TPU v7x, 128 devices: a whole 4x4x4 slice. The times are simulated.
128 devices in a mesh: batch: 32 (over z, y, core), rows: 4 (over x).
Axes of the slice: x: 4, y: 4, z: 4, core: 2. Of those that a mesh axis runs over, the one named last changes fastest.
Arguments:
- features: bfloat16 [768, 14, 14, 1024], P(('batch', 'rows')), may hold values from -12 to 12
- grads: bfloat16 [768, 14, 14, 256], P(('batch', 'rows')), may hold values from -12 to 12
- kernel: bfloat16 [3, 3, 256, 1024], replicated, may hold values from -0.125 to 0.125
- vectors: float32 [16, 64, 64], replicated, may hold values from -1 to 1, as said below
- values: float32 [16, 64], replicated, may hold values from 0.05 to 2
Outputs:
- input_grad: bfloat16 [768, 14, 14, 1024], P(('batch', 'rows'))
- kernel_grad: float32 [1024, 3, 3, 256], P(('batch', 'rows'))
Inputs may be any that keep to these rules, and one draw needn't show every extreme that they name: `vectors`: each group's matrix is orthogonal.
All inputs are finite; a program needn't handle non-finite values.
Results may differ from a plain program's by a relative error of at most 0.015.
Values sent between devices are 32-bit elements; how exact they have to be, the bound alone decides.
No kernel may reach another device: no remote copies, remote signals or barrier semaphores. Data moves between devices by JAX's collectives and lax.ppermute only.
A program may use at most 128 MiB of HBM per device.

v0:
```python
import functools

import jax
import jax.numpy as jnp
from jax import lax
from jax.sharding import Mesh
from jax.sharding import PartitionSpec as P

BATCH = ("batch_0", "batch_1", "batch_2")
BATCH_ROWS = ("batch_0", "batch_1", "batch_2", "rows")


def one_axis_at_a_time(value, axes):
    return functools.reduce(lax.psum, axes, value)


def block_matrix(blocks):
    groups, group_size = (blocks.shape[0], blocks.shape[1])
    identity = jnp.eye(groups, dtype=jnp.float32)
    full = jnp.einsum("gh,gij->gihj", identity, blocks)
    return full.reshape(groups * group_size, groups * group_size)


def diagonal_blocks(full, groups, group_size):
    shaped = full.reshape(groups, group_size, groups, group_size)
    index = jnp.arange(groups)
    return shaped[index, :, index, :]


def gather_columns(padded, slab_rows, columns_count):
    outputs = padded.shape[3]
    pieces = [
        padded[
            :,
            2 - shift_row : 2 - shift_row + slab_rows,
            2 - shift_col : 2 - shift_col + columns_count,
            :,
        ]
        for shift_row in range(3)
        for shift_col in range(3)
    ]
    return jnp.concatenate(pieces, axis=3).reshape(-1, 9 * outputs)


def local(features, grads, kernel, vectors, values):
    images_here, slab_rows, columns_count, channels = features.shape
    outputs = grads.shape[3]
    groups, group_size = values.shape
    pixels = images_here * slab_rows * columns_count
    device_count = lax.axis_size(BATCH) * lax.axis_size("rows")
    pixel_total = 1.0 * pixels * device_count
    flat = features.reshape(pixels, channels)
    feature_part = jnp.sum(flat, axis=0, dtype=jnp.float32)
    padded = jnp.pad(grads, ((0, 0), (1, 1), (1, 1), (0, 0)))
    columns = gather_columns(padded, slab_rows, columns_count)
    back_grad = jnp.dot(
        columns, kernel.reshape(9 * outputs, channels), preferred_element_type=jnp.float32
    )
    back_low = back_grad.astype(jnp.bfloat16)
    raw_full = lax.dot_general(
        flat, back_low, (((0,), (0,)), ((), ())), preferred_element_type=jnp.float32
    )
    raw_part = diagonal_blocks(raw_full, groups, group_size)
    back_part = jnp.sum(back_grad, axis=0)
    sum_feature = one_axis_at_a_time(feature_part, BATCH_ROWS)
    raw_cov, back_total = lax.psum((raw_part, back_part), BATCH_ROWS)
    channel_mean = sum_feature / pixel_total
    scales = lax.rsqrt(values)
    whiten = jnp.einsum("gij,gj,gkj->gik", vectors, scales, vectors)
    whiten_low = block_matrix(whiten).astype(jnp.bfloat16)
    centered_low = (flat - channel_mean).astype(jnp.bfloat16)
    whitened = jnp.dot(centered_low, whiten_low, preferred_element_type=jnp.float32).astype(
        jnp.bfloat16
    )
    per_device = channels // device_count
    weight_total = lax.psum(
        lax.dot_general(
            whitened, columns, (((0,), (0,)), ((), ())), preferred_element_type=jnp.float32
        ),
        BATCH_ROWS,
    )
    first_row = lax.axis_index(BATCH_ROWS) * per_device
    weight_share = lax.dynamic_slice_in_dim(weight_total, first_row, per_device, 0)
    cov_grad = (
        raw_cov
        - channel_mean.reshape(groups, group_size)[:, :, None]
        * back_total.reshape(groups, group_size)[:, None, :]
    )
    rotated = jnp.einsum("gki,gkl,glj->gij", vectors, cov_grad, vectors)
    symmetric = 0.5 * (rotated + jnp.swapaxes(rotated, 1, 2))
    roots = jnp.sqrt(values)
    factor = -(scales[:, :, None] * scales[:, None, :]) / (roots[:, :, None] + roots[:, None, :])
    sigma_grad = jnp.einsum("gik,gkl,gjl->gij", vectors, symmetric * factor, vectors)
    sigma_low = block_matrix(2.0 / pixel_total * sigma_grad).astype(jnp.bfloat16)
    stacked = jnp.concatenate([whiten_low, sigma_low], axis=0)
    shifted_low = (back_grad - back_total / pixel_total).astype(jnp.bfloat16)
    joined = jnp.concatenate([shifted_low, centered_low], axis=1)
    result = jnp.dot(joined, stacked, preferred_element_type=jnp.float32)
    input_grad = result.reshape(features.shape).astype(jnp.bfloat16)
    kernel_grad = weight_share.reshape(per_device, 3, 3, outputs)
    return (input_grad, kernel_grad)


def solution(mesh):
    finer = Mesh(
        mesh.devices.reshape(4, 4, 2, mesh.shape["rows"]), ("batch_0", "batch_1", "batch_2", "rows")
    )
    placed = (P(BATCH_ROWS, None, None, None), P(BATCH_ROWS, None, None, None), P(), P(), P())
    return jax.shard_map(
        local,
        mesh=finer,
        in_specs=placed,
        out_specs=(P(BATCH_ROWS, None, None, None), P(BATCH_ROWS, None, None, None)),
        check_vma=False,
    )
```

profile of v0, /device:TPU:0, one launch (start us, length us, event | category | flops | bytes accessed | tf_op | source)
XLA Modules:
  0.0 337.9 jit_solution(16871516216707155375)
XLA Ops:
  7.2 0.0 copy-start.1
  7.2 0.0 all-reduce.4.cloned.1.call-start
  7.2 4.9 %reshape.41 = bf16[1176,1024]{1,0:T(8,128)(2,1)} reshape(bf16[6,14,14,1024]{3,2,1,0:T(8,128)(2,1)} %param.5) | data formatting | bytes 4816896 | tf_op jit(solution)/shard_map/reshape | solution.py:52
  12.1 0.0 copy-done.1
  12.1 0.6 convert_reduce_fusion
  12.7 1.1 slice_dynamic-update-slice_fusion.7
  13.8 1.0 slice_dynamic-update-slice_fusion.6
  14.8 1.2 slice_dynamic-update-slice_fusion.5
  16.0 1.1 slice_dynamic-update-slice_fusion.4
  17.1 0.9 constant_dynamic-update-slice_fusion
  18.0 1.1 slice_dynamic-update-slice_fusion.3
  19.1 1.1 slice_dynamic-update-slice_fusion.2
  20.3 1.0 slice_dynamic-update-slice_fusion.1
  21.2 1.2 slice_dynamic-update-slice_fusion
  22.4 9.2 %reshape.39 = bf16[1176,2304]{1,0:T(8,128)(2,1)} reshape(bf16[6,14,14,2304]{3,2,1,0:T(8,128)(2,1)} %slice_dynamic-update-slice_fusion) | data formatting | bytes 10838016 | tf_op jit(solution)/shard_map/reshape | solution.py:42
  31.6 9.4 %fusion.63 = (f32[1024]{0:T(1024)S(1)}, f32[1176,1024]{1,0:T(8,128)S(1)}) fusion(bf16[1176,2304]{1,0:T(8,128)(2,1)} %reshape.39, bf16[2304,1024]{1,0:T(8,128)(2,1)} %bitcast.38), kind=kOutput, calls=%fused_computation.64 | convolution fusion | flops 5550267392 | bytes 14958592 | tf_op jit(solution)/shard_map/dot_general | solution.py:56
  41.0 2.2 copy-done.5
  43.2 4.4 %fusion.17 = f32[1024,1024]{0,1:T(8,128)} fusion(bf16[1176,1024]{1,0:T(8,128)(2,1)S(1)} %copy-done.2, f32[1176,1024]{1,0:T(8,128)S(1)} %get-tuple-element.7), kind=kOutput, calls=%fused_computation.21 | convolution fusion | flops 2467454976 | bytes 11419648 | tf_op jit(solution)/shard_map/dot_general | solution.py:60
  47.6 7.3 %reshape.42 = f32[16,64,16,64]{1,0,3,2:T(8,128)} reshape(f32[1024,1024]{0,1:T(8,128)} %fusion.17) | data formatting | bytes 8388608 | tf_op jit(solution)/shard_map/reshape | solution.py:25
  54.9 8.7 %copy.10 = f32[16,64,16,64]{3,1,2,0:T(8,128)} copy(f32[16,64,16,64]{1,0,3,2:T(8,128)} %reshape.42) | data formatting | bytes 8388608 | tf_op jit(solution)/shard_map/reshape | solution.py:25
  63.6 11.8 %psum.50 = f32[1024]{0:T(1024)S(1)} all-reduce(f32[1024]{0:T(1024)S(1)} %convert_reduce_fusion), channel_id=1, replica_groups=mesh['batch_0'=4,'batch_1'=4,'batch_2'=2,'rows'=4] {'batch_0'}, use_global_device_ids=true, to_apply=%region_3.4 | all-reduce | flops 1024 | bytes 8192 | tf_op jit(solution)/shard_map/psum | solution.py:14
  75.4 10.7 %psum.51 = f32[1024]{0:T(1024)S(1)} all-reduce(f32[1024]{0:T(1024)S(1)} %psum.50), channel_id=1, replica_groups=mesh['batch_0'=4,'batch_1'=4,'batch_2'=2,'rows'=4] {'batch_1'}, use_global_device_ids=true, to_apply=%region_4.5 | all-reduce | flops 1024 | bytes 8192 | tf_op jit(solution)/shard_map/psum | solution.py:14
  86.2 2.5 psum.52
  88.6 10.5 %psum.53 = f32[1024]{0:T(1024)S(1)} all-reduce(f32[1024]{0:T(1024)S(1)} %psum.52), channel_id=1, replica_groups=mesh['batch_0'=4,'batch_1'=4,'batch_2'=2,'rows'=4] {'rows'}, use_global_device_ids=true, to_apply=%region_6.7 | all-reduce | flops 1024 | bytes 8192 | tf_op jit(solution)/shard_map/psum | solution.py:14
  99.1 0.0 copy-start.4
  99.1 2.3 fusion
  101.4 3.5 %convert_element_type.69 = bf16[1176,1024]{1,0:T(8,128)(2,1)S(1)} reshape(bf16[6,14,14,1024]{3,2,1,0:T(8,128)(2,1)} %fusion) | data formatting | bytes 4816896 | tf_op jit(solution)/shard_map/convert_element_type | solution.py:71
  105.0 1.1 convolution_bitcast_fusion
  106.0 2.1 copy.9
  108.1 4.0 %fusion.5 = bf16[16,64,16,64]{3,2,1,0:T(8,128)(2,1)} fusion(f32[16,16]{1,0:T(8,128)S(1)} %fusion.58, f32[16,64,64]{2,1,0:T(8,128)} %copy.9), kind=kLoop, calls=%fused_computation.12 | loop fusion | flops 2097152 | bytes 2360320 | tf_op jit(solution)/shard_map/convert_element_type | solution.py:70
  112.1 6.5 %convert_element_type.61 = bf16[1024,1024]{1,0:T(8,128)(2,1)} reshape(bf16[16,64,16,64]{3,2,1,0:T(8,128)(2,1)} %fusion.5) | data formatting | bytes 4194304 | tf_op jit(solution)/shard_map/convert_element_type | solution.py:70
  118.6 4.8 %gather_fusion = f32[16,64,64]{2,1,0:T(8,128)} fusion(f32[16,64,16,64]{3,1,2,0:T(8,128)} %copy.10, s32[16]{0:T(128)S(1)} %or_bitcast_fusion), kind=kCustom, calls=%fused_computation | custom fusion | bytes 524416 | tf_op jit(solution)/shard_map/gather | solution.py:27
  123.4 15.0 %fusion.25 = f32[1024,2304]{1,0:T(8,128)} fusion(bf16[1176,2304]{1,0:T(8,128)(2,1)} %reshape.39, bf16[1176,1024]{1,0:T(8,128)(2,1)S(1)} %convert_element_type.69, bf16[1024,1024]{1,0:T(8,128)(2,1)} %convert_element_type.61), kind=kOutput, calls=%fused_computation.27 | convolution fusion | flops 8016519168 | bytes 19361792 | tf_op jit(solution)/shard_map/dot_general | solution.py:77
  138.4 0.0 all-reduce.4.cloned.1.call-update
  138.4 0.1 mul.53
  138.5 63.5 %psum.49 = f32[1024]{0:T(1024)S(1)} all-reduce(f32[1024]{0:T(1024)S(1)} %get-tuple-element.6), channel_id=1, replica_groups=mesh['batch_0'=4,'batch_1'=4,'batch_2'=2,'rows'=4] {'batch_0','batch_1',..., use_global_device_ids=true, to_apply=%region_1.2 | all-reduce | flops 1024 | bytes 8192 | tf_op jit(solution)/shard_map/psum | solution.py:66
  201.9 0.1 mul.55
  202.0 2.1 subtract_convert_fusion
  204.1 3.1 subtract_convert_fusion.1
  207.2 90.6 %all-reduce.4.cloned.1.call-done = (f32[16,64,64]{2,1,0:T(8,128)}, f32[1024,2304]{1,0:T(8,128)}) async-done(((f32[16,64,64]{2,1,0:T(8,128)}, f32[1024,2304]{1,0:T(8,128)}), (f32[16,64,64]{2,1,0:T(8,128)}, f32[1024,2304]{1,0:T(8,128)})) %all-reduce.4.cloned.1.call-update) | async-done | bytes 9699344 | tf_op jit(solution)/shard_map/psum | solution.py:66
  297.7 2.4 fusion.22
  300.1 2.0 copy.11
  302.2 2.7 convolution_multiply_fusion
  304.8 4.1 %fusion.6 = bf16[16,64,16,64]{3,2,1,0:T(8,128)(2,1)} fusion(f32[16,64,64]{2,1,0:T(8,128)} %convolution_multiply_fusion, f32[16,16]{1,0:T(8,128)S(1)} %fusion.58), kind=kLoop, calls=%fused_computation.13 | loop fusion | flops 2097152 | bytes 2360320 | tf_op jit(solution)/shard_map/convert_element_type | solution.py:94
  308.9 6.5 %convert_element_type.65 = bf16[1024,1024]{1,0:T(8,128)(2,1)} reshape(bf16[16,64,16,64]{3,2,1,0:T(8,128)(2,1)} %fusion.6) | data formatting | bytes 4194304 | tf_op jit(solution)/shard_map/convert_element_type | solution.py:94
  315.3 9.5 %fusion.10 = bf16[1176,1024]{1,0:T(8,128)(2,1)} fusion(bf16[1024,1024]{1,0:T(8,128)(2,1)} %convert_element_type.65, bf16[1024,1024]{1,0:T(8,128)(2,1)} %convert_element_type.61, bf16[1176,1024]{1,0:T(8,128)(2,1)} %subtract_convert_fusion, bf16[1176,1024]{1,0:T(8,128)(2,1)S(1)} %subtract_convert_fusion.1), kind=kOutput, calls=%fused_computation.17 | convolution fusion | flops 4951728128 | bytes 11419648 | tf_op jit(solution)/shard_map/dot_general | solution.py:98
  324.9 4.6 %convert_element_type.67 = bf16[6,14,14,1024]{3,2,1,0:T(8,128)(2,1)} reshape(bf16[1176,1024]{1,0:T(8,128)(2,1)} %fusion.10) | data formatting | bytes 4816896 | tf_op jit(solution)/shard_map/convert_element_type | solution.py:99
  329.5 1.5 constant_dynamic-slice_fusion
  (15 shorter events, 0.0 us)
Async XLA Ops:
  7.2 4.9 %copy-start.1 = (bf16[6,14,14,1024]{3,2,1,0:T(8,128)(2,1)S(1)}, bf16[6,14,14,1024]{3,2,1,0:T(8,128)(2,1)}, u32[]{:S(2)}) copy-start(bf16[6,14,14,1024]{3,2,1,0:T(8,128)(2,1)} %param.5) | copy-start | bytes 7225348
  7.2 5.5 %copy-start = (bf16[6,14,14,256]{3,2,1,0:T(8,128)(2,1)S(1)}, bf16[6,14,14,256]{3,2,1,0:T(8,128)(2,1)}, u32[]{:S(2)}) copy-start(bf16[6,14,14,256]{3,2,1,0:T(8,128)(2,1)} %param.6) | copy-start | bytes 1806340
  7.2 290.6 %all-reduce.4.cloned.1.call-start = ((), (), s32[]{:S(2)}) async-start(), calls=%async_computation | async-start | bytes 19922944 | tf_op jit(solution)/shard_map/psum | solution.py:66
  31.6 11.6 %copy-start.2 = (bf16[1176,1024]{1,0:T(8,128)(2,1)S(1)}, bf16[1176,1024]{1,0:T(8,128)(2,1)}, u32[]{:S(2)}) copy-start(bf16[1176,1024]{1,0:T(8,128)(2,1)} %reshape.41) | copy-start | bytes 7225348
  41.0 2.2 copy-start.5
  99.1 5.9 %copy-start.6 = (f32[16,64]{1,0:T(8,128)S(1)}, f32[16,64]{1,0:T(8,128)}, u32[]{:S(2)}) copy-start(f32[16,64]{1,0:T(8,128)} %param.9) | copy-start | bytes 12292
  99.1 5.9 %copy-start.4 = (f32[16,64,64]{2,1,0:T(8,128)S(1)}, f32[16,64,64]{2,1,0:T(8,128)}, u32[]{:S(2)}) copy-start(f32[16,64,64]{2,1,0:T(8,128)} %param.8) | copy-start | bytes 786436
  138.4 63.6 %copy-start.3 = (bf16[1176,1024]{1,0:T(8,128)(2,1)S(1)}, bf16[1176,1024]{1,0:T(8,128)(2,1)}, u32[]{:S(2)}) copy-start(bf16[1176,1024]{1,0:T(8,128)(2,1)} %reshape.41) | copy-start | bytes 7225348
Sparse Core Ops, SparseCore 0:
  138.5 159.1 all-reduce.3
where the time goes:
time: 340 us; the launch traced here: 338 us
  blocking collectives  99 us (29%)
  waiting for transfers between devices  90.6 us (27%)
  local copies, waits for them, and re-layouts  73.6 us (22%)
  matrix products  44.4 us (13%)
  other arithmetic  16.1 us (5%)
  between operations  14.1 us (4%)
    psum x1, waiting for transfers between devices, local(): raw_cov, back_total = lax.psum((raw_part, back_part), BATCH_ROWS)  90.6 us
    psum x1, blocking collectives, local(): raw_cov, back_total = lax.psum((raw_part, back_part), BATCH_ROWS)  63.5 us
    psum x4, blocking collectives, one_axis_at_a_time(): return functools.reduce(lax.psum, axes, value)  35.5 us
    reshape x2, local copies, waits for them, and re-layouts, diagonal_blocks(): shaped = full.reshape(groups, group_size, groups, group_size)  16 us
    dot_general x1, matrix products, local(): lax.dot_general(whitened, columns, (((0,), (0,)), ((), ())), preferred_el...  15 us
    unnamed x22, local copies, waits for them, and re-layouts  10.7 us
    dot_general x1, matrix products, local(): result = jnp.dot(joined, stacked, preferred_element_type=jnp.float32)  9.55 us
    dot_general x1, matrix products, local(): jnp.dot(columns, kernel.reshape(9 * outputs, channels), preferred_element...  9.36 us
  transfers between devices with their start and end apart: 1, of which 1 were waited for; matrix products, arithmetic and copies ran while one was open for 2% of the time, Pallas kernels for 0%

commit v1 on v0

v1 whole, which is shorter than its diff:
```python
import jax
import jax.numpy as jnp
import numpy as np
from jax import lax
from jax.experimental import pallas as pl
from jax.experimental.pallas import tpu as pltpu
from jax.sharding import Mesh
from jax.sharding import PartitionSpec as P

ALL = ("z", "y", "c", "x")
SIZE = {"z": 4, "y": 4, "c": 2, "x": 4}
STRIDE = {"z": 32, "y": 8, "c": 4, "x": 1}
RING = ((0, 3, 1, 2), (0, 1, 3, 2))
F32 = jnp.float32
BF16 = jnp.bfloat16
HIGHEST = lax.Precision.HIGHEST
IMAGES, H, W, D, O = 6, 14, 14, 1024, 256
ROWS = IMAGES * H * 16
PIXELS = IMAGES * H * W
TOTAL = 128.0 * PIXELS
VMEM_LIMIT = 60 << 20


def nt(a, b, precision=None):
    return lax.dot_general(
        a, b, (((1,), (1,)), ((), ())), precision=precision, preferred_element_type=F32
    )


def tn(a, b, precision=None):
    return lax.dot_general(
        a, b, (((0,), (0,)), ((), ())), precision=precision, preferred_element_type=F32
    )


def nn(a, b, precision=None):
    return lax.dot_general(
        a, b, (((1,), (0,)), ((), ())), precision=precision, preferred_element_type=F32
    )


def same_group(shape):
    row = lax.broadcasted_iota(jnp.int32, shape, 0)
    col = lax.broadcasted_iota(jnp.int32, shape, 1)
    return lax.div(row, 64) == lax.div(col, 64)


def block_vectors(vectors_ref, z):
    four = vectors_ref[4 * z : 4 * z + 4].reshape(256, 64)
    wide = jnp.concatenate([four, four, four, four], axis=1)
    return jnp.where(same_group((256, 256)), wide, 0.0)


def as_column(row):
    return jnp.broadcast_to(row, (256, 256)).T


def prep_kernel(
    features, grads, vectors, values, cols, xc, wht, u, sums, whiten, wide, wp32
):
    for z in range(4):
        basis = block_vectors(vectors, z)
        scale = lax.rsqrt(values[0:1, 256 * z : 256 * z + 256])
        full = nt(basis * scale, basis, HIGHEST)
        whiten[z] = full.astype(BF16)
        for c in range(2):
            spot = RING[c].index(z)
            for row, (y, x) in enumerate((y, x) for y in RING[c] for x in RING[c]):
                channel = y * 64 + c * 32 + x * 8
                wp32[4 * c + spot, row * 8 : row * 8 + 8, :] = full[channel : channel + 8, :]
    wide[...] = jnp.zeros_like(wide)
    inside = lax.broadcasted_iota(jnp.int32, (H, 16, O), 1) < W
    for b in range(IMAGES):
        wide[:, 8 : 8 + W, :] = grads[b].astype(F32)
        for c in range(3):
            shifted = wide[:, 9 - c : 25 - c, :]
            if c == 2:
                shifted = jnp.where(inside, shifted, 0.0)
            shifted = shifted.astype(BF16)
            for a in range(3):
                lane = (3 * a + c) * O
                first, last = b * H + max(0, a - 1), b * H + H - max(0, 1 - a)
                start = max(0, 1 - a)
                cols[first:last, :, lane : lane + O] = shifted[start : start + last - first]
                if a == 0:
                    cols[b * H + H - 1, :, lane : lane + O] = jnp.zeros((16, O), BF16)
                if a == 2:
                    cols[b * H, :, lane : lane + O] = jnp.zeros((16, O), BF16)
    total = jnp.zeros((1, D), F32)
    for b in range(IMAGES):
        total = total + jnp.sum(
            jnp.sum(features[b].astype(F32), axis=0), axis=0, keepdims=True
        )
    sums[...] = total
    mean = total * (1.0 / PIXELS)
    xc[...] = jnp.zeros_like(xc)
    for b in range(IMAGES):
        xc[b * H : b * H + H, 0:W, :] = (features[b].astype(F32) - mean[None]).astype(BF16)
    high = mean.astype(BF16)
    rest = mean - high.astype(F32)
    middle = rest.astype(BF16)
    low = (rest - middle.astype(F32)).astype(BF16)
    pad = lax.broadcasted_iota(jnp.int32, (16, D), 0)
    head = xc[0].astype(F32)
    head = jnp.where(pad == 14, high.astype(F32), jnp.where(pad == 15, middle.astype(F32), head))
    xc[0] = head.astype(BF16)
    head = xc[1].astype(F32)
    xc[1] = jnp.where(pad == 14, low.astype(F32), head).astype(BF16)
    for k in range(8):
        c, spot = k // 4, k % 4
        z = RING[c][spot]
        chunk = xc[:, :, 256 * z : 256 * z + 256].reshape(ROWS, 256)
        part = nt(wp32[k].astype(BF16), chunk)
        wht[128 * k : 128 * k + 128, :] = part.astype(BF16)
        shift = part[:, 14:15] + part[:, 15:16] + part[:, 30:31]
        u[128 * k : 128 * k + 128, :] = jnp.broadcast_to(shift, (128, 128))
    wht[1024:1040, :] = jnp.ones((16, ROWS), BF16)


def prep(features, grads, vectors, values):
    return pl.pallas_call(
        prep_kernel,
        out_shape=(
            jax.ShapeDtypeStruct((IMAGES * H, 16, 9 * O), BF16),
            jax.ShapeDtypeStruct((IMAGES * H, 16, D), BF16),
            jax.ShapeDtypeStruct((1040, ROWS), BF16),
            jax.ShapeDtypeStruct((1024, 128), F32),
            jax.ShapeDtypeStruct((1, D), F32),
            jax.ShapeDtypeStruct((4, 256, 256), BF16),
        ),
        scratch_shapes=[pltpu.VMEM((H, 32, O), F32), pltpu.VMEM((8, 128, 256), F32)],
        compiler_params=pltpu.CompilerParams(vmem_limit_bytes=VMEM_LIMIT),
        name="prep",
    )(features, grads, vectors, values)


def weight_kernel(wht, cols, u, out, colsum):
    full = nn(wht[...], cols[...])
    ones = full[1024:1032, :]
    colsum[...] = ones
    for k in range(6):
        lanes = slice(128 * k, 128 * k + 128)
        out[:, lanes] = full[0:1024, lanes] + u[...] * ones[0:1, lanes]


def weight_part(wht, cols, u, a):
    return pl.pallas_call(
        weight_kernel,
        grid=(1,),
        in_specs=[
            pl.BlockSpec((1040, ROWS), lambda i: (0, 0)),
            pl.BlockSpec((ROWS, 768), lambda i: (0, a)),
            pl.BlockSpec((1024, 128), lambda i: (0, 0)),
        ],
        out_specs=(
            pl.BlockSpec((1024, 768), lambda i: (0, 0)),
            pl.BlockSpec((8, 768), lambda i: (0, 0)),
        ),
        out_shape=(
            jax.ShapeDtypeStruct((1024, 768), F32),
            jax.ShapeDtypeStruct((8, 768), F32),
        ),
        compiler_params=pltpu.CompilerParams(vmem_limit_bytes=VMEM_LIMIT),
        name="weight_part",
    )(wht, cols, u)


def back_kernel(cols, kernel, xc, sums, sum0, sum1, sum2, dev, payload):
    z = pl.program_id(0)
    back = nn(cols[...], kernel[...])
    total = jnp.sum(back, axis=0, keepdims=True)
    real = lax.rem(lax.broadcasted_iota(jnp.int32, (ROWS, 256), 0), 16) < W
    low = jnp.where(real, back - total * (1.0 / PIXELS), 0.0).astype(BF16)
    dev[...] = low
    cov = tn(xc[...], low) + as_column(sums[...] * (1.0 / PIXELS)) * total
    group = lax.div(lax.broadcasted_iota(jnp.int32, (64, 256), 1), 64)
    packed = cov[0:64]
    for k in range(1, 4):
        packed = jnp.where(group == k, cov[64 * k : 64 * k + 64], packed)
    payload[0:64, :] = packed
    row = lax.broadcasted_iota(jnp.int32, (8, 256), 0)
    tail = jnp.where(row == 0, total, jnp.where(row == 1, sums[...], 0.0))
    for a, part in enumerate((sum0, sum1, sum2)):
        tail = jnp.where((row == 2 + a) & (z < 3), part[0:1, :], tail)
    payload[64:72, :] = tail


def back_part(cols, kernel, xc, sums, parts):
    last = lambda z: (0, jnp.minimum(z, 2))
    column = lambda z: (0, z)
    return pl.pallas_call(
        back_kernel,
        grid=(4,),
        in_specs=[
            pl.BlockSpec((ROWS, 9 * O), lambda z: (0, 0)),
            pl.BlockSpec((9 * O, 256), column),
            pl.BlockSpec((ROWS, 256), column),
            pl.BlockSpec((1, 256), column),
            pl.BlockSpec((8, 256), last),
            pl.BlockSpec((8, 256), last),
            pl.BlockSpec((8, 256), last),
        ],
        out_specs=(pl.BlockSpec((ROWS, 256), column), pl.BlockSpec((72, 256), column)),
        out_shape=(
            jax.ShapeDtypeStruct((ROWS, D), BF16),
            jax.ShapeDtypeStruct((72, D), F32),
        ),
        compiler_params=pltpu.CompilerParams(vmem_limit_bytes=VMEM_LIMIT),
        name="back_part",
    )(cols, kernel, xc, sums, *parts)


def final_kernel(
    dev, xc, payload, own, vectors, values, whiten, out, shift, sigma, row_vector
):
    @pl.when(pl.program_id(0) == 0)
    def _():
        for z in range(4):
            lanes = slice(256 * z, 256 * z + 256)
            basis = block_vectors(vectors, z)
            total = payload[64:65, lanes]
            mean = payload[65:66, lanes] * (1.0 / TOTAL)
            same = same_group((256, 256))
            stack = payload[0:64, lanes]
            raw = jnp.concatenate([stack, stack, stack, stack], axis=0)
            cov = jnp.where(same, raw - as_column(mean) * total, 0.0)
            rotated = nn(tn(basis, cov, HIGHEST), basis, HIGHEST)
            symmetric = 0.5 * (rotated + rotated.T)
            value = values[0:1, lanes]
            scale, root = lax.rsqrt(value), jnp.sqrt(value)
            factor = -(as_column(scale) * scale) / (as_column(root) + root)
            inner = jnp.where(same, symmetric * factor, 0.0)
            grad = nt(nn(basis, inner, HIGHEST), basis, HIGHEST)
            low = (grad * (2.0 / TOTAL)).astype(BF16)
            sigma[z] = low
            whiten_z = whiten[z].astype(F32)
            own_total, own_mean = own[64:65, lanes], own[65:66, lanes] * (1.0 / PIXELS)
            eight = lambda row: jnp.broadcast_to(row, (8, 256))
            row_vector[0:8, lanes] = nn(
                eight(own_total * (1.0 / PIXELS) - total * (1.0 / TOTAL)), whiten_z, HIGHEST
            ) + nn(eight(own_mean - mean), low.astype(F32), HIGHEST)
            shift[0:8, lanes] = nn(eight(mean), whiten_z, HIGHEST)

    for z in range(4):
        lanes = slice(256 * z, 256 * z + 256)
        result = nn(dev[:, lanes], whiten[z]) + nn(xc[:, lanes], sigma[z])
        result = result + row_vector[0:1, lanes]
        out[0, :, :, lanes] = result.astype(BF16).reshape(H, 16, 256)[:, 0:W, :]


def final_part(dev, xc, payload, own, vectors, values, whiten):
    return pl.pallas_call(
        final_kernel,
        grid=(IMAGES,),
        in_specs=[
            pl.BlockSpec((H * 16, D), lambda b: (b, 0)),
            pl.BlockSpec((H * 16, D), lambda b: (b, 0)),
            pl.BlockSpec((72, D), lambda b: (0, 0)),
            pl.BlockSpec((72, D), lambda b: (0, 0)),
            pl.BlockSpec((16, 64, 64), lambda b: (0, 0, 0)),
            pl.BlockSpec((1, D), lambda b: (0, 0)),
            pl.BlockSpec((4, 256, 256), lambda b: (0, 0, 0)),
        ],
        out_specs=(
            pl.BlockSpec((1, H, W, D), lambda b: (b, 0, 0, 0)),
            pl.BlockSpec((8, D), lambda b: (0, 0)),
        ),
        out_shape=(
            jax.ShapeDtypeStruct((IMAGES, H, W, D), BF16),
            jax.ShapeDtypeStruct((8, D), F32),
        ),
        scratch_shapes=[pltpu.VMEM((4, 256, 256), BF16), pltpu.VMEM((8, D), F32)],
        compiler_params=pltpu.CompilerParams(vmem_limit_bytes=VMEM_LIMIT),
        name="final_part",
    )(dev, xc, payload, own, vectors, values, whiten)


def permutation(move):
    pairs = []
    for device in range(128):
        at = {k: (device // STRIDE[k]) % SIZE[k] for k in ALL}
        move(at)
        pairs.append((device, sum(at[k] * STRIDE[k] for k in ALL)))
    return pairs


def exchange(value, move):
    return lax.ppermute(value, ALL, permutation(move))


def other_core(at):
    at["c"] ^= 1


def ring(axis, step):
    def move(at):
        at[axis] ^= (1, 3)[(step + at["c"]) % 2]

    return move


def split(value, dim, bit):
    keep = lax.dynamic_index_in_dim(value, bit, dim, keepdims=False)
    send = lax.dynamic_index_in_dim(value, 1 - bit, dim, keepdims=False)
    return keep, send


def local(features, grads, kernel, vectors, values):
    core = lax.axis_index("c")
    bits = {}
    for axis in "xyz":
        i = lax.axis_index(axis)
        a, b = (i ^ (i >> 1)) & 1, i >> 1
        bits[axis] = (jnp.where(core == 0, a, b), jnp.where(core == 0, b, a))
    flat_values = values.reshape(1, D)
    cols, xc, wht, u, sums, whiten = prep(features, grads, vectors, flat_values)
    cols, xc = cols.reshape(ROWS, 9 * O), xc.reshape(ROWS, D)

    parts, colsums = [], []
    for a in range(3):
        part, colsum = weight_part(wht, cols, u, a)
        colsums.append(colsum)
        keep, send = split(part.reshape(2, 512, 768), 0, core)
        parts.append((keep + exchange(send, other_core)).reshape(2, 2, 2, 2, 2, 2, 8, 768))
    dev, own = back_part(cols, kernel.reshape(9 * O, D), xc, sums, colsums)

    low, high = own[:, :512], own[:, 512:]
    mine = jnp.where(core == 0, low, high) + exchange(
        jnp.where(core == 0, high, low), other_core
    )
    for axis in "xyz":
        for step in range(2):
            mine = mine + exchange(mine, ring(axis, step))
    theirs = exchange(mine, other_core)
    payload = jnp.concatenate(
        [jnp.where(core == 0, mine, theirs), jnp.where(core == 0, theirs, mine)], axis=1
    )

    names = [["z1", "z2", "y1", "y2", "x1", "x2"] for _ in range(3)]
    for turn in range(3):
        parts = list(lax.optimization_barrier(tuple(parts)))
        for a in range(3):
            axis = "xyz"[(a + turn) % 3]
            dim = names[a].index(axis + "1")
            names[a].pop(dim)
            keep, send = split(parts[a], dim, bits[axis][0])
            parts[a] = keep + exchange(send, ring(axis, 0))
    share = jnp.stack(parts, axis=3)
    order = ["z", "y", "x"]
    for axis in "xyz":
        dim = order.index(axis)
        order.pop(dim)
        keep, send = split(share, dim, bits[axis][1])
        share = keep + exchange(send, ring(axis, 1))

    input_grad, shift = final_part(dev, xc, payload, own, vectors, flat_values, whiten)
    me = lax.axis_index(ALL)
    mine8 = lax.dynamic_slice(shift, (0, me * 8), (1, 8)).reshape(1, 8, 1)
    share = share - mine8 * payload[66:69, None, :768]
    kernel_grad = share.transpose(1, 0, 2).reshape(8, 3, 3, O)
    return input_grad, kernel_grad


def solution(mesh):
    finer = Mesh(mesh.devices.reshape(4, 4, 2, 4), ALL)
    split_all = P(ALL, None, None, None)
    return jax.shard_map(
        local,
        mesh=finer,
        in_specs=(split_all, split_all, P(), P(), P()),
        out_specs=(split_all, split_all),
        check_vma=False,
    )
```

time: 340 us -> 163 us (0.48)
  blocking collectives: 99 us -> 0 us
  Pallas kernels: 0 us -> 63.8 us
  local copies, waits for them, and re-layouts: 73.6 us -> 14.9 us
  waiting for transfers between devices: 90.6 us -> 36.6 us
  matrix products: 44.4 us -> 0 us
  starting transfers between devices: 0.04 us -> 28.9 us
  between operations: 14.1 us -> 0.95 us
    psum x5 -> x0, blocking collectives: 99 us -> none  [the longest x1 63.5 us: local(): raw_cov, back_total = lax.psum((raw_part, back_part), BATCH_ROWS)]
    psum x1 -> x0, waiting for transfers between devices: 90.6 us -> none  [local(): raw_cov, back_total = lax.psum((raw_part, back_part), BATCH_ROWS)]
    pallas_call x0 -> x6, Pallas kernels: none -> 63.8 us  [the longest x3 22 us: weight_part(): pl.pallas_call(weight_kernel, grid=(1,), in_specs=[pl.BlockSpec((1040, RO...]
    dot_general x7 -> x0, matrix products: 44.4 us -> none  [the longest x1 15 us: local(): lax.dot_general(whitened, columns, (((0,), (0,)), ((), ())), preferred_el...]
    ppermute x0 -> x23, waiting for transfers between devices: none -> 36.6 us  [exchange(): return lax.ppermute(value, ALL, permutation(move))]
    ppermute x0 -> x23, starting transfers between devices: none -> 28.9 us  [exchange(): return lax.ppermute(value, ALL, permutation(move))]
    reshape x4 -> x1, local copies, waits for them, and re-layouts: 30.1 us -> 1.36 us  [local(): flat_values = values.reshape(1, D)]
    convert_element_type x4 -> x0, local copies, waits for them, and re-layouts: 21.1 us -> none  [the longest x1 6.52 us: local(): whiten_low = block_matrix(whiten).astype(jnp.bfloat16)]
  transfers between devices with their start and end apart: 1 -> 23, of which waited for: 1 -> 12; matrix products, arithmetic and copies ran while one was open for 2% -> 17% of each run, Pallas kernels for 0% -> 29%
where the time goes in v1:
time: 163 us; the launch traced here: 162 us
  Pallas kernels  63.8 us (39%)
  waiting for transfers between devices  36.6 us (22%)
  starting transfers between devices  28.9 us (18%)
  other arithmetic  16.8 us (10%)
  local copies, waits for them, and re-layouts  14.9 us (9%)
    ppermute x23, waiting for transfers between devices, exchange(): return lax.ppermute(value, ALL, permutation(move))  36.6 us
    ppermute x23, starting transfers between devices, exchange(): return lax.ppermute(value, ALL, permutation(move))  28.9 us
    pallas_call x3, Pallas kernels, weight_part(): pl.pallas_call(weight_kernel, grid=(1,), in_specs=[pl.BlockSpec((1040, RO...  22 us
    pallas_call x1, Pallas kernels, final_part(): pl.pallas_call(final_kernel, grid=(IMAGES,), in_specs=[pl.BlockSpec((H *...  16.1 us
    pallas_call x1, Pallas kernels, back_part(): pl.pallas_call(back_kernel, grid=(4,), in_specs=[pl.BlockSpec((ROWS, 9 *...  16 us
    squeeze x15, local copies, waits for them, and re-layouts, split(): send = lax.dynamic_index_in_dim(value, 1 - bit, dim, keepdims=False)  11.9 us
    pallas_call x1, Pallas kernels, prep(): pl.pallas_call(prep_kernel, out_shape=(jax.ShapeDtypeStruct((IMAGES * H,...  9.58 us
    add x3, other arithmetic, local(): keep + exchange(send, other_core)  6.11 us
  transfers between devices with their start and end apart: 23, of which 12 were waited for; matrix products, arithmetic and copies ran while one was open for 17% of the time, Pallas kernels for 29%

profile of v1, /device:TPU:0, one launch (start us, length us, event | category | flops | bytes accessed | tf_op | source)
XLA Modules:
  0.0 161.9 jit_solution(8516139629713929574)
XLA Ops:
  0.6 1.4 reshape.40.values
  2.0 9.6 %prep.1 = (bf16[84,16,2304]{2,1,0:T(8,128)(2,1)}, bf16[84,16,1024]{2,1,0:T(8,128)(2,1)}, bf16[1040,1344]{1,0:T(8,128)(2,1)}, f32[1024,128]{1,0:T(8,128)}, f32[1,...) custom-call(bf16[6,14,14,1024]{3,2,1,0:T(8,128)(2,1)} %features.1, bf16[6,14,14,256]{3,2,1,0:T(8,128)(2,1)} %grads.1, ...), custom_call_target="tpu_custom_call" | custom-call | tf_op jit(solution)/shard_map/prep/pallas_call | solution.py:121
  11.6 7.3 %weight_part.5 = (f32[1024,768]{1,0:T(8,128)}, f32[8,768]{1,0:T(8,128)}) custom-call(bf16[1040,1344]{1,0:T(8,128)(2,1)} %get-tuple-element.30.wht, bf16[1344,2304]{1,0:T(8,128)(2,1)} %bitcast.88, f32[1024,128]{1,0:T(8,128)} %get-tuple-element.31.u), custom_call_target="tpu_custom_call" | custom-call | tf_op jit(solution)/shard_map/weight_part/pallas_call | solution.py:147
  18.9 1.5 dynamic-slice_bitcast_fusion
  20.5 7.4 %weight_part.4 = (f32[1024,768]{1,0:T(8,128)}, f32[8,768]{1,0:T(8,128)}) custom-call(bf16[1040,1344]{1,0:T(8,128)(2,1)} %get-tuple-element.30.wht, bf16[1344,2304]{1,0:T(8,128)(2,1)} %bitcast.89, f32[1024,128]{1,0:T(8,128)} %get-tuple-element.31.u), custom_call_target="tpu_custom_call" | custom-call | tf_op jit(solution)/shard_map/weight_part/pallas_call | solution.py:147
  27.9 2.7 %dynamic-slice_bitcast_fusion.1 = f32[512,768]{1,0:T(8,128)} fusion(f32[2,512,768]{2,1,0:T(8,128)} %bitcast.103, s32[]{:T(128)S(6)} %select_n.119), kind=kLoop, calls=%fused_computation.4 | loop fusion | bytes 3145732 | tf_op jit(solution)/shard_map/jit(dynamic_index_in_dim)/squeeze | solution.py:304
  31.0 7.3 %weight_part.3 = (f32[1024,768]{1,0:T(8,128)}, f32[8,768]{1,0:T(8,128)}) custom-call(bf16[1040,1344]{1,0:T(8,128)(2,1)} %get-tuple-element.30.wht, bf16[1344,2304]{1,0:T(8,128)(2,1)} %bitcast.90, f32[1024,128]{1,0:T(8,128)} %get-tuple-element.31.u), custom_call_target="tpu_custom_call" | custom-call | tf_op jit(solution)/shard_map/weight_part/pallas_call | solution.py:147
  38.3 2.7 %dynamic-slice_bitcast_fusion.2 = f32[512,768]{1,0:T(8,128)} fusion(f32[2,512,768]{2,1,0:T(8,128)} %bitcast.105, s32[]{:T(128)S(6)} %select_n.119), kind=kLoop, calls=%fused_computation.5 | loop fusion | bytes 3145732 | tf_op jit(solution)/shard_map/jit(dynamic_index_in_dim)/squeeze | solution.py:304
  41.0 16.0 %back_part.1 = (bf16[1344,1024]{1,0:T(8,128)(2,1)}, f32[72,1024]{1,0:T(8,128)}) custom-call(bf16[1344,2304]{1,0:T(8,128)(2,1)} %bitcast.91, bf16[2304,1024]{1,0:T(8,128)(2,1)} %bitcast.100, bf16[1344,1024]{1,0:T(8,128)(2,1)} %bitcast.92, f32[1,1024]{1,0:T(1,128)} %get-tuple-element.29.sums, f32[8,768]{1,0:T(8,128)} %get-tuple-element.32.sum0, ...), custom_call_target="tpu_custom_call" | custom-call | tf_op jit(solution)/shard_map/back_part/pallas_call | solution.py:191
  57.1 1.0 slice_select_fusion
  58.6 1.0 collective-permute-done
  59.6 1.0 select_add_fusion
  60.7 1.7 %collective-permute-start.1 = (f32[72,512]{1,0:T(8,128)S(1)}, f32[72,512]{1,0:T(8,128)}, u32[]{:S(2)}, u32[]{:S(2)}) collective-permute-start(f32[72,512]{1,0:T(8,128)S(1)} %select_add_fusion), channel_id=1, source_target_pairs={{0,1},{1,0},{2,3},{3,2},{4,7},{5,6},{6,5},{7,4},{8,9},{9,8},{10,11... | collective-permute-start | bytes 442376 | tf_op jit(solution)/shard_map/ppermute | solution.py:288
  62.3 1.6 bitcast_add_fusion
  64.0 1.8 %bitcast_add_fusion.1 = f32[512,768]{1,0:T(8,128)S(1)} fusion(f32[512,768]{1,0:T(8,128)} %collective-permute-done.9, f32[2,512,768]{2,1,0:T(8,128)S(1)} %bitcast.104, s32[]{:T(128)S(6)} %select_n.118), kind=kLoop, calls=%fused_computation.1 | loop fusion | flops 393216 | bytes 4718596 | tf_op jit(solution)/shard_map/add | solution.py:324
  66.3 2.8 %bitcast_add_fusion.2 = f32[512,768]{1,0:T(8,128)} fusion(f32[512,768]{1,0:T(8,128)} %collective-permute-done.8, f32[2,512,768]{2,1,0:T(8,128)S(1)} %bitcast.106, s32[]{:T(128)S(6)} %select_n.118), kind=kLoop, calls=%fused_computation.2 | loop fusion | flops 393216 | bytes 4718596 | tf_op jit(solution)/shard_map/add | solution.py:324
  69.0 0.9 dynamic-slice_bitcast_fusion.3
  70.0 1.9 %collective-permute-start.13 = (f32[2,2,2,2,2,8,768]{6,5,4,3,2,1,0:T(8,128)}, f32[2,2,2,2,2,8,768]{6,5,4,3,2,1,0:T(8,128)}, u32[]{:S(2)}, u32[]{:S(2)}) collective-permute-start(f32[2,2,2,2,2,8,768]{6,5,4,3,2,1,0:T(8,128)} %dynamic-slice_bitcast_fusion.3), channel_id=1, source_target_pairs={{0,32},{1,33},{2,34},{3,35},{4,100},{5,101},{6,102},{7,103},{8,40}... | collective-permute-start | bytes 2359304 | tf_op jit(solution)/shard_map/ppermute | solution.py:288
  71.9 0.9 add.157
  72.8 2.2 %collective-permute-start.2 = (f32[72,512]{1,0:T(8,128)S(1)}, f32[72,512]{1,0:T(8,128)S(1)}, u32[]{:S(2)}, u32[]{:S(2)}) collective-permute-start(f32[72,512]{1,0:T(8,128)S(1)} %add.157), channel_id=1, source_target_pairs={{0,3},{1,2},{2,1},{3,0},{4,5},{5,4},{6,7},{7,6},{8,11},{9,10},{10,... | collective-permute-start | bytes 442376 | tf_op jit(solution)/shard_map/ppermute | solution.py:288
  75.1 1.0 dynamic-slice_bitcast_fusion.4
  76.1 1.6 collective-permute-start.12
  77.7 1.6 collective-permute-done.2
  79.3 1.7 %collective-permute-start.3 = (f32[72,512]{1,0:T(8,128)S(1)}, f32[72,512]{1,0:T(8,128)S(1)}, u32[]{:S(2)}, u32[]{:S(2)}) collective-permute-start(f32[72,512]{1,0:T(8,128)S(1)} %add.158), channel_id=1, source_target_pairs={{0,8},{1,9},{2,10},{3,11},{4,28},{5,29},{6,30},{7,31},{8,0},{9,1},... | collective-permute-start | bytes 442376 | tf_op jit(solution)/shard_map/ppermute | solution.py:288
  81.0 2.1 %dynamic-slice_bitcast_fusion.5 = f32[2,2,2,2,2,8,768]{6,5,4,3,2,1,0:T(8,128)} fusion(f32[2,2,2,2,2,2,8,768]{7,6,5,4,3,2,1,0:T(8,128)} %bitcast.98, s32[]{:T(128)S(6)} %select_n.122), kind=kLoop, calls=%fused_computation.11 | loop fusion | bytes 1572868 | tf_op jit(solution)/shard_map/jit(dynamic_index_in_dim)/squeeze | solution.py:304
  83.1 6.8 %collective-permute-done.3 = f32[72,512]{1,0:T(8,128)S(1)} collective-permute-done((f32[72,512]{1,0:T(8,128)S(1)}, f32[72,512]{1,0:T(8,128)S(1)}, u32[]{:S(2)}, u32[]{:S(2)}) %collective-permute-start.3) | collective-permute-done | bytes 147488 | tf_op jit(solution)/shard_map/ppermute | solution.py:288
  89.9 3.1 %collective-permute-start.4 = (f32[72,512]{1,0:T(8,128)S(1)}, f32[72,512]{1,0:T(8,128)S(1)}, u32[]{:S(2)}, u32[]{:S(2)}) collective-permute-start(f32[72,512]{1,0:T(8,128)S(1)} %add.159), channel_id=1, source_target_pairs={{0,24},{1,25},{2,26},{3,27},{4,12},{5,13},{6,14},{7,15},{8,16},{9,... | collective-permute-start | bytes 442376 | tf_op jit(solution)/shard_map/ppermute | solution.py:288
  93.0 3.3 %collective-permute-done.4 = f32[72,512]{1,0:T(8,128)S(1)} collective-permute-done((f32[72,512]{1,0:T(8,128)S(1)}, f32[72,512]{1,0:T(8,128)S(1)}, u32[]{:S(2)}, u32[]{:S(2)}) %collective-permute-start.4) | collective-permute-done | bytes 147488 | tf_op jit(solution)/shard_map/ppermute | solution.py:288
  96.6 1.2 bitcast_add_fusion.3
  97.8 1.5 bitcast_add_fusion.4
  99.7 1.2 bitcast_add_fusion.5
  101.7 4.1 %collective-permute-start.6 = (f32[72,512]{1,0:T(8,128)S(1)}, f32[72,512]{1,0:T(8,128)}, u32[]{:S(2)}, u32[]{:S(2)}) collective-permute-start(f32[72,512]{1,0:T(8,128)S(1)} %add.161), channel_id=1, source_target_pairs={{0,96},{1,97},{2,98},{3,99},{4,36},{5,37},{6,38},{7,39},{8,104},{9... | collective-permute-start | bytes 442376 | tf_op jit(solution)/shard_map/ppermute | solution.py:288
  105.8 0.8 dynamic-slice_bitcast_fusion.7
  106.6 4.0 %collective-permute-done.6 = f32[72,512]{1,0:T(8,128)} collective-permute-done((f32[72,512]{1,0:T(8,128)S(1)}, f32[72,512]{1,0:T(8,128)}, u32[]{:S(2)}, u32[]{:S(2)}) %collective-permute-start.6) | collective-permute-done | bytes 147488 | tf_op jit(solution)/shard_map/ppermute | solution.py:288
  110.6 0.9 add.162
  112.2 2.5 %collective-permute-done.15 = f32[2,2,2,2,8,768]{5,4,3,2,1,0:T(8,128)} collective-permute-done((f32[2,2,2,2,8,768]{5,4,3,2,1,0:T(8,128)}, f32[2,2,2,2,8,768]{5,4,3,2,1,0:T(8,128)}, u32[]{:S(2)}, u32[]{:S(2)}) %collective-permute-start.15) | collective-permute-done | bytes 393248 | tf_op jit(solution)/shard_map/ppermute | solution.py:288
  114.7 1.0 bitcast_add_fusion.7
  115.7 3.8 %collective-permute-done.14 = f32[2,2,2,2,8,768]{5,4,3,2,1,0:T(8,128)S(1)} collective-permute-done((f32[2,2,2,2,8,768]{5,4,3,2,1,0:T(8,128)S(1)}, f32[2,2,2,2,8,768]{5,4,3,2,1,0:T(8,128)S(1)}, u32[]{:S(2)}, u32[]{:S(2)}) %collective-permute-start.14) | collective-permute-done | bytes 393248 | tf_op jit(solution)/shard_map/ppermute | solution.py:288
  119.8 1.6 collective-permute-start.18
  121.4 0.8 collective-permute-start.19
  122.2 3.2 %collective-permute-done.17 = f32[2,2,2,8,768]{4,3,2,1,0:T(8,128)S(1)} collective-permute-done((f32[2,2,2,8,768]{4,3,2,1,0:T(8,128)S(1)}, f32[2,2,2,8,768]{4,3,2,1,0:T(8,128)S(1)}, u32[]{:S(2)}, u32[]{:S(2)}) %collective-permute-start.17) | collective-permute-done | bytes 196640 | tf_op jit(solution)/shard_map/ppermute | solution.py:288
  125.5 1.6 collective-permute-done.19
  127.2 1.1 collective-permute-start.20
  128.4 6.9 %collective-permute-done.20 = f32[2,2,3,8,768]{4,3,1,0,2:T(8,128)S(1)} collective-permute-done((f32[2,2,3,8,768]{4,3,1,0,2:T(8,128)S(1)}, f32[2,2,3,8,768]{4,3,1,0,2:T(8,128)S(1)}, u32[]{:S(2)}, u32[]{:S(2)}) %collective-permute-start.20) | collective-permute-done | bytes 294944 | tf_op jit(solution)/shard_map/ppermute | solution.py:288
  135.3 3.3 %collective-permute-start.21 = (f32[2,3,8,768]{3,2,0,1:T(8,128)S(1)}, f32[2,3,8,768]{3,2,0,1:T(8,128)S(1)}, u32[]{:S(2)}, u32[]{:S(2)}) collective-permute-start(f32[2,3,8,768]{3,2,0,1:T(8,128)S(1)} %dynamic-slice_bitcast_fusion.13), channel_id=1, source_target_pairs={{0,24},{1,25},{2,26},{3,27},{4,12},{5,13},{6,14},{7,15},{8,16},{9,... | collective-permute-start | bytes 442376 | tf_op jit(solution)/shard_map/ppermute | solution.py:288
  139.4 16.1 %final_part.1 = (bf16[6,14,14,1024]{3,2,1,0:T(8,128)(2,1)}, f32[8,1024]{1,0:T(8,128)}) custom-call(bf16[1344,1024]{1,0:T(8,128)(2,1)} %get-tuple-element.35.dev, bf16[1344,1024]{1,0:T(8,128)(2,1)} %bitcast.93, f32[72,1024]{1,0:T(8,128)} %pad_maximum_fusion.1.payload, f32[72,1024]{1,0:T(8,128)} %get-tuple-element.36.own, f32[16,64,64]{2,1,0:T(8,128)} %vectors.3, ...), custom_call_target="tpu_custom_call" | custom-call | tf_op jit(solution)/shard_map/final_part/pallas_call | solution.py:252
  155.6 3.3 %collective-permute-start.22 = (f32[3,8,768]{2,1,0:T(8,128)S(1)}, f32[3,8,768]{2,1,0:T(8,128)S(1)}, u32[]{:S(2)}, u32[]{:S(2)}) collective-permute-start(f32[3,8,768]{2,1,0:T(8,128)S(1)} %dynamic-slice_bitcast_fusion.14), channel_id=1, source_target_pairs={{0,96},{1,97},{2,98},{3,99},{4,36},{5,37},{6,38},{7,39},{8,104},{9... | collective-permute-start | bytes 221192 | tf_op jit(solution)/shard_map/ppermute | solution.py:288
  159.7 1.6 collective-permute-done.22
  (58 shorter events, 6.4 us)
Async XLA Ops:
  20.4 41.9 %collective-permute-start.10 = (f32[512,768]{1,0:T(8,128)S(1)}, f32[512,768]{1,0:T(8,128)S(1)}, u32[]{:S(2)}, u32[]{:S(2)}) collective-permute-start(f32[512,768]{1,0:T(8,128)S(1)} %dynamic-slice_bitcast_fusion), channel_id=1, source_target_pairs={{0,4},{1,5},{2,6},{3,7},{4,0},{5,1},{6,2},{7,3},{8,12},{9,13},{10,... | collective-permute-start | bytes 4718600 | tf_op jit(solution)/shard_map/ppermute | solution.py:288
  30.5 33.4 %collective-permute-start.9 = (f32[512,768]{1,0:T(8,128)}, f32[512,768]{1,0:T(8,128)}, u32[]{:S(2)}, u32[]{:S(2)}) collective-permute-start(f32[512,768]{1,0:T(8,128)} %dynamic-slice_bitcast_fusion.1), channel_id=1, source_target_pairs={{0,4},{1,5},{2,6},{3,7},{4,0},{5,1},{6,2},{7,3},{8,12},{9,13},{10,... | collective-permute-start | bytes 4718600 | tf_op jit(solution)/shard_map/ppermute | solution.py:288
  41.0 24.7 %collective-permute-start.8 = (f32[512,768]{1,0:T(8,128)}, f32[512,768]{1,0:T(8,128)}, u32[]{:S(2)}, u32[]{:S(2)}) collective-permute-start(f32[512,768]{1,0:T(8,128)} %dynamic-slice_bitcast_fusion.2), channel_id=1, source_target_pairs={{0,4},{1,5},{2,6},{3,7},{4,0},{5,1},{6,2},{7,3},{8,12},{9,13},{10,... | collective-permute-start | bytes 4718600 | tf_op jit(solution)/shard_map/ppermute | solution.py:288
  58.1 1.6 collective-permute-start
  60.7 3.3 %copy-start.1 = (f32[1024,768]{1,0:T(8,128)S(1)}, f32[1024,768]{1,0:T(8,128)}, u32[]{:S(2)}) copy-start(f32[1024,768]{1,0:T(8,128)} %get-tuple-element.40) | copy-start | bytes 9437188
  60.7 11.2 %collective-permute-start.1 = (f32[72,512]{1,0:T(8,128)S(1)}, f32[72,512]{1,0:T(8,128)}, u32[]{:S(2)}, u32[]{:S(2)}) collective-permute-start(f32[72,512]{1,0:T(8,128)S(1)} %select_add_fusion), channel_id=1, source_target_pairs={{0,1},{1,0},{2,3},{3,2},{4,7},{5,6},{6,5},{7,4},{8,9},{9,8},{10,11... | collective-permute-start | bytes 442376 | tf_op jit(solution)/shard_map/ppermute | solution.py:288
  63.9 2.4 %copy-start.2 = (f32[1024,768]{1,0:T(8,128)S(1)}, f32[1024,768]{1,0:T(8,128)}, u32[]{:S(2)}) copy-start(f32[1024,768]{1,0:T(8,128)} %get-tuple-element.39) | copy-start | bytes 9437188
  70.0 26.6 %collective-permute-start.13 = (f32[2,2,2,2,2,8,768]{6,5,4,3,2,1,0:T(8,128)}, f32[2,2,2,2,2,8,768]{6,5,4,3,2,1,0:T(8,128)}, u32[]{:S(2)}, u32[]{:S(2)}) collective-permute-start(f32[2,2,2,2,2,8,768]{6,5,4,3,2,1,0:T(8,128)} %dynamic-slice_bitcast_fusion.3), channel_id=1, source_target_pairs={{0,32},{1,33},{2,34},{3,35},{4,100},{5,101},{6,102},{7,103},{8,40}... | collective-permute-start | bytes 2359304 | tf_op jit(solution)/shard_map/ppermute | solution.py:288
  72.8 6.4 %collective-permute-start.2 = (f32[72,512]{1,0:T(8,128)S(1)}, f32[72,512]{1,0:T(8,128)S(1)}, u32[]{:S(2)}, u32[]{:S(2)}) collective-permute-start(f32[72,512]{1,0:T(8,128)S(1)} %add.157), channel_id=1, source_target_pairs={{0,3},{1,2},{2,1},{3,0},{4,5},{5,4},{6,7},{7,6},{8,11},{9,10},{10,... | collective-permute-start | bytes 442376 | tf_op jit(solution)/shard_map/ppermute | solution.py:288
  76.1 21.7 %collective-permute-start.12 = (f32[2,2,2,2,2,8,768]{6,5,4,3,2,1,0:T(8,128)}, f32[2,2,2,2,2,8,768]{6,5,4,3,2,1,0:T(8,128)}, u32[]{:S(2)}, u32[]{:S(2)}) collective-permute-start(f32[2,2,2,2,2,8,768]{6,5,4,3,2,1,0:T(8,128)} %dynamic-slice_bitcast_fusion.4), channel_id=1, source_target_pairs={{0,8},{1,9},{2,10},{3,11},{4,28},{5,29},{6,30},{7,31},{8,0},{9,1},... | collective-permute-start | bytes 2359304 | tf_op jit(solution)/shard_map/ppermute | solution.py:288
  79.3 10.6 %collective-permute-start.3 = (f32[72,512]{1,0:T(8,128)S(1)}, f32[72,512]{1,0:T(8,128)S(1)}, u32[]{:S(2)}, u32[]{:S(2)}) collective-permute-start(f32[72,512]{1,0:T(8,128)S(1)} %add.158), channel_id=1, source_target_pairs={{0,8},{1,9},{2,10},{3,11},{4,28},{5,29},{6,30},{7,31},{8,0},{9,1},... | collective-permute-start | bytes 442376 | tf_op jit(solution)/shard_map/ppermute | solution.py:288
  83.1 16.3 %collective-permute-start.11 = (f32[2,2,2,2,2,8,768]{6,5,4,3,2,1,0:T(8,128)}, f32[2,2,2,2,2,8,768]{6,5,4,3,2,1,0:T(8,128)}, u32[]{:S(2)}, u32[]{:S(2)}) collective-permute-start(f32[2,2,2,2,2,8,768]{6,5,4,3,2,1,0:T(8,128)} %dynamic-slice_bitcast_fusion.5), channel_id=1, source_target_pairs={{0,1},{1,0},{2,3},{3,2},{4,7},{5,6},{6,5},{7,4},{8,9},{9,8},{10,11... | collective-permute-start | bytes 2359304 | tf_op jit(solution)/shard_map/ppermute | solution.py:288
  89.9 6.4 %collective-permute-start.4 = (f32[72,512]{1,0:T(8,128)S(1)}, f32[72,512]{1,0:T(8,128)S(1)}, u32[]{:S(2)}, u32[]{:S(2)}) collective-permute-start(f32[72,512]{1,0:T(8,128)S(1)} %add.159), channel_id=1, source_target_pairs={{0,24},{1,25},{2,26},{3,27},{4,12},{5,13},{6,14},{7,15},{8,16},{9,... | collective-permute-start | bytes 442376 | tf_op jit(solution)/shard_map/ppermute | solution.py:288
  96.4 5.3 %collective-permute-start.5 = (f32[72,512]{1,0:T(8,128)S(1)}, f32[72,512]{1,0:T(8,128)S(1)}, u32[]{:S(2)}, u32[]{:S(2)}) collective-permute-start(f32[72,512]{1,0:T(8,128)S(1)} %add.160), channel_id=1, source_target_pairs={{0,32},{1,33},{2,34},{3,35},{4,100},{5,101},{6,102},{7,103},{8,40}... | collective-permute-start | bytes 442376 | tf_op jit(solution)/shard_map/ppermute | solution.py:288
  97.8 3.2 %copy-start.3 = (f32[2,2,2,2,2,8,768]{6,5,4,3,2,1,0:T(8,128)}, f32[2,2,2,2,2,8,768]{6,5,4,3,2,1,0:T(8,128)S(1)}, u32[]{:S(2)}) copy-start(f32[2,2,2,2,2,8,768]{6,5,4,3,2,1,0:T(8,128)S(1)} %bitcast_add_fusion.3) | copy-start | bytes 2359300
  97.8 1.9 %copy-start = (f32[512,768]{1,0:T(8,128)S(1)}, f32[512,768]{1,0:T(8,128)}, u32[]{:S(2)}) copy-start(f32[512,768]{1,0:T(8,128)} %bitcast_add_fusion.2) | copy-start | bytes 4718596
  101.0 11.1 %copy-start.4 = (f32[2,2,2,2,2,8,768]{6,5,4,3,2,1,0:T(8,128)S(1)}, f32[2,2,2,2,2,8,768]{6,5,4,3,2,1,0:T(8,128)}, u32[]{:S(2)}) copy-start(f32[2,2,2,2,2,8,768]{6,5,4,3,2,1,0:T(8,128)} %copy-done.3) | copy-start | bytes 2359300
  101.0 11.1 %collective-permute-start.16 = (f32[2,2,2,2,8,768]{5,4,3,2,1,0:T(8,128)S(1)}, f32[2,2,2,2,8,768]{5,4,3,2,1,0:T(8,128)S(1)}, u32[]{:S(2)}, u32[]{:S(2)}) collective-permute-start(f32[2,2,2,2,8,768]{5,4,3,2,1,0:T(8,128)S(1)} %dynamic-slice_bitcast_fusion.6), channel_id=1, source_target_pairs={{0,1},{1,0},{2,3},{3,2},{4,7},{5,6},{6,5},{7,4},{8,9},{9,8},{10,11... | collective-permute-start | bytes 1179656 | tf_op jit(solution)/shard_map/ppermute | solution.py:288
  101.7 8.9 %collective-permute-start.6 = (f32[72,512]{1,0:T(8,128)S(1)}, f32[72,512]{1,0:T(8,128)}, u32[]{:S(2)}, u32[]{:S(2)}) collective-permute-start(f32[72,512]{1,0:T(8,128)S(1)} %add.161), channel_id=1, source_target_pairs={{0,96},{1,97},{2,98},{3,99},{4,36},{5,37},{6,38},{7,39},{8,104},{9... | collective-permute-start | bytes 442376 | tf_op jit(solution)/shard_map/ppermute | solution.py:288
  106.6 8.1 %collective-permute-start.15 = (f32[2,2,2,2,8,768]{5,4,3,2,1,0:T(8,128)}, f32[2,2,2,2,8,768]{5,4,3,2,1,0:T(8,128)}, u32[]{:S(2)}, u32[]{:S(2)}) collective-permute-start(f32[2,2,2,2,8,768]{5,4,3,2,1,0:T(8,128)} %dynamic-slice_bitcast_fusion.7), channel_id=1, source_target_pairs={{0,32},{1,33},{2,34},{3,35},{4,100},{5,101},{6,102},{7,103},{8,40}... | collective-permute-start | bytes 1179656 | tf_op jit(solution)/shard_map/ppermute | solution.py:288
  111.6 16.8 %collective-permute-start.7 = (f32[72,512]{1,0:T(8,128)S(1)}, f32[72,512]{1,0:T(8,128)S(1)}, u32[]{:S(2)}, u32[]{:S(2)}) collective-permute-start(f32[72,512]{1,0:T(8,128)S(1)} %add.162), channel_id=1, source_target_pairs={{0,4},{1,5},{2,6},{3,7},{4,0},{5,1},{6,2},{7,3},{8,12},{9,13},{10,... | collective-permute-start | bytes 442376 | tf_op jit(solution)/shard_map/ppermute | solution.py:288
  111.7 7.9 %collective-permute-start.14 = (f32[2,2,2,2,8,768]{5,4,3,2,1,0:T(8,128)S(1)}, f32[2,2,2,2,8,768]{5,4,3,2,1,0:T(8,128)S(1)}, u32[]{:S(2)}, u32[]{:S(2)}) collective-permute-start(f32[2,2,2,2,8,768]{5,4,3,2,1,0:T(8,128)S(1)} %dynamic-slice_bitcast_fusion.8), channel_id=1, source_target_pairs={{0,8},{1,9},{2,10},{3,11},{4,28},{5,29},{6,30},{7,31},{8,0},{9,1},... | collective-permute-start | bytes 1179656 | tf_op jit(solution)/shard_map/ppermute | solution.py:288
  119.6 5.8 %collective-permute-start.17 = (f32[2,2,2,8,768]{4,3,2,1,0:T(8,128)S(1)}, f32[2,2,2,8,768]{4,3,2,1,0:T(8,128)S(1)}, u32[]{:S(2)}, u32[]{:S(2)}) collective-permute-start(f32[2,2,2,8,768]{4,3,2,1,0:T(8,128)S(1)} %dynamic-slice_bitcast_fusion.12), channel_id=1, source_target_pairs={{0,32},{1,33},{2,34},{3,35},{4,100},{5,101},{6,102},{7,103},{8,40}... | collective-permute-start | bytes 589832 | tf_op jit(solution)/shard_map/ppermute | solution.py:288
  119.8 5.7 %collective-permute-start.18 = (f32[2,2,2,8,768]{4,3,2,1,0:T(8,128)S(1)}, f32[2,2,2,8,768]{4,3,2,1,0:T(8,128)S(1)}, u32[]{:S(2)}, u32[]{:S(2)}) collective-permute-start(f32[2,2,2,8,768]{4,3,2,1,0:T(8,128)S(1)} %dynamic-slice_bitcast_fusion.11), channel_id=1, source_target_pairs={{0,1},{1,0},{2,3},{3,2},{4,7},{5,6},{6,5},{7,4},{8,9},{9,8},{10,11... | collective-permute-start | bytes 589832 | tf_op jit(solution)/shard_map/ppermute | solution.py:288
  121.4 5.7 %collective-permute-start.19 = (f32[2,2,2,8,768]{4,3,2,1,0:T(8,128)S(1)}, f32[2,2,2,8,768]{4,3,2,1,0:T(8,128)S(1)}, u32[]{:S(2)}, u32[]{:S(2)}) collective-permute-start(f32[2,2,2,8,768]{4,3,2,1,0:T(8,128)S(1)} %dynamic-slice_bitcast_fusion.10), channel_id=1, source_target_pairs={{0,8},{1,9},{2,10},{3,11},{4,28},{5,29},{6,30},{7,31},{8,0},{9,1},... | collective-permute-start | bytes 589832 | tf_op jit(solution)/shard_map/ppermute | solution.py:288
  127.2 8.0 %collective-permute-start.20 = (f32[2,2,3,8,768]{4,3,1,0,2:T(8,128)S(1)}, f32[2,2,3,8,768]{4,3,1,0,2:T(8,128)S(1)}, u32[]{:S(2)}, u32[]{:S(2)}) collective-permute-start(f32[2,2,3,8,768]{4,3,1,0,2:T(8,128)S(1)} %dynamic-slice_bitcast_fusion.9), channel_id=1, source_target_pairs={{0,3},{1,2},{2,1},{3,0},{4,5},{5,4},{6,7},{7,6},{8,11},{9,10},{10,... | collective-permute-start | bytes 884744 | tf_op jit(solution)/shard_map/ppermute | solution.py:288
  135.3 20.2 %collective-permute-start.21 = (f32[2,3,8,768]{3,2,0,1:T(8,128)S(1)}, f32[2,3,8,768]{3,2,0,1:T(8,128)S(1)}, u32[]{:S(2)}, u32[]{:S(2)}) collective-permute-start(f32[2,3,8,768]{3,2,0,1:T(8,128)S(1)} %dynamic-slice_bitcast_fusion.13), channel_id=1, source_target_pairs={{0,24},{1,25},{2,26},{3,27},{4,12},{5,13},{6,14},{7,15},{8,16},{9,... | collective-permute-start | bytes 442376 | tf_op jit(solution)/shard_map/ppermute | solution.py:288
  155.6 5.6 %collective-permute-start.22 = (f32[3,8,768]{2,1,0:T(8,128)S(1)}, f32[3,8,768]{2,1,0:T(8,128)S(1)}, u32[]{:S(2)}, u32[]{:S(2)}) collective-permute-start(f32[3,8,768]{2,1,0:T(8,128)S(1)} %dynamic-slice_bitcast_fusion.14), channel_id=1, source_target_pairs={{0,96},{1,97},{2,98},{3,99},{4,36},{5,37},{6,38},{7,39},{8,104},{9... | collective-permute-start | bytes 221192 | tf_op jit(solution)/shard_map/ppermute | solution.py:288

commit v2 on v1

--- a/solution.py
+++ b/solution.py
@@ -1,3 +1,5 @@
+import functools
+
 import jax
 import jax.numpy as jnp
 import numpy as np
@@ -18,7 +20,7 @@
 ROWS = IMAGES * H * 16
 PIXELS = IMAGES * H * W
 TOTAL = 128.0 * PIXELS
-VMEM_LIMIT = 60 << 20
+ON_CHIP = pl.BlockSpec(memory_space=pltpu.VMEM)
 
 
 def nt(a, b, precision=None):
@@ -55,19 +57,32 @@
     return jnp.broadcast_to(row, (256, 256)).T
 
 
+def place():
+    core = lax.axis_index("c")
+    spots = ([], [])
+    for axis in "zyx":
+        i = lax.axis_index(axis)
+        a, b = (i ^ (i >> 1)) & 1, i >> 1
+        spots[0].append(2 * a + b)
+        spots[1].append(2 * b + a)
+    return core, spots
+
+
 def prep_kernel(
     features, grads, vectors, values, cols, xc, wht, u, sums, whiten, wide, wp32
 ):
+    core, spots = place()
     for z in range(4):
         basis = block_vectors(vectors, z)
         scale = lax.rsqrt(values[0:1, 256 * z : 256 * z + 256])
         full = nt(basis * scale, basis, HIGHEST)
         whiten[z] = full.astype(BF16)
         for c in range(2):
-            spot = RING[c].index(z)
+            at_z, at_y, at_x = spots[c]
             for row, (y, x) in enumerate((y, x) for y in RING[c] for x in RING[c]):
                 channel = y * 64 + c * 32 + x * 8
-                wp32[4 * c + spot, row * 8 : row * 8 + 8, :] = full[channel : channel + 8, :]
+                row = pl.multiple_of(8 * (row ^ (4 * at_y + at_x)), 8)
+                wp32[4 * c + z, pl.ds(row, 8), :] = full[channel : channel + 8, :]
     wide[...] = jnp.zeros_like(wide)
     inside = lax.broadcasted_iota(jnp.int32, (H, 16, O), 1) < W
     for b in range(IMAGES):
@@ -107,13 +122,14 @@
     head = xc[1].astype(F32)
     xc[1] = jnp.where(pad == 14, low.astype(F32), head).astype(BF16)
     for k in range(8):
-        c, spot = k // 4, k % 4
-        z = RING[c][spot]
+        c, z = k // 4, k % 4
         chunk = xc[:, :, 256 * z : 256 * z + 256].reshape(ROWS, 256)
         part = nt(wp32[k].astype(BF16), chunk)
-        wht[128 * k : 128 * k + 128, :] = part.astype(BF16)
+        row = 4 * (c ^ core) + (RING[c].index(z) ^ spots[c][0])
+        row = pl.multiple_of(128 * row, 128)
+        wht[pl.ds(row, 128), :] = part.astype(BF16)
         shift = part[:, 14:15] + part[:, 15:16] + part[:, 30:31]
-        u[128 * k : 128 * k + 128, :] = jnp.broadcast_to(shift, (128, 128))
+        u[pl.ds(row, 128), :] = jnp.broadcast_to(shift, (128, 128))
     wht[1024:1040, :] = jnp.ones((16, ROWS), BF16)
 
 
@@ -128,40 +144,36 @@
             jax.ShapeDtypeStruct((1, D), F32),
             jax.ShapeDtypeStruct((4, 256, 256), BF16),
         ),
+        in_specs=[ON_CHIP] * 4,
+        out_specs=(ON_CHIP,) * 6,
         scratch_shapes=[pltpu.VMEM((H, 32, O), F32), pltpu.VMEM((8, 128, 256), F32)],
-        compiler_params=pltpu.CompilerParams(vmem_limit_bytes=VMEM_LIMIT),
+        compiler_params=pltpu.CompilerParams(vmem_limit_bytes=8 << 20),
         name="prep",
     )(features, grads, vectors, values)
 
 
-def weight_kernel(wht, cols, u, out, colsum):
-    full = nn(wht[...], cols[...])
+def weight_kernel(a, wht, cols, u, keep, send, colsum):
+    full = nn(wht[...], cols[:, 768 * a : 768 * a + 768])
     ones = full[1024:1032, :]
     colsum[...] = ones
     for k in range(6):
         lanes = slice(128 * k, 128 * k + 128)
-        out[:, lanes] = full[0:1024, lanes] + u[...] * ones[0:1, lanes]
+        keep[:, lanes] = full[0:512, lanes] + u[0:512] * ones[0:1, lanes]
+        send[:, lanes] = full[512:1024, lanes] + u[512:1024] * ones[0:1, lanes]
 
 
 def weight_part(wht, cols, u, a):
     return pl.pallas_call(
-        weight_kernel,
-        grid=(1,),
-        in_specs=[
-            pl.BlockSpec((1040, ROWS), lambda i: (0, 0)),
-            pl.BlockSpec((ROWS, 768), lambda i: (0, a)),
-            pl.BlockSpec((1024, 128), lambda i: (0, 0)),
-        ],
-        out_specs=(
-            pl.BlockSpec((1024, 768), lambda i: (0, 0)),
-            pl.BlockSpec((8, 768), lambda i: (0, 0)),
-        ),
+        functools.partial(weight_kernel, a),
+        in_specs=[ON_CHIP] * 3,
+        out_specs=(ON_CHIP,) * 3,
         out_shape=(
-            jax.ShapeDtypeStruct((1024, 768), F32),
+            jax.ShapeDtypeStruct((512, 768), F32),
+            jax.ShapeDtypeStruct((512, 768), F32),
             jax.ShapeDtypeStruct((8, 768), F32),
         ),
-        compiler_params=pltpu.CompilerParams(vmem_limit_bytes=VMEM_LIMIT),
-        name="weight_part",
+        compiler_params=pltpu.CompilerParams(vmem_limit_bytes=6 << 20),
+        name=f"weight_part_{a}",
     )(wht, cols, u)
 
 
@@ -192,7 +204,7 @@
         back_kernel,
         grid=(4,),
         in_specs=[
-            pl.BlockSpec((ROWS, 9 * O), lambda z: (0, 0)),
+            ON_CHIP,
             pl.BlockSpec((9 * O, 256), column),
             pl.BlockSpec((ROWS, 256), column),
             pl.BlockSpec((1, 256), column),
@@ -205,7 +217,7 @@
             jax.ShapeDtypeStruct((ROWS, D), BF16),
             jax.ShapeDtypeStruct((72, D), F32),
         ),
-        compiler_params=pltpu.CompilerParams(vmem_limit_bytes=VMEM_LIMIT),
+        compiler_params=pltpu.CompilerParams(vmem_limit_bytes=14 << 20),
         name="back_part",
     )(cols, kernel, xc, sums, *parts)
 
@@ -270,7 +282,7 @@
             jax.ShapeDtypeStruct((8, D), F32),
         ),
         scratch_shapes=[pltpu.VMEM((4, 256, 256), BF16), pltpu.VMEM((8, D), F32)],
-        compiler_params=pltpu.CompilerParams(vmem_limit_bytes=VMEM_LIMIT),
+        compiler_params=pltpu.CompilerParams(vmem_limit_bytes=10 << 20),
         name="final_part",
     )(dev, xc, payload, own, vectors, values, whiten)
 
@@ -299,28 +311,21 @@
     return move
 
 
-def split(value, dim, bit):
-    keep = lax.dynamic_index_in_dim(value, bit, dim, keepdims=False)
-    send = lax.dynamic_index_in_dim(value, 1 - bit, dim, keepdims=False)
-    return keep, send
+def halves(value, dim):
+    pick = lambda k: lax.index_in_dim(value, k, dim, keepdims=False)
+    return pick(0), pick(1)
 
 
 def local(features, grads, kernel, vectors, values):
     core = lax.axis_index("c")
-    bits = {}
-    for axis in "xyz":
-        i = lax.axis_index(axis)
-        a, b = (i ^ (i >> 1)) & 1, i >> 1
-        bits[axis] = (jnp.where(core == 0, a, b), jnp.where(core == 0, b, a))
     flat_values = values.reshape(1, D)
     cols, xc, wht, u, sums, whiten = prep(features, grads, vectors, flat_values)
     cols, xc = cols.reshape(ROWS, 9 * O), xc.reshape(ROWS, D)
 
     parts, colsums = [], []
     for a in range(3):
-        part, colsum = weight_part(wht, cols, u, a)
+        keep, send, colsum = weight_part(wht, cols, u, a)
         colsums.append(colsum)
-        keep, send = split(part.reshape(2, 512, 768), 0, core)
         parts.append((keep + exchange(send, other_core)).reshape(2, 2, 2, 2, 2, 2, 8, 768))
     dev, own = back_part(cols, kernel.reshape(9 * O, D), xc, sums, colsums)
 
@@ -343,14 +348,14 @@
             axis = "xyz"[(a + turn) % 3]
             dim = names[a].index(axis + "1")
             names[a].pop(dim)
-            keep, send = split(parts[a], dim, bits[axis][0])
+            keep, send = halves(parts[a], dim)
             parts[a] = keep + exchange(send, ring(axis, 0))
     share = jnp.stack(parts, axis=3)
     order = ["z", "y", "x"]
     for axis in "xyz":
         dim = order.index(axis)
         order.pop(dim)
-        keep, send = split(share, dim, bits[axis][1])
+        keep, send = halves(share, dim)
         share = keep + exchange(send, ring(axis, 1))
 
     input_grad, shift = final_part(dev, xc, payload, own, vectors, flat_values, whiten)

time: 163 us -> 138 us (0.85)
  Pallas kernels: 63.8 us -> 43.1 us
  other arithmetic: 16.8 us -> 8.5 us
  waiting for transfers between devices: 36.6 us -> 41.6 us
    pallas_call x4, Pallas kernels: 38 us -> 25.8 us  [the longest x3 12.9 us: weight_part(): pl.pallas_call(functools.partial(weight_kernel, a), in_specs=[ON_CHIP] *...]
    unnamed x10 -> x36, local copies, waits for them, and re-layouts: 0.93 us -> 13.2 us
    squeeze x15 -> x12, local copies, waits for them, and re-layouts: 11.9 us -> 1.05 us  [halves(): pick = lambda k: lax.index_in_dim(value, k, dim, keepdims=False)]
    pallas_call x1, Pallas kernels: 9.58 us -> 4.26 us  [prep(): pl.pallas_call(prep_kernel, out_shape=(jax.ShapeDtypeStruct((IMAGES * H,...]
    ppermute x23, waiting for transfers between devices: 36.6 us -> 41.6 us  [exchange(): return lax.ppermute(value, ALL, permutation(move))]
    add x6, other arithmetic: 5.11 us -> 0.48 us  [local(): parts[a] = keep + exchange(send, ring(axis, 0))]
    pallas_call x1, Pallas kernels: 16.1 us -> 13.1 us  [final_part(): pl.pallas_call(final_kernel, grid=(IMAGES,), in_specs=[pl.BlockSpec((H *...]
    add x6, other arithmetic: 1.95 us -> 0.13 us  [local(): mine = mine + exchange(mine, ring(axis, step))]
  transfers between devices with their start and end apart: 23 -> 23, of which waited for: 12 -> 15; matrix products, arithmetic and copies ran while one was open for 17% -> 6% of each run, Pallas kernels for 29% -> 25%
where the time goes in v2:
time: 138 us
  Pallas kernels  43.1 us (31%)
  waiting for transfers between devices  41.6 us (30%)
  starting transfers between devices  28.7 us (21%)
  local copies, waits for them, and re-layouts  15.1 us (11%)
  other arithmetic  8.5 us (6%)
    ppermute x23, waiting for transfers between devices, exchange(): return lax.ppermute(value, ALL, permutation(move))  41.6 us
    ppermute x23, starting transfers between devices, exchange(): return lax.ppermute(value, ALL, permutation(move))  28.7 us
    unnamed x36, local copies, waits for them, and re-layouts  13.2 us
    pallas_call x1, Pallas kernels, final_part(): pl.pallas_call(final_kernel, grid=(IMAGES,), in_specs=[pl.BlockSpec((H *...  13.1 us
    pallas_call x3, Pallas kernels, weight_part(): pl.pallas_call(functools.partial(weight_kernel, a), in_specs=[ON_CHIP] *...  12.9 us
    pallas_call x1, Pallas kernels, back_part(): pl.pallas_call(back_kernel, grid=(4,), in_specs=[ON_CHIP, pl.BlockSpec((9...  12.9 us
    add x3, other arithmetic, local(): keep + exchange(send, other_core)  4.92 us
    pallas_call x1, Pallas kernels, prep(): pl.pallas_call(prep_kernel, out_shape=(jax.ShapeDtypeStruct((IMAGES * H,...  4.26 us
  transfers between devices with their start and end apart: 23, of which 15 were waited for; matrix products, arithmetic and copies ran while one was open for 6% of the time, Pallas kernels for 25%

profile of v2, /device:TPU:0, one launch (start us, length us, event | category | flops | bytes accessed | tf_op | source)
XLA Modules:
  0.0 138.0 jit_solution(8081603289590298027)
XLA Ops:
  0.6 0.8 reshape.31.values
  1.4 1.8 %copy-done.3 = bf16[6,14,14,1024]{3,2,1,0:T(8,128)(2,1)S(1)} copy-done((bf16[6,14,14,1024]{3,2,1,0:T(8,128)(2,1)S(1)}, bf16[6,14,14,1024]{3,2,1,0:T(8,128)(2,1)}, u32[]{:S(2)}) %copy-start.3) | copy-done | bytes 2408472
  3.2 1.0 copy-done.6
  4.2 1.1 copy-done.14
  5.3 4.3 %prep.1 = (bf16[84,16,2304]{2,1,0:T(8,128)(2,1)S(1)}, bf16[84,16,1024]{2,1,0:T(8,128)(2,1)S(1)}, bf16[1040,1344]{1,0:T(8,128)(2,1)S(1)}, f32[1024,128]{1,0:T(8,1...) custom-call(bf16[6,14,14,1024]{3,2,1,0:T(8,128)(2,1)S(1)} %copy-done.3, ...), custom_call_target="tpu_custom_call" | custom-call | tf_op jit(solution)/shard_map/prep/pallas_call | solution.py:137
  9.6 4.3 %weight_part_2.1 = (f32[512,768]{1,0:T(8,128)S(1)}, f32[512,768]{1,0:T(8,128)}, f32[8,768]{1,0:T(8,128)S(1)}) custom-call(bf16[1040,1344]{1,0:T(8,128)(2,1)S(1)} %get-tuple-element.33.wht, bf16[1344,2304]{1,0:T(8,128)(2,1)S(1)} %bitcast.93, f32[1024,128]{1,0:T(8,128)S(1)} %get-tuple-element.34.u), custom_call_target="tpu_custom_call" | custom-call | tf_op jit(solution)/shard_map/weight_part_2/pallas_call | solution.py:166
  13.9 4.3 %weight_part_1.1 = (f32[512,768]{1,0:T(8,128)S(1)}, f32[512,768]{1,0:T(8,128)}, f32[8,768]{1,0:T(8,128)S(1)}) custom-call(bf16[1040,1344]{1,0:T(8,128)(2,1)S(1)} %get-tuple-element.33.wht, bf16[1344,2304]{1,0:T(8,128)(2,1)S(1)} %bitcast.94, f32[1024,128]{1,0:T(8,128)S(1)} %get-tuple-element.34.u), custom_call_target="tpu_custom_call" | custom-call | tf_op jit(solution)/shard_map/weight_part_1/pallas_call | solution.py:166
  18.2 0.5 collective-permute-start.9
  18.7 4.3 %weight_part_0.1 = (f32[512,768]{1,0:T(8,128)S(1)}, f32[512,768]{1,0:T(8,128)}, f32[8,768]{1,0:T(8,128)S(1)}) custom-call(bf16[1040,1344]{1,0:T(8,128)(2,1)S(1)} %get-tuple-element.33.wht, bf16[1344,2304]{1,0:T(8,128)(2,1)S(1)} %bitcast.95, f32[1024,128]{1,0:T(8,128)S(1)} %get-tuple-element.34.u), custom_call_target="tpu_custom_call" | custom-call | tf_op jit(solution)/shard_map/weight_part_0/pallas_call | solution.py:166
  23.1 1.2 copy-done.12
  24.2 2.8 %copy-done.1 = bf16[84,16,2304]{2,1,0:T(8,128)(2,1)S(1)} copy-done((bf16[84,16,2304]{2,1,0:T(8,128)(2,1)S(1)}, bf16[84,16,2304]{2,1,0:T(8,128)(2,1)}, u32[]{:S(2)}) %copy-start.1) | copy-done | bytes 6193176
  27.0 2.3 %copy-done.2 = bf16[3,3,256,1024]{3,2,1,0:T(8,128)(2,1)S(1)} copy-done((bf16[3,3,256,1024]{3,2,1,0:T(8,128)(2,1)S(1)}, bf16[3,3,256,1024]{3,2,1,0:T(8,128)(2,1)}, u32[]{:S(2)}) %copy-start.2) | copy-done | bytes 4718616
  29.3 12.9 %back_part.1 = (bf16[1344,1024]{1,0:T(8,128)(2,1)S(1)}, f32[72,1024]{1,0:T(8,128)S(1)}) custom-call(bf16[1344,2304]{1,0:T(8,128)(2,1)S(1)} %bitcast.96, bf16[2304,1024]{1,0:T(8,128)(2,1)S(1)} %bitcast.99, bf16[1344,1024]{1,0:T(8,128)(2,1)S(1)} %bitcast.97, f32[1,1024]{1,0:T(1,128)S(1)} %get-tuple-element.32.sums, f32[8,768]{1,0:T(8,128)S(1)} %get-tuple-element.35.sum0, ...), custom_call_target="tpu_custom_call" | custom-call | tf_op jit(solution)/shard_map/back_part/pallas_call | solution.py:203
  42.3 0.6 collective-permute-start
  42.8 1.0 collective-permute-done
  43.9 1.7 %collective-permute-start.1 = (f32[72,512]{1,0:T(8,128)S(1)}, f32[72,512]{1,0:T(8,128)S(1)}, u32[]{:S(2)}, u32[]{:S(2)}) collective-permute-start(f32[72,512]{1,0:T(8,128)S(1)} %select_add_fusion), channel_id=1, source_target_pairs={{0,1},{1,0},{2,3},{3,2},{4,7},{5,6},{6,5},{7,4},{8,9},{9,8},{10,11... | collective-permute-start | bytes 442376 | tf_op jit(solution)/shard_map/ppermute | solution.py:300
  45.5 3.6 %collective-permute-done.1 = f32[72,512]{1,0:T(8,128)S(1)} collective-permute-done((f32[72,512]{1,0:T(8,128)S(1)}, f32[72,512]{1,0:T(8,128)S(1)}, u32[]{:S(2)}, u32[]{:S(2)}) %collective-permute-start.1) | collective-permute-done | bytes 147488 | tf_op jit(solution)/shard_map/ppermute | solution.py:300
  49.1 2.9 %collective-permute-start.2 = (f32[72,512]{1,0:T(8,128)S(1)}, f32[72,512]{1,0:T(8,128)S(1)}, u32[]{:S(2)}, u32[]{:S(2)}) collective-permute-start(f32[72,512]{1,0:T(8,128)S(1)} %add.79), channel_id=1, source_target_pairs={{0,3},{1,2},{2,1},{3,0},{4,5},{5,4},{6,7},{7,6},{8,11},{9,10},{10,... | collective-permute-start | bytes 442376 | tf_op jit(solution)/shard_map/ppermute | solution.py:300
  52.1 3.5 %collective-permute-done.2 = f32[72,512]{1,0:T(8,128)S(1)} collective-permute-done((f32[72,512]{1,0:T(8,128)S(1)}, f32[72,512]{1,0:T(8,128)S(1)}, u32[]{:S(2)}, u32[]{:S(2)}) %collective-permute-start.2) | collective-permute-done | bytes 147488 | tf_op jit(solution)/shard_map/ppermute | solution.py:300
  55.6 1.7 %collective-permute-start.3 = (f32[72,512]{1,0:T(8,128)S(1)}, f32[72,512]{1,0:T(8,128)S(1)}, u32[]{:S(2)}, u32[]{:S(2)}) collective-permute-start(f32[72,512]{1,0:T(8,128)S(1)} %add.80), channel_id=1, source_target_pairs={{0,8},{1,9},{2,10},{3,11},{4,28},{5,29},{6,30},{7,31},{8,0},{9,1},... | collective-permute-start | bytes 442376 | tf_op jit(solution)/shard_map/ppermute | solution.py:300
  57.3 1.7 %add.87 = f32[512,768]{1,0:T(8,128)S(1)} add(f32[512,768]{1,0:T(8,128)S(1)} %copy-done.9, f32[512,768]{1,0:T(8,128)} %collective-permute-done.10) | non-fusion elementwise | flops 393216 | bytes 4718592 | tf_op jit(solution)/shard_map/add | solution.py:329
  59.2 1.7 %add.86 = f32[512,768]{1,0:T(8,128)S(1)} add(f32[512,768]{1,0:T(8,128)S(1)} %copy-done.11, f32[512,768]{1,0:T(8,128)} %collective-permute-done.9) | non-fusion elementwise | flops 393216 | bytes 4718592 | tf_op jit(solution)/shard_map/add | solution.py:329
  61.1 1.6 %add.85 = f32[512,768]{1,0:T(8,128)S(1)} add(f32[512,768]{1,0:T(8,128)S(1)} %copy-done.13, f32[512,768]{1,0:T(8,128)} %collective-permute-done.8) | non-fusion elementwise | flops 393216 | bytes 4718592 | tf_op jit(solution)/shard_map/add | solution.py:329
  62.7 2.0 %collective-permute-start.13 = (f32[2,2,2,2,2,8,768]{6,5,4,3,2,1,0:T(8,128)S(1)}, f32[2,2,2,2,2,8,768]{6,5,4,3,2,1,0:T(8,128)S(1)}, u32[]{:S(2)}, u32[]{:S(2)}) collective-permute-start(f32[2,2,2,2,2,8,768]{6,5,4,3,2,1,0:T(8,128)S(1)} %slice_bitcast_fusion.4), channel_id=1, source_target_pairs={{0,32},{1,33},{2,34},{3,35},{4,100},{5,101},{6,102},{7,103},{8,40}... | collective-permute-start | bytes 2359304 | tf_op jit(solution)/shard_map/ppermute | solution.py:300
  64.8 2.3 %collective-permute-start.4 = (f32[72,512]{1,0:T(8,128)S(1)}, f32[72,512]{1,0:T(8,128)S(1)}, u32[]{:S(2)}, u32[]{:S(2)}) collective-permute-start(f32[72,512]{1,0:T(8,128)S(1)} %add.81), channel_id=1, source_target_pairs={{0,24},{1,25},{2,26},{3,27},{4,12},{5,13},{6,14},{7,15},{8,16},{9,... | collective-permute-start | bytes 442376 | tf_op jit(solution)/shard_map/ppermute | solution.py:300
  67.1 0.8 collective-permute-start.12
  67.8 4.7 %collective-permute-done.4 = f32[72,512]{1,0:T(8,128)S(1)} collective-permute-done((f32[72,512]{1,0:T(8,128)S(1)}, f32[72,512]{1,0:T(8,128)S(1)}, u32[]{:S(2)}, u32[]{:S(2)}) %collective-permute-start.4) | collective-permute-done | bytes 147488 | tf_op jit(solution)/shard_map/ppermute | solution.py:300
  73.1 4.6 %collective-permute-done.5 = f32[72,512]{1,0:T(8,128)S(1)} collective-permute-done((f32[72,512]{1,0:T(8,128)S(1)}, f32[72,512]{1,0:T(8,128)S(1)}, u32[]{:S(2)}, u32[]{:S(2)}) %collective-permute-start.5) | collective-permute-done | bytes 147488 | tf_op jit(solution)/shard_map/ppermute | solution.py:300
  77.8 2.9 %collective-permute-start.6 = (f32[72,512]{1,0:T(8,128)S(1)}, f32[72,512]{1,0:T(8,128)S(1)}, u32[]{:S(2)}, u32[]{:S(2)}) collective-permute-start(f32[72,512]{1,0:T(8,128)S(1)} %add.83), channel_id=1, source_target_pairs={{0,96},{1,97},{2,98},{3,99},{4,36},{5,37},{6,38},{7,39},{8,104},{9... | collective-permute-start | bytes 442376 | tf_op jit(solution)/shard_map/ppermute | solution.py:300
  80.7 3.5 %collective-permute-done.6 = f32[72,512]{1,0:T(8,128)S(1)} collective-permute-done((f32[72,512]{1,0:T(8,128)S(1)}, f32[72,512]{1,0:T(8,128)S(1)}, u32[]{:S(2)}, u32[]{:S(2)}) %collective-permute-start.6) | collective-permute-done | bytes 147488 | tf_op jit(solution)/shard_map/ppermute | solution.py:300
  85.4 1.7 %collective-permute-start.15 = (f32[2,2,2,2,8,768]{5,4,3,1,0,2:T(8,128)S(1)}, f32[2,2,2,2,8,768]{5,4,3,1,0,2:T(8,128)S(1)}, u32[]{:S(2)}, u32[]{:S(2)}) collective-permute-start(f32[2,2,2,2,8,768]{5,4,3,1,0,2:T(8,128)S(1)} %slice_bitcast_fusion.7), channel_id=1, source_target_pairs={{0,32},{1,33},{2,34},{3,35},{4,100},{5,101},{6,102},{7,103},{8,40}... | collective-permute-start | bytes 1179656 | tf_op jit(solution)/shard_map/ppermute | solution.py:300
  87.3 5.9 %collective-permute-done.16 = f32[2,2,2,2,8,768]{5,4,3,2,1,0:T(8,128)S(1)} collective-permute-done((f32[2,2,2,2,8,768]{5,4,3,2,1,0:T(8,128)S(1)}, f32[2,2,2,2,8,768]{5,4,3,2,1,0:T(8,128)S(1)}, u32[]{:S(2)}, u32[]{:S(2)}) %collective-permute-start.16) | collective-permute-done | bytes 393248 | tf_op jit(solution)/shard_map/ppermute | solution.py:300
  93.3 1.7 %collective-permute-done.14 = f32[2,2,2,2,8,768]{5,4,3,2,1,0:T(8,128)S(1)} collective-permute-done((f32[2,2,2,2,8,768]{5,4,3,2,1,0:T(8,128)S(1)}, f32[2,2,2,2,8,768]{5,4,3,2,1,0:T(8,128)S(1)}, u32[]{:S(2)}, u32[]{:S(2)}) %collective-permute-start.14) | collective-permute-done | bytes 393248 | tf_op jit(solution)/shard_map/ppermute | solution.py:300
  95.2 2.1 %collective-permute-start.18 = (f32[2,2,2,8,768]{4,3,2,1,0:T(8,128)S(1)}, f32[2,2,2,8,768]{4,3,2,1,0:T(8,128)S(1)}, u32[]{:S(2)}, u32[]{:S(2)}) collective-permute-start(f32[2,2,2,8,768]{4,3,2,1,0:T(8,128)S(1)} %slice_bitcast_fusion.13), channel_id=1, source_target_pairs={{0,1},{1,0},{2,3},{3,2},{4,7},{5,6},{6,5},{7,4},{8,9},{9,8},{10,11... | collective-permute-start | bytes 589832 | tf_op jit(solution)/shard_map/ppermute | solution.py:300
  97.8 3.1 %collective-permute-done.19 = f32[2,2,2,8,768]{4,3,2,1,0:T(8,128)S(1)} collective-permute-done((f32[2,2,2,8,768]{4,3,2,1,0:T(8,128)S(1)}, f32[2,2,2,8,768]{4,3,2,1,0:T(8,128)S(1)}, u32[]{:S(2)}, u32[]{:S(2)}) %collective-permute-start.19) | collective-permute-done | bytes 196640 | tf_op jit(solution)/shard_map/ppermute | solution.py:300
  101.0 2.1 %collective-permute-done.17 = f32[2,2,2,8,768]{4,3,2,1,0:T(8,128)S(1)} collective-permute-done((f32[2,2,2,8,768]{4,3,2,1,0:T(8,128)S(1)}, f32[2,2,2,8,768]{4,3,2,1,0:T(8,128)S(1)}, u32[]{:S(2)}, u32[]{:S(2)}) %collective-permute-start.17) | collective-permute-done | bytes 196640 | tf_op jit(solution)/shard_map/ppermute | solution.py:300
  103.2 0.8 copy-done.17
  104.0 0.7 slice_bitcast_fusion.9
  104.7 2.8 %collective-permute-start.20 = (f32[2,2,3,8,768]{4,3,1,0,2:T(8,128)}, f32[2,2,3,8,768]{4,3,1,0,2:T(8,128)S(1)}, u32[]{:S(2)}, u32[]{:S(2)}) collective-permute-start(f32[2,2,3,8,768]{4,3,1,0,2:T(8,128)} %slice_bitcast_fusion.9), channel_id=1, source_target_pairs={{0,3},{1,2},{2,1},{3,0},{4,5},{5,4},{6,7},{7,6},{8,11},{9,10},{10,... | collective-permute-start | bytes 884744 | tf_op jit(solution)/shard_map/ppermute | solution.py:300
  107.5 1.0 broadcast_select_fusion.1
  108.5 4.3 %collective-permute-done.20 = f32[2,2,3,8,768]{4,3,1,0,2:T(8,128)S(1)} collective-permute-done((f32[2,2,3,8,768]{4,3,1,0,2:T(8,128)}, f32[2,2,3,8,768]{4,3,1,0,2:T(8,128)S(1)}, u32[]{:S(2)}, u32[]{:S(2)}) %collective-permute-start.20) | collective-permute-done | bytes 294944 | tf_op jit(solution)/shard_map/ppermute | solution.py:300
  112.8 1.0 fusion.3
  113.9 2.7 %collective-permute-start.21 = (f32[2,3,8,768]{3,2,0,1:T(8,128)S(1)}, f32[2,3,8,768]{3,2,0,1:T(8,128)S(1)}, u32[]{:S(2)}, u32[]{:S(2)}) collective-permute-start(f32[2,3,8,768]{3,2,0,1:T(8,128)S(1)} %slice_bitcast_fusion.15), channel_id=1, source_target_pairs={{0,24},{1,25},{2,26},{3,27},{4,12},{5,13},{6,14},{7,15},{8,16},{9,... | collective-permute-start | bytes 442376 | tf_op jit(solution)/shard_map/ppermute | solution.py:300
  116.7 1.8 %copy-done.5 = bf16[1344,1024]{1,0:T(8,128)(2,1)S(1)} copy-done((bf16[1344,1024]{1,0:T(8,128)(2,1)S(1)}, bf16[1344,1024]{1,0:T(8,128)(2,1)}, u32[]{:S(2)}) %copy-start.5) | copy-done | bytes 2752536
  118.4 13.1 %final_part.1 = (bf16[6,14,14,1024]{3,2,1,0:T(8,128)(2,1)}, f32[8,1024]{1,0:T(8,128)S(1)}) custom-call(bf16[1344,1024]{1,0:T(8,128)(2,1)S(1)} %copy-done.5, bf16[1344,1024]{1,0:T(8,128)(2,1)S(1)} %bitcast.98, f32[72,1024]{1,0:T(8,128)S(1)} %pad_maximum_fusion.1.payload, f32[72,1024]{1,0:T(8,128)S(1)} %get-tuple-element.39.own, f32[16,64,64]{2,1,0:T(8,128)S(1)} %copy-done.7, ...), custom_call_target="tpu_custom_call" | custom-call | tf_op jit(solution)/shard_map/final_part/pallas_call | solution.py:264
  131.6 2.7 %collective-permute-start.22 = (f32[3,8,768]{2,1,0:T(8,128)S(1)}, f32[3,8,768]{2,1,0:T(8,128)S(1)}, u32[]{:S(2)}, u32[]{:S(2)}) collective-permute-start(f32[3,8,768]{2,1,0:T(8,128)S(1)} %slice_bitcast_fusion.17), channel_id=1, source_target_pairs={{0,96},{1,97},{2,98},{3,99},{4,36},{5,37},{6,38},{7,39},{8,104},{9... | collective-permute-start | bytes 221192 | tf_op jit(solution)/shard_map/ppermute | solution.py:300
  134.3 2.9 %collective-permute-done.22 = f32[3,8,768]{2,1,0:T(8,128)S(1)} collective-permute-done((f32[3,8,768]{2,1,0:T(8,128)S(1)}, f32[3,8,768]{2,1,0:T(8,128)S(1)}, u32[]{:S(2)}, u32[]{:S(2)}) %collective-permute-start.22) | collective-permute-done | bytes 73760 | tf_op jit(solution)/shard_map/ppermute | solution.py:300
  137.2 0.7 fusion.10
  (81 shorter events, 3.6 us)
Async XLA Ops:
  1.4 1.8 %copy-start.3 = (bf16[6,14,14,1024]{3,2,1,0:T(8,128)(2,1)S(1)}, bf16[6,14,14,1024]{3,2,1,0:T(8,128)(2,1)}, u32[]{:S(2)}) copy-start(bf16[6,14,14,1024]{3,2,1,0:T(8,128)(2,1)} %features.1) | copy-start | bytes 7225348
  3.2 1.0 copy-start.6
  4.2 1.1 copy-start.14
  9.6 4.3 %copy-start.15 = (bf16[4,256,256]{2,1,0:T(8,128)(2,1)}, bf16[4,256,256]{2,1,0:T(8,128)(2,1)S(1)}, u32[]{:S(2)}) copy-start(bf16[4,256,256]{2,1,0:T(8,128)(2,1)S(1)} %get-tuple-element.40.whiten) | copy-start | bytes 1572868
  9.6 9.1 %copy-start = (bf16[84,16,2304]{2,1,0:T(8,128)(2,1)}, bf16[84,16,2304]{2,1,0:T(8,128)(2,1)S(1)}, u32[]{:S(2)}) copy-start(bf16[84,16,2304]{2,1,0:T(8,128)(2,1)S(1)} %get-tuple-element.30) | copy-start | bytes 18579460
  13.9 4.3 %copy-start.8 = (f32[512,768]{1,0:T(8,128)}, f32[512,768]{1,0:T(8,128)S(1)}, u32[]{:S(2)}) copy-start(f32[512,768]{1,0:T(8,128)S(1)} %get-tuple-element.46) | copy-start | bytes 4718596
  13.9 43.4 %collective-permute-start.10 = (f32[512,768]{1,0:T(8,128)}, f32[512,768]{1,0:T(8,128)}, u32[]{:S(2)}, u32[]{:S(2)}) collective-permute-start(f32[512,768]{1,0:T(8,128)} %get-tuple-element.47), channel_id=1, source_target_pairs={{0,4},{1,5},{2,6},{3,7},{4,0},{5,1},{6,2},{7,3},{8,12},{9,13},{10,... | collective-permute-start | bytes 4718600 | tf_op jit(solution)/shard_map/ppermute | solution.py:300
  18.2 4.8 %copy-start.10 = (f32[512,768]{1,0:T(8,128)}, f32[512,768]{1,0:T(8,128)S(1)}, u32[]{:S(2)}) copy-start(f32[512,768]{1,0:T(8,128)S(1)} %get-tuple-element.44) | copy-start | bytes 4718596
  18.2 40.8 %collective-permute-start.9 = (f32[512,768]{1,0:T(8,128)}, f32[512,768]{1,0:T(8,128)}, u32[]{:S(2)}, u32[]{:S(2)}) collective-permute-start(f32[512,768]{1,0:T(8,128)} %get-tuple-element.45), channel_id=1, source_target_pairs={{0,4},{1,5},{2,6},{3,7},{4,0},{5,1},{6,2},{7,3},{8,12},{9,13},{10,... | collective-permute-start | bytes 4718600 | tf_op jit(solution)/shard_map/ppermute | solution.py:300
  23.1 1.2 copy-start.12
  24.2 36.7 %collective-permute-start.8 = (f32[512,768]{1,0:T(8,128)}, f32[512,768]{1,0:T(8,128)}, u32[]{:S(2)}, u32[]{:S(2)}) collective-permute-start(f32[512,768]{1,0:T(8,128)} %get-tuple-element.43), channel_id=1, source_target_pairs={{0,4},{1,5},{2,6},{3,7},{4,0},{5,1},{6,2},{7,3},{8,12},{9,13},{10,... | collective-permute-start | bytes 4718600 | tf_op jit(solution)/shard_map/ppermute | solution.py:300
  24.2 2.8 %copy-start.1 = (bf16[84,16,2304]{2,1,0:T(8,128)(2,1)S(1)}, bf16[84,16,2304]{2,1,0:T(8,128)(2,1)}, u32[]{:S(2)}) copy-start(bf16[84,16,2304]{2,1,0:T(8,128)(2,1)} %copy-done) | copy-start | bytes 18579460
  27.0 2.3 %copy-start.2 = (bf16[3,3,256,1024]{3,2,1,0:T(8,128)(2,1)S(1)}, bf16[3,3,256,1024]{3,2,1,0:T(8,128)(2,1)}, u32[]{:S(2)}) copy-start(bf16[3,3,256,1024]{3,2,1,0:T(8,128)(2,1)} %param.7) | copy-start | bytes 14155780
  42.2 16.8 %copy-start.4 = (bf16[1344,1024]{1,0:T(8,128)(2,1)}, bf16[1344,1024]{1,0:T(8,128)(2,1)S(1)}, u32[]{:S(2)}) copy-start(bf16[1344,1024]{1,0:T(8,128)(2,1)S(1)} %get-tuple-element.38.dev) | copy-start | bytes 8257540
  42.2 15.1 %copy-start.9 = (f32[512,768]{1,0:T(8,128)S(1)}, f32[512,768]{1,0:T(8,128)}, u32[]{:S(2)}) copy-start(f32[512,768]{1,0:T(8,128)} %copy-done.8) | copy-start | bytes 4718596
  42.3 1.6 %collective-permute-start = (f32[72,512]{1,0:T(8,128)S(1)}, f32[72,512]{1,0:T(8,128)S(1)}, u32[]{:S(2)}, u32[]{:S(2)}) collective-permute-start(f32[72,512]{1,0:T(8,128)S(1)} %slice_select_fusion), channel_id=1, source_target_pairs={{0,4},{1,5},{2,6},{3,7},{4,0},{5,1},{6,2},{7,3},{8,12},{9,13},{10,... | collective-permute-start | bytes 442376 | tf_op jit(solution)/shard_map/ppermute | solution.py:300
  43.9 5.2 %collective-permute-start.1 = (f32[72,512]{1,0:T(8,128)S(1)}, f32[72,512]{1,0:T(8,128)S(1)}, u32[]{:S(2)}, u32[]{:S(2)}) collective-permute-start(f32[72,512]{1,0:T(8,128)S(1)} %select_add_fusion), channel_id=1, source_target_pairs={{0,1},{1,0},{2,3},{3,2},{4,7},{5,6},{6,5},{7,4},{8,9},{9,8},{10,11... | collective-permute-start | bytes 442376 | tf_op jit(solution)/shard_map/ppermute | solution.py:300
  49.1 6.4 %collective-permute-start.2 = (f32[72,512]{1,0:T(8,128)S(1)}, f32[72,512]{1,0:T(8,128)S(1)}, u32[]{:S(2)}, u32[]{:S(2)}) collective-permute-start(f32[72,512]{1,0:T(8,128)S(1)} %add.79), channel_id=1, source_target_pairs={{0,3},{1,2},{2,1},{3,0},{4,5},{5,4},{6,7},{7,6},{8,11},{9,10},{10,... | collective-permute-start | bytes 442376 | tf_op jit(solution)/shard_map/ppermute | solution.py:300
  55.6 9.1 %collective-permute-start.3 = (f32[72,512]{1,0:T(8,128)S(1)}, f32[72,512]{1,0:T(8,128)S(1)}, u32[]{:S(2)}, u32[]{:S(2)}) collective-permute-start(f32[72,512]{1,0:T(8,128)S(1)} %add.80), channel_id=1, source_target_pairs={{0,8},{1,9},{2,10},{3,11},{4,28},{5,29},{6,30},{7,31},{8,0},{9,1},... | collective-permute-start | bytes 442376 | tf_op jit(solution)/shard_map/ppermute | solution.py:300
  57.3 1.9 %copy-start.11 = (f32[512,768]{1,0:T(8,128)S(1)}, f32[512,768]{1,0:T(8,128)}, u32[]{:S(2)}) copy-start(f32[512,768]{1,0:T(8,128)} %copy-done.10) | copy-start | bytes 4718596
  59.2 1.9 %copy-start.13 = (f32[512,768]{1,0:T(8,128)S(1)}, f32[512,768]{1,0:T(8,128)}, u32[]{:S(2)}) copy-start(f32[512,768]{1,0:T(8,128)} %copy-done.12) | copy-start | bytes 4718596
  62.7 21.6 %collective-permute-start.13 = (f32[2,2,2,2,2,8,768]{6,5,4,3,2,1,0:T(8,128)S(1)}, f32[2,2,2,2,2,8,768]{6,5,4,3,2,1,0:T(8,128)S(1)}, u32[]{:S(2)}, u32[]{:S(2)}) collective-permute-start(f32[2,2,2,2,2,8,768]{6,5,4,3,2,1,0:T(8,128)S(1)} %slice_bitcast_fusion.4), channel_id=1, source_target_pairs={{0,32},{1,33},{2,34},{3,35},{4,100},{5,101},{6,102},{7,103},{8,40}... | collective-permute-start | bytes 2359304 | tf_op jit(solution)/shard_map/ppermute | solution.py:300
  64.8 7.8 %collective-permute-start.4 = (f32[72,512]{1,0:T(8,128)S(1)}, f32[72,512]{1,0:T(8,128)S(1)}, u32[]{:S(2)}, u32[]{:S(2)}) collective-permute-start(f32[72,512]{1,0:T(8,128)S(1)} %add.81), channel_id=1, source_target_pairs={{0,24},{1,25},{2,26},{3,27},{4,12},{5,13},{6,14},{7,15},{8,16},{9,... | collective-permute-start | bytes 442376 | tf_op jit(solution)/shard_map/ppermute | solution.py:300
  67.1 17.4 %collective-permute-start.12 = (f32[2,2,2,2,2,8,768]{6,5,4,2,1,3,0:T(8,128)S(1)}, f32[2,2,2,2,2,8,768]{6,5,4,2,1,3,0:T(8,128)S(1)}, u32[]{:S(2)}, u32[]{:S(2)}) collective-permute-start(f32[2,2,2,2,2,8,768]{6,5,4,2,1,3,0:T(8,128)S(1)} %slice_bitcast_fusion), channel_id=1, source_target_pairs={{0,8},{1,9},{2,10},{3,11},{4,28},{5,29},{6,30},{7,31},{8,0},{9,1},... | collective-permute-start | bytes 2359304 | tf_op jit(solution)/shard_map/ppermute | solution.py:300
  72.5 5.2 %collective-permute-start.5 = (f32[72,512]{1,0:T(8,128)S(1)}, f32[72,512]{1,0:T(8,128)S(1)}, u32[]{:S(2)}, u32[]{:S(2)}) collective-permute-start(f32[72,512]{1,0:T(8,128)S(1)} %add.82), channel_id=1, source_target_pairs={{0,32},{1,33},{2,34},{3,35},{4,100},{5,101},{6,102},{7,103},{8,40}... | collective-permute-start | bytes 442376 | tf_op jit(solution)/shard_map/ppermute | solution.py:300
  73.0 12.1 %collective-permute-start.11 = (f32[2,2,2,2,2,8,768]{6,5,4,3,1,0,2:T(8,128)S(1)}, f32[2,2,2,2,2,8,768]{6,5,4,3,1,0,2:T(8,128)S(1)}, u32[]{:S(2)}, u32[]{:S(2)}) collective-permute-start(f32[2,2,2,2,2,8,768]{6,5,4,3,1,0,2:T(8,128)S(1)} %slice_bitcast_fusion.2), channel_id=1, source_target_pairs={{0,1},{1,0},{2,3},{3,2},{4,7},{5,6},{6,5},{7,4},{8,9},{9,8},{10,11... | collective-permute-start | bytes 2359304 | tf_op jit(solution)/shard_map/ppermute | solution.py:300
  77.8 6.4 %collective-permute-start.6 = (f32[72,512]{1,0:T(8,128)S(1)}, f32[72,512]{1,0:T(8,128)S(1)}, u32[]{:S(2)}, u32[]{:S(2)}) collective-permute-start(f32[72,512]{1,0:T(8,128)S(1)} %add.83), channel_id=1, source_target_pairs={{0,96},{1,97},{2,98},{3,99},{4,36},{5,37},{6,38},{7,39},{8,104},{9... | collective-permute-start | bytes 442376 | tf_op jit(solution)/shard_map/ppermute | solution.py:300
  84.3 23.2 %collective-permute-start.7 = (f32[72,512]{1,0:T(8,128)S(1)}, f32[72,512]{1,0:T(8,128)}, u32[]{:S(2)}, u32[]{:S(2)}) collective-permute-start(f32[72,512]{1,0:T(8,128)S(1)} %add.84), channel_id=1, source_target_pairs={{0,4},{1,5},{2,6},{3,7},{4,0},{5,1},{6,2},{7,3},{8,12},{9,13},{10,... | collective-permute-start | bytes 442376 | tf_op jit(solution)/shard_map/ppermute | solution.py:300
  85.3 7.9 %collective-permute-start.16 = (f32[2,2,2,2,8,768]{5,4,3,2,1,0:T(8,128)S(1)}, f32[2,2,2,2,8,768]{5,4,3,2,1,0:T(8,128)S(1)}, u32[]{:S(2)}, u32[]{:S(2)}) collective-permute-start(f32[2,2,2,2,8,768]{5,4,3,2,1,0:T(8,128)S(1)} %slice_bitcast_fusion.6), channel_id=1, source_target_pairs={{0,1},{1,0},{2,3},{3,2},{4,7},{5,6},{6,5},{7,4},{8,9},{9,8},{10,11... | collective-permute-start | bytes 1179656 | tf_op jit(solution)/shard_map/ppermute | solution.py:300
  85.4 7.9 %collective-permute-start.15 = (f32[2,2,2,2,8,768]{5,4,3,1,0,2:T(8,128)S(1)}, f32[2,2,2,2,8,768]{5,4,3,1,0,2:T(8,128)S(1)}, u32[]{:S(2)}, u32[]{:S(2)}) collective-permute-start(f32[2,2,2,2,8,768]{5,4,3,1,0,2:T(8,128)S(1)} %slice_bitcast_fusion.7), channel_id=1, source_target_pairs={{0,32},{1,33},{2,34},{3,35},{4,100},{5,101},{6,102},{7,103},{8,40}... | collective-permute-start | bytes 1179656 | tf_op jit(solution)/shard_map/ppermute | solution.py:300
  87.2 7.9 %collective-permute-start.14 = (f32[2,2,2,2,8,768]{5,4,3,2,1,0:T(8,128)S(1)}, f32[2,2,2,2,8,768]{5,4,3,2,1,0:T(8,128)S(1)}, u32[]{:S(2)}, u32[]{:S(2)}) collective-permute-start(f32[2,2,2,2,8,768]{5,4,3,2,1,0:T(8,128)S(1)} %slice_bitcast_fusion.8), channel_id=1, source_target_pairs={{0,8},{1,9},{2,10},{3,11},{4,28},{5,29},{6,30},{7,31},{8,0},{9,1},... | collective-permute-start | bytes 1179656 | tf_op jit(solution)/shard_map/ppermute | solution.py:300
  95.1 5.7 %collective-permute-start.19 = (f32[2,2,2,8,768]{4,3,2,1,0:T(8,128)S(1)}, f32[2,2,2,8,768]{4,3,2,1,0:T(8,128)S(1)}, u32[]{:S(2)}, u32[]{:S(2)}) collective-permute-start(f32[2,2,2,8,768]{4,3,2,1,0:T(8,128)S(1)} %slice_bitcast_fusion.12), channel_id=1, source_target_pairs={{0,8},{1,9},{2,10},{3,11},{4,28},{5,29},{6,30},{7,31},{8,0},{9,1},... | collective-permute-start | bytes 589832 | tf_op jit(solution)/shard_map/ppermute | solution.py:300
  95.2 5.7 %collective-permute-start.18 = (f32[2,2,2,8,768]{4,3,2,1,0:T(8,128)S(1)}, f32[2,2,2,8,768]{4,3,2,1,0:T(8,128)S(1)}, u32[]{:S(2)}, u32[]{:S(2)}) collective-permute-start(f32[2,2,2,8,768]{4,3,2,1,0:T(8,128)S(1)} %slice_bitcast_fusion.13), channel_id=1, source_target_pairs={{0,1},{1,0},{2,3},{3,2},{4,7},{5,6},{6,5},{7,4},{8,9},{9,8},{10,11... | collective-permute-start | bytes 589832 | tf_op jit(solution)/shard_map/ppermute | solution.py:300
  97.3 5.8 %collective-permute-start.17 = (f32[2,2,2,8,768]{4,3,2,1,0:T(8,128)S(1)}, f32[2,2,2,8,768]{4,3,2,1,0:T(8,128)S(1)}, u32[]{:S(2)}, u32[]{:S(2)}) collective-permute-start(f32[2,2,2,8,768]{4,3,2,1,0:T(8,128)S(1)} %slice_bitcast_fusion.14), channel_id=1, source_target_pairs={{0,32},{1,33},{2,34},{3,35},{4,100},{5,101},{6,102},{7,103},{8,40}... | collective-permute-start | bytes 589832 | tf_op jit(solution)/shard_map/ppermute | solution.py:300
  103.1 0.8 copy-start.17
  104.7 8.1 %collective-permute-start.20 = (f32[2,2,3,8,768]{4,3,1,0,2:T(8,128)}, f32[2,2,3,8,768]{4,3,1,0,2:T(8,128)S(1)}, u32[]{:S(2)}, u32[]{:S(2)}) collective-permute-start(f32[2,2,3,8,768]{4,3,1,0,2:T(8,128)} %slice_bitcast_fusion.9), channel_id=1, source_target_pairs={{0,3},{1,2},{2,1},{3,0},{4,5},{5,4},{6,7},{7,6},{8,11},{9,10},{10,... | collective-permute-start | bytes 884744 | tf_op jit(solution)/shard_map/ppermute | solution.py:300
  107.5 9.2 %copy-start.7 = (f32[16,64,64]{2,1,0:T(8,128)S(1)}, f32[16,64,64]{2,1,0:T(8,128)}, u32[]{:S(2)}) copy-start(f32[16,64,64]{2,1,0:T(8,128)} %vectors.3) | copy-start | bytes 786436
  107.5 9.2 %copy-start.16 = (bf16[4,256,256]{2,1,0:T(8,128)(2,1)S(1)}, bf16[4,256,256]{2,1,0:T(8,128)(2,1)}, u32[]{:S(2)}) copy-start(bf16[4,256,256]{2,1,0:T(8,128)(2,1)} %copy-done.15) | copy-start | bytes 1572868
  113.9 17.7 %collective-permute-start.21 = (f32[2,3,8,768]{3,2,0,1:T(8,128)S(1)}, f32[2,3,8,768]{3,2,0,1:T(8,128)S(1)}, u32[]{:S(2)}, u32[]{:S(2)}) collective-permute-start(f32[2,3,8,768]{3,2,0,1:T(8,128)S(1)} %slice_bitcast_fusion.15), channel_id=1, source_target_pairs={{0,24},{1,25},{2,26},{3,27},{4,12},{5,13},{6,14},{7,15},{8,16},{9,... | collective-permute-start | bytes 442376 | tf_op jit(solution)/shard_map/ppermute | solution.py:300
  116.7 1.8 %copy-start.5 = (bf16[1344,1024]{1,0:T(8,128)(2,1)S(1)}, bf16[1344,1024]{1,0:T(8,128)(2,1)}, u32[]{:S(2)}) copy-start(bf16[1344,1024]{1,0:T(8,128)(2,1)} %copy-done.4) | copy-start | bytes 8257540
  131.6 5.6 %collective-permute-start.22 = (f32[3,8,768]{2,1,0:T(8,128)S(1)}, f32[3,8,768]{2,1,0:T(8,128)S(1)}, u32[]{:S(2)}, u32[]{:S(2)}) collective-permute-start(f32[3,8,768]{2,1,0:T(8,128)S(1)} %slice_bitcast_fusion.17), channel_id=1, source_target_pairs={{0,96},{1,97},{2,98},{3,99},{4,36},{5,37},{6,38},{7,39},{8,104},{9... | collective-permute-start | bytes 221192 | tf_op jit(solution)/shard_map/ppermute | solution.py:300

commit v3 on v2

v3 whole, which is shorter than its diff:
```python
import functools

import jax
import jax.numpy as jnp
import numpy as np
from jax import lax
from jax.experimental import pallas as pl
from jax.experimental.pallas import tpu as pltpu
from jax.sharding import Mesh
from jax.sharding import PartitionSpec as P

ALL = ("z", "y", "c", "x")
SIZE = {"z": 4, "y": 4, "c": 2, "x": 4}
STRIDE = {"z": 32, "y": 8, "c": 4, "x": 1}
RING = ((0, 3, 1, 2), (0, 1, 3, 2))
F32 = jnp.float32
BF16 = jnp.bfloat16
IMAGES, H, W, D, O = 6, 14, 14, 1024, 256
ROWS = IMAGES * H * 16
PIXELS = IMAGES * H * W
TOTAL = 128.0 * PIXELS
ON_CHIP = pl.BlockSpec(memory_space=pltpu.VMEM)
IN_HBM = pl.BlockSpec(memory_space=pltpu.HBM)


def nt(a, b):
    return lax.dot_general(
        a, b, (((1,), (1,)), ((), ())), preferred_element_type=F32
    )


def tn(a, b):
    return lax.dot_general(
        a, b, (((0,), (0,)), ((), ())), preferred_element_type=F32
    )


def nn(a, b):
    return lax.dot_general(
        a, b, (((1,), (0,)), ((), ())), preferred_element_type=F32
    )


def same_group():
    row = lax.broadcasted_iota(jnp.int32, (256, 256), 0)
    col = lax.broadcasted_iota(jnp.int32, (256, 256), 1)
    return (row >> 6) == (col >> 6)


def block_vectors(vectors, z, same):
    four = vectors[4 * z : 4 * z + 4].reshape(256, 64)
    return jnp.where(same, jnp.concatenate([four, four, four, four], axis=1), 0.0)


def value_row(values, z):
    return jnp.concatenate([values[4 * z + g : 4 * z + g + 1, :] for g in range(4)], axis=1)


def columns_of(rows):
    rows = rows + [jnp.zeros((1, 256), F32)] * (8 - len(rows))
    return jnp.concatenate(rows, axis=0).T


def pieces(a, n):
    out = []
    for _ in range(n):
        out.append(a.astype(BF16))
        a = a - out[-1].astype(F32)
    return out


def fine(dot, a, b):
    a_high, a_low = pieces(a, 2)
    b_high, b_low = pieces(b, 2)
    return dot(a_high, b_high) + (dot(a_high, b_low) + dot(a_low, b_high))


def place():
    core = lax.axis_index("c")
    spots = ([], [])
    for axis in "zyx":
        i = lax.axis_index(axis)
        a, b = (i ^ (i >> 1)) & 1, i >> 1
        spots[0].append(2 * a + b)
        spots[1].append(2 * b + a)
    return core, spots


def prep_kernel(
    features_hbm,
    grads_hbm,
    vectors_hbm,
    values,
    cols,
    xc,
    wht,
    u,
    sums,
    whiten,
    wide,
    wp32,
    features,
    grads,
    vectors,
    arrived,
):
    copies = [
        pltpu.make_async_copy(source, target, arrived.at[k])
        for k, (source, target) in enumerate(
            ((vectors_hbm, vectors), (grads_hbm, grads), (features_hbm, features))
        )
    ]
    for copy in copies:
        copy.start()
    core, spots = place()
    same = same_group()
    wide[...] = jnp.zeros_like(wide)
    xc[...] = jnp.zeros_like(xc)
    wht[1024:1040, :] = jnp.ones((16, ROWS), BF16)
    copies[0].wait()
    for z in range(4):
        basis = block_vectors(vectors, z, same)
        scale = lax.rsqrt(value_row(values, z))
        full = fine(nt, basis * scale, basis)
        whiten[z] = full.astype(BF16)
        for c in range(2):
            at_z, at_y, at_x = spots[c]
            for row, (y, x) in enumerate((y, x) for y in RING[c] for x in RING[c]):
                channel = y * 64 + c * 32 + x * 8
                row = pl.multiple_of(8 * (row ^ (4 * at_y + at_x)), 8)
                wp32[4 * c + z, pl.ds(row, 8), :] = full[channel : channel + 8, :]
    copies[1].wait()
    inside = lax.broadcasted_iota(jnp.int32, (H, 16, O), 1) < W
    for b in range(IMAGES):
        wide[:, 8 : 8 + W, :] = grads[b].astype(F32)
        for c in range(3):
            shifted = wide[:, 9 - c : 25 - c, :]
            if c == 2:
                shifted = jnp.where(inside, shifted, 0.0)
            shifted = shifted.astype(BF16)
            for a in range(3):
                lane = (3 * a + c) * O
                first, last = b * H + max(0, a - 1), b * H + H - max(0, 1 - a)
                start = max(0, 1 - a)
                cols[first:last, :, lane : lane + O] = shifted[start : start + last - first]
                if a == 0:
                    cols[b * H + H - 1, :, lane : lane + O] = jnp.zeros((16, O), BF16)
                if a == 2:
                    cols[b * H, :, lane : lane + O] = jnp.zeros((16, O), BF16)
    copies[2].wait()
    total = jnp.zeros((1, D), F32)
    for b in range(IMAGES):
        total = total + jnp.sum(
            jnp.sum(features[b].astype(F32), axis=0), axis=0, keepdims=True
        )
    sums[...] = total
    mean = total * (1.0 / PIXELS)
    for b in range(IMAGES):
        xc[b * H : b * H + H, 0:W, :] = (features[b].astype(F32) - mean[None]).astype(BF16)
    high, middle, low = pieces(mean, 3)
    pad = lax.broadcasted_iota(jnp.int32, (16, D), 0)
    head = xc[0].astype(F32)
    head = jnp.where(pad == 14, high.astype(F32), jnp.where(pad == 15, middle.astype(F32), head))
    xc[0] = head.astype(BF16)
    head = xc[1].astype(F32)
    xc[1] = jnp.where(pad == 14, low.astype(F32), head).astype(BF16)
    for k in range(8):
        c, z = k // 4, k % 4
        chunk = xc[:, :, 256 * z : 256 * z + 256].reshape(ROWS, 256)
        part = nt(wp32[k].astype(BF16), chunk)
        row = 4 * (c ^ core) + (RING[c].index(z) ^ spots[c][0])
        row = pl.multiple_of(128 * row, 128)
        wht[pl.ds(row, 128), :] = part.astype(BF16)
        shift = part[:, 14:15] + part[:, 15:16] + part[:, 30:31]
        u[pl.ds(row, 128), :] = jnp.broadcast_to(shift, (128, 128))


def prep(features, grads, vectors, values):
    return pl.pallas_call(
        prep_kernel,
        out_shape=(
            jax.ShapeDtypeStruct((IMAGES * H, 16, 9 * O), BF16),
            jax.ShapeDtypeStruct((IMAGES * H, 16, D), BF16),
            jax.ShapeDtypeStruct((1040, ROWS), BF16),
            jax.ShapeDtypeStruct((1024, 128), F32),
            jax.ShapeDtypeStruct((1, D), F32),
            jax.ShapeDtypeStruct((4, 256, 256), BF16),
        ),
        in_specs=[IN_HBM] * 3 + [ON_CHIP],
        out_specs=(ON_CHIP,) * 6,
        scratch_shapes=[
            pltpu.VMEM((H, 32, O), F32),
            pltpu.VMEM((8, 128, 256), F32),
            pltpu.VMEM((IMAGES, H, W, D), BF16),
            pltpu.VMEM((IMAGES, H, W, O), BF16),
            pltpu.VMEM((16, 64, 64), F32),
            pltpu.SemaphoreType.DMA((3,)),
        ],
        compiler_params=pltpu.CompilerParams(vmem_limit_bytes=10 << 20),
        name="prep",
    )(features, grads, vectors, values)


def weight_kernel(a, wht, cols, u, keep, send, colsum):
    for n in range(3):
        start = 768 * a + 256 * n
        full = nn(wht[...], cols[:, start : start + 256])
        colsum[:, 256 * n : 256 * n + 256] = full[1024:1032, :]
        for k in range(2):
            ones = full[1024:1025, 128 * k : 128 * k + 128]
            lanes = slice(256 * n + 128 * k, 256 * n + 128 * k + 128)
            part = full[0:1024, 128 * k : 128 * k + 128] + u[...] * ones
            keep[:, lanes] = part[0:512]
            send[:, lanes] = part[512:1024]


def weight_part(wht, cols, u, a):
    return pl.pallas_call(
        functools.partial(weight_kernel, a),
        in_specs=[ON_CHIP] * 3,
        out_specs=(ON_CHIP,) * 3,
        out_shape=(
            jax.ShapeDtypeStruct((512, 768), F32),
            jax.ShapeDtypeStruct((512, 768), F32),
            jax.ShapeDtypeStruct((8, 768), F32),
        ),
        compiler_params=pltpu.CompilerParams(vmem_limit_bytes=6 << 20),
        name=f"weight_part_{a}",
    )(wht, cols, u)


def back_kernel(
    cols,
    kernel_hbm,
    xc,
    sums,
    sum0,
    sum1,
    sum2,
    vectors,
    values,
    dev,
    payload,
    mine,
    theirs,
    bases,
    factors,
    kernel,
    arrived,
):
    copies = [
        pltpu.make_async_copy(
            kernel_hbm.at[:, pl.ds(256 * z, 256)], kernel.at[z], arrived.at[z]
        )
        for z in range(4)
    ]
    for copy in copies:
        copy.start()
    same = same_group()
    real = (lax.broadcasted_iota(jnp.int32, (ROWS, 256), 0) & 15) < W
    group = lax.broadcasted_iota(jnp.int32, (64, 256), 1) >> 6
    row = lax.broadcasted_iota(jnp.int32, (8, 256), 0)
    for z in range(4):
        lanes = slice(256 * z, 256 * z + 256)
        copies[z].wait()
        back = nn(cols[...], kernel[z])
        total = jnp.sum(back, axis=0, keepdims=True)
        low = jnp.where(real, back - total * (1.0 / PIXELS), 0.0).astype(BF16)
        dev[:, lanes] = low
        value = value_row(values, z)
        scale, root = lax.rsqrt(value), jnp.sqrt(value)
        tall = columns_of([sums[:, lanes] * (1.0 / PIXELS), scale, root])
        cov = tn(xc[:, lanes], low) + tall[:, 0:1] * total
        packed = cov[0:64]
        for k in range(1, 4):
            packed = jnp.where(group == k, cov[64 * k : 64 * k + 64], packed)
        payload[0:64, lanes] = packed
        tail = jnp.where(row == 0, total, jnp.where(row == 1, sums[:, lanes], 0.0))
        if z < 3:
            for a, part in enumerate((sum0, sum1, sum2)):
                tail = jnp.where(row == 2 + a, part[0:1, lanes], tail)
        payload[64:72, lanes] = tail
        bases[z] = block_vectors(vectors, z, same)
        factor = -(tall[:, 1:2] * scale) / (tall[:, 2:3] + root)
        factors[z] = jnp.where(same, factor, 0.0)
    for c in range(2):

        @pl.when(lax.axis_index("c") == c)
        def _():
            mine[...] = payload[:, 512 * c : 512 * c + 512]
            theirs[...] = payload[:, 512 - 512 * c : 1024 - 512 * c]


def back_part(cols, kernel, xc, sums, colsums, vectors, values):
    return pl.pallas_call(
        back_kernel,
        in_specs=[ON_CHIP, IN_HBM] + [ON_CHIP] * 7,
        out_specs=(ON_CHIP,) * 6,
        out_shape=(
            jax.ShapeDtypeStruct((ROWS, D), BF16),
            jax.ShapeDtypeStruct((72, D), F32),
            jax.ShapeDtypeStruct((72, 512), F32),
            jax.ShapeDtypeStruct((72, 512), F32),
            jax.ShapeDtypeStruct((4, 256, 256), F32),
            jax.ShapeDtypeStruct((4, 256, 256), F32),
        ),
        scratch_shapes=[
            pltpu.VMEM((4, 9 * O, 256), BF16),
            pltpu.SemaphoreType.DMA((4,)),
        ],
        compiler_params=pltpu.CompilerParams(vmem_limit_bytes=14 << 20),
        name="back_part",
    )(cols, kernel, xc, sums, *colsums, vectors, values)


def final_kernel(
    dev,
    xc,
    mine,
    theirs,
    own,
    bases,
    factors,
    whiten,
    out,
    fix,
    payload,
    shift,
    sigma,
    row_vector,
):
    image = pl.program_id(0)

    @pl.when(image == 0)
    def _():
        for c in range(2):

            @pl.when(lax.axis_index("c") == c)
            def _():
                payload[:, 512 * c : 512 * c + 512] = mine[...]
                payload[:, 512 - 512 * c : 1024 - 512 * c] = theirs[...]

        for z in range(4):
            lanes = slice(256 * z, 256 * z + 256)
            basis = bases[z]
            total = payload[64:65, lanes]
            mean = payload[65:66, lanes] * (1.0 / TOTAL)
            stack = payload[0:64, lanes]
            raw = jnp.concatenate([stack, stack, stack, stack], axis=0)
            cov = raw - columns_of([mean])[:, 0:1] * total
            rotated = fine(nn, fine(tn, basis, cov), basis)
            inner = 0.5 * (rotated + rotated.T) * factors[z]
            grad = fine(nt, fine(nn, basis, inner), basis)
            sigma[z] = (grad * (2.0 / TOTAL)).astype(BF16)
            moved = own[64:65, lanes] * (1.0 / PIXELS) - total * (1.0 / TOTAL)
            offset = own[65:66, lanes] * (1.0 / PIXELS) - mean
            empty = [jnp.zeros((1, 256), BF16)]
            stacked = jnp.concatenate(pieces(moved, 3) + pieces(mean, 3) + empty * 2, axis=0)
            through = nn(stacked, whiten[z])
            stacked = jnp.concatenate(pieces(offset, 3) + empty * 5, axis=0)
            other = nn(stacked, sigma[z])
            row_vector[0:1, lanes] = (
                jnp.sum(through[0:3], axis=0, keepdims=True)
                + jnp.sum(other[0:3], axis=0, keepdims=True)
            )
            shift[0:1, lanes] = jnp.sum(through[3:6], axis=0, keepdims=True)
        first = 8 * sum(STRIDE[axis] * lax.axis_index(axis) for axis in ALL)
        lane = lax.broadcasted_iota(jnp.int32, (8, D), 1)
        row = lax.broadcasted_iota(jnp.int32, (8, D), 0)
        chosen = jnp.where(lane == row + first, shift[...], 0.0)
        chosen = jnp.sum(chosen, axis=1, keepdims=True)
        for a in range(3):
            fix[a] = chosen * payload[66 + a : 67 + a, 0:768]

    rows = pl.ds(pl.multiple_of(image * (H * 16), H * 16), H * 16)
    for z in range(4):
        lanes = slice(256 * z, 256 * z + 256)
        result = nn(dev[rows, lanes], whiten[z]) + nn(xc[rows, lanes], sigma[z])
        result = result + row_vector[0:1, lanes]
        out[0, :, :, lanes] = result.astype(BF16).reshape(H, 16, 256)[:, 0:W, :]


def final_part(dev, xc, mine, theirs, own, bases, factors, whiten):
    return pl.pallas_call(
        final_kernel,
        grid=(IMAGES,),
        in_specs=[ON_CHIP] * 8,
        out_specs=(pl.BlockSpec((1, H, W, D), lambda b: (b, 0, 0, 0)), ON_CHIP),
        out_shape=(
            jax.ShapeDtypeStruct((IMAGES, H, W, D), BF16),
            jax.ShapeDtypeStruct((3, 8, 768), F32),
        ),
        scratch_shapes=[
            pltpu.VMEM((72, D), F32),
            pltpu.VMEM((1, D), F32),
            pltpu.VMEM((4, 256, 256), BF16),
            pltpu.VMEM((1, D), F32),
        ],
        compiler_params=pltpu.CompilerParams(vmem_limit_bytes=10 << 20),
        name="final_part",
    )(dev, xc, mine, theirs, own, bases, factors, whiten)


def permutation(move):
    pairs = []
    for device in range(128):
        at = {k: (device // STRIDE[k]) % SIZE[k] for k in ALL}
        move(at)
        pairs.append((device, sum(at[k] * STRIDE[k] for k in ALL)))
    return pairs


def exchange(value, move):
    return lax.ppermute(value, ALL, permutation(move))


def other_core(at):
    at["c"] ^= 1


def ring(axis, step):
    def move(at):
        at[axis] ^= (1, 3)[(step + at["c"]) % 2]

    return move


def halves(value, dim):
    pick = lambda k: lax.index_in_dim(value, k, dim, keepdims=False)
    return pick(0), pick(1)


def local(features, grads, kernel, vectors, values):
    stay = lambda array: pltpu.with_memory_space_constraint(array, pltpu.HBM)
    cols, xc, wht, u, sums, whiten = prep(stay(features), stay(grads), stay(vectors), values)
    cols, xc = cols.reshape(ROWS, 9 * O), xc.reshape(ROWS, D)

    parts, colsums = [], []
    for a in range(3):
        keep, send, colsum = weight_part(wht, cols, u, a)
        colsums.append(colsum)
        parts.append((keep + exchange(send, other_core)).reshape(2, 2, 2, 2, 2, 2, 8, 768))
    cols, *parts = lax.optimization_barrier((cols, *parts))
    dev, own, mine, theirs, bases, factors = back_part(
        cols, stay(kernel.reshape(9 * O, D)), xc, sums, colsums, vectors, values
    )
    mine = mine + exchange(theirs, other_core)

    names = [["z1", "z2", "y1", "y2", "x1", "x2"] for _ in range(3)]
    for turn in range(3):
        for a in range(3):
            axis = "xyz"[(a + turn) % 3]
            dim = names[a].index(axis + "1")
            names[a].pop(dim)
            keep, send = halves(parts[a], dim)
            parts[a] = keep + exchange(send, ring(axis, 0))
        if turn == 0:
            mine, *parts = lax.optimization_barrier((mine, *parts))
            for axis in "xyz":
                for step in range(2):
                    mine = mine + exchange(mine, ring(axis, step))
            theirs = exchange(mine, other_core)
    share = jnp.stack(parts, axis=3)
    order = ["z", "y", "x"]
    for axis in "xyz":
        dim = order.index(axis)
        order.pop(dim)
        keep, send = halves(share, dim)
        share = keep + exchange(send, ring(axis, 1))

    input_grad, fix = final_part(dev, xc, mine, theirs, own, bases, factors, whiten)
    kernel_grad = (share - fix).transpose(1, 0, 2).reshape(8, 3, 3, O)
    return input_grad, kernel_grad


def solution(mesh):
    finer = Mesh(mesh.devices.reshape(4, 4, 2, 4), ALL)
    split_all = P(ALL, None, None, None)
    return jax.shard_map(
        local,
        mesh=finer,
        in_specs=(split_all, split_all, P(), P(), P()),
        out_specs=(split_all, split_all),
        check_vma=False,
    )
```

time: 138 us -> 99.9 us (0.72)
  local copies, waits for them, and re-layouts: 15.1 us -> 1.07 us
  starting transfers between devices: 28.7 us -> 19.5 us
  waiting for transfers between devices: 41.6 us -> 34.5 us
  other arithmetic: 8.5 us -> 2.07 us
  Pallas kernels: 43.1 us -> 41.5 us
    unnamed x36 -> x4, local copies, waits for them, and re-layouts: 13.2 us -> 0.7 us
    ppermute x23, starting transfers between devices: 28.7 us -> 19.5 us  [exchange(): return lax.ppermute(value, ALL, permutation(move))]
    ppermute x23, waiting for transfers between devices: 41.6 us -> 34.5 us  [exchange(): return lax.ppermute(value, ALL, permutation(move))]
    add x3, other arithmetic: 4.92 us -> 0.56 us  [local(): keep + exchange(send, other_core)]
    pallas_call x3, Pallas kernels: 12.9 us -> 9.34 us  [weight_part(): pl.pallas_call(functools.partial(weight_kernel, a), in_specs=[ON_CHIP] *...]
  transfers between devices with their start and end apart: 23 -> 23, of which waited for: 15 -> 13; matrix products, arithmetic and copies ran while one was open for 6% -> 1% of each run, Pallas kernels for 25% -> 33%
where the time goes in v3:
time: 99.9 us; the launch traced here: 99.7 us
  Pallas kernels  41.5 us (42%)
  waiting for transfers between devices  34.5 us (35%)
  starting transfers between devices  19.5 us (20%)
  other arithmetic  2.07 us (2%)
  local copies, waits for them, and re-layouts  1.07 us (1%)
    ppermute x23, waiting for transfers between devices, exchange(): return lax.ppermute(value, ALL, permutation(move))  34.5 us
    ppermute x23, starting transfers between devices, exchange(): return lax.ppermute(value, ALL, permutation(move))  19.5 us
    pallas_call x1, Pallas kernels, back_part(): pl.pallas_call(back_kernel, in_specs=[ON_CHIP, IN_HBM] + [ON_CHIP] * 7, o...  18.3 us
    pallas_call x3, Pallas kernels, weight_part(): pl.pallas_call(functools.partial(weight_kernel, a), in_specs=[ON_CHIP] *...  9.34 us
    pallas_call x1, Pallas kernels, final_part(): pl.pallas_call(final_kernel, grid=(IMAGES,), in_specs=[ON_CHIP] * 8, out_...  8.79 us
    pallas_call x1, Pallas kernels, prep(): pl.pallas_call(prep_kernel, out_shape=(jax.ShapeDtypeStruct((IMAGES * H,...  5.12 us
  transfers between devices with their start and end apart: 23, of which 13 were waited for; matrix products, arithmetic and copies ran while one was open for 1% of the time, Pallas kernels for 33%

profile of v3, /device:TPU:0, one launch (start us, length us, event | category | flops | bytes accessed | tf_op | source)
XLA Modules:
  0.0 99.7 jit_solution(7694016157203325214)
XLA Ops:
  0.6 0.7 copy-done.1
  1.3 5.1 %prep.1 = (bf16[84,16,2304]{2,1,0:T(8,128)(2,1)S(1)}, bf16[84,16,1024]{2,1,0:T(8,128)(2,1)S(1)}, bf16[1040,1344]{1,0:T(8,128)(2,1)S(1)}, f32[1024,128]{1,0:T(8,1...) custom-call(bf16[6,14,14,1024]{3,2,1,0:T(8,128)(2,1)} %features_hbm.1, ...), custom_call_target="tpu_custom_call" | custom-call | tf_op jit(solution)/shard_map/prep/pallas_call | solution.py:179
  6.5 3.1 %weight_part_2.1 = (f32[512,768]{1,0:T(8,128)S(1)}, f32[512,768]{1,0:T(8,128)S(1)}, f32[8,768]{1,0:T(8,128)S(1)}) custom-call(bf16[1040,1344]{1,0:T(8,128)(2,1)S(1)} %get-tuple-element.34.wht, bf16[1344,2304]{1,0:T(8,128)(2,1)S(1)} %bitcast.89, f32[1024,128]{1,0:T(8,128)S(1)} %get-tuple-element.35.u), custom_call_target="tpu_custom_call" | custom-call | tf_op jit(solution)/shard_map/weight_part_2/pallas_call | solution.py:218
  9.6 0.1 collective-permute-start.2
  9.7 3.1 %weight_part_1.1 = (f32[512,768]{1,0:T(8,128)S(1)}, f32[512,768]{1,0:T(8,128)S(1)}, f32[8,768]{1,0:T(8,128)S(1)}) custom-call(bf16[1040,1344]{1,0:T(8,128)(2,1)S(1)} %get-tuple-element.34.wht, bf16[1344,2304]{1,0:T(8,128)(2,1)S(1)} %bitcast.90, f32[1024,128]{1,0:T(8,128)S(1)} %get-tuple-element.35.u), custom_call_target="tpu_custom_call" | custom-call | tf_op jit(solution)/shard_map/weight_part_1/pallas_call | solution.py:218
  12.8 0.6 collective-permute-start.1
  13.4 3.1 %weight_part_0.1 = (f32[512,768]{1,0:T(8,128)S(1)}, f32[512,768]{1,0:T(8,128)S(1)}, f32[8,768]{1,0:T(8,128)S(1)}) custom-call(bf16[1040,1344]{1,0:T(8,128)(2,1)S(1)} %get-tuple-element.34.wht, bf16[1344,2304]{1,0:T(8,128)(2,1)S(1)} %bitcast.91, f32[1024,128]{1,0:T(8,128)S(1)} %get-tuple-element.35.u), custom_call_target="tpu_custom_call" | custom-call | tf_op jit(solution)/shard_map/weight_part_0/pallas_call | solution.py:218
  16.5 0.1 collective-permute-start
  16.6 0.2 add.68
  16.8 0.2 add.67
  17.0 3.0 %collective-permute-done = f32[512,768]{1,0:T(8,128)S(1)} collective-permute-done((f32[512,768]{1,0:T(8,128)S(1)}, f32[512,768]{1,0:T(8,128)S(1)}, u32[]{:S(2)}, u32[]{:S(2)}) %collective-permute-start) | collective-permute-done | bytes 1572896 | tf_op jit(solution)/shard_map/ppermute | solution.py:414
  20.0 0.2 add.66
  20.3 2.1 %collective-permute-start.6 = (f32[2,2,2,2,2,8,768]{6,5,0,2,4,1,3:T(8,128)S(1)}, f32[2,2,2,2,2,8,768]{6,5,0,2,4,1,3:T(8,128)S(1)}, u32[]{:S(2)}, u32[]{:S(2)}) collective-permute-start(f32[2,2,2,2,2,8,768]{6,5,0,2,4,1,3:T(8,128)S(1)} %slice_bitcast_fusion), channel_id=1, source_target_pairs={{0,32},{1,33},{2,34},{3,35},{4,100},{5,101},{6,102},{7,103},{8,40}... | collective-permute-start | bytes 2359304 | tf_op jit(solution)/shard_map/ppermute | solution.py:414
  22.4 1.7 %collective-permute-start.5 = (f32[2,2,2,2,2,8,768]{6,5,1,2,4,3,0:T(8,128)S(1)}, f32[2,2,2,2,2,8,768]{6,5,1,2,4,3,0:T(8,128)S(1)}, u32[]{:S(2)}, u32[]{:S(2)}) collective-permute-start(f32[2,2,2,2,2,8,768]{6,5,1,2,4,3,0:T(8,128)S(1)} %slice_bitcast_fusion.2), channel_id=1, source_target_pairs={{0,8},{1,9},{2,10},{3,11},{4,28},{5,29},{6,30},{7,31},{8,0},{9,1},... | collective-permute-start | bytes 2359304 | tf_op jit(solution)/shard_map/ppermute | solution.py:414
  24.1 1.7 %collective-permute-start.4 = (f32[2,2,2,2,2,8,768]{6,5,1,3,4,0,2:T(8,128)S(1)}, f32[2,2,2,2,2,8,768]{6,5,1,3,4,0,2:T(8,128)S(1)}, u32[]{:S(2)}, u32[]{:S(2)}) collective-permute-start(f32[2,2,2,2,2,8,768]{6,5,1,3,4,0,2:T(8,128)S(1)} %slice_bitcast_fusion.4), channel_id=1, source_target_pairs={{0,1},{1,0},{2,3},{3,2},{4,7},{5,6},{6,5},{7,4},{8,9},{9,8},{10,11... | collective-permute-start | bytes 2359304 | tf_op jit(solution)/shard_map/ppermute | solution.py:414
  25.9 18.3 %back_part.1 = (bf16[1344,1024]{1,0:T(8,128)(2,1)S(1)}, f32[72,1024]{1,0:T(8,128)S(1)}, f32[72,512]{1,0:T(8,128)S(1)}, f32[72,512]{1,0:T(8,128)S(1)}, f32[4,256,...) custom-call(bf16[1344,2304]{1,0:T(8,128)(2,1)S(1)} %bitcast.92, bf16[2304,1024]{1,0:T(8,128)(2,1)} %bitcast.101, ...), custom_call_target="tpu_custom_call" | custom-call | tf_op jit(solution)/shard_map/back_part/pallas_call | solution.py:295
  44.2 4.2 %collective-permute-start.3 = (f32[72,512]{1,0:T(8,128)S(1)}, f32[72,512]{1,0:T(8,128)S(1)}, u32[]{:S(2)}, u32[]{:S(2)}) collective-permute-start(f32[72,512]{1,0:T(8,128)S(1)} %get-tuple-element.50), channel_id=1, source_target_pairs={{0,4},{1,5},{2,6},{3,7},{4,0},{5,1},{6,2},{7,3},{8,12},{9,13},{10,... | collective-permute-start | bytes 442376 | tf_op jit(solution)/shard_map/ppermute | solution.py:414
  48.4 1.0 %collective-permute-done.3 = f32[72,512]{1,0:T(8,128)S(1)} collective-permute-done((f32[72,512]{1,0:T(8,128)S(1)}, f32[72,512]{1,0:T(8,128)S(1)}, u32[]{:S(2)}, u32[]{:S(2)}) %collective-permute-start.3) | collective-permute-done | bytes 147488 | tf_op jit(solution)/shard_map/ppermute | solution.py:414
  49.4 0.1 fusion
  49.6 0.1 fusion.1
  49.7 0.1 fusion.2
  49.9 0.2 collective-permute-start.14
  50.1 0.2 collective-permute-start.7
  50.3 0.1 collective-permute-start.16
  50.4 4.8 %collective-permute-done.7 = f32[72,512]{1,0:T(8,128)S(1)} collective-permute-done((f32[72,512]{1,0:T(8,128)S(1)}, f32[72,512]{1,0:T(8,128)S(1)}, u32[]{:S(2)}, u32[]{:S(2)}) %collective-permute-start.7) | collective-permute-done | bytes 147488 | tf_op jit(solution)/shard_map/ppermute | solution.py:414
  55.2 0.6 collective-permute-start.8
  55.8 0.6 collective-permute-start.18
  56.4 6.8 %collective-permute-done.8 = f32[72,512]{1,0:T(8,128)S(1)} collective-permute-done((f32[72,512]{1,0:T(8,128)S(1)}, f32[72,512]{1,0:T(8,128)S(1)}, u32[]{:S(2)}, u32[]{:S(2)}) %collective-permute-start.8) | collective-permute-done | bytes 147488 | tf_op jit(solution)/shard_map/ppermute | solution.py:414
  63.3 2.0 %collective-permute-start.9 = (f32[72,512]{1,0:T(8,128)S(1)}, f32[72,512]{1,0:T(8,128)S(1)}, u32[]{:S(2)}, u32[]{:S(2)}) collective-permute-start(f32[72,512]{1,0:T(8,128)S(1)} %add.74), channel_id=1, source_target_pairs={{0,8},{1,9},{2,10},{3,11},{4,28},{5,29},{6,30},{7,31},{8,0},{9,1},... | collective-permute-start | bytes 442376 | tf_op jit(solution)/shard_map/ppermute | solution.py:414
  65.4 0.1 collective-permute-start.15
  65.8 0.2 collective-permute-start.19
  66.0 2.6 %collective-permute-done.9 = f32[72,512]{1,0:T(8,128)S(1)} collective-permute-done((f32[72,512]{1,0:T(8,128)S(1)}, f32[72,512]{1,0:T(8,128)S(1)}, u32[]{:S(2)}, u32[]{:S(2)}) %collective-permute-start.9) | collective-permute-done | bytes 147488 | tf_op jit(solution)/shard_map/ppermute | solution.py:414
  68.6 0.2 collective-permute-start.10
  68.8 2.4 %collective-permute-done.15 = f32[2,2,2,8,768]{4,3,0,1,2:T(8,128)S(1)} collective-permute-done((f32[2,2,2,8,768]{4,3,0,1,2:T(8,128)S(1)}, f32[2,2,2,8,768]{4,3,0,1,2:T(8,128)S(1)}, u32[]{:S(2)}, u32[]{:S(2)}) %collective-permute-start.15) | collective-permute-done | bytes 196640 | tf_op jit(solution)/shard_map/ppermute | solution.py:414
  71.2 0.2 collective-permute-done.17
  71.4 1.7 %collective-permute-done.19 = f32[2,2,2,8,768]{4,3,0,1,2:T(8,128)S(1)} collective-permute-done((f32[2,2,2,8,768]{4,3,0,1,2:T(8,128)S(1)}, f32[2,2,2,8,768]{4,3,0,1,2:T(8,128)S(1)}, u32[]{:S(2)}, u32[]{:S(2)}) %collective-permute-start.19) | collective-permute-done | bytes 196640 | tf_op jit(solution)/shard_map/ppermute | solution.py:414
  73.2 1.1 %collective-permute-start.20 = (f32[2,2,3,8,768]{4,3,2,0,1:T(8,128)S(1)}, f32[2,2,3,8,768]{4,3,2,0,1:T(8,128)S(1)}, u32[]{:S(2)}, u32[]{:S(2)}) collective-permute-start(f32[2,2,3,8,768]{4,3,2,0,1:T(8,128)S(1)} %slice_bitcast_fusion.9), channel_id=1, source_target_pairs={{0,3},{1,2},{2,1},{3,0},{4,5},{5,4},{6,7},{7,6},{8,11},{9,10},{10,... | collective-permute-start | bytes 884744 | tf_op jit(solution)/shard_map/ppermute | solution.py:414
  74.3 0.8 collective-permute-done.10
  75.1 0.1 collective-permute-start.11
  75.2 5.1 %collective-permute-done.11 = f32[72,512]{1,0:T(8,128)S(1)} collective-permute-done((f32[72,512]{1,0:T(8,128)S(1)}, f32[72,512]{1,0:T(8,128)S(1)}, u32[]{:S(2)}, u32[]{:S(2)}) %collective-permute-start.11) | collective-permute-done | bytes 147488 | tf_op jit(solution)/shard_map/ppermute | solution.py:414
  80.3 0.3 collective-permute-start.12
  80.6 0.6 collective-permute-done.20
  81.3 0.8 collective-permute-start.21
  82.1 4.7 %collective-permute-done.12 = f32[72,512]{1,0:T(8,128)S(1)} collective-permute-done((f32[72,512]{1,0:T(8,128)S(1)}, f32[72,512]{1,0:T(8,128)S(1)}, u32[]{:S(2)}, u32[]{:S(2)}) %collective-permute-start.12) | collective-permute-done | bytes 147488 | tf_op jit(solution)/shard_map/ppermute | solution.py:414
  86.9 0.8 collective-permute-done.21
  87.7 2.5 %collective-permute-start.22 = (f32[3,8,768]{2,1,0:T(8,128)S(1)}, f32[3,8,768]{2,1,0:T(8,128)S(1)}, u32[]{:S(2)}, u32[]{:S(2)}) collective-permute-start(f32[3,8,768]{2,1,0:T(8,128)S(1)} %slice_bitcast_fusion.19), channel_id=1, source_target_pairs={{0,96},{1,97},{2,98},{3,99},{4,36},{5,37},{6,38},{7,39},{8,104},{9... | collective-permute-start | bytes 221192 | tf_op jit(solution)/shard_map/ppermute | solution.py:414
  90.2 8.8 %final_part.1 = (bf16[6,14,14,1024]{3,2,1,0:T(8,128)(2,1)}, f32[3,8,768]{2,1,0:T(8,128)S(1)}) custom-call(bf16[1344,1024]{1,0:T(8,128)(2,1)S(1)} %get-tuple-element.48.dev, bf16[1344,1024]{1,0:T(8,128)(2,1)S(1)} %bitcast.94, f32[72,512]{1,0:T(8,128)S(1)} %add.78.mine, f32[72,512]{1,0:T(8,128)S(1)} %collective-permute-done.13.theirs, ...), custom_call_target="tpu_custom_call" | custom-call | tf_op jit(solution)/shard_map/final_part/pallas_call | solution.py:384
  99.0 0.6 fusion.12
  (43 shorter events, 1.1 us)
Async XLA Ops:
  0.6 0.7 copy-start.1
  9.6 7.0 %collective-permute-start.2 = (f32[512,768]{1,0:T(8,128)S(1)}, f32[512,768]{1,0:T(8,128)S(1)}, u32[]{:S(2)}, u32[]{:S(2)}) collective-permute-start(f32[512,768]{1,0:T(8,128)S(1)} %get-tuple-element.41), channel_id=1, source_target_pairs={{0,4},{1,5},{2,6},{3,7},{4,0},{5,1},{6,2},{7,3},{8,12},{9,13},{10,... | collective-permute-start | bytes 4718600 | tf_op jit(solution)/shard_map/ppermute | solution.py:414
  12.8 4.0 %collective-permute-start.1 = (f32[512,768]{1,0:T(8,128)S(1)}, f32[512,768]{1,0:T(8,128)S(1)}, u32[]{:S(2)}, u32[]{:S(2)}) collective-permute-start(f32[512,768]{1,0:T(8,128)S(1)} %get-tuple-element.39), channel_id=1, source_target_pairs={{0,4},{1,5},{2,6},{3,7},{4,0},{5,1},{6,2},{7,3},{8,12},{9,13},{10,... | collective-permute-start | bytes 4718600 | tf_op jit(solution)/shard_map/ppermute | solution.py:414
  16.5 3.5 %collective-permute-start = (f32[512,768]{1,0:T(8,128)S(1)}, f32[512,768]{1,0:T(8,128)S(1)}, u32[]{:S(2)}, u32[]{:S(2)}) collective-permute-start(f32[512,768]{1,0:T(8,128)S(1)} %get-tuple-element.37), channel_id=1, source_target_pairs={{0,4},{1,5},{2,6},{3,7},{4,0},{5,1},{6,2},{7,3},{8,12},{9,13},{10,... | collective-permute-start | bytes 4718600 | tf_op jit(solution)/shard_map/ppermute | solution.py:414
  20.2 5.7 %copy-start = (f32[16,64,64]{2,1,0:T(8,128)S(1)}, f32[16,64,64]{2,1,0:T(8,128)}, u32[]{:S(2)}) copy-start(f32[16,64,64]{2,1,0:T(8,128)} %vectors.1) | copy-start | bytes 786436
  20.3 29.2 %collective-permute-start.6 = (f32[2,2,2,2,2,8,768]{6,5,0,2,4,1,3:T(8,128)S(1)}, f32[2,2,2,2,2,8,768]{6,5,0,2,4,1,3:T(8,128)S(1)}, u32[]{:S(2)}, u32[]{:S(2)}) collective-permute-start(f32[2,2,2,2,2,8,768]{6,5,0,2,4,1,3:T(8,128)S(1)} %slice_bitcast_fusion), channel_id=1, source_target_pairs={{0,32},{1,33},{2,34},{3,35},{4,100},{5,101},{6,102},{7,103},{8,40}... | collective-permute-start | bytes 2359304 | tf_op jit(solution)/shard_map/ppermute | solution.py:414
  22.4 27.1 %collective-permute-start.5 = (f32[2,2,2,2,2,8,768]{6,5,1,2,4,3,0:T(8,128)S(1)}, f32[2,2,2,2,2,8,768]{6,5,1,2,4,3,0:T(8,128)S(1)}, u32[]{:S(2)}, u32[]{:S(2)}) collective-permute-start(f32[2,2,2,2,2,8,768]{6,5,1,2,4,3,0:T(8,128)S(1)} %slice_bitcast_fusion.2), channel_id=1, source_target_pairs={{0,8},{1,9},{2,10},{3,11},{4,28},{5,29},{6,30},{7,31},{8,0},{9,1},... | collective-permute-start | bytes 2359304 | tf_op jit(solution)/shard_map/ppermute | solution.py:414
  24.1 25.5 %collective-permute-start.4 = (f32[2,2,2,2,2,8,768]{6,5,1,3,4,0,2:T(8,128)S(1)}, f32[2,2,2,2,2,8,768]{6,5,1,3,4,0,2:T(8,128)S(1)}, u32[]{:S(2)}, u32[]{:S(2)}) collective-permute-start(f32[2,2,2,2,2,8,768]{6,5,1,3,4,0,2:T(8,128)S(1)} %slice_bitcast_fusion.4), channel_id=1, source_target_pairs={{0,1},{1,0},{2,3},{3,2},{4,7},{5,6},{6,5},{7,4},{8,9},{9,8},{10,11... | collective-permute-start | bytes 2359304 | tf_op jit(solution)/shard_map/ppermute | solution.py:414
  44.2 5.2 %collective-permute-start.3 = (f32[72,512]{1,0:T(8,128)S(1)}, f32[72,512]{1,0:T(8,128)S(1)}, u32[]{:S(2)}, u32[]{:S(2)}) collective-permute-start(f32[72,512]{1,0:T(8,128)S(1)} %get-tuple-element.50), channel_id=1, source_target_pairs={{0,4},{1,5},{2,6},{3,7},{4,0},{5,1},{6,2},{7,3},{8,12},{9,13},{10,... | collective-permute-start | bytes 442376 | tf_op jit(solution)/shard_map/ppermute | solution.py:414
  49.9 15.5 %collective-permute-start.14 = (f32[2,2,2,2,8,768]{5,4,1,2,3,0:T(8,128)S(1)}, f32[2,2,2,2,8,768]{5,4,1,2,3,0:T(8,128)S(1)}, u32[]{:S(2)}, u32[]{:S(2)}) collective-permute-start(f32[2,2,2,2,8,768]{5,4,1,2,3,0:T(8,128)S(1)} %slice_bitcast_fusion.8), channel_id=1, source_target_pairs={{0,8},{1,9},{2,10},{3,11},{4,28},{5,29},{6,30},{7,31},{8,0},{9,1},... | collective-permute-start | bytes 1179656 | tf_op jit(solution)/shard_map/ppermute | solution.py:414
  50.1 5.1 %collective-permute-start.7 = (f32[72,512]{1,0:T(8,128)S(1)}, f32[72,512]{1,0:T(8,128)S(1)}, u32[]{:S(2)}, u32[]{:S(2)}) collective-permute-start(f32[72,512]{1,0:T(8,128)S(1)} %add.69), channel_id=1, source_target_pairs={{0,1},{1,0},{2,3},{3,2},{4,7},{5,6},{6,5},{7,4},{8,9},{9,8},{10,11... | collective-permute-start | bytes 442376 | tf_op jit(solution)/shard_map/ppermute | solution.py:414
  50.3 15.1 %collective-permute-start.16 = (f32[2,2,2,2,8,768]{5,4,0,1,3,2:T(8,128)S(1)}, f32[2,2,2,2,8,768]{5,4,0,1,3,2:T(8,128)S(1)}, u32[]{:S(2)}, u32[]{:S(2)}) collective-permute-start(f32[2,2,2,2,8,768]{5,4,0,1,3,2:T(8,128)S(1)} %slice_bitcast_fusion.7), channel_id=1, source_target_pairs={{0,32},{1,33},{2,34},{3,35},{4,100},{5,101},{6,102},{7,103},{8,40}... | collective-permute-start | bytes 1179656 | tf_op jit(solution)/shard_map/ppermute | solution.py:414
  55.2 8.0 %collective-permute-start.8 = (f32[72,512]{1,0:T(8,128)S(1)}, f32[72,512]{1,0:T(8,128)S(1)}, u32[]{:S(2)}, u32[]{:S(2)}) collective-permute-start(f32[72,512]{1,0:T(8,128)S(1)} %add.73), channel_id=1, source_target_pairs={{0,3},{1,2},{2,1},{3,0},{4,5},{5,4},{6,7},{7,6},{8,11},{9,10},{10,... | collective-permute-start | bytes 442376 | tf_op jit(solution)/shard_map/ppermute | solution.py:414
  55.8 9.8 %collective-permute-start.18 = (f32[2,2,2,2,8,768]{5,4,0,2,3,1:T(8,128)S(1)}, f32[2,2,2,2,8,768]{5,4,0,2,3,1:T(8,128)S(1)}, u32[]{:S(2)}, u32[]{:S(2)}) collective-permute-start(f32[2,2,2,2,8,768]{5,4,0,2,3,1:T(8,128)S(1)} %slice_bitcast_fusion.6), channel_id=1, source_target_pairs={{0,1},{1,0},{2,3},{3,2},{4,7},{5,6},{6,5},{7,4},{8,9},{9,8},{10,11... | collective-permute-start | bytes 1179656 | tf_op jit(solution)/shard_map/ppermute | solution.py:414
  63.3 5.3 %collective-permute-start.9 = (f32[72,512]{1,0:T(8,128)S(1)}, f32[72,512]{1,0:T(8,128)S(1)}, u32[]{:S(2)}, u32[]{:S(2)}) collective-permute-start(f32[72,512]{1,0:T(8,128)S(1)} %add.74), channel_id=1, source_target_pairs={{0,8},{1,9},{2,10},{3,11},{4,28},{5,29},{6,30},{7,31},{8,0},{9,1},... | collective-permute-start | bytes 442376 | tf_op jit(solution)/shard_map/ppermute | solution.py:414
  65.4 5.8 %collective-permute-start.15 = (f32[2,2,2,8,768]{4,3,0,1,2:T(8,128)S(1)}, f32[2,2,2,8,768]{4,3,0,1,2:T(8,128)S(1)}, u32[]{:S(2)}, u32[]{:S(2)}) collective-permute-start(f32[2,2,2,8,768]{4,3,0,1,2:T(8,128)S(1)} %slice_bitcast_fusion.15), channel_id=1, source_target_pairs={{0,32},{1,33},{2,34},{3,35},{4,100},{5,101},{6,102},{7,103},{8,40}... | collective-permute-start | bytes 589832 | tf_op jit(solution)/shard_map/ppermute | solution.py:414
  65.6 5.7 %collective-permute-start.17 = (f32[2,2,2,8,768]{4,3,0,1,2:T(8,128)S(1)}, f32[2,2,2,8,768]{4,3,0,1,2:T(8,128)S(1)}, u32[]{:S(2)}, u32[]{:S(2)}) collective-permute-start(f32[2,2,2,8,768]{4,3,0,1,2:T(8,128)S(1)} %slice_bitcast_fusion.13), channel_id=1, source_target_pairs={{0,1},{1,0},{2,3},{3,2},{4,7},{5,6},{6,5},{7,4},{8,9},{9,8},{10,11... | collective-permute-start | bytes 589832 | tf_op jit(solution)/shard_map/ppermute | solution.py:414
  65.8 7.3 %collective-permute-start.19 = (f32[2,2,2,8,768]{4,3,0,1,2:T(8,128)S(1)}, f32[2,2,2,8,768]{4,3,0,1,2:T(8,128)S(1)}, u32[]{:S(2)}, u32[]{:S(2)}) collective-permute-start(f32[2,2,2,8,768]{4,3,0,1,2:T(8,128)S(1)} %slice_bitcast_fusion.11), channel_id=1, source_target_pairs={{0,8},{1,9},{2,10},{3,11},{4,28},{5,29},{6,30},{7,31},{8,0},{9,1},... | collective-permute-start | bytes 589832 | tf_op jit(solution)/shard_map/ppermute | solution.py:414
  68.6 6.4 %collective-permute-start.10 = (f32[72,512]{1,0:T(8,128)S(1)}, f32[72,512]{1,0:T(8,128)S(1)}, u32[]{:S(2)}, u32[]{:S(2)}) collective-permute-start(f32[72,512]{1,0:T(8,128)S(1)} %add.75), channel_id=1, source_target_pairs={{0,24},{1,25},{2,26},{3,27},{4,12},{5,13},{6,14},{7,15},{8,16},{9,... | collective-permute-start | bytes 442376 | tf_op jit(solution)/shard_map/ppermute | solution.py:414
  73.2 8.0 %collective-permute-start.20 = (f32[2,2,3,8,768]{4,3,2,0,1:T(8,128)S(1)}, f32[2,2,3,8,768]{4,3,2,0,1:T(8,128)S(1)}, u32[]{:S(2)}, u32[]{:S(2)}) collective-permute-start(f32[2,2,3,8,768]{4,3,2,0,1:T(8,128)S(1)} %slice_bitcast_fusion.9), channel_id=1, source_target_pairs={{0,3},{1,2},{2,1},{3,0},{4,5},{5,4},{6,7},{7,6},{8,11},{9,10},{10,... | collective-permute-start | bytes 884744 | tf_op jit(solution)/shard_map/ppermute | solution.py:414
  75.1 5.2 %collective-permute-start.11 = (f32[72,512]{1,0:T(8,128)S(1)}, f32[72,512]{1,0:T(8,128)S(1)}, u32[]{:S(2)}, u32[]{:S(2)}) collective-permute-start(f32[72,512]{1,0:T(8,128)S(1)} %add.76), channel_id=1, source_target_pairs={{0,32},{1,33},{2,34},{3,35},{4,100},{5,101},{6,102},{7,103},{8,40}... | collective-permute-start | bytes 442376 | tf_op jit(solution)/shard_map/ppermute | solution.py:414
  80.3 6.4 %collective-permute-start.12 = (f32[72,512]{1,0:T(8,128)S(1)}, f32[72,512]{1,0:T(8,128)S(1)}, u32[]{:S(2)}, u32[]{:S(2)}) collective-permute-start(f32[72,512]{1,0:T(8,128)S(1)} %add.77), channel_id=1, source_target_pairs={{0,96},{1,97},{2,98},{3,99},{4,36},{5,37},{6,38},{7,39},{8,104},{9... | collective-permute-start | bytes 442376 | tf_op jit(solution)/shard_map/ppermute | solution.py:414
  81.3 6.4 %collective-permute-start.21 = (f32[2,3,8,768]{3,2,1,0:T(8,128)S(1)}, f32[2,3,8,768]{3,2,1,0:T(8,128)S(1)}, u32[]{:S(2)}, u32[]{:S(2)}) collective-permute-start(f32[2,3,8,768]{3,2,1,0:T(8,128)S(1)} %slice_bitcast_fusion.17), channel_id=1, source_target_pairs={{0,24},{1,25},{2,26},{3,27},{4,12},{5,13},{6,14},{7,15},{8,16},{9,... | collective-permute-start | bytes 442376 | tf_op jit(solution)/shard_map/ppermute | solution.py:414
  86.8 3.5 %collective-permute-start.13 = (f32[72,512]{1,0:T(8,128)S(1)}, f32[72,512]{1,0:T(8,128)S(1)}, u32[]{:S(2)}, u32[]{:S(2)}) collective-permute-start(f32[72,512]{1,0:T(8,128)S(1)} %add.78.mine), channel_id=1, source_target_pairs={{0,4},{1,5},{2,6},{3,7},{4,0},{5,1},{6,2},{7,3},{8,12},{9,13},{10,... | collective-permute-start | bytes 442376 | tf_op jit(solution)/shard_map/ppermute | solution.py:414
  87.7 11.3 %collective-permute-start.22 = (f32[3,8,768]{2,1,0:T(8,128)S(1)}, f32[3,8,768]{2,1,0:T(8,128)S(1)}, u32[]{:S(2)}, u32[]{:S(2)}) collective-permute-start(f32[3,8,768]{2,1,0:T(8,128)S(1)} %slice_bitcast_fusion.19), channel_id=1, source_target_pairs={{0,96},{1,97},{2,98},{3,99},{4,36},{5,37},{6,38},{7,39},{8,104},{9... | collective-permute-start | bytes 221192 | tf_op jit(solution)/shard_map/ppermute | solution.py:414

commit v4 on v3

--- a/solution.py
+++ b/solution.py
@@ -201,7 +201,9 @@
     )(features, grads, vectors, values)
 
 
-def weight_kernel(a, wht, cols, u, keep, send, colsum):
+def weight_kernel(a, wht, cols, u, kernel_hbm, keep, send, colsum, slab, arrived):
+    copy = pltpu.make_async_copy(kernel_hbm.at[pl.ds(768 * a, 768)], slab, arrived)
+    copy.start()
     for n in range(3):
         start = 768 * a + 256 * n
         full = nn(wht[...], cols[:, start : start + 256])
@@ -212,26 +214,45 @@
             part = full[0:1024, 128 * k : 128 * k + 128] + u[...] * ones
             keep[:, lanes] = part[0:512]
             send[:, lanes] = part[512:1024]
-
-
-def weight_part(wht, cols, u, a):
+    copy.wait()
+
+
+def weight_part(wht, cols, u, kernel, a):
     return pl.pallas_call(
         functools.partial(weight_kernel, a),
-        in_specs=[ON_CHIP] * 3,
-        out_specs=(ON_CHIP,) * 3,
+        in_specs=[ON_CHIP] * 3 + [IN_HBM],
+        out_specs=(ON_CHIP,) * 4,
         out_shape=(
             jax.ShapeDtypeStruct((512, 768), F32),
             jax.ShapeDtypeStruct((512, 768), F32),
             jax.ShapeDtypeStruct((8, 768), F32),
+            jax.ShapeDtypeStruct((768, D), BF16),
         ),
+        scratch_shapes=[pltpu.SemaphoreType.DMA],
         compiler_params=pltpu.CompilerParams(vmem_limit_bytes=6 << 20),
         name=f"weight_part_{a}",
-    )(wht, cols, u)
+    )(wht, cols, u, kernel)
+
+
+def pack(block, payload, first):
+    block[:, 0:256] = payload[0:48, first : first + 256]
+    block[:, 256:512] = payload[0:48, first + 256 : first + 512]
+    block[0:24, 512:768] = payload[48:72, first : first + 256]
+    block[24:48, 512:768] = payload[48:72, first + 256 : first + 512]
+
+
+def unpack(block, payload, first):
+    payload[0:48, first : first + 256] = block[:, 0:256]
+    payload[0:48, first + 256 : first + 512] = block[:, 256:512]
+    payload[48:72, first : first + 256] = block[0:24, 512:768]
+    payload[48:72, first + 256 : first + 512] = block[24:48, 512:768]
 
 
 def back_kernel(
     cols,
-    kernel_hbm,
+    slab0,
+    slab1,
+    slab2,
     xc,
     sums,
     sum0,
@@ -240,30 +261,22 @@
     vectors,
     values,
     dev,
-    payload,
+    own,
     mine,
     theirs,
     bases,
     factors,
-    kernel,
-    arrived,
+    payload,
 ):
-    copies = [
-        pltpu.make_async_copy(
-            kernel_hbm.at[:, pl.ds(256 * z, 256)], kernel.at[z], arrived.at[z]
-        )
-        for z in range(4)
-    ]
-    for copy in copies:
-        copy.start()
     same = same_group()
     real = (lax.broadcasted_iota(jnp.int32, (ROWS, 256), 0) & 15) < W
     group = lax.broadcasted_iota(jnp.int32, (64, 256), 1) >> 6
     row = lax.broadcasted_iota(jnp.int32, (8, 256), 0)
     for z in range(4):
         lanes = slice(256 * z, 256 * z + 256)
-        copies[z].wait()
-        back = nn(cols[...], kernel[z])
+        back = nn(cols[:, 0:768], slab0[:, lanes])
+        back = back + nn(cols[:, 768:1536], slab1[:, lanes])
+        back = back + nn(cols[:, 1536:2304], slab2[:, lanes])
         total = jnp.sum(back, axis=0, keepdims=True)
         low = jnp.where(real, back - total * (1.0 / PIXELS), 0.0).astype(BF16)
         dev[:, lanes] = low
@@ -280,6 +293,7 @@
             for a, part in enumerate((sum0, sum1, sum2)):
                 tail = jnp.where(row == 2 + a, part[0:1, lanes], tail)
         payload[64:72, lanes] = tail
+        own[:, lanes] = tail
         bases[z] = block_vectors(vectors, z, same)
         factor = -(tall[:, 1:2] * scale) / (tall[:, 2:3] + root)
         factors[z] = jnp.where(same, factor, 0.0)
@@ -287,30 +301,27 @@
 
         @pl.when(lax.axis_index("c") == c)
         def _():
-            mine[...] = payload[:, 512 * c : 512 * c + 512]
-            theirs[...] = payload[:, 512 - 512 * c : 1024 - 512 * c]
-
-
-def back_part(cols, kernel, xc, sums, colsums, vectors, values):
+            pack(mine, payload, 512 * c)
+            pack(theirs, payload, 512 - 512 * c)
+
+
+def back_part(cols, slabs, xc, sums, colsums, vectors, values):
     return pl.pallas_call(
         back_kernel,
-        in_specs=[ON_CHIP, IN_HBM] + [ON_CHIP] * 7,
+        in_specs=[ON_CHIP] * 11,
         out_specs=(ON_CHIP,) * 6,
         out_shape=(
             jax.ShapeDtypeStruct((ROWS, D), BF16),
-            jax.ShapeDtypeStruct((72, D), F32),
-            jax.ShapeDtypeStruct((72, 512), F32),
-            jax.ShapeDtypeStruct((72, 512), F32),
+            jax.ShapeDtypeStruct((8, D), F32),
+            jax.ShapeDtypeStruct((48, 768), F32),
+            jax.ShapeDtypeStruct((48, 768), F32),
             jax.ShapeDtypeStruct((4, 256, 256), F32),
             jax.ShapeDtypeStruct((4, 256, 256), F32),
         ),
-        scratch_shapes=[
-            pltpu.VMEM((4, 9 * O, 256), BF16),
-            pltpu.SemaphoreType.DMA((4,)),
-        ],
+        scratch_shapes=[pltpu.VMEM((72, D), F32)],
         compiler_params=pltpu.CompilerParams(vmem_limit_bytes=14 << 20),
         name="back_part",
-    )(cols, kernel, xc, sums, *colsums, vectors, values)
+    )(cols, *slabs, xc, sums, *colsums, vectors, values)
 
 
 def final_kernel(
@@ -328,64 +339,66 @@
     shift,
     sigma,
     row_vector,
+    done,
+    sent,
 ):
-    image = pl.program_id(0)
-
-    @pl.when(image == 0)
-    def _():
-        for c in range(2):
-
-            @pl.when(lax.axis_index("c") == c)
-            def _():
-                payload[:, 512 * c : 512 * c + 512] = mine[...]
-                payload[:, 512 - 512 * c : 1024 - 512 * c] = theirs[...]
-
+    for c in range(2):
+
+        @pl.when(lax.axis_index("c") == c)
+        def _():
+            unpack(mine, payload, 512 * c)
+            unpack(theirs, payload, 512 - 512 * c)
+
+    for z in range(4):
+        lanes = slice(256 * z, 256 * z + 256)
+        basis = bases[z]
+        total = payload[64:65, lanes]
+        mean = payload[65:66, lanes] * (1.0 / TOTAL)
+        stack = payload[0:64, lanes]
+        raw = jnp.concatenate([stack, stack, stack, stack], axis=0)
+        cov = raw - columns_of([mean])[:, 0:1] * total
+        rotated = fine(nn, fine(tn, basis, cov), basis)
+        inner = 0.5 * (rotated + rotated.T) * factors[z]
+        grad = fine(nt, fine(nn, basis, inner), basis)
+        sigma[z] = (grad * (2.0 / TOTAL)).astype(BF16)
+        moved = own[0:1, lanes] * (1.0 / PIXELS) - total * (1.0 / TOTAL)
+        offset = own[1:2, lanes] * (1.0 / PIXELS) - mean
+        empty = [jnp.zeros((1, 256), BF16)]
+        stacked = jnp.concatenate(pieces(moved, 3) + pieces(mean, 3) + empty * 2, axis=0)
+        through = nn(stacked, whiten[z])
+        stacked = jnp.concatenate(pieces(offset, 3) + empty * 5, axis=0)
+        other = nn(stacked, sigma[z])
+        row_vector[0:1, lanes] = (
+            jnp.sum(through[0:3], axis=0, keepdims=True)
+            + jnp.sum(other[0:3], axis=0, keepdims=True)
+        )
+        shift[0:1, lanes] = jnp.sum(through[3:6], axis=0, keepdims=True)
+    first = 8 * sum(STRIDE[axis] * lax.axis_index(axis) for axis in ALL)
+    lane = lax.broadcasted_iota(jnp.int32, (8, D), 1)
+    row = lax.broadcasted_iota(jnp.int32, (8, D), 0)
+    chosen = jnp.where(lane == row + first, shift[...], 0.0)
+    chosen = jnp.sum(chosen, axis=1, keepdims=True)
+    for a in range(3):
+        fix[a] = chosen * payload[66 + a : 67 + a, 0:768]
+    copies = []
+    for b in range(IMAGES):
+        rows = slice(H * 16 * b, H * 16 * b + H * 16)
         for z in range(4):
             lanes = slice(256 * z, 256 * z + 256)
-            basis = bases[z]
-            total = payload[64:65, lanes]
-            mean = payload[65:66, lanes] * (1.0 / TOTAL)
-            stack = payload[0:64, lanes]
-            raw = jnp.concatenate([stack, stack, stack, stack], axis=0)
-            cov = raw - columns_of([mean])[:, 0:1] * total
-            rotated = fine(nn, fine(tn, basis, cov), basis)
-            inner = 0.5 * (rotated + rotated.T) * factors[z]
-            grad = fine(nt, fine(nn, basis, inner), basis)
-            sigma[z] = (grad * (2.0 / TOTAL)).astype(BF16)
-            moved = own[64:65, lanes] * (1.0 / PIXELS) - total * (1.0 / TOTAL)
-            offset = own[65:66, lanes] * (1.0 / PIXELS) - mean
-            empty = [jnp.zeros((1, 256), BF16)]
-            stacked = jnp.concatenate(pieces(moved, 3) + pieces(mean, 3) + empty * 2, axis=0)
-            through = nn(stacked, whiten[z])
-            stacked = jnp.concatenate(pieces(offset, 3) + empty * 5, axis=0)
-            other = nn(stacked, sigma[z])
-            row_vector[0:1, lanes] = (
-                jnp.sum(through[0:3], axis=0, keepdims=True)
-                + jnp.sum(other[0:3], axis=0, keepdims=True)
-            )
-            shift[0:1, lanes] = jnp.sum(through[3:6], axis=0, keepdims=True)
-        first = 8 * sum(STRIDE[axis] * lax.axis_index(axis) for axis in ALL)
-        lane = lax.broadcasted_iota(jnp.int32, (8, D), 1)
-        row = lax.broadcasted_iota(jnp.int32, (8, D), 0)
-        chosen = jnp.where(lane == row + first, shift[...], 0.0)
-        chosen = jnp.sum(chosen, axis=1, keepdims=True)
-        for a in range(3):
-            fix[a] = chosen * payload[66 + a : 67 + a, 0:768]
-
-    rows = pl.ds(pl.multiple_of(image * (H * 16), H * 16), H * 16)
-    for z in range(4):
-        lanes = slice(256 * z, 256 * z + 256)
-        result = nn(dev[rows, lanes], whiten[z]) + nn(xc[rows, lanes], sigma[z])
-        result = result + row_vector[0:1, lanes]
-        out[0, :, :, lanes] = result.astype(BF16).reshape(H, 16, 256)[:, 0:W, :]
+            result = nn(dev[rows, lanes], whiten[z]) + nn(xc[rows, lanes], sigma[z])
+            result = result + row_vector[0:1, lanes]
+            done[b, :, :, lanes] = result.astype(BF16).reshape(H, 16, 256)[:, 0:W, :]
+        copies.append(pltpu.make_async_copy(done.at[b], out.at[b], sent.at[b]))
+        copies[-1].start()
+    for copy in copies:
+        copy.wait()
 
 
 def final_part(dev, xc, mine, theirs, own, bases, factors, whiten):
     return pl.pallas_call(
         final_kernel,
-        grid=(IMAGES,),
         in_specs=[ON_CHIP] * 8,
-        out_specs=(pl.BlockSpec((1, H, W, D), lambda b: (b, 0, 0, 0)), ON_CHIP),
+        out_specs=(IN_HBM, ON_CHIP),
         out_shape=(
             jax.ShapeDtypeStruct((IMAGES, H, W, D), BF16),
             jax.ShapeDtypeStruct((3, 8, 768), F32),
@@ -395,8 +408,10 @@
             pltpu.VMEM((1, D), F32),
             pltpu.VMEM((4, 256, 256), BF16),
             pltpu.VMEM((1, D), F32),
+            pltpu.VMEM((IMAGES, H, W, D), BF16),
+            pltpu.SemaphoreType.DMA((IMAGES,)),
         ],
-        compiler_params=pltpu.CompilerParams(vmem_limit_bytes=10 << 20),
+        compiler_params=pltpu.CompilerParams(vmem_limit_bytes=12 << 20),
         name="final_part",
     )(dev, xc, mine, theirs, own, bases, factors, whiten)
 
@@ -430,19 +445,28 @@
     return pick(0), pick(1)
 
 
+def joint(part, send, mine, move):
+    rows = send.size // 768
+    message = jnp.concatenate([send.reshape(rows, 768), mine], axis=0)
+    message = exchange(message, move)
+    return part + message[:rows].reshape(part.shape), mine + message[rows:]
+
+
 def local(features, grads, kernel, vectors, values):
     stay = lambda array: pltpu.with_memory_space_constraint(array, pltpu.HBM)
     cols, xc, wht, u, sums, whiten = prep(stay(features), stay(grads), stay(vectors), values)
     cols, xc = cols.reshape(ROWS, 9 * O), xc.reshape(ROWS, D)
-
-    parts, colsums = [], []
+    kernel = stay(kernel.reshape(9 * O, D))
+
+    parts, colsums, slabs = [], [], []
     for a in range(3):
-        keep, send, colsum = weight_part(wht, cols, u, a)
+        keep, send, colsum, slab = weight_part(wht, cols, u, kernel, a)
         colsums.append(colsum)
+        slabs.append(slab)
         parts.append((keep + exchange(send, other_core)).reshape(2, 2, 2, 2, 2, 2, 8, 768))
-    cols, *parts = lax.optimization_barrier((cols, *parts))
+    cols = lax.optimization_barrier((cols, *parts))[0]
     dev, own, mine, theirs, bases, factors = back_part(
-        cols, stay(kernel.reshape(9 * O, D)), xc, sums, colsums, vectors, values
+        cols, slabs, xc, sums, colsums, vectors, values
     )
     mine = mine + exchange(theirs, other_core)
 
@@ -453,20 +477,21 @@
             dim = names[a].index(axis + "1")
             names[a].pop(dim)
             keep, send = halves(parts[a], dim)
-            parts[a] = keep + exchange(send, ring(axis, 0))
+            if turn > 0 and a == 0:
+                parts[a], mine = joint(keep, send, mine, ring(axis, 0))
+            else:
+                parts[a] = keep + exchange(send, ring(axis, 0))
         if turn == 0:
             mine, *parts = lax.optimization_barrier((mine, *parts))
-            for axis in "xyz":
-                for step in range(2):
-                    mine = mine + exchange(mine, ring(axis, step))
-            theirs = exchange(mine, other_core)
-    share = jnp.stack(parts, axis=3)
-    order = ["z", "y", "x"]
+            mine = mine + exchange(mine, ring("x", 0))
+    share = jnp.stack(parts, axis=0)
+    order = ["a", "z", "y", "x"]
     for axis in "xyz":
         dim = order.index(axis)
         order.pop(dim)
         keep, send = halves(share, dim)
-        share = keep + exchange(send, ring(axis, 1))
+        share, mine = joint(keep, send, mine, ring(axis, 1))
+    theirs = exchange(mine, other_core)
 
     input_grad, fix = final_part(dev, xc, mine, theirs, own, bases, factors, whiten)
     kernel_grad = (share - fix).transpose(1, 0, 2).reshape(8, 3, 3, O)

time: 99.9 us -> 108 us (1.081)
  waiting for transfers between devices: 34.5 us -> 46.1 us
  Pallas kernels: 41.5 us -> 38.2 us
  starting transfers between devices: 19.5 us -> 18 us
    ppermute x23 -> x18, waiting for transfers between devices: 34.5 us -> 46.1 us  [exchange(): return lax.ppermute(value, ALL, permutation(move))]
    pallas_call x2, Pallas kernels: 27.1 us -> 23.7 us  [the longest x1 16.3 us: back_part(): pl.pallas_call(back_kernel, in_specs=[ON_CHIP] * 11, out_specs=(ON_CHIP,)...]
    ppermute x23 -> x18, starting transfers between devices: 19.5 us -> 18 us  [exchange(): return lax.ppermute(value, ALL, permutation(move))]
  transfers between devices with their start and end apart: 23 -> 18, of which waited for: 13 -> 9; matrix products, arithmetic and copies ran while one was open for 1% -> 2% of each run, Pallas kernels for 33% -> 21%
where the time goes in v4:
time: 108 us; the launch traced here: 107 us
  waiting for transfers between devices  46.1 us (43%)
  Pallas kernels  38.2 us (35%)
  starting transfers between devices  18 us (17%)
  other arithmetic  2.16 us (2%)
  local copies, waits for them, and re-layouts  1.54 us (1%)
  between operations  1.08 us (1%)
    ppermute x18, waiting for transfers between devices, exchange(): return lax.ppermute(value, ALL, permutation(move))  46.1 us
    ppermute x18, starting transfers between devices, exchange(): return lax.ppermute(value, ALL, permutation(move))  18 us
    pallas_call x1, Pallas kernels, back_part(): pl.pallas_call(back_kernel, in_specs=[ON_CHIP] * 11, out_specs=(ON_CHIP,)...  16.3 us
    pallas_call x3, Pallas kernels, weight_part(): pl.pallas_call(functools.partial(weight_kernel, a), in_specs=[ON_CHIP] *...  9.38 us
    pallas_call x1, Pallas kernels, final_part(): pl.pallas_call(final_kernel, in_specs=[ON_CHIP] * 8, out_specs=(IN_HBM, O...  7.36 us
    pallas_call x1, Pallas kernels, prep(): pl.pallas_call(prep_kernel, out_shape=(jax.ShapeDtypeStruct((IMAGES * H,...  5.12 us
  transfers between devices with their start and end apart: 18, of which 9 were waited for; matrix products, arithmetic and copies ran while one was open for 2% of the time, Pallas kernels for 21%

profile of v4, /device:TPU:0, one launch (start us, length us, event | category | flops | bytes accessed | tf_op | source)
XLA Modules:
  0.0 107.1 jit_solution(3419391974613857382)
XLA Ops:
  0.6 0.7 copy-done.1
  1.3 5.1 %prep.1 = (bf16[84,16,2304]{2,1,0:T(8,128)(2,1)S(1)}, bf16[84,16,1024]{2,1,0:T(8,128)(2,1)S(1)}, bf16[1040,1344]{1,0:T(8,128)(2,1)S(1)}, f32[1024,128]{1,0:T(8,1...) custom-call(bf16[6,14,14,1024]{3,2,1,0:T(8,128)(2,1)} %features_hbm.1, ...), custom_call_target="tpu_custom_call" | custom-call | tf_op jit(solution)/shard_map/prep/pallas_call | solution.py:179
  6.5 3.1 %weight_part_2.1 = (f32[512,768]{1,0:T(8,128)S(1)}, f32[512,768]{1,0:T(8,128)S(1)}, f32[8,768]{1,0:T(8,128)S(1)}, bf16[768,1024]{1,0:T(8,128)(2,1)S(1)}) custom-call(bf16[1040,1344]{1,0:T(8,128)(2,1)S(1)} %get-tuple-element.34.wht, bf16[1344,2304]{1,0:T(8,128)(2,1)S(1)} %bitcast.82, f32[1024,128]{1,0:T(8,128)S(1)} %get-tuple-element.35.u, ...), custom_call_target="tpu_custom_call" | custom-call | tf_op jit(solution)/shard_map/weight_part_2/pallas_call | solution.py:221
  9.6 0.1 collective-permute-start.5
  9.7 3.1 %weight_part_0.1 = (f32[512,768]{1,0:T(8,128)S(1)}, f32[512,768]{1,0:T(8,128)S(1)}, f32[8,768]{1,0:T(8,128)S(1)}, bf16[768,1024]{1,0:T(8,128)(2,1)S(1)}) custom-call(bf16[1040,1344]{1,0:T(8,128)(2,1)S(1)} %get-tuple-element.34.wht, bf16[1344,2304]{1,0:T(8,128)(2,1)S(1)} %bitcast.83, f32[1024,128]{1,0:T(8,128)S(1)} %get-tuple-element.35.u, ...), custom_call_target="tpu_custom_call" | custom-call | tf_op jit(solution)/shard_map/weight_part_0/pallas_call | solution.py:221
  12.8 0.6 collective-permute-start
  13.4 3.1 %weight_part_1.1 = (f32[512,768]{1,0:T(8,128)S(1)}, f32[512,768]{1,0:T(8,128)S(1)}, f32[8,768]{1,0:T(8,128)S(1)}, bf16[768,1024]{1,0:T(8,128)(2,1)S(1)}) custom-call(bf16[1040,1344]{1,0:T(8,128)(2,1)S(1)} %get-tuple-element.34.wht, bf16[1344,2304]{1,0:T(8,128)(2,1)S(1)} %bitcast.84, f32[1024,128]{1,0:T(8,128)S(1)} %get-tuple-element.35.u, ...), custom_call_target="tpu_custom_call" | custom-call | tf_op jit(solution)/shard_map/weight_part_1/pallas_call | solution.py:221
  16.5 0.1 collective-permute-start.1
  16.6 0.2 add.72
  16.8 0.1 fusion.10
  16.9 0.1 copy.19
  17.0 2.1 %collective-permute-start.6 = (f32[2,2,2,2,2,8,768]{6,5,0,2,4,1,3:T(8,128)S(1)}, f32[2,2,2,2,2,8,768]{6,5,0,2,4,1,3:T(8,128)S(1)}, u32[]{:S(2)}, u32[]{:S(2)}) collective-permute-start(f32[2,2,2,2,2,8,768]{6,5,0,2,4,1,3:T(8,128)S(1)} %copy.19), channel_id=1, source_target_pairs={{0,32},{1,33},{2,34},{3,35},{4,100},{5,101},{6,102},{7,103},{8,40}... | collective-permute-start | bytes 2359304 | tf_op jit(solution)/shard_map/ppermute | solution.py:429
  19.1 0.2 add.67
  19.3 0.1 fusion.12
  19.4 0.1 copy.47
  19.5 1.7 %collective-permute-start.3 = (f32[2,2,2,2,2,8,768]{6,5,0,1,3,4,2:T(8,128)S(1)}, f32[2,2,2,2,2,8,768]{6,5,0,1,3,4,2:T(8,128)S(1)}, u32[]{:S(2)}, u32[]{:S(2)}) collective-permute-start(f32[2,2,2,2,2,8,768]{6,5,0,1,3,4,2:T(8,128)S(1)} %bitcast.99), channel_id=1, source_target_pairs={{0,1},{1,0},{2,3},{3,2},{4,7},{5,6},{6,5},{7,4},{8,9},{9,8},{10,11... | collective-permute-start | bytes 2359304 | tf_op jit(solution)/shard_map/ppermute | solution.py:429
  21.2 0.2 add.68
  21.4 0.1 fusion.11
  21.6 0.1 copy.46
  21.7 1.7 %collective-permute-start.4 = (f32[2,2,2,2,2,8,768]{6,5,1,2,4,3,0:T(8,128)S(1)}, f32[2,2,2,2,2,8,768]{6,5,1,2,4,3,0:T(8,128)S(1)}, u32[]{:S(2)}, u32[]{:S(2)}) collective-permute-start(f32[2,2,2,2,2,8,768]{6,5,1,2,4,3,0:T(8,128)S(1)} %bitcast.100), channel_id=1, source_target_pairs={{0,8},{1,9},{2,10},{3,11},{4,28},{5,29},{6,30},{7,31},{8,0},{9,1},... | collective-permute-start | bytes 2359304 | tf_op jit(solution)/shard_map/ppermute | solution.py:429
  23.3 16.3 %back_part.1 = (bf16[1344,1024]{1,0:T(8,128)(2,1)S(1)}, f32[8,1024]{1,0:T(8,128)S(1)}, f32[48,768]{1,0:T(8,128)S(1)}, f32[48,768]{1,0:T(8,128)S(1)}, f32[4,256,2...) custom-call(bf16[1344,2304]{1,0:T(8,128)(2,1)S(1)} %bitcast.85, bf16[768,1024]{1,0:T(8,128)(2,1)S(1)} %get-tuple-element.41.slab0, ...), custom_call_target="tpu_custom_call" | custom-call | tf_op jit(solution)/shard_map/back_part/pallas_call | solution.py:309
  39.7 4.5 %collective-permute-start.2 = (f32[48,768]{1,0:T(8,128)S(1)}, f32[48,768]{1,0:T(8,128)S(1)}, u32[]{:S(2)}, u32[]{:S(2)}) collective-permute-start(f32[48,768]{1,0:T(8,128)S(1)} %get-tuple-element.51), channel_id=1, source_target_pairs={{0,4},{1,5},{2,6},{3,7},{4,0},{5,1},{6,2},{7,3},{8,12},{9,13},{10,... | collective-permute-start | bytes 442376 | tf_op jit(solution)/shard_map/ppermute | solution.py:429
  44.2 1.0 collective-permute-done.2
  45.3 0.1 copy_add_fusion
  45.4 0.1 fusion.1
  45.5 0.1 fusion
  45.7 0.5 collective-permute-start.12
  46.2 1.8 %collective-permute-start.7 = (f32[48,768]{1,0:T(8,128)S(1)}, f32[48,768]{1,0:T(8,128)S(1)}, u32[]{:S(2)}, u32[]{:S(2)}) collective-permute-start(f32[48,768]{1,0:T(8,128)S(1)} %add.69), channel_id=1, source_target_pairs={{0,1},{1,0},{2,3},{3,2},{4,7},{5,6},{6,5},{7,4},{8,9},{9,8},{10,11... | collective-permute-start | bytes 442376 | tf_op jit(solution)/shard_map/ppermute | solution.py:429
  48.1 0.1 collective-permute-start.10
  48.2 7.1 %collective-permute-done.7 = f32[48,768]{1,0:T(8,128)S(1)} collective-permute-done((f32[48,768]{1,0:T(8,128)S(1)}, f32[48,768]{1,0:T(8,128)S(1)}, u32[]{:S(2)}, u32[]{:S(2)}) %collective-permute-start.7) | collective-permute-done | bytes 147488 | tf_op jit(solution)/shard_map/ppermute | solution.py:429
  55.4 0.2 collective-permute-start.8
  55.7 2.0 %collective-permute-start.13 = (f32[2,2,2,8,768]{4,3,0,1,2:T(8,128)S(1)}, f32[2,2,2,8,768]{4,3,0,1,2:T(8,128)S(1)}, u32[]{:S(2)}, u32[]{:S(2)}) collective-permute-start(f32[2,2,2,8,768]{4,3,0,1,2:T(8,128)S(1)} %slice_bitcast_fusion.3), channel_id=1, source_target_pairs={{0,8},{1,9},{2,10},{3,11},{4,28},{5,29},{6,30},{7,31},{8,0},{9,1},... | collective-permute-start | bytes 589832 | tf_op jit(solution)/shard_map/ppermute | solution.py:429
  57.6 0.1 bitcast_add_fusion.1
  57.7 0.3 collective-permute-start.11
  58.0 6.8 %collective-permute-done.8 = f32[176,768]{1,0:T(8,128)S(1)} collective-permute-done((f32[176,768]{1,0:T(8,128)S(1)}, f32[176,768]{1,0:T(8,128)S(1)}, u32[]{:S(2)}, u32[]{:S(2)}) %collective-permute-start.8) | collective-permute-done | bytes 540704 | tf_op jit(solution)/shard_map/ppermute | solution.py:429
  65.0 0.1 collective-permute-start.9
  65.1 1.8 %collective-permute-done.13 = f32[2,2,2,8,768]{4,3,0,1,2:T(8,128)S(1)} collective-permute-done((f32[2,2,2,8,768]{4,3,0,1,2:T(8,128)S(1)}, f32[2,2,2,8,768]{4,3,0,1,2:T(8,128)S(1)}, u32[]{:S(2)}, u32[]{:S(2)}) %collective-permute-start.13) | collective-permute-done | bytes 196640 | tf_op jit(solution)/shard_map/ppermute | solution.py:429
  67.0 5.3 %collective-permute-done.9 = f32[112,768]{1,0:T(8,128)S(1)} collective-permute-done((f32[112,768]{1,0:T(8,128)S(1)}, f32[112,768]{1,0:T(8,128)S(1)}, u32[]{:S(2)}, u32[]{:S(2)}) %collective-permute-start.9) | collective-permute-done | bytes 344096 | tf_op jit(solution)/shard_map/ppermute | solution.py:429
  72.6 0.6 collective-permute-start.14
  73.1 9.0 %collective-permute-done.14 = f32[144,768]{1,0:T(8,128)S(1)} collective-permute-done((f32[144,768]{1,0:T(8,128)S(1)}, f32[144,768]{1,0:T(8,128)S(1)}, u32[]{:S(2)}, u32[]{:S(2)}) %collective-permute-start.14) | collective-permute-done | bytes 442400 | tf_op jit(solution)/shard_map/ppermute | solution.py:429
  82.3 1.2 %collective-permute-start.15 = (f32[96,768]{1,0:T(8,128)S(1)}, f32[96,768]{1,0:T(8,128)S(1)}, u32[]{:S(2)}, u32[]{:S(2)}) collective-permute-start(f32[96,768]{1,0:T(8,128)S(1)} %pad_maximum_fusion.4), channel_id=1, source_target_pairs={{0,24},{1,25},{2,26},{3,27},{4,12},{5,13},{6,14},{7,15},{8,16},{9,... | collective-permute-start | bytes 884744 | tf_op jit(solution)/shard_map/ppermute | solution.py:429
  83.5 6.8 %collective-permute-done.15 = f32[96,768]{1,0:T(8,128)S(1)} collective-permute-done((f32[96,768]{1,0:T(8,128)S(1)}, f32[96,768]{1,0:T(8,128)S(1)}, u32[]{:S(2)}, u32[]{:S(2)}) %collective-permute-start.15) | collective-permute-done | bytes 294944 | tf_op jit(solution)/shard_map/ppermute | solution.py:429
  90.4 0.4 collective-permute-start.16
  90.8 6.8 %collective-permute-done.16 = f32[72,768]{1,0:T(8,128)S(1)} collective-permute-done((f32[72,768]{1,0:T(8,128)S(1)}, f32[72,768]{1,0:T(8,128)S(1)}, u32[]{:S(2)}, u32[]{:S(2)}) %collective-permute-start.16) | collective-permute-done | bytes 221216 | tf_op jit(solution)/shard_map/ppermute | solution.py:429
  97.7 0.1 collective-permute-start.17
  97.8 1.4 %collective-permute-done.17.theirs = f32[48,768]{1,0:T(8,128)S(1)} collective-permute-done((f32[48,768]{1,0:T(8,128)S(1)}, f32[48,768]{1,0:T(8,128)S(1)}, u32[]{:S(2)}, u32[]{:S(2)}) %collective-permute-start.17) | collective-permute-done | bytes 147488 | tf_op jit(solution)/shard_map/ppermute | solution.py:429
  99.1 7.4 %final_part.1 = (bf16[6,14,14,1024]{3,2,1,0:T(8,128)(2,1)}, f32[3,8,768]{2,1,0:T(8,128)S(1)}) custom-call(bf16[1344,1024]{1,0:T(8,128)(2,1)S(1)} %get-tuple-element.49.dev, bf16[1344,1024]{1,0:T(8,128)(2,1)S(1)} %bitcast.87, f32[48,768]{1,0:T(8,128)S(1)} %slice_add_fusion.1.mine, f32[48,768]{1,0:T(8,128)S(1)} %collective-permute-done.17.theirs, ...), custom_call_target="tpu_custom_call" | custom-call | tf_op jit(solution)/shard_map/final_part/pallas_call | solution.py:398
  106.5 0.6 fusion.9
  (50 shorter events, 0.9 us)
Async XLA Ops:
  0.6 0.7 copy-start.1
  9.6 7.0 %collective-permute-start.5 = (f32[512,768]{1,0:T(8,128)S(1)}, f32[512,768]{1,0:T(8,128)S(1)}, u32[]{:S(2)}, u32[]{:S(2)}) collective-permute-start(f32[512,768]{1,0:T(8,128)S(1)} %get-tuple-element.53), channel_id=1, source_target_pairs={{0,4},{1,5},{2,6},{3,7},{4,0},{5,1},{6,2},{7,3},{8,12},{9,13},{10,... | collective-permute-start | bytes 4718600 | tf_op jit(solution)/shard_map/ppermute | solution.py:429
  12.8 6.3 %collective-permute-start = (f32[512,768]{1,0:T(8,128)S(1)}, f32[512,768]{1,0:T(8,128)S(1)}, u32[]{:S(2)}, u32[]{:S(2)}) collective-permute-start(f32[512,768]{1,0:T(8,128)S(1)} %get-tuple-element.37), channel_id=1, source_target_pairs={{0,4},{1,5},{2,6},{3,7},{4,0},{5,1},{6,2},{7,3},{8,12},{9,13},{10,... | collective-permute-start | bytes 4718600 | tf_op jit(solution)/shard_map/ppermute | solution.py:429
  16.5 4.7 %collective-permute-start.1 = (f32[512,768]{1,0:T(8,128)S(1)}, f32[512,768]{1,0:T(8,128)S(1)}, u32[]{:S(2)}, u32[]{:S(2)}) collective-permute-start(f32[512,768]{1,0:T(8,128)S(1)} %get-tuple-element.39), channel_id=1, source_target_pairs={{0,4},{1,5},{2,6},{3,7},{4,0},{5,1},{6,2},{7,3},{8,12},{9,13},{10,... | collective-permute-start | bytes 4718600 | tf_op jit(solution)/shard_map/ppermute | solution.py:429
  17.0 28.2 %collective-permute-start.6 = (f32[2,2,2,2,2,8,768]{6,5,0,2,4,1,3:T(8,128)S(1)}, f32[2,2,2,2,2,8,768]{6,5,0,2,4,1,3:T(8,128)S(1)}, u32[]{:S(2)}, u32[]{:S(2)}) collective-permute-start(f32[2,2,2,2,2,8,768]{6,5,0,2,4,1,3:T(8,128)S(1)} %copy.19), channel_id=1, source_target_pairs={{0,32},{1,33},{2,34},{3,35},{4,100},{5,101},{6,102},{7,103},{8,40}... | collective-permute-start | bytes 2359304 | tf_op jit(solution)/shard_map/ppermute | solution.py:429
  19.5 25.9 %collective-permute-start.3 = (f32[2,2,2,2,2,8,768]{6,5,0,1,3,4,2:T(8,128)S(1)}, f32[2,2,2,2,2,8,768]{6,5,0,1,3,4,2:T(8,128)S(1)}, u32[]{:S(2)}, u32[]{:S(2)}) collective-permute-start(f32[2,2,2,2,2,8,768]{6,5,0,1,3,4,2:T(8,128)S(1)} %bitcast.99), channel_id=1, source_target_pairs={{0,1},{1,0},{2,3},{3,2},{4,7},{5,6},{6,5},{7,4},{8,9},{9,8},{10,11... | collective-permute-start | bytes 2359304 | tf_op jit(solution)/shard_map/ppermute | solution.py:429
  21.6 1.8 %copy-start = (f32[16,64,64]{2,1,0:T(8,128)S(1)}, f32[16,64,64]{2,1,0:T(8,128)}, u32[]{:S(2)}) copy-start(f32[16,64,64]{2,1,0:T(8,128)} %vectors.1) | copy-start | bytes 786436
  21.6 1.8 %copy-start.2 = (f32[16,64]{1,0:T(8,128)S(1)}, f32[16,64]{1,0:T(8,128)}, u32[]{:S(2)}) copy-start(f32[16,64]{1,0:T(8,128)} %values.3) | copy-start | bytes 12292
  21.7 23.8 %collective-permute-start.4 = (f32[2,2,2,2,2,8,768]{6,5,1,2,4,3,0:T(8,128)S(1)}, f32[2,2,2,2,2,8,768]{6,5,1,2,4,3,0:T(8,128)S(1)}, u32[]{:S(2)}, u32[]{:S(2)}) collective-permute-start(f32[2,2,2,2,2,8,768]{6,5,1,2,4,3,0:T(8,128)S(1)} %bitcast.100), channel_id=1, source_target_pairs={{0,8},{1,9},{2,10},{3,11},{4,28},{5,29},{6,30},{7,31},{8,0},{9,1},... | collective-permute-start | bytes 2359304 | tf_op jit(solution)/shard_map/ppermute | solution.py:429
  39.7 5.6 %collective-permute-start.2 = (f32[48,768]{1,0:T(8,128)S(1)}, f32[48,768]{1,0:T(8,128)S(1)}, u32[]{:S(2)}, u32[]{:S(2)}) collective-permute-start(f32[48,768]{1,0:T(8,128)S(1)} %get-tuple-element.51), channel_id=1, source_target_pairs={{0,4},{1,5},{2,6},{3,7},{4,0},{5,1},{6,2},{7,3},{8,12},{9,13},{10,... | collective-permute-start | bytes 442376 | tf_op jit(solution)/shard_map/ppermute | solution.py:429
  45.7 9.9 %collective-permute-start.12 = (f32[2,2,2,2,8,768]{5,4,0,2,3,1:T(8,128)S(1)}, f32[2,2,2,2,8,768]{5,4,0,2,3,1:T(8,128)S(1)}, u32[]{:S(2)}, u32[]{:S(2)}) collective-permute-start(f32[2,2,2,2,8,768]{5,4,0,2,3,1:T(8,128)S(1)} %slice_bitcast_fusion), channel_id=1, source_target_pairs={{0,1},{1,0},{2,3},{3,2},{4,7},{5,6},{6,5},{7,4},{8,9},{9,8},{10,11... | collective-permute-start | bytes 1179656 | tf_op jit(solution)/shard_map/ppermute | solution.py:429
  46.2 9.1 %collective-permute-start.7 = (f32[48,768]{1,0:T(8,128)S(1)}, f32[48,768]{1,0:T(8,128)S(1)}, u32[]{:S(2)}, u32[]{:S(2)}) collective-permute-start(f32[48,768]{1,0:T(8,128)S(1)} %add.69), channel_id=1, source_target_pairs={{0,1},{1,0},{2,3},{3,2},{4,7},{5,6},{6,5},{7,4},{8,9},{9,8},{10,11... | collective-permute-start | bytes 442376 | tf_op jit(solution)/shard_map/ppermute | solution.py:429
  48.1 9.6 %collective-permute-start.10 = (f32[2,2,2,2,8,768]{5,4,0,1,3,2:T(8,128)S(1)}, f32[2,2,2,2,8,768]{5,4,0,1,3,2:T(8,128)S(1)}, u32[]{:S(2)}, u32[]{:S(2)}) collective-permute-start(f32[2,2,2,2,8,768]{5,4,0,1,3,2:T(8,128)S(1)} %slice_bitcast_fusion.1), channel_id=1, source_target_pairs={{0,32},{1,33},{2,34},{3,35},{4,100},{5,101},{6,102},{7,103},{8,40}... | collective-permute-start | bytes 1179656 | tf_op jit(solution)/shard_map/ppermute | solution.py:429
  55.4 9.4 %collective-permute-start.8 = (f32[176,768]{1,0:T(8,128)S(1)}, f32[176,768]{1,0:T(8,128)S(1)}, u32[]{:S(2)}, u32[]{:S(2)}) collective-permute-start(f32[176,768]{1,0:T(8,128)S(1)} %pad_maximum_fusion.1), channel_id=1, source_target_pairs={{0,8},{1,9},{2,10},{3,11},{4,28},{5,29},{6,30},{7,31},{8,0},{9,1},... | collective-permute-start | bytes 1622024 | tf_op jit(solution)/shard_map/ppermute | solution.py:429
  55.7 11.2 %collective-permute-start.13 = (f32[2,2,2,8,768]{4,3,0,1,2:T(8,128)S(1)}, f32[2,2,2,8,768]{4,3,0,1,2:T(8,128)S(1)}, u32[]{:S(2)}, u32[]{:S(2)}) collective-permute-start(f32[2,2,2,8,768]{4,3,0,1,2:T(8,128)S(1)} %slice_bitcast_fusion.3), channel_id=1, source_target_pairs={{0,8},{1,9},{2,10},{3,11},{4,28},{5,29},{6,30},{7,31},{8,0},{9,1},... | collective-permute-start | bytes 589832 | tf_op jit(solution)/shard_map/ppermute | solution.py:429
  57.7 9.2 %collective-permute-start.11 = (f32[2,2,2,8,768]{4,3,0,1,2:T(8,128)S(1)}, f32[2,2,2,8,768]{4,3,0,1,2:T(8,128)S(1)}, u32[]{:S(2)}, u32[]{:S(2)}) collective-permute-start(f32[2,2,2,8,768]{4,3,0,1,2:T(8,128)S(1)} %slice_bitcast_fusion.5), channel_id=1, source_target_pairs={{0,1},{1,0},{2,3},{3,2},{4,7},{5,6},{6,5},{7,4},{8,9},{9,8},{10,11... | collective-permute-start | bytes 589832 | tf_op jit(solution)/shard_map/ppermute | solution.py:429
  65.0 7.3 %collective-permute-start.9 = (f32[112,768]{1,0:T(8,128)S(1)}, f32[112,768]{1,0:T(8,128)S(1)}, u32[]{:S(2)}, u32[]{:S(2)}) collective-permute-start(f32[112,768]{1,0:T(8,128)S(1)} %pad_maximum_fusion.3), channel_id=1, source_target_pairs={{0,32},{1,33},{2,34},{3,35},{4,100},{5,101},{6,102},{7,103},{8,40}... | collective-permute-start | bytes 1032200 | tf_op jit(solution)/shard_map/ppermute | solution.py:429
  72.6 9.6 %collective-permute-start.14 = (f32[144,768]{1,0:T(8,128)S(1)}, f32[144,768]{1,0:T(8,128)S(1)}, u32[]{:S(2)}, u32[]{:S(2)}) collective-permute-start(f32[144,768]{1,0:T(8,128)S(1)} %pad_maximum_fusion.2), channel_id=1, source_target_pairs={{0,3},{1,2},{2,1},{3,0},{4,5},{5,4},{6,7},{7,6},{8,11},{9,10},{10,... | collective-permute-start | bytes 1327112 | tf_op jit(solution)/shard_map/ppermute | solution.py:429
  82.3 8.0 %collective-permute-start.15 = (f32[96,768]{1,0:T(8,128)S(1)}, f32[96,768]{1,0:T(8,128)S(1)}, u32[]{:S(2)}, u32[]{:S(2)}) collective-permute-start(f32[96,768]{1,0:T(8,128)S(1)} %pad_maximum_fusion.4), channel_id=1, source_target_pairs={{0,24},{1,25},{2,26},{3,27},{4,12},{5,13},{6,14},{7,15},{8,16},{9,... | collective-permute-start | bytes 884744 | tf_op jit(solution)/shard_map/ppermute | solution.py:429
  90.4 7.2 %collective-permute-start.16 = (f32[72,768]{1,0:T(8,128)S(1)}, f32[72,768]{1,0:T(8,128)S(1)}, u32[]{:S(2)}, u32[]{:S(2)}) collective-permute-start(f32[72,768]{1,0:T(8,128)S(1)} %pad_maximum_fusion.5), channel_id=1, source_target_pairs={{0,96},{1,97},{2,98},{3,99},{4,36},{5,37},{6,38},{7,39},{8,104},{9... | collective-permute-start | bytes 663560 | tf_op jit(solution)/shard_map/ppermute | solution.py:429
  97.7 1.5 %collective-permute-start.17 = (f32[48,768]{1,0:T(8,128)S(1)}, f32[48,768]{1,0:T(8,128)S(1)}, u32[]{:S(2)}, u32[]{:S(2)}) collective-permute-start(f32[48,768]{1,0:T(8,128)S(1)} %slice_add_fusion.1.mine), channel_id=1, source_target_pairs={{0,4},{1,5},{2,6},{3,7},{4,0},{5,1},{6,2},{7,3},{8,12},{9,13},{10,... | collective-permute-start | bytes 442376 | tf_op jit(solution)/shard_map/ppermute | solution.py:429

commit v5 on v4

--- a/solution.py
+++ b/solution.py
@@ -70,8 +70,8 @@
 
 
 def fine(dot, a, b):
-    a_high, a_low = pieces(a, 2)
-    b_high, b_low = pieces(b, 2)
+    a_high, a_low = a if isinstance(a, tuple) else pieces(a, 2)
+    b_high, b_low = b if isinstance(b, tuple) else pieces(b, 2)
     return dot(a_high, b_high) + (dot(a_high, b_low) + dot(a_low, b_high))
 
 
@@ -234,20 +234,6 @@
     )(wht, cols, u, kernel)
 
 
-def pack(block, payload, first):
-    block[:, 0:256] = payload[0:48, first : first + 256]
-    block[:, 256:512] = payload[0:48, first + 256 : first + 512]
-    block[0:24, 512:768] = payload[48:72, first : first + 256]
-    block[24:48, 512:768] = payload[48:72, first + 256 : first + 512]
-
-
-def unpack(block, payload, first):
-    payload[0:48, first : first + 256] = block[:, 0:256]
-    payload[0:48, first + 256 : first + 512] = block[:, 256:512]
-    payload[48:72, first : first + 256] = block[0:24, 512:768]
-    payload[48:72, first + 256 : first + 512] = block[24:48, 512:768]
-
-
 def back_kernel(
     cols,
     slab0,
@@ -266,12 +252,20 @@
     theirs,
     bases,
     factors,
-    payload,
+    blocks,
 ):
     same = same_group()
+    eye = lax.broadcasted_iota(jnp.int32, (256, 256), 0) == lax.broadcasted_iota(
+        jnp.int32, (256, 256), 1
+    )
+    eye = jnp.where(eye, 1.0, 0.0).astype(BF16)
     real = (lax.broadcasted_iota(jnp.int32, (ROWS, 256), 0) & 15) < W
     group = lax.broadcasted_iota(jnp.int32, (64, 256), 1) >> 6
+    below = lax.broadcasted_iota(jnp.int32, (64, 256), 0) - (
+        lax.broadcasted_iota(jnp.int32, (64, 256), 1) & 63
+    )
     row = lax.broadcasted_iota(jnp.int32, (8, 256), 0)
+    upper = None
     for z in range(4):
         lanes = slice(256 * z, 256 * z + 256)
         back = nn(cols[:, 0:768], slab0[:, lanes])
@@ -283,26 +277,32 @@
         value = value_row(values, z)
         scale, root = lax.rsqrt(value), jnp.sqrt(value)
         tall = columns_of([sums[:, lanes] * (1.0 / PIXELS), scale, root])
-        cov = tn(xc[:, lanes], low) + tall[:, 0:1] * total
+        turned = nt(eye, xc[:, lanes]).astype(BF16)
+        cov = nn(turned, low) + tall[:, 0:1] * total
+        cov = 0.5 * (cov + cov.T)
         packed = cov[0:64]
         for k in range(1, 4):
             packed = jnp.where(group == k, cov[64 * k : 64 * k + 64], packed)
-        payload[0:64, lanes] = packed
+        if z % 2 == 0:
+            upper = packed
+        else:
+            blocks[z // 2, 0:64, :] = jnp.where(below <= 0, upper, packed)
+        diagonal = jnp.sum(jnp.where(below == 0, packed, 0.0), axis=0, keepdims=True)
         tail = jnp.where(row == 0, total, jnp.where(row == 1, sums[:, lanes], 0.0))
+        tail = jnp.where(row == 5, diagonal, tail)
         if z < 3:
             for a, part in enumerate((sum0, sum1, sum2)):
                 tail = jnp.where(row == 2 + a, part[0:1, lanes], tail)
-        payload[64:72, lanes] = tail
         own[:, lanes] = tail
-        bases[z] = block_vectors(vectors, z, same)
+        blocks[z // 2, 64 + 8 * (z % 2) : 72 + 8 * (z % 2), :] = tail
+        basis = block_vectors(vectors, z, same)
+        for k, piece in enumerate(pieces(basis, 2) + pieces(basis.T, 2)):
+            bases[z, k] = piece
         factor = -(tall[:, 1:2] * scale) / (tall[:, 2:3] + root)
         factors[z] = jnp.where(same, factor, 0.0)
-    for c in range(2):
-
-        @pl.when(lax.axis_index("c") == c)
-        def _():
-            pack(mine, payload, 512 * c)
-            pack(theirs, payload, 512 - 512 * c)
+    core = lax.axis_index("c")
+    mine[...] = blocks[core]
+    theirs[...] = blocks[1 - core]
 
 
 def back_part(cols, slabs, xc, sums, colsums, vectors, values):
@@ -313,12 +313,12 @@
         out_shape=(
             jax.ShapeDtypeStruct((ROWS, D), BF16),
             jax.ShapeDtypeStruct((8, D), F32),
-            jax.ShapeDtypeStruct((48, 768), F32),
-            jax.ShapeDtypeStruct((48, 768), F32),
-            jax.ShapeDtypeStruct((4, 256, 256), F32),
+            jax.ShapeDtypeStruct((80, 256), F32),
+            jax.ShapeDtypeStruct((80, 256), F32),
+            jax.ShapeDtypeStruct((4, 4, 256, 256), BF16),
             jax.ShapeDtypeStruct((4, 256, 256), F32),
         ),
-        scratch_shapes=[pltpu.VMEM((72, D), F32)],
+        scratch_shapes=[pltpu.VMEM((2, 80, 256), F32)],
         compiler_params=pltpu.CompilerParams(vmem_limit_bytes=14 << 20),
         name="back_part",
     )(cols, *slabs, xc, sums, *colsums, vectors, values)
@@ -335,31 +335,36 @@
     whiten,
     out,
     fix,
-    payload,
+    blocks,
     shift,
     sigma,
     row_vector,
     done,
     sent,
 ):
-    for c in range(2):
-
-        @pl.when(lax.axis_index("c") == c)
-        def _():
-            unpack(mine, payload, 512 * c)
-            unpack(theirs, payload, 512 - 512 * c)
-
+    core = lax.axis_index("c")
+    blocks[core] = mine[...]
+    blocks[1 - core] = theirs[...]
+    below = (lax.broadcasted_iota(jnp.int32, (256, 256), 0) & 63) - (
+        lax.broadcasted_iota(jnp.int32, (256, 256), 1) & 63
+    )
     for z in range(4):
         lanes = slice(256 * z, 256 * z + 256)
-        basis = bases[z]
-        total = payload[64:65, lanes]
-        mean = payload[65:66, lanes] * (1.0 / TOTAL)
-        stack = payload[0:64, lanes]
-        raw = jnp.concatenate([stack, stack, stack, stack], axis=0)
-        cov = raw - columns_of([mean])[:, 0:1] * total
-        rotated = fine(nn, fine(tn, basis, cov), basis)
-        inner = 0.5 * (rotated + rotated.T) * factors[z]
-        grad = fine(nt, fine(nn, basis, inner), basis)
+        start = 64 + 8 * (z % 2)
+        tail = blocks[z // 2, start : start + 8, :]
+        total, mean = tail[0:1], tail[1:2] * (1.0 / TOTAL)
+        packed = blocks[z // 2, 0:64, :]
+        square = jnp.concatenate([packed, packed, packed, packed], axis=0)
+        if z % 2 == 0:
+            raw = jnp.where(below <= 0, square, square.T)
+        else:
+            raw = jnp.where(below > 0, square, square.T)
+            raw = jnp.where(below == 0, tail[5:6], raw)
+        tall = columns_of([total, mean])
+        cov = raw - 0.5 * (tall[:, 1:2] * total + tall[:, 0:1] * mean)
+        basis, turned = (bases[z, 0], bases[z, 1]), (bases[z, 2], bases[z, 3])
+        rotated = fine(nn, turned, fine(nn, cov, basis))
+        grad = fine(nn, basis, fine(nn, rotated * factors[z], turned))
         sigma[z] = (grad * (2.0 / TOTAL)).astype(BF16)
         moved = own[0:1, lanes] * (1.0 / PIXELS) - total * (1.0 / TOTAL)
         offset = own[1:2, lanes] * (1.0 / PIXELS) - mean
@@ -379,7 +384,9 @@
     chosen = jnp.where(lane == row + first, shift[...], 0.0)
     chosen = jnp.sum(chosen, axis=1, keepdims=True)
     for a in range(3):
-        fix[a] = chosen * payload[66 + a : 67 + a, 0:768]
+        for z in range(3):
+            start = 66 + 8 * (z % 2) + a
+            fix[a, :, 256 * z : 256 * z + 256] = chosen * blocks[z // 2, start : start + 1, :]
     copies = []
     for b in range(IMAGES):
         rows = slice(H * 16 * b, H * 16 * b + H * 16)
@@ -404,7 +411,7 @@
             jax.ShapeDtypeStruct((3, 8, 768), F32),
         ),
         scratch_shapes=[
-            pltpu.VMEM((72, D), F32),
+            pltpu.VMEM((2, 80, 256), F32),
             pltpu.VMEM((1, D), F32),
             pltpu.VMEM((4, 256, 256), BF16),
             pltpu.VMEM((1, D), F32),
@@ -445,13 +452,6 @@
     return pick(0), pick(1)
 
 
-def joint(part, send, mine, move):
-    rows = send.size // 768
-    message = jnp.concatenate([send.reshape(rows, 768), mine], axis=0)
-    message = exchange(message, move)
-    return part + message[:rows].reshape(part.shape), mine + message[rows:]
-
-
 def local(features, grads, kernel, vectors, values):
     stay = lambda array: pltpu.with_memory_space_constraint(array, pltpu.HBM)
     cols, xc, wht, u, sums, whiten = prep(stay(features), stay(grads), stay(vectors), values)
@@ -471,27 +471,44 @@
     mine = mine + exchange(theirs, other_core)
 
     names = [["z1", "z2", "y1", "y2", "x1", "x2"] for _ in range(3)]
-    for turn in range(3):
+
+    def turn(k):
         for a in range(3):
-            axis = "xyz"[(a + turn) % 3]
+            axis = "xyz"[(a + k) % 3]
             dim = names[a].index(axis + "1")
             names[a].pop(dim)
             keep, send = halves(parts[a], dim)
-            if turn > 0 and a == 0:
-                parts[a], mine = joint(keep, send, mine, ring(axis, 0))
-            else:
-                parts[a] = keep + exchange(send, ring(axis, 0))
-        if turn == 0:
-            mine, *parts = lax.optimization_barrier((mine, *parts))
-            mine = mine + exchange(mine, ring("x", 0))
-    share = jnp.stack(parts, axis=0)
-    order = ["a", "z", "y", "x"]
-    for axis in "xyz":
+            parts[a] = keep + exchange(send, ring(axis, 0))
+
+    moves = [ring(axis, step) for axis in "xyz" for step in range(2)]
+
+    def after(value, *others):
+        return lax.optimization_barrier((value, *others))[0]
+
+    turn(0)
+    mine, *parts = lax.optimization_barrier((mine, *parts))
+    one = mine + exchange(mine, moves[0])
+    two = one + exchange(one, moves[1])
+    turn(1)
+    two, *parts = lax.optimization_barrier((two, *parts))
+    three = two + exchange(two, moves[2])
+    four = three + exchange(three, moves[3])
+    turn(2)
+    share = after(jnp.stack(parts, axis=3), three)
+    four = after(four, share)
+    five = four + exchange(four, moves[4])
+    order = ["z", "y", "x"]
+    for axis, ahead in (("x", None), ("y", four), ("z", five)):
+        if ahead is not None:
+            share = after(share, ahead)
         dim = order.index(axis)
         order.pop(dim)
         keep, send = halves(share, dim)
-        share, mine = joint(keep, send, mine, ring(axis, 1))
-    theirs = exchange(mine, other_core)
+        share = keep + exchange(send, ring(axis, 1))
+        if axis == "x":
+            five = after(five, share)
+            six = five + exchange(five, moves[5])
+    mine, theirs = six, exchange(six, other_core)
 
     input_grad, fix = final_part(dev, xc, mine, theirs, own, bases, factors, whiten)
     kernel_grad = (share - fix).transpose(1, 0, 2).reshape(8, 3, 3, O)

time: 108 us -> 96.4 us (0.89)
  waiting for transfers between devices: 46.1 us -> 29.7 us
  starting transfers between devices: 18 us -> 22.9 us
    ppermute x18 -> x23, waiting for transfers between devices: 46.1 us -> 29.7 us  [exchange(): return lax.ppermute(value, ALL, permutation(move))]
    ppermute x18 -> x23, starting transfers between devices: 18 us -> 22.9 us  [exchange(): return lax.ppermute(value, ALL, permutation(move))]
  transfers between devices with their start and end apart: 18 -> 23, of which waited for: 9 -> 12; matrix products, arithmetic and copies ran while one was open for 2% -> 2% of each run, Pallas kernels for 21% -> 31%
where the time goes in v5:
time: 96.4 us; the launch traced here: 95.2 us
  Pallas kernels  38.2 us (40%)
  waiting for transfers between devices  29.7 us (31%)
  starting transfers between devices  22.9 us (24%)
  other arithmetic  1.93 us (2%)
  local copies, waits for them, and re-layouts  1.46 us (2%)
  between operations  0.99 us (1%)
    ppermute x23, waiting for transfers between devices, exchange(): return lax.ppermute(value, ALL, permutation(move))  29.7 us
    ppermute x23, starting transfers between devices, exchange(): return lax.ppermute(value, ALL, permutation(move))  22.9 us
    pallas_call x1, Pallas kernels, back_part(): pl.pallas_call(back_kernel, in_specs=[ON_CHIP] * 11, out_specs=(ON_CHIP,)...  16.7 us
    pallas_call x3, Pallas kernels, weight_part(): pl.pallas_call(functools.partial(weight_kernel, a), in_specs=[ON_CHIP] *...  9.38 us
    pallas_call x1, Pallas kernels, final_part(): pl.pallas_call(final_kernel, in_specs=[ON_CHIP] * 8, out_specs=(IN_HBM, O...  7 us
    pallas_call x1, Pallas kernels, prep(): pl.pallas_call(prep_kernel, out_shape=(jax.ShapeDtypeStruct((IMAGES * H,...  5.12 us
  transfers between devices with their start and end apart: 23, of which 12 were waited for; matrix products, arithmetic and copies ran while one was open for 2% of the time, Pallas kernels for 31%

profile of v5, /device:TPU:0, one launch (start us, length us, event | category | flops | bytes accessed | tf_op | source)
XLA Modules:
  0.0 95.2 jit_solution(13496142409693143396)
XLA Ops:
  0.6 0.7 copy-done.1
  1.3 5.1 %prep.1 = (bf16[84,16,2304]{2,1,0:T(8,128)(2,1)S(1)}, bf16[84,16,1024]{2,1,0:T(8,128)(2,1)S(1)}, bf16[1040,1344]{1,0:T(8,128)(2,1)S(1)}, f32[1024,128]{1,0:T(8,1...) custom-call(bf16[6,14,14,1024]{3,2,1,0:T(8,128)(2,1)} %features_hbm.1, ...), custom_call_target="tpu_custom_call" | custom-call | tf_op jit(solution)/shard_map/prep/pallas_call | solution.py:179
  6.5 3.1 %weight_part_2.1 = (f32[512,768]{1,0:T(8,128)S(1)}, f32[512,768]{1,0:T(8,128)S(1)}, f32[8,768]{1,0:T(8,128)S(1)}, bf16[768,1024]{1,0:T(8,128)(2,1)S(1)}) custom-call(bf16[1040,1344]{1,0:T(8,128)(2,1)S(1)} %get-tuple-element.43.wht, bf16[1344,2304]{1,0:T(8,128)(2,1)S(1)} %bitcast.74, f32[1024,128]{1,0:T(8,128)S(1)} %get-tuple-element.44.u, ...), custom_call_target="tpu_custom_call" | custom-call | tf_op jit(solution)/shard_map/weight_part_2/pallas_call | solution.py:221
  9.7 3.1 %weight_part_0.1 = (f32[512,768]{1,0:T(8,128)S(1)}, f32[512,768]{1,0:T(8,128)S(1)}, f32[8,768]{1,0:T(8,128)S(1)}, bf16[768,1024]{1,0:T(8,128)(2,1)S(1)}) custom-call(bf16[1040,1344]{1,0:T(8,128)(2,1)S(1)} %get-tuple-element.43.wht, bf16[1344,2304]{1,0:T(8,128)(2,1)S(1)} %bitcast.75, f32[1024,128]{1,0:T(8,128)S(1)} %get-tuple-element.44.u, ...), custom_call_target="tpu_custom_call" | custom-call | tf_op jit(solution)/shard_map/weight_part_0/pallas_call | solution.py:221
  12.8 0.6 collective-permute-start
  13.4 3.1 %weight_part_1.1 = (f32[512,768]{1,0:T(8,128)S(1)}, f32[512,768]{1,0:T(8,128)S(1)}, f32[8,768]{1,0:T(8,128)S(1)}, bf16[768,1024]{1,0:T(8,128)(2,1)S(1)}) custom-call(bf16[1040,1344]{1,0:T(8,128)(2,1)S(1)} %get-tuple-element.43.wht, bf16[1344,2304]{1,0:T(8,128)(2,1)S(1)} %bitcast.76, f32[1024,128]{1,0:T(8,128)S(1)} %get-tuple-element.44.u, ...), custom_call_target="tpu_custom_call" | custom-call | tf_op jit(solution)/shard_map/weight_part_1/pallas_call | solution.py:221
  16.5 0.1 collective-permute-start.1
  16.6 0.2 add.71
  16.8 0.1 fusion.6
  17.0 2.1 %collective-permute-start.6 = (f32[2,2,2,2,2,8,768]{6,5,0,2,4,1,3:T(8,128)S(1)}, f32[2,2,2,2,2,8,768]{6,5,0,2,4,1,3:T(8,128)S(1)}, u32[]{:S(2)}, u32[]{:S(2)}) collective-permute-start(f32[2,2,2,2,2,8,768]{6,5,0,2,4,1,3:T(8,128)S(1)} %copy.11), channel_id=1, source_target_pairs={{0,32},{1,33},{2,34},{3,35},{4,100},{5,101},{6,102},{7,103},{8,40}... | collective-permute-start | bytes 2359304 | tf_op jit(solution)/shard_map/ppermute | solution.py:436
  19.1 0.2 add.66
  19.3 0.1 fusion.8
  19.5 1.7 %collective-permute-start.3 = (f32[2,2,2,2,2,8,768]{6,5,1,3,4,0,2:T(8,128)S(1)}, f32[2,2,2,2,2,8,768]{6,5,1,3,4,0,2:T(8,128)S(1)}, u32[]{:S(2)}, u32[]{:S(2)}) collective-permute-start(f32[2,2,2,2,2,8,768]{6,5,1,3,4,0,2:T(8,128)S(1)} %bitcast.87), channel_id=1, source_target_pairs={{0,1},{1,0},{2,3},{3,2},{4,7},{5,6},{6,5},{7,4},{8,9},{9,8},{10,11... | collective-permute-start | bytes 2359304 | tf_op jit(solution)/shard_map/ppermute | solution.py:436
  21.3 0.2 add.67
  21.5 0.1 fusion.7
  21.7 1.7 %collective-permute-start.4 = (f32[2,2,2,2,2,8,768]{6,5,1,2,4,3,0:T(8,128)S(1)}, f32[2,2,2,2,2,8,768]{6,5,1,2,4,3,0:T(8,128)S(1)}, u32[]{:S(2)}, u32[]{:S(2)}) collective-permute-start(f32[2,2,2,2,2,8,768]{6,5,1,2,4,3,0:T(8,128)S(1)} %bitcast.88), channel_id=1, source_target_pairs={{0,8},{1,9},{2,10},{3,11},{4,28},{5,29},{6,30},{7,31},{8,0},{9,1},... | collective-permute-start | bytes 2359304 | tf_op jit(solution)/shard_map/ppermute | solution.py:436
  23.4 16.7 %back_part.1 = (bf16[1344,1024]{1,0:T(8,128)(2,1)S(1)}, f32[8,1024]{1,0:T(8,128)S(1)}, f32[80,256]{1,0:T(8,128)S(1)}, f32[80,256]{1,0:T(8,128)S(1)}, bf16[4,4,25...) custom-call(bf16[1344,2304]{1,0:T(8,128)(2,1)S(1)} %bitcast.77, bf16[768,1024]{1,0:T(8,128)(2,1)S(1)} %get-tuple-element.50.slab0, ...), custom_call_target="tpu_custom_call" | custom-call | tf_op jit(solution)/shard_map/back_part/pallas_call | solution.py:309
  40.1 4.8 %collective-permute-start.2 = (f32[80,256]{1,0:T(8,128)S(1)}, f32[80,256]{1,0:T(8,128)S(1)}, u32[]{:S(2)}, u32[]{:S(2)}) collective-permute-start(f32[80,256]{1,0:T(8,128)S(1)} %get-tuple-element.60), channel_id=1, source_target_pairs={{0,4},{1,5},{2,6},{3,7},{4,0},{5,1},{6,2},{7,3},{8,12},{9,13},{10,... | collective-permute-start | bytes 245768 | tf_op jit(solution)/shard_map/ppermute | solution.py:436
  44.8 0.9 collective-permute-done.2
  45.8 0.1 copy_add_fusion
  45.9 0.1 fusion.1
  46.0 0.1 fusion
  46.1 0.3 collective-permute-start.7
  46.5 1.9 %collective-permute-start.11 = (f32[2,2,2,2,8,768]{5,4,0,2,3,1:T(8,128)S(1)}, f32[2,2,2,2,8,768]{5,4,0,2,3,1:T(8,128)S(1)}, u32[]{:S(2)}, u32[]{:S(2)}) collective-permute-start(f32[2,2,2,2,8,768]{5,4,0,2,3,1:T(8,128)S(1)} %slice_bitcast_fusion), channel_id=1, source_target_pairs={{0,1},{1,0},{2,3},{3,2},{4,7},{5,6},{6,5},{7,4},{8,9},{9,8},{10,11... | collective-permute-start | bytes 1179656 | tf_op jit(solution)/shard_map/ppermute | solution.py:436
  48.5 2.2 %collective-permute-done.7 = f32[80,256]{1,0:T(8,128)S(1)} collective-permute-done((f32[80,256]{1,0:T(8,128)S(1)}, f32[80,256]{1,0:T(8,128)S(1)}, u32[]{:S(2)}, u32[]{:S(2)}) %collective-permute-start.7) | collective-permute-done | bytes 81952 | tf_op jit(solution)/shard_map/ppermute | solution.py:436
  50.7 0.6 collective-permute-start.8
  51.2 0.2 collective-permute-start.9
  51.5 4.9 %collective-permute-done.8 = f32[80,256]{1,0:T(8,128)S(1)} collective-permute-done((f32[80,256]{1,0:T(8,128)S(1)}, f32[80,256]{1,0:T(8,128)S(1)}, u32[]{:S(2)}, u32[]{:S(2)}) %collective-permute-start.8) | collective-permute-done | bytes 81952 | tf_op jit(solution)/shard_map/ppermute | solution.py:436
  56.5 2.6 %collective-permute-done.9 = f32[2,2,2,2,8,768]{5,4,1,2,3,0:T(8,128)S(1)} collective-permute-done((f32[2,2,2,2,8,768]{5,4,1,2,3,0:T(8,128)S(1)}, f32[2,2,2,2,8,768]{5,4,1,2,3,0:T(8,128)S(1)}, u32[]{:S(2)}, u32[]{:S(2)}) %collective-permute-start.9) | collective-permute-done | bytes 393248 | tf_op jit(solution)/shard_map/ppermute | solution.py:436
  59.2 0.2 collective-permute-start.12
  59.4 2.0 %collective-permute-start.16 = (f32[2,2,2,8,768]{4,3,0,1,2:T(8,128)S(1)}, f32[2,2,2,8,768]{4,3,0,1,2:T(8,128)S(1)}, u32[]{:S(2)}, u32[]{:S(2)}) collective-permute-start(f32[2,2,2,8,768]{4,3,0,1,2:T(8,128)S(1)} %slice_bitcast_fusion.4), channel_id=1, source_target_pairs={{0,8},{1,9},{2,10},{3,11},{4,28},{5,29},{6,30},{7,31},{8,0},{9,1},... | collective-permute-start | bytes 589832 | tf_op jit(solution)/shard_map/ppermute | solution.py:436
  61.4 0.4 collective-permute-start.15
  61.8 1.9 %collective-permute-done.12 = f32[80,256]{1,0:T(8,128)S(1)} collective-permute-done((f32[80,256]{1,0:T(8,128)S(1)}, f32[80,256]{1,0:T(8,128)S(1)}, u32[]{:S(2)}, u32[]{:S(2)}) %collective-permute-start.12) | collective-permute-done | bytes 81952 | tf_op jit(solution)/shard_map/ppermute | solution.py:436
  63.7 2.1 %collective-permute-done.16 = f32[2,2,2,8,768]{4,3,0,1,2:T(8,128)S(1)} collective-permute-done((f32[2,2,2,8,768]{4,3,0,1,2:T(8,128)S(1)}, f32[2,2,2,8,768]{4,3,0,1,2:T(8,128)S(1)}, u32[]{:S(2)}, u32[]{:S(2)}) %collective-permute-start.16) | collective-permute-done | bytes 196640 | tf_op jit(solution)/shard_map/ppermute | solution.py:436
  65.8 1.3 %collective-permute-done.15 = f32[2,2,2,8,768]{4,3,0,1,2:T(8,128)S(1)} collective-permute-done((f32[2,2,2,8,768]{4,3,0,1,2:T(8,128)S(1)}, f32[2,2,2,8,768]{4,3,0,1,2:T(8,128)S(1)}, u32[]{:S(2)}, u32[]{:S(2)}) %collective-permute-start.15) | collective-permute-done | bytes 196640 | tf_op jit(solution)/shard_map/ppermute | solution.py:436
  67.2 0.3 collective-permute-done.14
  67.5 2.7 %collective-permute-start.18 = (f32[2,2,3,8,768]{4,3,2,0,1:T(8,128)S(1)}, f32[2,2,3,8,768]{4,3,2,0,1:T(8,128)S(1)}, u32[]{:S(2)}, u32[]{:S(2)}) collective-permute-start(f32[2,2,3,8,768]{4,3,2,0,1:T(8,128)S(1)} %slice_bitcast_fusion.3), channel_id=1, source_target_pairs={{0,3},{1,2},{2,1},{3,0},{4,5},{5,4},{6,7},{7,6},{8,11},{9,10},{10,... | collective-permute-start | bytes 884744 | tf_op jit(solution)/shard_map/ppermute | solution.py:436
  70.2 1.1 %collective-permute-start.13 = (f32[80,256]{1,0:T(8,128)S(1)}, f32[80,256]{1,0:T(8,128)S(1)}, u32[]{:S(2)}, u32[]{:S(2)}) collective-permute-start(f32[80,256]{1,0:T(8,128)S(1)} %add.78), channel_id=1, source_target_pairs={{0,24},{1,25},{2,26},{3,27},{4,12},{5,13},{6,14},{7,15},{8,16},{9,... | collective-permute-start | bytes 245768 | tf_op jit(solution)/shard_map/ppermute | solution.py:436
  71.3 4.5 %collective-permute-done.13 = f32[80,256]{1,0:T(8,128)S(1)} collective-permute-done((f32[80,256]{1,0:T(8,128)S(1)}, f32[80,256]{1,0:T(8,128)S(1)}, u32[]{:S(2)}, u32[]{:S(2)}) %collective-permute-start.13) | collective-permute-done | bytes 81952 | tf_op jit(solution)/shard_map/ppermute | solution.py:436
  75.9 0.1 collective-permute-start.17
  76.0 1.2 %collective-permute-start.21 = (f32[2,3,8,768]{3,2,1,0:T(8,128)S(1)}, f32[2,3,8,768]{3,2,1,0:T(8,128)S(1)}, u32[]{:S(2)}, u32[]{:S(2)}) collective-permute-start(f32[2,3,8,768]{3,2,1,0:T(8,128)S(1)} %slice_bitcast_fusion.7), channel_id=1, source_target_pairs={{0,24},{1,25},{2,26},{3,27},{4,12},{5,13},{6,14},{7,15},{8,16},{9,... | collective-permute-start | bytes 442376 | tf_op jit(solution)/shard_map/ppermute | solution.py:436
  77.2 3.1 %collective-permute-done.17 = f32[80,256]{1,0:T(8,128)S(1)} collective-permute-done((f32[80,256]{1,0:T(8,128)S(1)}, f32[80,256]{1,0:T(8,128)S(1)}, u32[]{:S(2)}, u32[]{:S(2)}) %collective-permute-start.17) | collective-permute-done | bytes 81952 | tf_op jit(solution)/shard_map/ppermute | solution.py:436
  80.4 0.6 collective-permute-start.19
  81.0 5.2 %collective-permute-done.19 = f32[80,256]{1,0:T(8,128)S(1)} collective-permute-done((f32[80,256]{1,0:T(8,128)S(1)}, f32[80,256]{1,0:T(8,128)S(1)}, u32[]{:S(2)}, u32[]{:S(2)}) %collective-permute-start.19) | collective-permute-done | bytes 81952 | tf_op jit(solution)/shard_map/ppermute | solution.py:436
  86.3 0.6 collective-permute-start.22
  86.8 0.6 collective-permute-done.20.theirs
  87.5 7.0 %final_part.1 = (bf16[6,14,14,1024]{3,2,1,0:T(8,128)(2,1)}, f32[3,8,768]{2,1,0:T(8,128)S(1)}) custom-call(bf16[1344,1024]{1,0:T(8,128)(2,1)S(1)} %get-tuple-element.58.dev, bf16[1344,1024]{1,0:T(8,128)(2,1)S(1)} %bitcast.79, f32[80,256]{1,0:T(8,128)S(1)} %add.85.mine, f32[80,256]{1,0:T(8,128)S(1)} %collective-permute-done.20.theirs, ...), custom_call_target="tpu_custom_call" | custom-call | tf_op jit(solution)/shard_map/final_part/pallas_call | solution.py:405
  94.5 0.6 fusion.5
  (48 shorter events, 1.1 us)
Async XLA Ops:
  0.6 0.7 copy-start.1
  9.6 7.0 %collective-permute-start.5 = (f32[512,768]{1,0:T(8,128)S(1)}, f32[512,768]{1,0:T(8,128)S(1)}, u32[]{:S(2)}, u32[]{:S(2)}) collective-permute-start(f32[512,768]{1,0:T(8,128)S(1)} %get-tuple-element.62), channel_id=1, source_target_pairs={{0,4},{1,5},{2,6},{3,7},{4,0},{5,1},{6,2},{7,3},{8,12},{9,13},{10,... | collective-permute-start | bytes 4718600 | tf_op jit(solution)/shard_map/ppermute | solution.py:436
  12.8 6.3 %collective-permute-start = (f32[512,768]{1,0:T(8,128)S(1)}, f32[512,768]{1,0:T(8,128)S(1)}, u32[]{:S(2)}, u32[]{:S(2)}) collective-permute-start(f32[512,768]{1,0:T(8,128)S(1)} %get-tuple-element.46), channel_id=1, source_target_pairs={{0,4},{1,5},{2,6},{3,7},{4,0},{5,1},{6,2},{7,3},{8,12},{9,13},{10,... | collective-permute-start | bytes 4718600 | tf_op jit(solution)/shard_map/ppermute | solution.py:436
  16.5 4.7 %collective-permute-start.1 = (f32[512,768]{1,0:T(8,128)S(1)}, f32[512,768]{1,0:T(8,128)S(1)}, u32[]{:S(2)}, u32[]{:S(2)}) collective-permute-start(f32[512,768]{1,0:T(8,128)S(1)} %get-tuple-element.48), channel_id=1, source_target_pairs={{0,4},{1,5},{2,6},{3,7},{4,0},{5,1},{6,2},{7,3},{8,12},{9,13},{10,... | collective-permute-start | bytes 4718600 | tf_op jit(solution)/shard_map/ppermute | solution.py:436
  17.0 28.8 %collective-permute-start.6 = (f32[2,2,2,2,2,8,768]{6,5,0,2,4,1,3:T(8,128)S(1)}, f32[2,2,2,2,2,8,768]{6,5,0,2,4,1,3:T(8,128)S(1)}, u32[]{:S(2)}, u32[]{:S(2)}) collective-permute-start(f32[2,2,2,2,2,8,768]{6,5,0,2,4,1,3:T(8,128)S(1)} %copy.11), channel_id=1, source_target_pairs={{0,32},{1,33},{2,34},{3,35},{4,100},{5,101},{6,102},{7,103},{8,40}... | collective-permute-start | bytes 2359304 | tf_op jit(solution)/shard_map/ppermute | solution.py:436
  19.5 26.4 %collective-permute-start.3 = (f32[2,2,2,2,2,8,768]{6,5,1,3,4,0,2:T(8,128)S(1)}, f32[2,2,2,2,2,8,768]{6,5,1,3,4,0,2:T(8,128)S(1)}, u32[]{:S(2)}, u32[]{:S(2)}) collective-permute-start(f32[2,2,2,2,2,8,768]{6,5,1,3,4,0,2:T(8,128)S(1)} %bitcast.87), channel_id=1, source_target_pairs={{0,1},{1,0},{2,3},{3,2},{4,7},{5,6},{6,5},{7,4},{8,9},{9,8},{10,11... | collective-permute-start | bytes 2359304 | tf_op jit(solution)/shard_map/ppermute | solution.py:436
  21.6 1.8 %copy-start = (f32[16,64,64]{2,1,0:T(8,128)S(1)}, f32[16,64,64]{2,1,0:T(8,128)}, u32[]{:S(2)}) copy-start(f32[16,64,64]{2,1,0:T(8,128)} %vectors.1) | copy-start | bytes 786436
  21.6 1.8 %copy-start.2 = (f32[16,64]{1,0:T(8,128)S(1)}, f32[16,64]{1,0:T(8,128)}, u32[]{:S(2)}) copy-start(f32[16,64]{1,0:T(8,128)} %values.3) | copy-start | bytes 12292
  21.7 24.3 %collective-permute-start.4 = (f32[2,2,2,2,2,8,768]{6,5,1,2,4,3,0:T(8,128)S(1)}, f32[2,2,2,2,2,8,768]{6,5,1,2,4,3,0:T(8,128)S(1)}, u32[]{:S(2)}, u32[]{:S(2)}) collective-permute-start(f32[2,2,2,2,2,8,768]{6,5,1,2,4,3,0:T(8,128)S(1)} %bitcast.88), channel_id=1, source_target_pairs={{0,8},{1,9},{2,10},{3,11},{4,28},{5,29},{6,30},{7,31},{8,0},{9,1},... | collective-permute-start | bytes 2359304 | tf_op jit(solution)/shard_map/ppermute | solution.py:436
  40.1 5.7 %collective-permute-start.2 = (f32[80,256]{1,0:T(8,128)S(1)}, f32[80,256]{1,0:T(8,128)S(1)}, u32[]{:S(2)}, u32[]{:S(2)}) collective-permute-start(f32[80,256]{1,0:T(8,128)S(1)} %get-tuple-element.60), channel_id=1, source_target_pairs={{0,4},{1,5},{2,6},{3,7},{4,0},{5,1},{6,2},{7,3},{8,12},{9,13},{10,... | collective-permute-start | bytes 245768 | tf_op jit(solution)/shard_map/ppermute | solution.py:436
  46.1 4.5 %collective-permute-start.7 = (f32[80,256]{1,0:T(8,128)S(1)}, f32[80,256]{1,0:T(8,128)S(1)}, u32[]{:S(2)}, u32[]{:S(2)}) collective-permute-start(f32[80,256]{1,0:T(8,128)S(1)} %add.68), channel_id=1, source_target_pairs={{0,1},{1,0},{2,3},{3,2},{4,7},{5,6},{6,5},{7,4},{8,9},{9,8},{10,11... | collective-permute-start | bytes 245768 | tf_op jit(solution)/shard_map/ppermute | solution.py:436
  46.5 10.0 %collective-permute-start.11 = (f32[2,2,2,2,8,768]{5,4,0,2,3,1:T(8,128)S(1)}, f32[2,2,2,2,8,768]{5,4,0,2,3,1:T(8,128)S(1)}, u32[]{:S(2)}, u32[]{:S(2)}) collective-permute-start(f32[2,2,2,2,8,768]{5,4,0,2,3,1:T(8,128)S(1)} %slice_bitcast_fusion), channel_id=1, source_target_pairs={{0,1},{1,0},{2,3},{3,2},{4,7},{5,6},{6,5},{7,4},{8,9},{9,8},{10,11... | collective-permute-start | bytes 1179656 | tf_op jit(solution)/shard_map/ppermute | solution.py:436
  48.4 8.1 %collective-permute-start.10 = (f32[2,2,2,2,8,768]{5,4,0,1,3,2:T(8,128)S(1)}, f32[2,2,2,2,8,768]{5,4,0,1,3,2:T(8,128)S(1)}, u32[]{:S(2)}, u32[]{:S(2)}) collective-permute-start(f32[2,2,2,2,8,768]{5,4,0,1,3,2:T(8,128)S(1)} %slice_bitcast_fusion.1), channel_id=1, source_target_pairs={{0,32},{1,33},{2,34},{3,35},{4,100},{5,101},{6,102},{7,103},{8,40}... | collective-permute-start | bytes 1179656 | tf_op jit(solution)/shard_map/ppermute | solution.py:436
  50.7 5.7 %collective-permute-start.8 = (f32[80,256]{1,0:T(8,128)S(1)}, f32[80,256]{1,0:T(8,128)S(1)}, u32[]{:S(2)}, u32[]{:S(2)}) collective-permute-start(f32[80,256]{1,0:T(8,128)S(1)} %add.73), channel_id=1, source_target_pairs={{0,3},{1,2},{2,1},{3,0},{4,5},{5,4},{6,7},{7,6},{8,11},{9,10},{10,... | collective-permute-start | bytes 245768 | tf_op jit(solution)/shard_map/ppermute | solution.py:436
  51.2 7.9 %collective-permute-start.9 = (f32[2,2,2,2,8,768]{5,4,1,2,3,0:T(8,128)S(1)}, f32[2,2,2,2,8,768]{5,4,1,2,3,0:T(8,128)S(1)}, u32[]{:S(2)}, u32[]{:S(2)}) collective-permute-start(f32[2,2,2,2,8,768]{5,4,1,2,3,0:T(8,128)S(1)} %slice_bitcast_fusion.2), channel_id=1, source_target_pairs={{0,8},{1,9},{2,10},{3,11},{4,28},{5,29},{6,30},{7,31},{8,0},{9,1},... | collective-permute-start | bytes 1179656 | tf_op jit(solution)/shard_map/ppermute | solution.py:436
  59.2 4.5 %collective-permute-start.12 = (f32[80,256]{1,0:T(8,128)S(1)}, f32[80,256]{1,0:T(8,128)S(1)}, u32[]{:S(2)}, u32[]{:S(2)}) collective-permute-start(f32[80,256]{1,0:T(8,128)S(1)} %add.74), channel_id=1, source_target_pairs={{0,8},{1,9},{2,10},{3,11},{4,28},{5,29},{6,30},{7,31},{8,0},{9,1},... | collective-permute-start | bytes 245768 | tf_op jit(solution)/shard_map/ppermute | solution.py:436
  59.4 6.4 %collective-permute-start.16 = (f32[2,2,2,8,768]{4,3,0,1,2:T(8,128)S(1)}, f32[2,2,2,8,768]{4,3,0,1,2:T(8,128)S(1)}, u32[]{:S(2)}, u32[]{:S(2)}) collective-permute-start(f32[2,2,2,8,768]{4,3,0,1,2:T(8,128)S(1)} %slice_bitcast_fusion.4), channel_id=1, source_target_pairs={{0,8},{1,9},{2,10},{3,11},{4,28},{5,29},{6,30},{7,31},{8,0},{9,1},... | collective-permute-start | bytes 589832 | tf_op jit(solution)/shard_map/ppermute | solution.py:436
  61.4 5.7 %collective-permute-start.15 = (f32[2,2,2,8,768]{4,3,0,1,2:T(8,128)S(1)}, f32[2,2,2,8,768]{4,3,0,1,2:T(8,128)S(1)}, u32[]{:S(2)}, u32[]{:S(2)}) collective-permute-start(f32[2,2,2,8,768]{4,3,0,1,2:T(8,128)S(1)} %slice_bitcast_fusion.5), channel_id=1, source_target_pairs={{0,1},{1,0},{2,3},{3,2},{4,7},{5,6},{6,5},{7,4},{8,9},{9,8},{10,11... | collective-permute-start | bytes 589832 | tf_op jit(solution)/shard_map/ppermute | solution.py:436
  61.8 5.7 %collective-permute-start.14 = (f32[2,2,2,8,768]{4,3,0,1,2:T(8,128)S(1)}, f32[2,2,2,8,768]{4,3,0,1,2:T(8,128)S(1)}, u32[]{:S(2)}, u32[]{:S(2)}) collective-permute-start(f32[2,2,2,8,768]{4,3,0,1,2:T(8,128)S(1)} %slice_bitcast_fusion.6), channel_id=1, source_target_pairs={{0,32},{1,33},{2,34},{3,35},{4,100},{5,101},{6,102},{7,103},{8,40}... | collective-permute-start | bytes 589832 | tf_op jit(solution)/shard_map/ppermute | solution.py:436
  67.5 8.4 %collective-permute-start.18 = (f32[2,2,3,8,768]{4,3,2,0,1:T(8,128)S(1)}, f32[2,2,3,8,768]{4,3,2,0,1:T(8,128)S(1)}, u32[]{:S(2)}, u32[]{:S(2)}) collective-permute-start(f32[2,2,3,8,768]{4,3,2,0,1:T(8,128)S(1)} %slice_bitcast_fusion.3), channel_id=1, source_target_pairs={{0,3},{1,2},{2,1},{3,0},{4,5},{5,4},{6,7},{7,6},{8,11},{9,10},{10,... | collective-permute-start | bytes 884744 | tf_op jit(solution)/shard_map/ppermute | solution.py:436
  70.2 5.7 %collective-permute-start.13 = (f32[80,256]{1,0:T(8,128)S(1)}, f32[80,256]{1,0:T(8,128)S(1)}, u32[]{:S(2)}, u32[]{:S(2)}) collective-permute-start(f32[80,256]{1,0:T(8,128)S(1)} %add.78), channel_id=1, source_target_pairs={{0,24},{1,25},{2,26},{3,27},{4,12},{5,13},{6,14},{7,15},{8,16},{9,... | collective-permute-start | bytes 245768 | tf_op jit(solution)/shard_map/ppermute | solution.py:436
  75.9 4.5 %collective-permute-start.17 = (f32[80,256]{1,0:T(8,128)S(1)}, f32[80,256]{1,0:T(8,128)S(1)}, u32[]{:S(2)}, u32[]{:S(2)}) collective-permute-start(f32[80,256]{1,0:T(8,128)S(1)} %add.79), channel_id=1, source_target_pairs={{0,32},{1,33},{2,34},{3,35},{4,100},{5,101},{6,102},{7,103},{8,40}... | collective-permute-start | bytes 245768 | tf_op jit(solution)/shard_map/ppermute | solution.py:436
  76.0 10.2 %collective-permute-start.21 = (f32[2,3,8,768]{3,2,1,0:T(8,128)S(1)}, f32[2,3,8,768]{3,2,1,0:T(8,128)S(1)}, u32[]{:S(2)}, u32[]{:S(2)}) collective-permute-start(f32[2,3,8,768]{3,2,1,0:T(8,128)S(1)} %slice_bitcast_fusion.7), channel_id=1, source_target_pairs={{0,24},{1,25},{2,26},{3,27},{4,12},{5,13},{6,14},{7,15},{8,16},{9,... | collective-permute-start | bytes 442376 | tf_op jit(solution)/shard_map/ppermute | solution.py:436
  80.4 5.7 %collective-permute-start.19 = (f32[80,256]{1,0:T(8,128)S(1)}, f32[80,256]{1,0:T(8,128)S(1)}, u32[]{:S(2)}, u32[]{:S(2)}) collective-permute-start(f32[80,256]{1,0:T(8,128)S(1)} %add.83), channel_id=1, source_target_pairs={{0,96},{1,97},{2,98},{3,99},{4,36},{5,37},{6,38},{7,39},{8,104},{9... | collective-permute-start | bytes 245768 | tf_op jit(solution)/shard_map/ppermute | solution.py:436
  86.1 1.4 %collective-permute-start.20 = (f32[80,256]{1,0:T(8,128)S(1)}, f32[80,256]{1,0:T(8,128)S(1)}, u32[]{:S(2)}, u32[]{:S(2)}) collective-permute-start(f32[80,256]{1,0:T(8,128)S(1)} %add.85.mine), channel_id=1, source_target_pairs={{0,4},{1,5},{2,6},{3,7},{4,0},{5,1},{6,2},{7,3},{8,12},{9,13},{10,... | collective-permute-start | bytes 245768 | tf_op jit(solution)/shard_map/ppermute | solution.py:436
  86.3 8.2 %collective-permute-start.22 = (f32[3,8,768]{2,1,0:T(8,128)S(1)}, f32[3,8,768]{2,1,0:T(8,128)S(1)}, u32[]{:S(2)}, u32[]{:S(2)}) collective-permute-start(f32[3,8,768]{2,1,0:T(8,128)S(1)} %slice_bitcast_fusion.8), channel_id=1, source_target_pairs={{0,96},{1,97},{2,98},{3,99},{4,36},{5,37},{6,38},{7,39},{8,104},{9... | collective-permute-start | bytes 221192 | tf_op jit(solution)/shard_map/ppermute | solution.py:436

commit v6 on v5

--- a/solution.py
+++ b/solution.py
@@ -253,12 +253,9 @@
     bases,
     factors,
     blocks,
+    tails,
 ):
     same = same_group()
-    eye = lax.broadcasted_iota(jnp.int32, (256, 256), 0) == lax.broadcasted_iota(
-        jnp.int32, (256, 256), 1
-    )
-    eye = jnp.where(eye, 1.0, 0.0).astype(BF16)
     real = (lax.broadcasted_iota(jnp.int32, (ROWS, 256), 0) & 15) < W
     group = lax.broadcasted_iota(jnp.int32, (64, 256), 1) >> 6
     below = lax.broadcasted_iota(jnp.int32, (64, 256), 0) - (
@@ -274,11 +271,14 @@
         total = jnp.sum(back, axis=0, keepdims=True)
         low = jnp.where(real, back - total * (1.0 / PIXELS), 0.0).astype(BF16)
         dev[:, lanes] = low
+        tails[z : z + 1, :] = total
+    for z in range(4):
+        lanes = slice(256 * z, 256 * z + 256)
+        total = tails[z : z + 1, :]
         value = value_row(values, z)
         scale, root = lax.rsqrt(value), jnp.sqrt(value)
         tall = columns_of([sums[:, lanes] * (1.0 / PIXELS), scale, root])
-        turned = nt(eye, xc[:, lanes]).astype(BF16)
-        cov = nn(turned, low) + tall[:, 0:1] * total
+        cov = tn(xc[:, lanes], dev[:, lanes]) + tall[:, 0:1] * total
         cov = 0.5 * (cov + cov.T)
         packed = cov[0:64]
         for k in range(1, 4):
@@ -318,7 +318,7 @@
             jax.ShapeDtypeStruct((4, 4, 256, 256), BF16),
             jax.ShapeDtypeStruct((4, 256, 256), F32),
         ),
-        scratch_shapes=[pltpu.VMEM((2, 80, 256), F32)],
+        scratch_shapes=[pltpu.VMEM((2, 80, 256), F32), pltpu.VMEM((8, 256), F32)],
         compiler_params=pltpu.CompilerParams(vmem_limit_bytes=14 << 20),
         name="back_part",
     )(cols, *slabs, xc, sums, *colsums, vectors, values)
@@ -494,20 +494,18 @@
     three = two + exchange(two, moves[2])
     four = three + exchange(three, moves[3])
     turn(2)
-    share = after(jnp.stack(parts, axis=3), three)
-    four = after(four, share)
+    share = after(jnp.stack(parts, axis=3), four)
     five = four + exchange(four, moves[4])
     order = ["z", "y", "x"]
-    for axis, ahead in (("x", None), ("y", four), ("z", five)):
-        if ahead is not None:
-            share = after(share, ahead)
+    for axis in "xyz":
+        if axis == "y":
+            share = after(share, five)
+            six = after(five, share)
+            six = six + exchange(six, moves[5])
         dim = order.index(axis)
         order.pop(dim)
         keep, send = halves(share, dim)
         share = keep + exchange(send, ring(axis, 1))
-        if axis == "x":
-            five = after(five, share)
-            six = five + exchange(five, moves[5])
     mine, theirs = six, exchange(six, other_core)
 
     input_grad, fix = final_part(dev, xc, mine, theirs, own, bases, factors, whiten)

time: 96.4 us -> 89.3 us (0.926)
  Pallas kernels: 38.2 us -> 30.5 us
  starting transfers between devices: 22.9 us -> 27 us
  waiting for transfers between devices: 29.7 us -> 27 us
    pallas_call x1, Pallas kernels: 16.7 us -> 8.98 us  [back_part(): pl.pallas_call(back_kernel, in_specs=[ON_CHIP] * 11, out_specs=(ON_CHIP,)...]
    ppermute x23, starting transfers between devices: 22.9 us -> 27 us  [exchange(): return lax.ppermute(value, ALL, permutation(move))]
    ppermute x23, waiting for transfers between devices: 29.7 us -> 27 us  [exchange(): return lax.ppermute(value, ALL, permutation(move))]
  transfers between devices with their start and end apart: 23 -> 23, of which waited for: 12 -> 11; matrix products, arithmetic and copies ran while one was open for 2% -> 2% of each run, Pallas kernels for 31% -> 25%
where the time goes in v6:
time: 89.3 us; the launch traced here: 88.9 us
  Pallas kernels  30.5 us (34%)
  starting transfers between devices  27 us (30%)
  waiting for transfers between devices  27 us (30%)
  other arithmetic  1.93 us (2%)
  local copies, waits for them, and re-layouts  1.46 us (2%)
  between operations  0.98 us (1%)
    ppermute x23, waiting for transfers between devices, exchange(): return lax.ppermute(value, ALL, permutation(move))  27 us
    ppermute x23, starting transfers between devices, exchange(): return lax.ppermute(value, ALL, permutation(move))  27 us
    pallas_call x3, Pallas kernels, weight_part(): pl.pallas_call(functools.partial(weight_kernel, a), in_specs=[ON_CHIP] *...  9.38 us
    pallas_call x1, Pallas kernels, back_part(): pl.pallas_call(back_kernel, in_specs=[ON_CHIP] * 11, out_specs=(ON_CHIP,)...  8.98 us
    pallas_call x1, Pallas kernels, final_part(): pl.pallas_call(final_kernel, in_specs=[ON_CHIP] * 8, out_specs=(IN_HBM, O...  7 us
    pallas_call x1, Pallas kernels, prep(): pl.pallas_call(prep_kernel, out_shape=(jax.ShapeDtypeStruct((IMAGES * H,...  5.12 us
  transfers between devices with their start and end apart: 23, of which 11 were waited for; matrix products, arithmetic and copies ran while one was open for 2% of the time, Pallas kernels for 25%

profile of v6, /device:TPU:0, one launch (start us, length us, event | category | flops | bytes accessed | tf_op | source)
XLA Modules:
  0.0 88.9 jit_solution(12653248059520444664)
XLA Ops:
  0.6 0.7 copy-done.1
  1.3 5.1 %prep.1 = (bf16[84,16,2304]{2,1,0:T(8,128)(2,1)S(1)}, bf16[84,16,1024]{2,1,0:T(8,128)(2,1)S(1)}, bf16[1040,1344]{1,0:T(8,128)(2,1)S(1)}, f32[1024,128]{1,0:T(8,1...) custom-call(bf16[6,14,14,1024]{3,2,1,0:T(8,128)(2,1)} %features_hbm.1, ...), custom_call_target="tpu_custom_call" | custom-call | tf_op jit(solution)/shard_map/prep/pallas_call | solution.py:179
  6.5 3.1 %weight_part_2.1 = (f32[512,768]{1,0:T(8,128)S(1)}, f32[512,768]{1,0:T(8,128)S(1)}, f32[8,768]{1,0:T(8,128)S(1)}, bf16[768,1024]{1,0:T(8,128)(2,1)S(1)}) custom-call(bf16[1040,1344]{1,0:T(8,128)(2,1)S(1)} %get-tuple-element.41.wht, bf16[1344,2304]{1,0:T(8,128)(2,1)S(1)} %bitcast.76, f32[1024,128]{1,0:T(8,128)S(1)} %get-tuple-element.42.u, ...), custom_call_target="tpu_custom_call" | custom-call | tf_op jit(solution)/shard_map/weight_part_2/pallas_call | solution.py:221
  9.7 3.1 %weight_part_0.1 = (f32[512,768]{1,0:T(8,128)S(1)}, f32[512,768]{1,0:T(8,128)S(1)}, f32[8,768]{1,0:T(8,128)S(1)}, bf16[768,1024]{1,0:T(8,128)(2,1)S(1)}) custom-call(bf16[1040,1344]{1,0:T(8,128)(2,1)S(1)} %get-tuple-element.41.wht, bf16[1344,2304]{1,0:T(8,128)(2,1)S(1)} %bitcast.77, f32[1024,128]{1,0:T(8,128)S(1)} %get-tuple-element.42.u, ...), custom_call_target="tpu_custom_call" | custom-call | tf_op jit(solution)/shard_map/weight_part_0/pallas_call | solution.py:221
  12.8 0.6 collective-permute-start
  13.4 3.1 %weight_part_1.1 = (f32[512,768]{1,0:T(8,128)S(1)}, f32[512,768]{1,0:T(8,128)S(1)}, f32[8,768]{1,0:T(8,128)S(1)}, bf16[768,1024]{1,0:T(8,128)(2,1)S(1)}) custom-call(bf16[1040,1344]{1,0:T(8,128)(2,1)S(1)} %get-tuple-element.41.wht, bf16[1344,2304]{1,0:T(8,128)(2,1)S(1)} %bitcast.78, f32[1024,128]{1,0:T(8,128)S(1)} %get-tuple-element.42.u, ...), custom_call_target="tpu_custom_call" | custom-call | tf_op jit(solution)/shard_map/weight_part_1/pallas_call | solution.py:221
  16.5 0.1 collective-permute-start.1
  16.6 0.2 add.71
  16.8 0.1 fusion.7
  17.0 2.1 %collective-permute-start.6 = (f32[2,2,2,2,2,8,768]{6,5,0,2,4,1,3:T(8,128)S(1)}, f32[2,2,2,2,2,8,768]{6,5,0,2,4,1,3:T(8,128)S(1)}, u32[]{:S(2)}, u32[]{:S(2)}) collective-permute-start(f32[2,2,2,2,2,8,768]{6,5,0,2,4,1,3:T(8,128)S(1)} %copy.11), channel_id=1, source_target_pairs={{0,32},{1,33},{2,34},{3,35},{4,100},{5,101},{6,102},{7,103},{8,40}... | collective-permute-start | bytes 2359304 | tf_op jit(solution)/shard_map/ppermute | solution.py:436
  19.1 0.2 add.66
  19.3 0.1 fusion.9
  19.5 1.7 %collective-permute-start.3 = (f32[2,2,2,2,2,8,768]{6,5,1,3,4,0,2:T(8,128)S(1)}, f32[2,2,2,2,2,8,768]{6,5,1,3,4,0,2:T(8,128)S(1)}, u32[]{:S(2)}, u32[]{:S(2)}) collective-permute-start(f32[2,2,2,2,2,8,768]{6,5,1,3,4,0,2:T(8,128)S(1)} %bitcast.89), channel_id=1, source_target_pairs={{0,1},{1,0},{2,3},{3,2},{4,7},{5,6},{6,5},{7,4},{8,9},{9,8},{10,11... | collective-permute-start | bytes 2359304 | tf_op jit(solution)/shard_map/ppermute | solution.py:436
  21.3 0.2 add.67
  21.5 0.1 fusion.8
  21.7 1.7 %collective-permute-start.4 = (f32[2,2,2,2,2,8,768]{6,5,1,2,4,3,0:T(8,128)S(1)}, f32[2,2,2,2,2,8,768]{6,5,1,2,4,3,0:T(8,128)S(1)}, u32[]{:S(2)}, u32[]{:S(2)}) collective-permute-start(f32[2,2,2,2,2,8,768]{6,5,1,2,4,3,0:T(8,128)S(1)} %bitcast.90), channel_id=1, source_target_pairs={{0,8},{1,9},{2,10},{3,11},{4,28},{5,29},{6,30},{7,31},{8,0},{9,1},... | collective-permute-start | bytes 2359304 | tf_op jit(solution)/shard_map/ppermute | solution.py:436
  23.4 9.0 %back_part.1 = (bf16[1344,1024]{1,0:T(8,128)(2,1)S(1)}, f32[8,1024]{1,0:T(8,128)S(1)}, f32[80,256]{1,0:T(8,128)S(1)}, f32[80,256]{1,0:T(8,128)S(1)}, bf16[4,4,25...) custom-call(bf16[1344,2304]{1,0:T(8,128)(2,1)S(1)} %bitcast.79, bf16[768,1024]{1,0:T(8,128)(2,1)S(1)} %get-tuple-element.48.slab0, ...), custom_call_target="tpu_custom_call" | custom-call | tf_op jit(solution)/shard_map/back_part/pallas_call | solution.py:309
  32.4 4.6 %collective-permute-start.2 = (f32[80,256]{1,0:T(8,128)S(1)}, f32[80,256]{1,0:T(8,128)S(1)}, u32[]{:S(2)}, u32[]{:S(2)}) collective-permute-start(f32[80,256]{1,0:T(8,128)S(1)} %get-tuple-element.58), channel_id=1, source_target_pairs={{0,4},{1,5},{2,6},{3,7},{4,0},{5,1},{6,2},{7,3},{8,12},{9,13},{10,... | collective-permute-start | bytes 245768 | tf_op jit(solution)/shard_map/ppermute | solution.py:436
  36.9 0.9 %collective-permute-done.2 = f32[80,256]{1,0:T(8,128)S(1)} collective-permute-done((f32[80,256]{1,0:T(8,128)S(1)}, f32[80,256]{1,0:T(8,128)S(1)}, u32[]{:S(2)}, u32[]{:S(2)}) %collective-permute-start.2) | collective-permute-done | bytes 81952 | tf_op jit(solution)/shard_map/ppermute | solution.py:436
  37.9 0.1 copy_add_fusion
  38.0 0.1 fusion.1
  38.1 0.1 fusion
  38.2 0.3 collective-permute-start.7
  38.5 1.9 %collective-permute-start.11 = (f32[2,2,2,2,8,768]{5,4,0,2,3,1:T(8,128)S(1)}, f32[2,2,2,2,8,768]{5,4,0,2,3,1:T(8,128)S(1)}, u32[]{:S(2)}, u32[]{:S(2)}) collective-permute-start(f32[2,2,2,2,8,768]{5,4,0,2,3,1:T(8,128)S(1)} %slice_bitcast_fusion), channel_id=1, source_target_pairs={{0,1},{1,0},{2,3},{3,2},{4,7},{5,6},{6,5},{7,4},{8,9},{9,8},{10,11... | collective-permute-start | bytes 1179656 | tf_op jit(solution)/shard_map/ppermute | solution.py:436
  40.5 0.1 collective-permute-start.10
  40.6 2.2 %collective-permute-done.7 = f32[80,256]{1,0:T(8,128)S(1)} collective-permute-done((f32[80,256]{1,0:T(8,128)S(1)}, f32[80,256]{1,0:T(8,128)S(1)}, u32[]{:S(2)}, u32[]{:S(2)}) %collective-permute-start.7) | collective-permute-done | bytes 81952 | tf_op jit(solution)/shard_map/ppermute | solution.py:436
  42.7 0.5 collective-permute-start.8
  43.3 0.2 collective-permute-start.9
  43.5 4.9 %collective-permute-done.8 = f32[80,256]{1,0:T(8,128)S(1)} collective-permute-done((f32[80,256]{1,0:T(8,128)S(1)}, f32[80,256]{1,0:T(8,128)S(1)}, u32[]{:S(2)}, u32[]{:S(2)}) %collective-permute-start.8) | collective-permute-done | bytes 81952 | tf_op jit(solution)/shard_map/ppermute | solution.py:436
  48.6 2.5 %collective-permute-done.9 = f32[2,2,2,2,8,768]{5,4,1,2,3,0:T(8,128)S(1)} collective-permute-done((f32[2,2,2,2,8,768]{5,4,1,2,3,0:T(8,128)S(1)}, f32[2,2,2,2,8,768]{5,4,1,2,3,0:T(8,128)S(1)}, u32[]{:S(2)}, u32[]{:S(2)}) %collective-permute-start.9) | collective-permute-done | bytes 393248 | tf_op jit(solution)/shard_map/ppermute | solution.py:436
  51.2 0.2 collective-permute-start.12
  51.5 2.0 %collective-permute-start.17 = (f32[2,2,2,8,768]{4,3,0,1,2:T(8,128)S(1)}, f32[2,2,2,8,768]{4,3,0,1,2:T(8,128)S(1)}, u32[]{:S(2)}, u32[]{:S(2)}) collective-permute-start(f32[2,2,2,8,768]{4,3,0,1,2:T(8,128)S(1)} %slice_bitcast_fusion.4), channel_id=1, source_target_pairs={{0,8},{1,9},{2,10},{3,11},{4,28},{5,29},{6,30},{7,31},{8,0},{9,1},... | collective-permute-start | bytes 589832 | tf_op jit(solution)/shard_map/ppermute | solution.py:436
  53.5 2.3 %collective-permute-done.12 = f32[80,256]{1,0:T(8,128)S(1)} collective-permute-done((f32[80,256]{1,0:T(8,128)S(1)}, f32[80,256]{1,0:T(8,128)S(1)}, u32[]{:S(2)}, u32[]{:S(2)}) %collective-permute-start.12) | collective-permute-done | bytes 81952 | tf_op jit(solution)/shard_map/ppermute | solution.py:436
  55.8 1.2 %collective-permute-start.13 = (f32[80,256]{1,0:T(8,128)S(1)}, f32[80,256]{1,0:T(8,128)S(1)}, u32[]{:S(2)}, u32[]{:S(2)}) collective-permute-start(f32[80,256]{1,0:T(8,128)S(1)} %add.78), channel_id=1, source_target_pairs={{0,24},{1,25},{2,26},{3,27},{4,12},{5,13},{6,14},{7,15},{8,16},{9,... | collective-permute-start | bytes 245768 | tf_op jit(solution)/shard_map/ppermute | solution.py:436
  57.0 0.3 collective-permute-start.16
  57.4 0.5 collective-permute-start.15
  57.9 3.6 %collective-permute-done.13 = f32[80,256]{1,0:T(8,128)S(1)} collective-permute-done((f32[80,256]{1,0:T(8,128)S(1)}, f32[80,256]{1,0:T(8,128)S(1)}, u32[]{:S(2)}, u32[]{:S(2)}) %collective-permute-start.13) | collective-permute-done | bytes 81952 | tf_op jit(solution)/shard_map/ppermute | solution.py:436
  61.6 1.2 %collective-permute-done.16 = f32[2,2,2,8,768]{4,3,0,1,2:T(8,128)S(1)} collective-permute-done((f32[2,2,2,8,768]{4,3,0,1,2:T(8,128)S(1)}, f32[2,2,2,8,768]{4,3,0,1,2:T(8,128)S(1)}, u32[]{:S(2)}, u32[]{:S(2)}) %collective-permute-start.16) | collective-permute-done | bytes 196640 | tf_op jit(solution)/shard_map/ppermute | solution.py:436
  62.8 0.2 collective-permute-done.15
  63.1 2.7 %collective-permute-start.18 = (f32[2,2,3,8,768]{4,3,2,0,1:T(8,128)S(1)}, f32[2,2,3,8,768]{4,3,2,0,1:T(8,128)S(1)}, u32[]{:S(2)}, u32[]{:S(2)}) collective-permute-start(f32[2,2,3,8,768]{4,3,2,0,1:T(8,128)S(1)} %slice_bitcast_fusion.3), channel_id=1, source_target_pairs={{0,3},{1,2},{2,1},{3,0},{4,5},{5,4},{6,7},{7,6},{8,11},{9,10},{10,... | collective-permute-start | bytes 884744 | tf_op jit(solution)/shard_map/ppermute | solution.py:436
  65.8 4.4 %collective-permute-done.14 = f32[80,256]{1,0:T(8,128)S(1)} collective-permute-done((f32[80,256]{1,0:T(8,128)S(1)}, f32[80,256]{1,0:T(8,128)S(1)}, u32[]{:S(2)}, u32[]{:S(2)}) %collective-permute-start.14) | collective-permute-done | bytes 81952 | tf_op jit(solution)/shard_map/ppermute | solution.py:436
  70.2 0.9 %collective-permute-done.18 = f32[2,2,3,8,768]{4,3,2,0,1:T(8,128)S(1)} collective-permute-done((f32[2,2,3,8,768]{4,3,2,0,1:T(8,128)S(1)}, f32[2,2,3,8,768]{4,3,2,0,1:T(8,128)S(1)}, u32[]{:S(2)}, u32[]{:S(2)}) %collective-permute-start.18) | collective-permute-done | bytes 294944 | tf_op jit(solution)/shard_map/ppermute | solution.py:436
  71.2 2.2 %collective-permute-start.21 = (f32[2,3,8,768]{3,2,1,0:T(8,128)S(1)}, f32[2,3,8,768]{3,2,1,0:T(8,128)S(1)}, u32[]{:S(2)}, u32[]{:S(2)}) collective-permute-start(f32[2,3,8,768]{3,2,1,0:T(8,128)S(1)} %slice_bitcast_fusion.7), channel_id=1, source_target_pairs={{0,24},{1,25},{2,26},{3,27},{4,12},{5,13},{6,14},{7,15},{8,16},{9,... | collective-permute-start | bytes 442376 | tf_op jit(solution)/shard_map/ppermute | solution.py:436
  73.4 1.9 %collective-permute-start.19 = (f32[80,256]{1,0:T(8,128)S(1)}, f32[80,256]{1,0:T(8,128)S(1)}, u32[]{:S(2)}, u32[]{:S(2)}) collective-permute-start(f32[80,256]{1,0:T(8,128)S(1)} %add.80), channel_id=1, source_target_pairs={{0,96},{1,97},{2,98},{3,99},{4,36},{5,37},{6,38},{7,39},{8,104},{9... | collective-permute-start | bytes 245768 | tf_op jit(solution)/shard_map/ppermute | solution.py:436
  75.3 3.7 %collective-permute-done.19 = f32[80,256]{1,0:T(8,128)S(1)} collective-permute-done((f32[80,256]{1,0:T(8,128)S(1)}, f32[80,256]{1,0:T(8,128)S(1)}, u32[]{:S(2)}, u32[]{:S(2)}) %collective-permute-start.19) | collective-permute-done | bytes 81952 | tf_op jit(solution)/shard_map/ppermute | solution.py:436
  79.2 2.0 %collective-permute-start.22 = (f32[3,8,768]{2,1,0:T(8,128)S(1)}, f32[3,8,768]{2,1,0:T(8,128)S(1)}, u32[]{:S(2)}, u32[]{:S(2)}) collective-permute-start(f32[3,8,768]{2,1,0:T(8,128)S(1)} %slice_bitcast_fusion.8), channel_id=1, source_target_pairs={{0,96},{1,97},{2,98},{3,99},{4,36},{5,37},{6,38},{7,39},{8,104},{9... | collective-permute-start | bytes 221192 | tf_op jit(solution)/shard_map/ppermute | solution.py:436
  81.2 7.0 %final_part.1 = (bf16[6,14,14,1024]{3,2,1,0:T(8,128)(2,1)}, f32[3,8,768]{2,1,0:T(8,128)S(1)}) custom-call(bf16[1344,1024]{1,0:T(8,128)(2,1)S(1)} %get-tuple-element.56.dev, bf16[1344,1024]{1,0:T(8,128)(2,1)S(1)} %bitcast.81, f32[80,256]{1,0:T(8,128)S(1)} %add.85.mine, f32[80,256]{1,0:T(8,128)S(1)} %collective-permute-done.20.theirs, ...), custom_call_target="tpu_custom_call" | custom-call | tf_op jit(solution)/shard_map/final_part/pallas_call | solution.py:405
  88.2 0.6 fusion.6
  (48 shorter events, 1.0 us)
Async XLA Ops:
  0.6 0.7 copy-start.1
  9.6 7.0 %collective-permute-start.5 = (f32[512,768]{1,0:T(8,128)S(1)}, f32[512,768]{1,0:T(8,128)S(1)}, u32[]{:S(2)}, u32[]{:S(2)}) collective-permute-start(f32[512,768]{1,0:T(8,128)S(1)} %get-tuple-element.60), channel_id=1, source_target_pairs={{0,4},{1,5},{2,6},{3,7},{4,0},{5,1},{6,2},{7,3},{8,12},{9,13},{10,... | collective-permute-start | bytes 4718600 | tf_op jit(solution)/shard_map/ppermute | solution.py:436
  12.8 6.3 %collective-permute-start = (f32[512,768]{1,0:T(8,128)S(1)}, f32[512,768]{1,0:T(8,128)S(1)}, u32[]{:S(2)}, u32[]{:S(2)}) collective-permute-start(f32[512,768]{1,0:T(8,128)S(1)} %get-tuple-element.44), channel_id=1, source_target_pairs={{0,4},{1,5},{2,6},{3,7},{4,0},{5,1},{6,2},{7,3},{8,12},{9,13},{10,... | collective-permute-start | bytes 4718600 | tf_op jit(solution)/shard_map/ppermute | solution.py:436
  16.5 4.7 %collective-permute-start.1 = (f32[512,768]{1,0:T(8,128)S(1)}, f32[512,768]{1,0:T(8,128)S(1)}, u32[]{:S(2)}, u32[]{:S(2)}) collective-permute-start(f32[512,768]{1,0:T(8,128)S(1)} %get-tuple-element.46), channel_id=1, source_target_pairs={{0,4},{1,5},{2,6},{3,7},{4,0},{5,1},{6,2},{7,3},{8,12},{9,13},{10,... | collective-permute-start | bytes 4718600 | tf_op jit(solution)/shard_map/ppermute | solution.py:436
  17.0 20.8 %collective-permute-start.6 = (f32[2,2,2,2,2,8,768]{6,5,0,2,4,1,3:T(8,128)S(1)}, f32[2,2,2,2,2,8,768]{6,5,0,2,4,1,3:T(8,128)S(1)}, u32[]{:S(2)}, u32[]{:S(2)}) collective-permute-start(f32[2,2,2,2,2,8,768]{6,5,0,2,4,1,3:T(8,128)S(1)} %copy.11), channel_id=1, source_target_pairs={{0,32},{1,33},{2,34},{3,35},{4,100},{5,101},{6,102},{7,103},{8,40}... | collective-permute-start | bytes 2359304 | tf_op jit(solution)/shard_map/ppermute | solution.py:436
  19.5 18.5 %collective-permute-start.3 = (f32[2,2,2,2,2,8,768]{6,5,1,3,4,0,2:T(8,128)S(1)}, f32[2,2,2,2,2,8,768]{6,5,1,3,4,0,2:T(8,128)S(1)}, u32[]{:S(2)}, u32[]{:S(2)}) collective-permute-start(f32[2,2,2,2,2,8,768]{6,5,1,3,4,0,2:T(8,128)S(1)} %bitcast.89), channel_id=1, source_target_pairs={{0,1},{1,0},{2,3},{3,2},{4,7},{5,6},{6,5},{7,4},{8,9},{9,8},{10,11... | collective-permute-start | bytes 2359304 | tf_op jit(solution)/shard_map/ppermute | solution.py:436
  21.6 1.8 %copy-start = (f32[16,64,64]{2,1,0:T(8,128)S(1)}, f32[16,64,64]{2,1,0:T(8,128)}, u32[]{:S(2)}) copy-start(f32[16,64,64]{2,1,0:T(8,128)} %vectors.1) | copy-start | bytes 786436
  21.6 1.8 %copy-start.2 = (f32[16,64]{1,0:T(8,128)S(1)}, f32[16,64]{1,0:T(8,128)}, u32[]{:S(2)}) copy-start(f32[16,64]{1,0:T(8,128)} %values.3) | copy-start | bytes 12292
  21.7 16.4 %collective-permute-start.4 = (f32[2,2,2,2,2,8,768]{6,5,1,2,4,3,0:T(8,128)S(1)}, f32[2,2,2,2,2,8,768]{6,5,1,2,4,3,0:T(8,128)S(1)}, u32[]{:S(2)}, u32[]{:S(2)}) collective-permute-start(f32[2,2,2,2,2,8,768]{6,5,1,2,4,3,0:T(8,128)S(1)} %bitcast.90), channel_id=1, source_target_pairs={{0,8},{1,9},{2,10},{3,11},{4,28},{5,29},{6,30},{7,31},{8,0},{9,1},... | collective-permute-start | bytes 2359304 | tf_op jit(solution)/shard_map/ppermute | solution.py:436
  32.4 5.5 %collective-permute-start.2 = (f32[80,256]{1,0:T(8,128)S(1)}, f32[80,256]{1,0:T(8,128)S(1)}, u32[]{:S(2)}, u32[]{:S(2)}) collective-permute-start(f32[80,256]{1,0:T(8,128)S(1)} %get-tuple-element.58), channel_id=1, source_target_pairs={{0,4},{1,5},{2,6},{3,7},{4,0},{5,1},{6,2},{7,3},{8,12},{9,13},{10,... | collective-permute-start | bytes 245768 | tf_op jit(solution)/shard_map/ppermute | solution.py:436
  38.2 4.5 %collective-permute-start.7 = (f32[80,256]{1,0:T(8,128)S(1)}, f32[80,256]{1,0:T(8,128)S(1)}, u32[]{:S(2)}, u32[]{:S(2)}) collective-permute-start(f32[80,256]{1,0:T(8,128)S(1)} %add.68), channel_id=1, source_target_pairs={{0,1},{1,0},{2,3},{3,2},{4,7},{5,6},{6,5},{7,4},{8,9},{9,8},{10,11... | collective-permute-start | bytes 245768 | tf_op jit(solution)/shard_map/ppermute | solution.py:436
  38.5 10.0 %collective-permute-start.11 = (f32[2,2,2,2,8,768]{5,4,0,2,3,1:T(8,128)S(1)}, f32[2,2,2,2,8,768]{5,4,0,2,3,1:T(8,128)S(1)}, u32[]{:S(2)}, u32[]{:S(2)}) collective-permute-start(f32[2,2,2,2,8,768]{5,4,0,2,3,1:T(8,128)S(1)} %slice_bitcast_fusion), channel_id=1, source_target_pairs={{0,1},{1,0},{2,3},{3,2},{4,7},{5,6},{6,5},{7,4},{8,9},{9,8},{10,11... | collective-permute-start | bytes 1179656 | tf_op jit(solution)/shard_map/ppermute | solution.py:436
  40.5 8.1 %collective-permute-start.10 = (f32[2,2,2,2,8,768]{5,4,0,1,3,2:T(8,128)S(1)}, f32[2,2,2,2,8,768]{5,4,0,1,3,2:T(8,128)S(1)}, u32[]{:S(2)}, u32[]{:S(2)}) collective-permute-start(f32[2,2,2,2,8,768]{5,4,0,1,3,2:T(8,128)S(1)} %slice_bitcast_fusion.1), channel_id=1, source_target_pairs={{0,32},{1,33},{2,34},{3,35},{4,100},{5,101},{6,102},{7,103},{8,40}... | collective-permute-start | bytes 1179656 | tf_op jit(solution)/shard_map/ppermute | solution.py:436
  42.7 5.7 %collective-permute-start.8 = (f32[80,256]{1,0:T(8,128)S(1)}, f32[80,256]{1,0:T(8,128)S(1)}, u32[]{:S(2)}, u32[]{:S(2)}) collective-permute-start(f32[80,256]{1,0:T(8,128)S(1)} %add.73), channel_id=1, source_target_pairs={{0,3},{1,2},{2,1},{3,0},{4,5},{5,4},{6,7},{7,6},{8,11},{9,10},{10,... | collective-permute-start | bytes 245768 | tf_op jit(solution)/shard_map/ppermute | solution.py:436
  43.3 7.9 %collective-permute-start.9 = (f32[2,2,2,2,8,768]{5,4,1,2,3,0:T(8,128)S(1)}, f32[2,2,2,2,8,768]{5,4,1,2,3,0:T(8,128)S(1)}, u32[]{:S(2)}, u32[]{:S(2)}) collective-permute-start(f32[2,2,2,2,8,768]{5,4,1,2,3,0:T(8,128)S(1)} %slice_bitcast_fusion.2), channel_id=1, source_target_pairs={{0,8},{1,9},{2,10},{3,11},{4,28},{5,29},{6,30},{7,31},{8,0},{9,1},... | collective-permute-start | bytes 1179656 | tf_op jit(solution)/shard_map/ppermute | solution.py:436
  51.2 4.5 %collective-permute-start.12 = (f32[80,256]{1,0:T(8,128)S(1)}, f32[80,256]{1,0:T(8,128)S(1)}, u32[]{:S(2)}, u32[]{:S(2)}) collective-permute-start(f32[80,256]{1,0:T(8,128)S(1)} %add.74), channel_id=1, source_target_pairs={{0,8},{1,9},{2,10},{3,11},{4,28},{5,29},{6,30},{7,31},{8,0},{9,1},... | collective-permute-start | bytes 245768 | tf_op jit(solution)/shard_map/ppermute | solution.py:436
  51.5 10.0 %collective-permute-start.17 = (f32[2,2,2,8,768]{4,3,0,1,2:T(8,128)S(1)}, f32[2,2,2,8,768]{4,3,0,1,2:T(8,128)S(1)}, u32[]{:S(2)}, u32[]{:S(2)}) collective-permute-start(f32[2,2,2,8,768]{4,3,0,1,2:T(8,128)S(1)} %slice_bitcast_fusion.4), channel_id=1, source_target_pairs={{0,8},{1,9},{2,10},{3,11},{4,28},{5,29},{6,30},{7,31},{8,0},{9,1},... | collective-permute-start | bytes 589832 | tf_op jit(solution)/shard_map/ppermute | solution.py:436
  55.8 5.7 %collective-permute-start.13 = (f32[80,256]{1,0:T(8,128)S(1)}, f32[80,256]{1,0:T(8,128)S(1)}, u32[]{:S(2)}, u32[]{:S(2)}) collective-permute-start(f32[80,256]{1,0:T(8,128)S(1)} %add.78), channel_id=1, source_target_pairs={{0,24},{1,25},{2,26},{3,27},{4,12},{5,13},{6,14},{7,15},{8,16},{9,... | collective-permute-start | bytes 245768 | tf_op jit(solution)/shard_map/ppermute | solution.py:436
  57.0 5.7 %collective-permute-start.16 = (f32[2,2,2,8,768]{4,3,0,1,2:T(8,128)S(1)}, f32[2,2,2,8,768]{4,3,0,1,2:T(8,128)S(1)}, u32[]{:S(2)}, u32[]{:S(2)}) collective-permute-start(f32[2,2,2,8,768]{4,3,0,1,2:T(8,128)S(1)} %slice_bitcast_fusion.5), channel_id=1, source_target_pairs={{0,1},{1,0},{2,3},{3,2},{4,7},{5,6},{6,5},{7,4},{8,9},{9,8},{10,11... | collective-permute-start | bytes 589832 | tf_op jit(solution)/shard_map/ppermute | solution.py:436
  57.4 5.7 %collective-permute-start.15 = (f32[2,2,2,8,768]{4,3,0,1,2:T(8,128)S(1)}, f32[2,2,2,8,768]{4,3,0,1,2:T(8,128)S(1)}, u32[]{:S(2)}, u32[]{:S(2)}) collective-permute-start(f32[2,2,2,8,768]{4,3,0,1,2:T(8,128)S(1)} %slice_bitcast_fusion.6), channel_id=1, source_target_pairs={{0,32},{1,33},{2,34},{3,35},{4,100},{5,101},{6,102},{7,103},{8,40}... | collective-permute-start | bytes 589832 | tf_op jit(solution)/shard_map/ppermute | solution.py:436
  63.1 8.0 %collective-permute-start.18 = (f32[2,2,3,8,768]{4,3,2,0,1:T(8,128)S(1)}, f32[2,2,3,8,768]{4,3,2,0,1:T(8,128)S(1)}, u32[]{:S(2)}, u32[]{:S(2)}) collective-permute-start(f32[2,2,3,8,768]{4,3,2,0,1:T(8,128)S(1)} %slice_bitcast_fusion.3), channel_id=1, source_target_pairs={{0,3},{1,2},{2,1},{3,0},{4,5},{5,4},{6,7},{7,6},{8,11},{9,10},{10,... | collective-permute-start | bytes 884744 | tf_op jit(solution)/shard_map/ppermute | solution.py:436
  65.8 4.4 %collective-permute-start.14 = (f32[80,256]{1,0:T(8,128)S(1)}, f32[80,256]{1,0:T(8,128)S(1)}, u32[]{:S(2)}, u32[]{:S(2)}) collective-permute-start(f32[80,256]{1,0:T(8,128)S(1)} %add.79), channel_id=1, source_target_pairs={{0,32},{1,33},{2,34},{3,35},{4,100},{5,101},{6,102},{7,103},{8,40}... | collective-permute-start | bytes 245768 | tf_op jit(solution)/shard_map/ppermute | solution.py:436
  71.2 8.0 %collective-permute-start.21 = (f32[2,3,8,768]{3,2,1,0:T(8,128)S(1)}, f32[2,3,8,768]{3,2,1,0:T(8,128)S(1)}, u32[]{:S(2)}, u32[]{:S(2)}) collective-permute-start(f32[2,3,8,768]{3,2,1,0:T(8,128)S(1)} %slice_bitcast_fusion.7), channel_id=1, source_target_pairs={{0,24},{1,25},{2,26},{3,27},{4,12},{5,13},{6,14},{7,15},{8,16},{9,... | collective-permute-start | bytes 442376 | tf_op jit(solution)/shard_map/ppermute | solution.py:436
  73.4 5.7 %collective-permute-start.19 = (f32[80,256]{1,0:T(8,128)S(1)}, f32[80,256]{1,0:T(8,128)S(1)}, u32[]{:S(2)}, u32[]{:S(2)}) collective-permute-start(f32[80,256]{1,0:T(8,128)S(1)} %add.80), channel_id=1, source_target_pairs={{0,96},{1,97},{2,98},{3,99},{4,36},{5,37},{6,38},{7,39},{8,104},{9... | collective-permute-start | bytes 245768 | tf_op jit(solution)/shard_map/ppermute | solution.py:436
  79.0 2.1 %collective-permute-start.20 = (f32[80,256]{1,0:T(8,128)S(1)}, f32[80,256]{1,0:T(8,128)S(1)}, u32[]{:S(2)}, u32[]{:S(2)}) collective-permute-start(f32[80,256]{1,0:T(8,128)S(1)} %add.85.mine), channel_id=1, source_target_pairs={{0,4},{1,5},{2,6},{3,7},{4,0},{5,1},{6,2},{7,3},{8,12},{9,13},{10,... | collective-permute-start | bytes 245768 | tf_op jit(solution)/shard_map/ppermute | solution.py:436
  79.2 9.0 %collective-permute-start.22 = (f32[3,8,768]{2,1,0:T(8,128)S(1)}, f32[3,8,768]{2,1,0:T(8,128)S(1)}, u32[]{:S(2)}, u32[]{:S(2)}) collective-permute-start(f32[3,8,768]{2,1,0:T(8,128)S(1)} %slice_bitcast_fusion.8), channel_id=1, source_target_pairs={{0,96},{1,97},{2,98},{3,99},{4,36},{5,37},{6,38},{7,39},{8,104},{9... | collective-permute-start | bytes 221192 | tf_op jit(solution)/shard_map/ppermute | solution.py:436

commit v7 on v6

--- a/solution.py
+++ b/solution.py
@@ -12,11 +12,14 @@
 ALL = ("z", "y", "c", "x")
 SIZE = {"z": 4, "y": 4, "c": 2, "x": 4}
 STRIDE = {"z": 32, "y": 8, "c": 4, "x": 1}
-RING = ((0, 3, 1, 2), (0, 1, 3, 2))
+ORDERS = ((0, 3, 1, 2), (0, 1, 3, 2))
+FLIP = {"z": 0, "y": 1, "x": 0}
+RING = [{axis: ORDERS[(c + FLIP[axis]) % 2] for axis in "zyx"} for c in range(2)]
 F32 = jnp.float32
 BF16 = jnp.bfloat16
 IMAGES, H, W, D, O = 6, 14, 14, 1024, 256
 ROWS = IMAGES * H * 16
+WIDE = 9 * O // 2
 PIXELS = IMAGES * H * W
 TOTAL = 128.0 * PIXELS
 ON_CHIP = pl.BlockSpec(memory_space=pltpu.VMEM)
@@ -81,8 +84,8 @@
     for axis in "zyx":
         i = lax.axis_index(axis)
         a, b = (i ^ (i >> 1)) & 1, i >> 1
-        spots[0].append(2 * a + b)
-        spots[1].append(2 * b + a)
+        for c in range(2):
+            spots[c].append(2 * a + b if (c + FLIP[axis]) % 2 == 0 else 2 * b + a)
     return core, spots
 
 
@@ -125,7 +128,8 @@
         whiten[z] = full.astype(BF16)
         for c in range(2):
             at_z, at_y, at_x = spots[c]
-            for row, (y, x) in enumerate((y, x) for y in RING[c] for x in RING[c]):
+            order = [(y, x) for y in RING[c]["y"] for x in RING[c]["x"]]
+            for row, (y, x) in enumerate(order):
                 channel = y * 64 + c * 32 + x * 8
                 row = pl.multiple_of(8 * (row ^ (4 * at_y + at_x)), 8)
                 wp32[4 * c + z, pl.ds(row, 8), :] = full[channel : channel + 8, :]
@@ -168,7 +172,7 @@
         c, z = k // 4, k % 4
         chunk = xc[:, :, 256 * z : 256 * z + 256].reshape(ROWS, 256)
         part = nt(wp32[k].astype(BF16), chunk)
-        row = 4 * (c ^ core) + (RING[c].index(z) ^ spots[c][0])
+        row = 4 * (c ^ core) + (RING[c]["z"].index(z) ^ spots[c][0])
         row = pl.multiple_of(128 * row, 128)
         wht[pl.ds(row, 128), :] = part.astype(BF16)
         shift = part[:, 14:15] + part[:, 15:16] + part[:, 30:31]
@@ -202,15 +206,14 @@
 
 
 def weight_kernel(a, wht, cols, u, kernel_hbm, keep, send, colsum, slab, arrived):
-    copy = pltpu.make_async_copy(kernel_hbm.at[pl.ds(768 * a, 768)], slab, arrived)
+    copy = pltpu.make_async_copy(kernel_hbm.at[pl.ds(WIDE * a, WIDE)], slab, arrived)
     copy.start()
-    for n in range(3):
-        start = 768 * a + 256 * n
-        full = nn(wht[...], cols[:, start : start + 256])
-        colsum[:, 256 * n : 256 * n + 256] = full[1024:1032, :]
-        for k in range(2):
+    for start, size in ((0, 256), (256, 256), (512, 256), (768, 384)):
+        full = nn(wht[...], cols[:, WIDE * a + start : WIDE * a + start + size])
+        colsum[:, start : start + size] = full[1024:1032, :]
+        for k in range(size // 128):
             ones = full[1024:1025, 128 * k : 128 * k + 128]
-            lanes = slice(256 * n + 128 * k, 256 * n + 128 * k + 128)
+            lanes = slice(start + 128 * k, start + 128 * k + 128)
             part = full[0:1024, 128 * k : 128 * k + 128] + u[...] * ones
             keep[:, lanes] = part[0:512]
             send[:, lanes] = part[512:1024]
@@ -223,27 +226,33 @@
         in_specs=[ON_CHIP] * 3 + [IN_HBM],
         out_specs=(ON_CHIP,) * 4,
         out_shape=(
-            jax.ShapeDtypeStruct((512, 768), F32),
-            jax.ShapeDtypeStruct((512, 768), F32),
-            jax.ShapeDtypeStruct((8, 768), F32),
-            jax.ShapeDtypeStruct((768, D), BF16),
+            jax.ShapeDtypeStruct((512, WIDE), F32),
+            jax.ShapeDtypeStruct((512, WIDE), F32),
+            jax.ShapeDtypeStruct((8, WIDE), F32),
+            jax.ShapeDtypeStruct((WIDE, D), BF16),
         ),
         scratch_shapes=[pltpu.SemaphoreType.DMA],
-        compiler_params=pltpu.CompilerParams(vmem_limit_bytes=6 << 20),
+        compiler_params=pltpu.CompilerParams(vmem_limit_bytes=8 << 20),
         name=f"weight_part_{a}",
     )(wht, cols, u, kernel)
+
+
+def pair_of_lanes(sums, a, c):
+    first = (3 * a + c) * 2
+    row = [
+        sums[q // 9][0:1, 128 * (q % 9) : 128 * (q % 9) + 128] for q in (first, first + 1)
+    ]
+    return jnp.concatenate(row, axis=1)
 
 
 def back_kernel(
     cols,
     slab0,
     slab1,
-    slab2,
     xc,
     sums,
     sum0,
     sum1,
-    sum2,
     vectors,
     values,
     dev,
@@ -265,9 +274,8 @@
     upper = None
     for z in range(4):
         lanes = slice(256 * z, 256 * z + 256)
-        back = nn(cols[:, 0:768], slab0[:, lanes])
-        back = back + nn(cols[:, 768:1536], slab1[:, lanes])
-        back = back + nn(cols[:, 1536:2304], slab2[:, lanes])
+        back = nn(cols[:, 0:WIDE], slab0[:, lanes])
+        back = back + nn(cols[:, WIDE : 2 * WIDE], slab1[:, lanes])
         total = jnp.sum(back, axis=0, keepdims=True)
         low = jnp.where(real, back - total * (1.0 / PIXELS), 0.0).astype(BF16)
         dev[:, lanes] = low
@@ -291,8 +299,8 @@
         tail = jnp.where(row == 0, total, jnp.where(row == 1, sums[:, lanes], 0.0))
         tail = jnp.where(row == 5, diagonal, tail)
         if z < 3:
-            for a, part in enumerate((sum0, sum1, sum2)):
-                tail = jnp.where(row == 2 + a, part[0:1, lanes], tail)
+            for a in range(3):
+                tail = jnp.where(row == 2 + a, pair_of_lanes((sum0, sum1), a, z), tail)
         own[:, lanes] = tail
         blocks[z // 2, 64 + 8 * (z % 2) : 72 + 8 * (z % 2), :] = tail
         basis = block_vectors(vectors, z, same)
@@ -308,7 +316,7 @@
 def back_part(cols, slabs, xc, sums, colsums, vectors, values):
     return pl.pallas_call(
         back_kernel,
-        in_specs=[ON_CHIP] * 11,
+        in_specs=[ON_CHIP] * 9,
         out_specs=(ON_CHIP,) * 6,
         out_shape=(
             jax.ShapeDtypeStruct((ROWS, D), BF16),
@@ -348,34 +356,42 @@
     below = (lax.broadcasted_iota(jnp.int32, (256, 256), 0) & 63) - (
         lax.broadcasted_iota(jnp.int32, (256, 256), 1) & 63
     )
-    for z in range(4):
-        lanes = slice(256 * z, 256 * z + 256)
+    every = range(4)
+    chunk = [slice(256 * z, 256 * z + 256) for z in every]
+    total, mean, covs = [], [], []
+    for z in every:
         start = 64 + 8 * (z % 2)
         tail = blocks[z // 2, start : start + 8, :]
-        total, mean = tail[0:1], tail[1:2] * (1.0 / TOTAL)
+        total.append(tail[0:1])
+        mean.append(tail[1:2] * (1.0 / TOTAL))
         packed = blocks[z // 2, 0:64, :]
         square = jnp.concatenate([packed, packed, packed, packed], axis=0)
         if z % 2 == 0:
             raw = jnp.where(below <= 0, square, square.T)
         else:
             raw = jnp.where(below > 0, square, square.T)
-            raw = jnp.where(below == 0, tail[5:6], raw)
-        tall = columns_of([total, mean])
-        cov = raw - 0.5 * (tall[:, 1:2] * total + tall[:, 0:1] * mean)
-        basis, turned = (bases[z, 0], bases[z, 1]), (bases[z, 2], bases[z, 3])
-        rotated = fine(nn, turned, fine(nn, cov, basis))
-        grad = fine(nn, basis, fine(nn, rotated * factors[z], turned))
-        sigma[z] = (grad * (2.0 / TOTAL)).astype(BF16)
-        moved = own[0:1, lanes] * (1.0 / PIXELS) - total * (1.0 / TOTAL)
-        offset = own[1:2, lanes] * (1.0 / PIXELS) - mean
+            raw = jnp.where(below == 0, blocks[z // 2, start + 5 : start + 6, :], raw)
+        tall = columns_of([total[z], mean[z]])
+        covs.append(raw - 0.5 * (tall[:, 1:2] * total[z] + tall[:, 0:1] * mean[z]))
+    basis = [(bases[z, 0], bases[z, 1]) for z in every]
+    turned = [(bases[z, 2], bases[z, 3]) for z in every]
+    grads = [fine(nn, covs[z], basis[z]) for z in every]
+    grads = [fine(nn, turned[z], grads[z]) * factors[z] for z in every]
+    grads = [fine(nn, grads[z], turned[z]) for z in every]
+    grads = [fine(nn, basis[z], grads[z]) for z in every]
+    for z in every:
+        sigma[z] = (grads[z] * (2.0 / TOTAL)).astype(BF16)
+    for z in every:
+        lanes = chunk[z]
+        moved = own[0:1, lanes] * (1.0 / PIXELS) - total[z] * (1.0 / TOTAL)
+        offset = own[1:2, lanes] * (1.0 / PIXELS) - mean[z]
         empty = [jnp.zeros((1, 256), BF16)]
-        stacked = jnp.concatenate(pieces(moved, 3) + pieces(mean, 3) + empty * 2, axis=0)
+        stacked = jnp.concatenate(pieces(moved, 3) + pieces(mean[z], 3) + empty * 2, axis=0)
         through = nn(stacked, whiten[z])
         stacked = jnp.concatenate(pieces(offset, 3) + empty * 5, axis=0)
         other = nn(stacked, sigma[z])
-        row_vector[0:1, lanes] = (
-            jnp.sum(through[0:3], axis=0, keepdims=True)
-            + jnp.sum(other[0:3], axis=0, keepdims=True)
+        row_vector[0:1, lanes] = jnp.sum(through[0:3], axis=0, keepdims=True) + jnp.sum(
+            other[0:3], axis=0, keepdims=True
         )
         shift[0:1, lanes] = jnp.sum(through[3:6], axis=0, keepdims=True)
     first = 8 * sum(STRIDE[axis] * lax.axis_index(axis) for axis in ALL)
@@ -386,7 +402,11 @@
     for a in range(3):
         for z in range(3):
             start = 66 + 8 * (z % 2) + a
-            fix[a, :, 256 * z : 256 * z + 256] = chosen * blocks[z // 2, start : start + 1, :]
+            both = chosen * blocks[z // 2, start : start + 1, :]
+            for k in range(2):
+                q = (3 * a + z) * 2 + k
+                lanes = slice(128 * (q % 9), 128 * (q % 9) + 128)
+                fix[q // 9, :, lanes] = both[:, 128 * k : 128 * k + 128]
     copies = []
     for b in range(IMAGES):
         rows = slice(H * 16 * b, H * 16 * b + H * 16)
@@ -408,7 +428,7 @@
         out_specs=(IN_HBM, ON_CHIP),
         out_shape=(
             jax.ShapeDtypeStruct((IMAGES, H, W, D), BF16),
-            jax.ShapeDtypeStruct((3, 8, 768), F32),
+            jax.ShapeDtypeStruct((2, 8, WIDE), F32),
         ),
         scratch_shapes=[
             pltpu.VMEM((2, 80, 256), F32),
@@ -442,7 +462,7 @@
 
 def ring(axis, step):
     def move(at):
-        at[axis] ^= (1, 3)[(step + at["c"]) % 2]
+        at[axis] ^= (1, 3)[(step + at["c"] + FLIP[axis]) % 2]
 
     return move
 
@@ -459,21 +479,21 @@
     kernel = stay(kernel.reshape(9 * O, D))
 
     parts, colsums, slabs = [], [], []
-    for a in range(3):
+    for a in range(2):
         keep, send, colsum, slab = weight_part(wht, cols, u, kernel, a)
         colsums.append(colsum)
         slabs.append(slab)
-        parts.append((keep + exchange(send, other_core)).reshape(2, 2, 2, 2, 2, 2, 8, 768))
+        parts.append((keep + exchange(send, other_core)).reshape(2, 2, 2, 2, 2, 2, 8, WIDE))
     cols = lax.optimization_barrier((cols, *parts))[0]
     dev, own, mine, theirs, bases, factors = back_part(
         cols, slabs, xc, sums, colsums, vectors, values
     )
     mine = mine + exchange(theirs, other_core)
 
-    names = [["z1", "z2", "y1", "y2", "x1", "x2"] for _ in range(3)]
+    names = [["z1", "z2", "y1", "y2", "x1", "x2"] for _ in range(2)]
 
     def turn(k):
-        for a in range(3):
+        for a in range(2):
             axis = "xyz"[(a + k) % 3]
             dim = names[a].index(axis + "1")
             names[a].pop(dim)
@@ -486,8 +506,8 @@
         return lax.optimization_barrier((value, *others))[0]
 
     turn(0)
-    mine, *parts = lax.optimization_barrier((mine, *parts))
     one = mine + exchange(mine, moves[0])
+    one, *parts = lax.optimization_barrier((one, *parts))
     two = one + exchange(one, moves[1])
     turn(1)
     two, *parts = lax.optimization_barrier((two, *parts))
@@ -509,7 +529,7 @@
     mine, theirs = six, exchange(six, other_core)
 
     input_grad, fix = final_part(dev, xc, mine, theirs, own, bases, factors, whiten)
-    kernel_grad = (share - fix).transpose(1, 0, 2).reshape(8, 3, 3, O)
+    kernel_grad = (share - fix).transpose(1, 0, 2).reshape(8, 9 * O).reshape(8, 3, 3, O)
     return input_grad, kernel_grad
 
 

time: 89.3 us -> 98.8 us (1.11)
  starting transfers between devices: 27 us -> 31.2 us
  waiting for transfers between devices: 27 us -> 31 us
  Pallas kernels: 30.5 us -> 32.3 us
    ppermute x23 -> x19, starting transfers between devices: 27 us -> 31.2 us  [exchange(): return lax.ppermute(value, ALL, permutation(move))]
    ppermute x23 -> x19, waiting for transfers between devices: 27 us -> 31 us  [exchange(): return lax.ppermute(value, ALL, permutation(move))]
    pallas_call x3 -> x2, Pallas kernels: 9.38 us -> 12.6 us  [weight_part(): pl.pallas_call(functools.partial(weight_kernel, a), in_specs=[ON_CHIP] *...]
    pallas_call x1, Pallas kernels: 7 us -> 4.84 us  [final_part(): pl.pallas_call(final_kernel, in_specs=[ON_CHIP] * 8, out_specs=(IN_HBM, O...]
  transfers between devices with their start and end apart: 23 -> 19, of which waited for: 11 -> 12; matrix products, arithmetic and copies ran while one was open for 2% -> 1% of each run, Pallas kernels for 25% -> 21%
where the time goes in v7:
time: 98.8 us; the launch traced here: 98.5 us
  Pallas kernels  32.3 us (33%)
  starting transfers between devices  31.2 us (32%)
  waiting for transfers between devices  31 us (31%)
  other arithmetic  1.82 us (2%)
  local copies, waits for them, and re-layouts  1.36 us (1%)
    ppermute x19, starting transfers between devices, exchange(): return lax.ppermute(value, ALL, permutation(move))  31.2 us
    ppermute x19, waiting for transfers between devices, exchange(): return lax.ppermute(value, ALL, permutation(move))  31 us
    pallas_call x2, Pallas kernels, weight_part(): pl.pallas_call(functools.partial(weight_kernel, a), in_specs=[ON_CHIP] *...  12.6 us
    pallas_call x1, Pallas kernels, back_part(): pl.pallas_call(back_kernel, in_specs=[ON_CHIP] * 9, out_specs=(ON_CHIP,)...  9.78 us
    pallas_call x1, Pallas kernels, prep(): pl.pallas_call(prep_kernel, out_shape=(jax.ShapeDtypeStruct((IMAGES * H,...  5.12 us
    pallas_call x1, Pallas kernels, final_part(): pl.pallas_call(final_kernel, in_specs=[ON_CHIP] * 8, out_specs=(IN_HBM, O...  4.84 us
  transfers between devices with their start and end apart: 19, of which 12 were waited for; matrix products, arithmetic and copies ran while one was open for 1% of the time, Pallas kernels for 21%

profile of v7, /device:TPU:0, one launch (start us, length us, event | category | flops | bytes accessed | tf_op | source)
XLA Modules:
  0.0 98.5 jit_solution(1350881485171976678)
XLA Ops:
  0.6 0.7 copy-done.1
  1.3 5.1 %prep.1 = (bf16[84,16,2304]{2,1,0:T(8,128)(2,1)S(1)}, bf16[84,16,1024]{2,1,0:T(8,128)(2,1)S(1)}, bf16[1040,1344]{1,0:T(8,128)(2,1)S(1)}, f32[1024,128]{1,0:T(8,1...) custom-call(bf16[6,14,14,1024]{3,2,1,0:T(8,128)(2,1)} %features_hbm.1, ...), custom_call_target="tpu_custom_call" | custom-call | tf_op jit(solution)/shard_map/prep/pallas_call | solution.py:183
  6.5 6.3 %weight_part_1.1 = (f32[512,1152]{1,0:T(8,128)S(1)}, f32[512,1152]{1,0:T(8,128)S(1)}, f32[8,1152]{1,0:T(8,128)S(1)}, bf16[1152,1024]{1,0:T(8,128)(2,1)S(1)}) custom-call(bf16[1040,1344]{1,0:T(8,128)(2,1)S(1)} %get-tuple-element.35.wht, bf16[1344,2304]{1,0:T(8,128)(2,1)S(1)} %bitcast.62, f32[1024,128]{1,0:T(8,128)S(1)} %get-tuple-element.36.u, ...), custom_call_target="tpu_custom_call" | custom-call | tf_op jit(solution)/shard_map/weight_part_1/pallas_call | solution.py:224
  12.8 0.1 collective-permute-start.1
  12.9 6.3 %weight_part_0.1 = (f32[512,1152]{1,0:T(8,128)S(1)}, f32[512,1152]{1,0:T(8,128)S(1)}, f32[8,1152]{1,0:T(8,128)S(1)}, bf16[1152,1024]{1,0:T(8,128)(2,1)S(1)}) custom-call(bf16[1040,1344]{1,0:T(8,128)(2,1)S(1)} %get-tuple-element.35.wht, bf16[1344,2304]{1,0:T(8,128)(2,1)S(1)} %bitcast.63, f32[1024,128]{1,0:T(8,128)S(1)} %get-tuple-element.36.u, ...), custom_call_target="tpu_custom_call" | custom-call | tf_op jit(solution)/shard_map/weight_part_0/pallas_call | solution.py:224
  19.2 0.8 collective-permute-start
  19.9 0.2 add.55
  20.2 0.2 fusion.6
  20.3 0.1 copy.23
  20.4 3.2 %collective-permute-start.5 = (f32[2,2,2,2,2,8,1152]{6,5,1,2,4,3,0:T(8,128)S(1)}, f32[2,2,2,2,2,8,1152]{6,5,1,2,4,3,0:T(8,128)S(1)}, u32[]{:S(2)}, u32[]{:S(2)}) collective-permute-start(f32[2,2,2,2,2,8,1152]{6,5,1,2,4,3,0:T(8,128)S(1)} %bitcast.71), channel_id=1, source_target_pairs={{0,24},{1,25},{2,26},{3,27},{4,12},{5,13},{6,14},{7,15},{8,16},{9,... | collective-permute-start | bytes 3538952 | tf_op jit(solution)/shard_map/ppermute | solution.py:456
  23.6 0.5 collective-permute-done
  24.1 0.2 add.54
  24.3 0.2 fusion.7
  24.5 0.1 copy.24
  24.6 1.7 %collective-permute-start.4 = (f32[2,2,2,2,2,8,1152]{6,5,1,3,4,0,2:T(8,128)S(1)}, f32[2,2,2,2,2,8,1152]{6,5,1,3,4,0,2:T(8,128)S(1)}, u32[]{:S(2)}, u32[]{:S(2)}) collective-permute-start(f32[2,2,2,2,2,8,1152]{6,5,1,3,4,0,2:T(8,128)S(1)} %bitcast.72), channel_id=1, source_target_pairs={{0,1},{1,0},{2,3},{3,2},{4,7},{5,6},{6,5},{7,4},{8,9},{9,8},{10,11... | collective-permute-start | bytes 3538952 | tf_op jit(solution)/shard_map/ppermute | solution.py:456
  26.3 9.8 %back_part.1 = (bf16[1344,1024]{1,0:T(8,128)(2,1)S(1)}, f32[8,1024]{1,0:T(8,128)S(1)}, f32[80,256]{1,0:T(8,128)S(1)}, f32[80,256]{1,0:T(8,128)S(1)}, bf16[4,4,25...) custom-call(bf16[1344,2304]{1,0:T(8,128)(2,1)S(1)} %bitcast.64, bf16[1152,1024]{1,0:T(8,128)(2,1)S(1)} %get-tuple-element.42.slab0, ...), custom_call_target="tpu_custom_call" | custom-call | tf_op jit(solution)/shard_map/back_part/pallas_call | solution.py:317
  36.0 1.4 %collective-permute-start.2 = (f32[80,256]{1,0:T(8,128)S(1)}, f32[80,256]{1,0:T(8,128)S(1)}, u32[]{:S(2)}, u32[]{:S(2)}) collective-permute-start(f32[80,256]{1,0:T(8,128)S(1)} %get-tuple-element.50), channel_id=1, source_target_pairs={{0,4},{1,5},{2,6},{3,7},{4,0},{5,1},{6,2},{7,3},{8,12},{9,13},{10,... | collective-permute-start | bytes 245768 | tf_op jit(solution)/shard_map/ppermute | solution.py:456
  37.5 0.9 collective-permute-done.2
  38.4 0.3 collective-permute-start.3
  38.7 4.2 %collective-permute-done.3 = f32[80,256]{1,0:T(8,128)S(1)} collective-permute-done((f32[80,256]{1,0:T(8,128)S(1)}, f32[80,256]{1,0:T(8,128)S(1)}, u32[]{:S(2)}, u32[]{:S(2)}) %collective-permute-start.3) | collective-permute-done | bytes 81952 | tf_op jit(solution)/shard_map/ppermute | solution.py:456
  43.0 0.1 fusion
  43.1 0.2 fusion.1
  43.3 2.0 %collective-permute-start.8 = (f32[2,2,2,2,8,1152]{5,4,0,1,3,2:T(8,128)S(1)}, f32[2,2,2,2,8,1152]{5,4,0,1,3,2:T(8,128)S(1)}, u32[]{:S(2)}, u32[]{:S(2)}) collective-permute-start(f32[2,2,2,2,8,1152]{5,4,0,1,3,2:T(8,128)S(1)} %slice_bitcast_fusion), channel_id=1, source_target_pairs={{0,32},{1,33},{2,34},{3,35},{4,100},{5,101},{6,102},{7,103},{8,40}... | collective-permute-start | bytes 1769480 | tf_op jit(solution)/shard_map/ppermute | solution.py:456
  45.3 1.7 %collective-permute-start.6 = (f32[80,256]{1,0:T(8,128)S(1)}, f32[80,256]{1,0:T(8,128)S(1)}, u32[]{:S(2)}, u32[]{:S(2)}) collective-permute-start(f32[80,256]{1,0:T(8,128)S(1)} %add.57), channel_id=1, source_target_pairs={{0,3},{1,2},{2,1},{3,0},{4,5},{5,4},{6,7},{7,6},{8,11},{9,10},{10,... | collective-permute-start | bytes 245768 | tf_op jit(solution)/shard_map/ppermute | solution.py:456
  47.0 3.1 %collective-permute-start.7 = (f32[2,2,2,2,8,1152]{5,4,1,2,3,0:T(8,128)S(1)}, f32[2,2,2,2,8,1152]{5,4,1,2,3,0:T(8,128)S(1)}, u32[]{:S(2)}, u32[]{:S(2)}) collective-permute-start(f32[2,2,2,2,8,1152]{5,4,1,2,3,0:T(8,128)S(1)} %slice_bitcast_fusion.1), channel_id=1, source_target_pairs={{0,24},{1,25},{2,26},{3,27},{4,12},{5,13},{6,14},{7,15},{8,16},{9,... | collective-permute-start | bytes 1769480 | tf_op jit(solution)/shard_map/ppermute | solution.py:456
  50.1 0.9 collective-permute-done.6
  51.0 2.3 %collective-permute-done.8 = f32[2,2,2,2,8,1152]{5,4,0,1,3,2:T(8,128)S(1)} collective-permute-done((f32[2,2,2,2,8,1152]{5,4,0,1,3,2:T(8,128)S(1)}, f32[2,2,2,2,8,1152]{5,4,0,1,3,2:T(8,128)S(1)}, u32[]{:S(2)}, u32[]{:S(2)}) %collective-permute-start.8) | collective-permute-done | bytes 589856 | tf_op jit(solution)/shard_map/ppermute | solution.py:456
  53.3 0.1 bitcast_add_fusion
  53.4 4.8 %collective-permute-done.7 = f32[2,2,2,2,8,1152]{5,4,1,2,3,0:T(8,128)S(1)} collective-permute-done((f32[2,2,2,2,8,1152]{5,4,1,2,3,0:T(8,128)S(1)}, f32[2,2,2,2,8,1152]{5,4,1,2,3,0:T(8,128)S(1)}, u32[]{:S(2)}, u32[]{:S(2)}) %collective-permute-start.7) | collective-permute-done | bytes 589856 | tf_op jit(solution)/shard_map/ppermute | solution.py:456
  58.2 0.1 bitcast_add_fusion.1
  58.3 3.1 %collective-permute-start.9 = (f32[80,256]{1,0:T(8,128)S(1)}, f32[80,256]{1,0:T(8,128)S(1)}, u32[]{:S(2)}, u32[]{:S(2)}) collective-permute-start(f32[80,256]{1,0:T(8,128)S(1)} %add.60), channel_id=1, source_target_pairs={{0,24},{1,25},{2,26},{3,27},{4,12},{5,13},{6,14},{7,15},{8,16},{9,... | collective-permute-start | bytes 245768 | tf_op jit(solution)/shard_map/ppermute | solution.py:456
  61.4 0.2 collective-permute-start.12
  61.6 2.4 %collective-permute-done.9 = f32[80,256]{1,0:T(8,128)S(1)} collective-permute-done((f32[80,256]{1,0:T(8,128)S(1)}, f32[80,256]{1,0:T(8,128)S(1)}, u32[]{:S(2)}, u32[]{:S(2)}) %collective-permute-start.9) | collective-permute-done | bytes 81952 | tf_op jit(solution)/shard_map/ppermute | solution.py:456
  64.0 0.1 collective-permute-start.10
  64.2 0.5 collective-permute-start.13
  64.7 3.9 %collective-permute-done.10 = f32[80,256]{1,0:T(8,128)S(1)} collective-permute-done((f32[80,256]{1,0:T(8,128)S(1)}, f32[80,256]{1,0:T(8,128)S(1)}, u32[]{:S(2)}, u32[]{:S(2)}) %collective-permute-start.10) | collective-permute-done | bytes 81952 | tf_op jit(solution)/shard_map/ppermute | solution.py:456
  68.6 2.6 %collective-permute-done.13 = f32[2,2,2,8,1152]{4,3,0,1,2:T(8,128)S(1)} collective-permute-done((f32[2,2,2,8,1152]{4,3,0,1,2:T(8,128)S(1)}, f32[2,2,2,8,1152]{4,3,0,1,2:T(8,128)S(1)}, u32[]{:S(2)}, u32[]{:S(2)}) %collective-permute-start.13) | collective-permute-done | bytes 294944 | tf_op jit(solution)/shard_map/ppermute | solution.py:456
  71.3 1.7 %collective-permute-start.14 = (f32[2,2,2,8,1152]{4,3,2,0,1:T(8,128)S(1)}, f32[2,2,2,8,1152]{4,3,2,0,1:T(8,128)S(1)}, u32[]{:S(2)}, u32[]{:S(2)}) collective-permute-start(f32[2,2,2,8,1152]{4,3,2,0,1:T(8,128)S(1)} %slice_bitcast_fusion.2), channel_id=1, source_target_pairs={{0,3},{1,2},{2,1},{3,0},{4,5},{5,4},{6,7},{7,6},{8,11},{9,10},{10,... | collective-permute-start | bytes 884744 | tf_op jit(solution)/shard_map/ppermute | solution.py:456
  72.9 0.2 collective-permute-start.11
  73.2 4.2 %collective-permute-done.11 = f32[80,256]{1,0:T(8,128)S(1)} collective-permute-done((f32[80,256]{1,0:T(8,128)S(1)}, f32[80,256]{1,0:T(8,128)S(1)}, u32[]{:S(2)}, u32[]{:S(2)}) %collective-permute-start.11) | collective-permute-done | bytes 81952 | tf_op jit(solution)/shard_map/ppermute | solution.py:456
  77.4 1.9 %collective-permute-done.14 = f32[2,2,2,8,1152]{4,3,2,0,1:T(8,128)S(1)} collective-permute-done((f32[2,2,2,8,1152]{4,3,2,0,1:T(8,128)S(1)}, f32[2,2,2,8,1152]{4,3,2,0,1:T(8,128)S(1)}, u32[]{:S(2)}, u32[]{:S(2)}) %collective-permute-start.14) | collective-permute-done | bytes 294944 | tf_op jit(solution)/shard_map/ppermute | solution.py:456
  79.4 2.1 %collective-permute-start.17 = (f32[2,2,8,1152]{3,2,1,0:T(8,128)S(1)}, f32[2,2,8,1152]{3,2,1,0:T(8,128)S(1)}, u32[]{:S(2)}, u32[]{:S(2)}) collective-permute-start(f32[2,2,8,1152]{3,2,1,0:T(8,128)S(1)} %slice_bitcast_fusion.5), channel_id=1, source_target_pairs={{0,8},{1,9},{2,10},{3,11},{4,28},{5,29},{6,30},{7,31},{8,0},{9,1},... | collective-permute-start | bytes 442376 | tf_op jit(solution)/shard_map/ppermute | solution.py:456
  81.5 5.6 %collective-permute-start.15 = (f32[80,256]{1,0:T(8,128)S(1)}, f32[80,256]{1,0:T(8,128)S(1)}, u32[]{:S(2)}, u32[]{:S(2)}) collective-permute-start(f32[80,256]{1,0:T(8,128)S(1)} %add.65), channel_id=1, source_target_pairs={{0,96},{1,97},{2,98},{3,99},{4,36},{5,37},{6,38},{7,39},{8,104},{9... | collective-permute-start | bytes 245768 | tf_op jit(solution)/shard_map/ppermute | solution.py:456
  87.1 2.4 %collective-permute-done.15 = f32[80,256]{1,0:T(8,128)S(1)} collective-permute-done((f32[80,256]{1,0:T(8,128)S(1)}, f32[80,256]{1,0:T(8,128)S(1)}, u32[]{:S(2)}, u32[]{:S(2)}) %collective-permute-start.15) | collective-permute-done | bytes 81952 | tf_op jit(solution)/shard_map/ppermute | solution.py:456
  89.6 0.1 collective-permute-start.16
  89.7 3.3 %collective-permute-start.18 = (f32[2,8,1152]{2,1,0:T(8,128)S(1)}, f32[2,8,1152]{2,1,0:T(8,128)S(1)}, u32[]{:S(2)}, u32[]{:S(2)}) collective-permute-start(f32[2,8,1152]{2,1,0:T(8,128)S(1)} %slice_bitcast_fusion.6), channel_id=1, source_target_pairs={{0,96},{1,97},{2,98},{3,99},{4,36},{5,37},{6,38},{7,39},{8,104},{9... | collective-permute-start | bytes 221192 | tf_op jit(solution)/shard_map/ppermute | solution.py:456
  93.0 4.8 %final_part.1 = (bf16[6,14,14,1024]{3,2,1,0:T(8,128)(2,1)}, f32[2,8,1152]{2,1,0:T(8,128)S(1)}) custom-call(bf16[1344,1024]{1,0:T(8,128)(2,1)S(1)} %get-tuple-element.48.dev, bf16[1344,1024]{1,0:T(8,128)(2,1)S(1)} %bitcast.66, f32[80,256]{1,0:T(8,128)S(1)} %add.69.mine, f32[80,256]{1,0:T(8,128)S(1)} %collective-permute-done.16.theirs, ...), custom_call_target="tpu_custom_call" | custom-call | tf_op jit(solution)/shard_map/final_part/pallas_call | solution.py:425
  97.9 0.6 fusion.5
  (31 shorter events, 0.4 us)
Async XLA Ops:
  0.6 0.7 copy-start.1
  12.8 7.2 %collective-permute-start.1 = (f32[512,1152]{1,0:T(8,128)S(1)}, f32[512,1152]{1,0:T(8,128)S(1)}, u32[]{:S(2)}, u32[]{:S(2)}) collective-permute-start(f32[512,1152]{1,0:T(8,128)S(1)} %get-tuple-element.40), channel_id=1, source_target_pairs={{0,4},{1,5},{2,6},{3,7},{4,0},{5,1},{6,2},{7,3},{8,12},{9,13},{10,... | collective-permute-start | bytes 7077896 | tf_op jit(solution)/shard_map/ppermute | solution.py:456
  19.2 4.9 %collective-permute-start = (f32[512,1152]{1,0:T(8,128)S(1)}, f32[512,1152]{1,0:T(8,128)S(1)}, u32[]{:S(2)}, u32[]{:S(2)}) collective-permute-start(f32[512,1152]{1,0:T(8,128)S(1)} %get-tuple-element.38), channel_id=1, source_target_pairs={{0,4},{1,5},{2,6},{3,7},{4,0},{5,1},{6,2},{7,3},{8,12},{9,13},{10,... | collective-permute-start | bytes 7077896 | tf_op jit(solution)/shard_map/ppermute | solution.py:456
  20.4 22.5 %collective-permute-start.5 = (f32[2,2,2,2,2,8,1152]{6,5,1,2,4,3,0:T(8,128)S(1)}, f32[2,2,2,2,2,8,1152]{6,5,1,2,4,3,0:T(8,128)S(1)}, u32[]{:S(2)}, u32[]{:S(2)}) collective-permute-start(f32[2,2,2,2,2,8,1152]{6,5,1,2,4,3,0:T(8,128)S(1)} %bitcast.71), channel_id=1, source_target_pairs={{0,24},{1,25},{2,26},{3,27},{4,12},{5,13},{6,14},{7,15},{8,16},{9,... | collective-permute-start | bytes 3538952 | tf_op jit(solution)/shard_map/ppermute | solution.py:456
  24.5 1.8 %copy-start = (f32[16,64,64]{2,1,0:T(8,128)S(1)}, f32[16,64,64]{2,1,0:T(8,128)}, u32[]{:S(2)}) copy-start(f32[16,64,64]{2,1,0:T(8,128)} %vectors.1) | copy-start | bytes 786436
  24.5 1.8 %copy-start.2 = (f32[16,64]{1,0:T(8,128)S(1)}, f32[16,64]{1,0:T(8,128)}, u32[]{:S(2)}) copy-start(f32[16,64]{1,0:T(8,128)} %values.3) | copy-start | bytes 12292
  24.6 18.5 %collective-permute-start.4 = (f32[2,2,2,2,2,8,1152]{6,5,1,3,4,0,2:T(8,128)S(1)}, f32[2,2,2,2,2,8,1152]{6,5,1,3,4,0,2:T(8,128)S(1)}, u32[]{:S(2)}, u32[]{:S(2)}) collective-permute-start(f32[2,2,2,2,2,8,1152]{6,5,1,3,4,0,2:T(8,128)S(1)} %bitcast.72), channel_id=1, source_target_pairs={{0,1},{1,0},{2,3},{3,2},{4,7},{5,6},{6,5},{7,4},{8,9},{9,8},{10,11... | collective-permute-start | bytes 3538952 | tf_op jit(solution)/shard_map/ppermute | solution.py:456
  36.0 2.4 %collective-permute-start.2 = (f32[80,256]{1,0:T(8,128)S(1)}, f32[80,256]{1,0:T(8,128)S(1)}, u32[]{:S(2)}, u32[]{:S(2)}) collective-permute-start(f32[80,256]{1,0:T(8,128)S(1)} %get-tuple-element.50), channel_id=1, source_target_pairs={{0,4},{1,5},{2,6},{3,7},{4,0},{5,1},{6,2},{7,3},{8,12},{9,13},{10,... | collective-permute-start | bytes 245768 | tf_op jit(solution)/shard_map/ppermute | solution.py:456
  38.4 4.5 %collective-permute-start.3 = (f32[80,256]{1,0:T(8,128)S(1)}, f32[80,256]{1,0:T(8,128)S(1)}, u32[]{:S(2)}, u32[]{:S(2)}) collective-permute-start(f32[80,256]{1,0:T(8,128)S(1)} %add.56), channel_id=1, source_target_pairs={{0,1},{1,0},{2,3},{3,2},{4,7},{5,6},{6,5},{7,4},{8,9},{9,8},{10,11... | collective-permute-start | bytes 245768 | tf_op jit(solution)/shard_map/ppermute | solution.py:456
  43.3 10.0 %collective-permute-start.8 = (f32[2,2,2,2,8,1152]{5,4,0,1,3,2:T(8,128)S(1)}, f32[2,2,2,2,8,1152]{5,4,0,1,3,2:T(8,128)S(1)}, u32[]{:S(2)}, u32[]{:S(2)}) collective-permute-start(f32[2,2,2,2,8,1152]{5,4,0,1,3,2:T(8,128)S(1)} %slice_bitcast_fusion), channel_id=1, source_target_pairs={{0,32},{1,33},{2,34},{3,35},{4,100},{5,101},{6,102},{7,103},{8,40}... | collective-permute-start | bytes 1769480 | tf_op jit(solution)/shard_map/ppermute | solution.py:456
  45.3 5.7 %collective-permute-start.6 = (f32[80,256]{1,0:T(8,128)S(1)}, f32[80,256]{1,0:T(8,128)S(1)}, u32[]{:S(2)}, u32[]{:S(2)}) collective-permute-start(f32[80,256]{1,0:T(8,128)S(1)} %add.57), channel_id=1, source_target_pairs={{0,3},{1,2},{2,1},{3,0},{4,5},{5,4},{6,7},{7,6},{8,11},{9,10},{10,... | collective-permute-start | bytes 245768 | tf_op jit(solution)/shard_map/ppermute | solution.py:456
  47.0 11.2 %collective-permute-start.7 = (f32[2,2,2,2,8,1152]{5,4,1,2,3,0:T(8,128)S(1)}, f32[2,2,2,2,8,1152]{5,4,1,2,3,0:T(8,128)S(1)}, u32[]{:S(2)}, u32[]{:S(2)}) collective-permute-start(f32[2,2,2,2,8,1152]{5,4,1,2,3,0:T(8,128)S(1)} %slice_bitcast_fusion.1), channel_id=1, source_target_pairs={{0,24},{1,25},{2,26},{3,27},{4,12},{5,13},{6,14},{7,15},{8,16},{9,... | collective-permute-start | bytes 1769480 | tf_op jit(solution)/shard_map/ppermute | solution.py:456
  58.3 5.7 %collective-permute-start.9 = (f32[80,256]{1,0:T(8,128)S(1)}, f32[80,256]{1,0:T(8,128)S(1)}, u32[]{:S(2)}, u32[]{:S(2)}) collective-permute-start(f32[80,256]{1,0:T(8,128)S(1)} %add.60), channel_id=1, source_target_pairs={{0,24},{1,25},{2,26},{3,27},{4,12},{5,13},{6,14},{7,15},{8,16},{9,... | collective-permute-start | bytes 245768 | tf_op jit(solution)/shard_map/ppermute | solution.py:456
  61.4 7.2 %collective-permute-start.12 = (f32[2,2,2,8,1152]{4,3,0,1,2:T(8,128)S(1)}, f32[2,2,2,8,1152]{4,3,0,1,2:T(8,128)S(1)}, u32[]{:S(2)}, u32[]{:S(2)}) collective-permute-start(f32[2,2,2,8,1152]{4,3,0,1,2:T(8,128)S(1)} %slice_bitcast_fusion.4), channel_id=1, source_target_pairs={{0,32},{1,33},{2,34},{3,35},{4,100},{5,101},{6,102},{7,103},{8,40}... | collective-permute-start | bytes 884744 | tf_op jit(solution)/shard_map/ppermute | solution.py:456
  64.0 4.5 %collective-permute-start.10 = (f32[80,256]{1,0:T(8,128)S(1)}, f32[80,256]{1,0:T(8,128)S(1)}, u32[]{:S(2)}, u32[]{:S(2)}) collective-permute-start(f32[80,256]{1,0:T(8,128)S(1)} %add.63), channel_id=1, source_target_pairs={{0,8},{1,9},{2,10},{3,11},{4,28},{5,29},{6,30},{7,31},{8,0},{9,1},... | collective-permute-start | bytes 245768 | tf_op jit(solution)/shard_map/ppermute | solution.py:456
  64.2 7.0 %collective-permute-start.13 = (f32[2,2,2,8,1152]{4,3,0,1,2:T(8,128)S(1)}, f32[2,2,2,8,1152]{4,3,0,1,2:T(8,128)S(1)}, u32[]{:S(2)}, u32[]{:S(2)}) collective-permute-start(f32[2,2,2,8,1152]{4,3,0,1,2:T(8,128)S(1)} %slice_bitcast_fusion.3), channel_id=1, source_target_pairs={{0,1},{1,0},{2,3},{3,2},{4,7},{5,6},{6,5},{7,4},{8,9},{9,8},{10,11... | collective-permute-start | bytes 884744 | tf_op jit(solution)/shard_map/ppermute | solution.py:456
  71.3 8.0 %collective-permute-start.14 = (f32[2,2,2,8,1152]{4,3,2,0,1:T(8,128)S(1)}, f32[2,2,2,8,1152]{4,3,2,0,1:T(8,128)S(1)}, u32[]{:S(2)}, u32[]{:S(2)}) collective-permute-start(f32[2,2,2,8,1152]{4,3,2,0,1:T(8,128)S(1)} %slice_bitcast_fusion.2), channel_id=1, source_target_pairs={{0,3},{1,2},{2,1},{3,0},{4,5},{5,4},{6,7},{7,6},{8,11},{9,10},{10,... | collective-permute-start | bytes 884744 | tf_op jit(solution)/shard_map/ppermute | solution.py:456
  72.9 4.4 %collective-permute-start.11 = (f32[80,256]{1,0:T(8,128)S(1)}, f32[80,256]{1,0:T(8,128)S(1)}, u32[]{:S(2)}, u32[]{:S(2)}) collective-permute-start(f32[80,256]{1,0:T(8,128)S(1)} %add.64), channel_id=1, source_target_pairs={{0,32},{1,33},{2,34},{3,35},{4,100},{5,101},{6,102},{7,103},{8,40}... | collective-permute-start | bytes 245768 | tf_op jit(solution)/shard_map/ppermute | solution.py:456
  79.4 10.3 %collective-permute-start.17 = (f32[2,2,8,1152]{3,2,1,0:T(8,128)S(1)}, f32[2,2,8,1152]{3,2,1,0:T(8,128)S(1)}, u32[]{:S(2)}, u32[]{:S(2)}) collective-permute-start(f32[2,2,8,1152]{3,2,1,0:T(8,128)S(1)} %slice_bitcast_fusion.5), channel_id=1, source_target_pairs={{0,8},{1,9},{2,10},{3,11},{4,28},{5,29},{6,30},{7,31},{8,0},{9,1},... | collective-permute-start | bytes 442376 | tf_op jit(solution)/shard_map/ppermute | solution.py:456
  81.5 8.1 %collective-permute-start.15 = (f32[80,256]{1,0:T(8,128)S(1)}, f32[80,256]{1,0:T(8,128)S(1)}, u32[]{:S(2)}, u32[]{:S(2)}) collective-permute-start(f32[80,256]{1,0:T(8,128)S(1)} %add.65), channel_id=1, source_target_pairs={{0,96},{1,97},{2,98},{3,99},{4,36},{5,37},{6,38},{7,39},{8,104},{9... | collective-permute-start | bytes 245768 | tf_op jit(solution)/shard_map/ppermute | solution.py:456
  89.6 3.5 %collective-permute-start.16 = (f32[80,256]{1,0:T(8,128)S(1)}, f32[80,256]{1,0:T(8,128)S(1)}, u32[]{:S(2)}, u32[]{:S(2)}) collective-permute-start(f32[80,256]{1,0:T(8,128)S(1)} %add.69.mine), channel_id=1, source_target_pairs={{0,4},{1,5},{2,6},{3,7},{4,0},{5,1},{6,2},{7,3},{8,12},{9,13},{10,... | collective-permute-start | bytes 245768 | tf_op jit(solution)/shard_map/ppermute | solution.py:456
  89.7 8.2 %collective-permute-start.18 = (f32[2,8,1152]{2,1,0:T(8,128)S(1)}, f32[2,8,1152]{2,1,0:T(8,128)S(1)}, u32[]{:S(2)}, u32[]{:S(2)}) collective-permute-start(f32[2,8,1152]{2,1,0:T(8,128)S(1)} %slice_bitcast_fusion.6), channel_id=1, source_target_pairs={{0,96},{1,97},{2,98},{3,99},{4,36},{5,37},{6,38},{7,39},{8,104},{9... | collective-permute-start | bytes 221192 | tf_op jit(solution)/shard_map/ppermute | solution.py:456

commit v8 on v6

--- a/solution.py
+++ b/solution.py
@@ -12,7 +12,9 @@
 ALL = ("z", "y", "c", "x")
 SIZE = {"z": 4, "y": 4, "c": 2, "x": 4}
 STRIDE = {"z": 32, "y": 8, "c": 4, "x": 1}
-RING = ((0, 3, 1, 2), (0, 1, 3, 2))
+ORDERS = ((0, 3, 1, 2), (0, 1, 3, 2))
+FLIP = {"z": 0, "y": 1, "x": 0}
+RING = [{axis: ORDERS[(c + FLIP[axis]) % 2] for axis in "zyx"} for c in range(2)]
 F32 = jnp.float32
 BF16 = jnp.bfloat16
 IMAGES, H, W, D, O = 6, 14, 14, 1024, 256
@@ -81,8 +83,8 @@
     for axis in "zyx":
         i = lax.axis_index(axis)
         a, b = (i ^ (i >> 1)) & 1, i >> 1
-        spots[0].append(2 * a + b)
-        spots[1].append(2 * b + a)
+        for c in range(2):
+            spots[c].append(2 * a + b if (c + FLIP[axis]) % 2 == 0 else 2 * b + a)
     return core, spots
 
 
@@ -90,7 +92,7 @@
     features_hbm,
     grads_hbm,
     vectors_hbm,
-    values,
+    values_hbm,
     cols,
     xc,
     wht,
@@ -102,13 +104,14 @@
     features,
     grads,
     vectors,
+    values,
     arrived,
 ):
+    moves = [(values_hbm, values), (vectors_hbm, vectors), (grads_hbm, grads)]
+    moves += [(features_hbm.at[b], features.at[b]) for b in range(IMAGES)]
     copies = [
         pltpu.make_async_copy(source, target, arrived.at[k])
-        for k, (source, target) in enumerate(
-            ((vectors_hbm, vectors), (grads_hbm, grads), (features_hbm, features))
-        )
+        for k, (source, target) in enumerate(moves)
     ]
     for copy in copies:
         copy.start()
@@ -118,6 +121,7 @@
     xc[...] = jnp.zeros_like(xc)
     wht[1024:1040, :] = jnp.ones((16, ROWS), BF16)
     copies[0].wait()
+    copies[1].wait()
     for z in range(4):
         basis = block_vectors(vectors, z, same)
         scale = lax.rsqrt(value_row(values, z))
@@ -125,11 +129,12 @@
         whiten[z] = full.astype(BF16)
         for c in range(2):
             at_z, at_y, at_x = spots[c]
-            for row, (y, x) in enumerate((y, x) for y in RING[c] for x in RING[c]):
+            order = [(y, x) for y in RING[c]["y"] for x in RING[c]["x"]]
+            for row, (y, x) in enumerate(order):
                 channel = y * 64 + c * 32 + x * 8
                 row = pl.multiple_of(8 * (row ^ (4 * at_y + at_x)), 8)
                 wp32[4 * c + z, pl.ds(row, 8), :] = full[channel : channel + 8, :]
-    copies[1].wait()
+    copies[2].wait()
     inside = lax.broadcasted_iota(jnp.int32, (H, 16, O), 1) < W
     for b in range(IMAGES):
         wide[:, 8 : 8 + W, :] = grads[b].astype(F32)
@@ -147,9 +152,9 @@
                     cols[b * H + H - 1, :, lane : lane + O] = jnp.zeros((16, O), BF16)
                 if a == 2:
                     cols[b * H, :, lane : lane + O] = jnp.zeros((16, O), BF16)
-    copies[2].wait()
     total = jnp.zeros((1, D), F32)
     for b in range(IMAGES):
+        copies[3 + b].wait()
         total = total + jnp.sum(
             jnp.sum(features[b].astype(F32), axis=0), axis=0, keepdims=True
         )
@@ -168,7 +173,7 @@
         c, z = k // 4, k % 4
         chunk = xc[:, :, 256 * z : 256 * z + 256].reshape(ROWS, 256)
         part = nt(wp32[k].astype(BF16), chunk)
-        row = 4 * (c ^ core) + (RING[c].index(z) ^ spots[c][0])
+        row = 4 * (c ^ core) + (RING[c]["z"].index(z) ^ spots[c][0])
         row = pl.multiple_of(128 * row, 128)
         wht[pl.ds(row, 128), :] = part.astype(BF16)
         shift = part[:, 14:15] + part[:, 15:16] + part[:, 30:31]
@@ -186,7 +191,7 @@
             jax.ShapeDtypeStruct((1, D), F32),
             jax.ShapeDtypeStruct((4, 256, 256), BF16),
         ),
-        in_specs=[IN_HBM] * 3 + [ON_CHIP],
+        in_specs=[IN_HBM] * 4,
         out_specs=(ON_CHIP,) * 6,
         scratch_shapes=[
             pltpu.VMEM((H, 32, O), F32),
@@ -194,7 +199,8 @@
             pltpu.VMEM((IMAGES, H, W, D), BF16),
             pltpu.VMEM((IMAGES, H, W, O), BF16),
             pltpu.VMEM((16, 64, 64), F32),
-            pltpu.SemaphoreType.DMA((3,)),
+            pltpu.VMEM((16, 64), F32),
+            pltpu.SemaphoreType.DMA((3 + IMAGES,)),
         ],
         compiler_params=pltpu.CompilerParams(vmem_limit_bytes=10 << 20),
         name="prep",
@@ -348,34 +354,42 @@
     below = (lax.broadcasted_iota(jnp.int32, (256, 256), 0) & 63) - (
         lax.broadcasted_iota(jnp.int32, (256, 256), 1) & 63
     )
-    for z in range(4):
-        lanes = slice(256 * z, 256 * z + 256)
+    every = range(4)
+    chunk = [slice(256 * z, 256 * z + 256) for z in every]
+    total, mean, covs = [], [], []
+    for z in every:
         start = 64 + 8 * (z % 2)
         tail = blocks[z // 2, start : start + 8, :]
-        total, mean = tail[0:1], tail[1:2] * (1.0 / TOTAL)
+        total.append(tail[0:1])
+        mean.append(tail[1:2] * (1.0 / TOTAL))
         packed = blocks[z // 2, 0:64, :]
         square = jnp.concatenate([packed, packed, packed, packed], axis=0)
         if z % 2 == 0:
             raw = jnp.where(below <= 0, square, square.T)
         else:
             raw = jnp.where(below > 0, square, square.T)
-            raw = jnp.where(below == 0, tail[5:6], raw)
-        tall = columns_of([total, mean])
-        cov = raw - 0.5 * (tall[:, 1:2] * total + tall[:, 0:1] * mean)
-        basis, turned = (bases[z, 0], bases[z, 1]), (bases[z, 2], bases[z, 3])
-        rotated = fine(nn, turned, fine(nn, cov, basis))
-        grad = fine(nn, basis, fine(nn, rotated * factors[z], turned))
-        sigma[z] = (grad * (2.0 / TOTAL)).astype(BF16)
-        moved = own[0:1, lanes] * (1.0 / PIXELS) - total * (1.0 / TOTAL)
-        offset = own[1:2, lanes] * (1.0 / PIXELS) - mean
+            raw = jnp.where(below == 0, blocks[z // 2, start + 5 : start + 6, :], raw)
+        tall = columns_of([total[z], mean[z]])
+        covs.append(raw - 0.5 * (tall[:, 1:2] * total[z] + tall[:, 0:1] * mean[z]))
+    basis = [(bases[z, 0], bases[z, 1]) for z in every]
+    turned = [(bases[z, 2], bases[z, 3]) for z in every]
+    grads = [fine(nn, covs[z], basis[z]) for z in every]
+    grads = [fine(nn, turned[z], grads[z]) * factors[z] for z in every]
+    grads = [fine(nn, grads[z], turned[z]) for z in every]
+    grads = [fine(nn, basis[z], grads[z]) for z in every]
+    for z in every:
+        sigma[z] = (grads[z] * (2.0 / TOTAL)).astype(BF16)
+    for z in every:
+        lanes = chunk[z]
+        moved = own[0:1, lanes] * (1.0 / PIXELS) - total[z] * (1.0 / TOTAL)
+        offset = own[1:2, lanes] * (1.0 / PIXELS) - mean[z]
         empty = [jnp.zeros((1, 256), BF16)]
-        stacked = jnp.concatenate(pieces(moved, 3) + pieces(mean, 3) + empty * 2, axis=0)
+        stacked = jnp.concatenate(pieces(moved, 3) + pieces(mean[z], 3) + empty * 2, axis=0)
         through = nn(stacked, whiten[z])
         stacked = jnp.concatenate(pieces(offset, 3) + empty * 5, axis=0)
         other = nn(stacked, sigma[z])
-        row_vector[0:1, lanes] = (
-            jnp.sum(through[0:3], axis=0, keepdims=True)
-            + jnp.sum(other[0:3], axis=0, keepdims=True)
+        row_vector[0:1, lanes] = jnp.sum(through[0:3], axis=0, keepdims=True) + jnp.sum(
+            other[0:3], axis=0, keepdims=True
         )
         shift[0:1, lanes] = jnp.sum(through[3:6], axis=0, keepdims=True)
     first = 8 * sum(STRIDE[axis] * lax.axis_index(axis) for axis in ALL)
@@ -442,7 +456,7 @@
 
 def ring(axis, step):
     def move(at):
-        at[axis] ^= (1, 3)[(step + at["c"]) % 2]
+        at[axis] ^= (1, 3)[(step + at["c"] + FLIP[axis]) % 2]
 
     return move
 
@@ -454,7 +468,9 @@
 
 def local(features, grads, kernel, vectors, values):
     stay = lambda array: pltpu.with_memory_space_constraint(array, pltpu.HBM)
-    cols, xc, wht, u, sums, whiten = prep(stay(features), stay(grads), stay(vectors), values)
+    cols, xc, wht, u, sums, whiten = prep(
+        stay(features), stay(grads), stay(vectors), stay(values)
+    )
     cols, xc = cols.reshape(ROWS, 9 * O), xc.reshape(ROWS, D)
     kernel = stay(kernel.reshape(9 * O, D))
 

time: 89.3 us -> 89.9 us (level)
  starting transfers between devices: 27 us -> 33.3 us
  waiting for transfers between devices: 27 us -> 24.3 us
  Pallas kernels: 30.5 us -> 28.5 us
    ppermute x23, starting transfers between devices: 27 us -> 33.3 us  [exchange(): return lax.ppermute(value, ALL, permutation(move))]
    ppermute x23, waiting for transfers between devices: 27 us -> 24.3 us  [exchange(): return lax.ppermute(value, ALL, permutation(move))]
    pallas_call x1, Pallas kernels: 7 us -> 4.92 us  [final_part(): pl.pallas_call(final_kernel, in_specs=[ON_CHIP] * 8, out_specs=(IN_HBM, O...]
  transfers between devices with their start and end apart: 23 -> 23, of which waited for: 11 -> 11; matrix products, arithmetic and copies ran while one was open for 2% -> 2% of each run, Pallas kernels for 25% -> 22%
where the time goes in v8:
time: 89.9 us; the launch traced here: 89.8 us
  starting transfers between devices  33.3 us (37%)
  Pallas kernels  28.5 us (32%)
  waiting for transfers between devices  24.3 us (27%)
  other arithmetic  1.93 us (2%)
  between operations  1 us (1%)
    ppermute x23, starting transfers between devices, exchange(): return lax.ppermute(value, ALL, permutation(move))  33.3 us
    ppermute x23, waiting for transfers between devices, exchange(): return lax.ppermute(value, ALL, permutation(move))  24.3 us
    pallas_call x3, Pallas kernels, weight_part(): pl.pallas_call(functools.partial(weight_kernel, a), in_specs=[ON_CHIP] *...  9.37 us
    pallas_call x1, Pallas kernels, back_part(): pl.pallas_call(back_kernel, in_specs=[ON_CHIP] * 11, out_specs=(ON_CHIP,)...  8.97 us
    pallas_call x1, Pallas kernels, prep(): pl.pallas_call(prep_kernel, out_shape=(jax.ShapeDtypeStruct((IMAGES * H,...  5.23 us
    pallas_call x1, Pallas kernels, final_part(): pl.pallas_call(final_kernel, in_specs=[ON_CHIP] * 8, out_specs=(IN_HBM, O...  4.92 us
  transfers between devices with their start and end apart: 23, of which 11 were waited for; matrix products, arithmetic and copies ran while one was open for 2% of the time, Pallas kernels for 22%

profile of v8, /device:TPU:0, one launch (start us, length us, event | category | flops | bytes accessed | tf_op | source)
XLA Modules:
  0.0 89.8 jit_solution(998957065377743322)
XLA Ops:
  0.6 5.2 %prep.1 = (bf16[84,16,2304]{2,1,0:T(8,128)(2,1)S(1)}, bf16[84,16,1024]{2,1,0:T(8,128)(2,1)S(1)}, bf16[1040,1344]{1,0:T(8,128)(2,1)S(1)}, f32[1024,128]{1,0:T(8,1...) custom-call(bf16[6,14,14,1024]{3,2,1,0:T(8,128)(2,1)} %features_hbm.1, ...), custom_call_target="tpu_custom_call" | custom-call | tf_op jit(solution)/shard_map/prep/pallas_call | solution.py:184
  5.9 3.1 %weight_part_2.1 = (f32[512,768]{1,0:T(8,128)S(1)}, f32[512,768]{1,0:T(8,128)S(1)}, f32[8,768]{1,0:T(8,128)S(1)}, bf16[768,1024]{1,0:T(8,128)(2,1)S(1)}) custom-call(bf16[1040,1344]{1,0:T(8,128)(2,1)S(1)} %get-tuple-element.41.wht, bf16[1344,2304]{1,0:T(8,128)(2,1)S(1)} %bitcast.76, f32[1024,128]{1,0:T(8,128)S(1)} %get-tuple-element.42.u, ...), custom_call_target="tpu_custom_call" | custom-call | tf_op jit(solution)/shard_map/weight_part_2/pallas_call | solution.py:227
  9.0 0.1 collective-permute-start.5
  9.1 3.1 %weight_part_0.1 = (f32[512,768]{1,0:T(8,128)S(1)}, f32[512,768]{1,0:T(8,128)S(1)}, f32[8,768]{1,0:T(8,128)S(1)}, bf16[768,1024]{1,0:T(8,128)(2,1)S(1)}) custom-call(bf16[1040,1344]{1,0:T(8,128)(2,1)S(1)} %get-tuple-element.41.wht, bf16[1344,2304]{1,0:T(8,128)(2,1)S(1)} %bitcast.77, f32[1024,128]{1,0:T(8,128)S(1)} %get-tuple-element.42.u, ...), custom_call_target="tpu_custom_call" | custom-call | tf_op jit(solution)/shard_map/weight_part_0/pallas_call | solution.py:227
  12.2 0.6 collective-permute-start
  12.8 3.1 %weight_part_1.1 = (f32[512,768]{1,0:T(8,128)S(1)}, f32[512,768]{1,0:T(8,128)S(1)}, f32[8,768]{1,0:T(8,128)S(1)}, bf16[768,1024]{1,0:T(8,128)(2,1)S(1)}) custom-call(bf16[1040,1344]{1,0:T(8,128)(2,1)S(1)} %get-tuple-element.41.wht, bf16[1344,2304]{1,0:T(8,128)(2,1)S(1)} %bitcast.78, f32[1024,128]{1,0:T(8,128)S(1)} %get-tuple-element.42.u, ...), custom_call_target="tpu_custom_call" | custom-call | tf_op jit(solution)/shard_map/weight_part_1/pallas_call | solution.py:227
  15.9 0.1 collective-permute-start.1
  16.0 0.2 add.71
  16.2 0.1 fusion.7
  16.4 2.1 %collective-permute-start.6 = (f32[2,2,2,2,2,8,768]{6,5,0,2,4,1,3:T(8,128)S(1)}, f32[2,2,2,2,2,8,768]{6,5,0,2,4,1,3:T(8,128)S(1)}, u32[]{:S(2)}, u32[]{:S(2)}) collective-permute-start(f32[2,2,2,2,2,8,768]{6,5,0,2,4,1,3:T(8,128)S(1)} %copy.11), channel_id=1, source_target_pairs={{0,32},{1,33},{2,34},{3,35},{4,100},{5,101},{6,102},{7,103},{8,40}... | collective-permute-start | bytes 2359304 | tf_op jit(solution)/shard_map/ppermute | solution.py:450
  18.5 0.2 add.66
  18.7 0.1 fusion.9
  18.9 1.7 %collective-permute-start.3 = (f32[2,2,2,2,2,8,768]{6,5,1,3,4,0,2:T(8,128)S(1)}, f32[2,2,2,2,2,8,768]{6,5,1,3,4,0,2:T(8,128)S(1)}, u32[]{:S(2)}, u32[]{:S(2)}) collective-permute-start(f32[2,2,2,2,2,8,768]{6,5,1,3,4,0,2:T(8,128)S(1)} %bitcast.89), channel_id=1, source_target_pairs={{0,1},{1,0},{2,3},{3,2},{4,7},{5,6},{6,5},{7,4},{8,9},{9,8},{10,11... | collective-permute-start | bytes 2359304 | tf_op jit(solution)/shard_map/ppermute | solution.py:450
  20.7 0.2 add.67
  20.9 0.1 fusion.8
  21.1 3.1 %collective-permute-start.4 = (f32[2,2,2,2,2,8,768]{6,5,1,2,4,3,0:T(8,128)S(1)}, f32[2,2,2,2,2,8,768]{6,5,1,2,4,3,0:T(8,128)S(1)}, u32[]{:S(2)}, u32[]{:S(2)}) collective-permute-start(f32[2,2,2,2,2,8,768]{6,5,1,2,4,3,0:T(8,128)S(1)} %bitcast.90), channel_id=1, source_target_pairs={{0,24},{1,25},{2,26},{3,27},{4,12},{5,13},{6,14},{7,15},{8,16},{9,... | collective-permute-start | bytes 2359304 | tf_op jit(solution)/shard_map/ppermute | solution.py:450
  24.2 9.0 %back_part.1 = (bf16[1344,1024]{1,0:T(8,128)(2,1)S(1)}, f32[8,1024]{1,0:T(8,128)S(1)}, f32[80,256]{1,0:T(8,128)S(1)}, f32[80,256]{1,0:T(8,128)S(1)}, bf16[4,4,25...) custom-call(bf16[1344,2304]{1,0:T(8,128)(2,1)S(1)} %bitcast.79, bf16[768,1024]{1,0:T(8,128)(2,1)S(1)} %get-tuple-element.48.slab0, ...), custom_call_target="tpu_custom_call" | custom-call | tf_op jit(solution)/shard_map/back_part/pallas_call | solution.py:315
  33.2 1.7 %collective-permute-start.2 = (f32[80,256]{1,0:T(8,128)S(1)}, f32[80,256]{1,0:T(8,128)S(1)}, u32[]{:S(2)}, u32[]{:S(2)}) collective-permute-start(f32[80,256]{1,0:T(8,128)S(1)} %get-tuple-element.58), channel_id=1, source_target_pairs={{0,4},{1,5},{2,6},{3,7},{4,0},{5,1},{6,2},{7,3},{8,12},{9,13},{10,... | collective-permute-start | bytes 245768 | tf_op jit(solution)/shard_map/ppermute | solution.py:450
  34.9 0.9 %collective-permute-done.2 = f32[80,256]{1,0:T(8,128)S(1)} collective-permute-done((f32[80,256]{1,0:T(8,128)S(1)}, f32[80,256]{1,0:T(8,128)S(1)}, u32[]{:S(2)}, u32[]{:S(2)}) %collective-permute-start.2) | collective-permute-done | bytes 81952 | tf_op jit(solution)/shard_map/ppermute | solution.py:450
  35.8 0.1 copy_add_fusion
  35.9 0.1 fusion.1
  36.0 0.1 fusion
  36.1 0.3 collective-permute-start.7
  36.5 1.9 %collective-permute-start.11 = (f32[2,2,2,2,8,768]{5,4,0,2,3,1:T(8,128)S(1)}, f32[2,2,2,2,8,768]{5,4,0,2,3,1:T(8,128)S(1)}, u32[]{:S(2)}, u32[]{:S(2)}) collective-permute-start(f32[2,2,2,2,8,768]{5,4,0,2,3,1:T(8,128)S(1)} %slice_bitcast_fusion), channel_id=1, source_target_pairs={{0,1},{1,0},{2,3},{3,2},{4,7},{5,6},{6,5},{7,4},{8,9},{9,8},{10,11... | collective-permute-start | bytes 1179656 | tf_op jit(solution)/shard_map/ppermute | solution.py:450
  38.4 0.1 collective-permute-start.10
  38.5 2.2 %collective-permute-done.7 = f32[80,256]{1,0:T(8,128)S(1)} collective-permute-done((f32[80,256]{1,0:T(8,128)S(1)}, f32[80,256]{1,0:T(8,128)S(1)}, u32[]{:S(2)}, u32[]{:S(2)}) %collective-permute-start.7) | collective-permute-done | bytes 81952 | tf_op jit(solution)/shard_map/ppermute | solution.py:450
  40.7 1.0 %collective-permute-start.8 = (f32[80,256]{1,0:T(8,128)S(1)}, f32[80,256]{1,0:T(8,128)S(1)}, u32[]{:S(2)}, u32[]{:S(2)}) collective-permute-start(f32[80,256]{1,0:T(8,128)S(1)} %add.73), channel_id=1, source_target_pairs={{0,3},{1,2},{2,1},{3,0},{4,5},{5,4},{6,7},{7,6},{8,11},{9,10},{10,... | collective-permute-start | bytes 245768 | tf_op jit(solution)/shard_map/ppermute | solution.py:450
  41.7 2.7 %collective-permute-start.9 = (f32[2,2,2,2,8,768]{5,4,1,2,3,0:T(8,128)S(1)}, f32[2,2,2,2,8,768]{5,4,1,2,3,0:T(8,128)S(1)}, u32[]{:S(2)}, u32[]{:S(2)}) collective-permute-start(f32[2,2,2,2,8,768]{5,4,1,2,3,0:T(8,128)S(1)} %slice_bitcast_fusion.2), channel_id=1, source_target_pairs={{0,24},{1,25},{2,26},{3,27},{4,12},{5,13},{6,14},{7,15},{8,16},{9,... | collective-permute-start | bytes 1179656 | tf_op jit(solution)/shard_map/ppermute | solution.py:450
  44.3 2.1 %collective-permute-done.8 = f32[80,256]{1,0:T(8,128)S(1)} collective-permute-done((f32[80,256]{1,0:T(8,128)S(1)}, f32[80,256]{1,0:T(8,128)S(1)}, u32[]{:S(2)}, u32[]{:S(2)}) %collective-permute-start.8) | collective-permute-done | bytes 81952 | tf_op jit(solution)/shard_map/ppermute | solution.py:450
  46.6 4.2 %collective-permute-done.9 = f32[2,2,2,2,8,768]{5,4,1,2,3,0:T(8,128)S(1)} collective-permute-done((f32[2,2,2,2,8,768]{5,4,1,2,3,0:T(8,128)S(1)}, f32[2,2,2,2,8,768]{5,4,1,2,3,0:T(8,128)S(1)}, u32[]{:S(2)}, u32[]{:S(2)}) %collective-permute-start.9) | collective-permute-done | bytes 393248 | tf_op jit(solution)/shard_map/ppermute | solution.py:450
  50.8 2.7 %collective-permute-start.12 = (f32[80,256]{1,0:T(8,128)S(1)}, f32[80,256]{1,0:T(8,128)S(1)}, u32[]{:S(2)}, u32[]{:S(2)}) collective-permute-start(f32[80,256]{1,0:T(8,128)S(1)} %add.74), channel_id=1, source_target_pairs={{0,24},{1,25},{2,26},{3,27},{4,12},{5,13},{6,14},{7,15},{8,16},{9,... | collective-permute-start | bytes 245768 | tf_op jit(solution)/shard_map/ppermute | solution.py:450
  53.5 0.7 collective-permute-start.17
  54.2 3.1 %collective-permute-done.12 = f32[80,256]{1,0:T(8,128)S(1)} collective-permute-done((f32[80,256]{1,0:T(8,128)S(1)}, f32[80,256]{1,0:T(8,128)S(1)}, u32[]{:S(2)}, u32[]{:S(2)}) %collective-permute-start.12) | collective-permute-done | bytes 81952 | tf_op jit(solution)/shard_map/ppermute | solution.py:450
  57.3 0.1 collective-permute-start.13
  57.4 0.1 collective-permute-start.16
  57.5 1.5 %collective-permute-start.15 = (f32[2,2,2,8,768]{4,3,0,1,2:T(8,128)S(1)}, f32[2,2,2,8,768]{4,3,0,1,2:T(8,128)S(1)}, u32[]{:S(2)}, u32[]{:S(2)}) collective-permute-start(f32[2,2,2,8,768]{4,3,0,1,2:T(8,128)S(1)} %slice_bitcast_fusion.6), channel_id=1, source_target_pairs={{0,32},{1,33},{2,34},{3,35},{4,100},{5,101},{6,102},{7,103},{8,40}... | collective-permute-start | bytes 589832 | tf_op jit(solution)/shard_map/ppermute | solution.py:450
  59.0 2.8 %collective-permute-done.13 = f32[80,256]{1,0:T(8,128)S(1)} collective-permute-done((f32[80,256]{1,0:T(8,128)S(1)}, f32[80,256]{1,0:T(8,128)S(1)}, u32[]{:S(2)}, u32[]{:S(2)}) %collective-permute-start.13) | collective-permute-done | bytes 81952 | tf_op jit(solution)/shard_map/ppermute | solution.py:450
  61.9 1.3 %collective-permute-done.16 = f32[2,2,2,8,768]{4,3,0,1,2:T(8,128)S(1)} collective-permute-done((f32[2,2,2,8,768]{4,3,0,1,2:T(8,128)S(1)}, f32[2,2,2,8,768]{4,3,0,1,2:T(8,128)S(1)}, u32[]{:S(2)}, u32[]{:S(2)}) %collective-permute-start.16) | collective-permute-done | bytes 196640 | tf_op jit(solution)/shard_map/ppermute | solution.py:450
  63.4 2.4 %collective-permute-start.18 = (f32[2,2,3,8,768]{4,3,2,0,1:T(8,128)S(1)}, f32[2,2,3,8,768]{4,3,2,0,1:T(8,128)S(1)}, u32[]{:S(2)}, u32[]{:S(2)}) collective-permute-start(f32[2,2,3,8,768]{4,3,2,0,1:T(8,128)S(1)} %slice_bitcast_fusion.3), channel_id=1, source_target_pairs={{0,3},{1,2},{2,1},{3,0},{4,5},{5,4},{6,7},{7,6},{8,11},{9,10},{10,... | collective-permute-start | bytes 884744 | tf_op jit(solution)/shard_map/ppermute | solution.py:450
  65.8 0.8 collective-permute-start.14
  66.6 3.7 %collective-permute-done.14 = f32[80,256]{1,0:T(8,128)S(1)} collective-permute-done((f32[80,256]{1,0:T(8,128)S(1)}, f32[80,256]{1,0:T(8,128)S(1)}, u32[]{:S(2)}, u32[]{:S(2)}) %collective-permute-start.14) | collective-permute-done | bytes 81952 | tf_op jit(solution)/shard_map/ppermute | solution.py:450
  70.2 1.2 %collective-permute-done.18 = f32[2,2,3,8,768]{4,3,2,0,1:T(8,128)S(1)} collective-permute-done((f32[2,2,3,8,768]{4,3,2,0,1:T(8,128)S(1)}, f32[2,2,3,8,768]{4,3,2,0,1:T(8,128)S(1)}, u32[]{:S(2)}, u32[]{:S(2)}) %collective-permute-start.18) | collective-permute-done | bytes 294944 | tf_op jit(solution)/shard_map/ppermute | solution.py:450
  71.4 4.0 %collective-permute-start.21 = (f32[2,3,8,768]{3,2,1,0:T(8,128)S(1)}, f32[2,3,8,768]{3,2,1,0:T(8,128)S(1)}, u32[]{:S(2)}, u32[]{:S(2)}) collective-permute-start(f32[2,3,8,768]{3,2,1,0:T(8,128)S(1)} %slice_bitcast_fusion.7), channel_id=1, source_target_pairs={{0,8},{1,9},{2,10},{3,11},{4,28},{5,29},{6,30},{7,31},{8,0},{9,1},... | collective-permute-start | bytes 442376 | tf_op jit(solution)/shard_map/ppermute | solution.py:450
  75.4 2.8 %collective-permute-start.19 = (f32[80,256]{1,0:T(8,128)S(1)}, f32[80,256]{1,0:T(8,128)S(1)}, u32[]{:S(2)}, u32[]{:S(2)}) collective-permute-start(f32[80,256]{1,0:T(8,128)S(1)} %add.80), channel_id=1, source_target_pairs={{0,96},{1,97},{2,98},{3,99},{4,36},{5,37},{6,38},{7,39},{8,104},{9... | collective-permute-start | bytes 245768 | tf_op jit(solution)/shard_map/ppermute | solution.py:450
  78.3 2.8 %collective-permute-done.19 = f32[80,256]{1,0:T(8,128)S(1)} collective-permute-done((f32[80,256]{1,0:T(8,128)S(1)}, f32[80,256]{1,0:T(8,128)S(1)}, u32[]{:S(2)}, u32[]{:S(2)}) %collective-permute-start.19) | collective-permute-done | bytes 81952 | tf_op jit(solution)/shard_map/ppermute | solution.py:450
  81.3 2.9 %collective-permute-start.22 = (f32[3,8,768]{2,1,0:T(8,128)S(1)}, f32[3,8,768]{2,1,0:T(8,128)S(1)}, u32[]{:S(2)}, u32[]{:S(2)}) collective-permute-start(f32[3,8,768]{2,1,0:T(8,128)S(1)} %slice_bitcast_fusion.8), channel_id=1, source_target_pairs={{0,96},{1,97},{2,98},{3,99},{4,36},{5,37},{6,38},{7,39},{8,104},{9... | collective-permute-start | bytes 221192 | tf_op jit(solution)/shard_map/ppermute | solution.py:450
  84.2 4.9 %final_part.1 = (bf16[6,14,14,1024]{3,2,1,0:T(8,128)(2,1)}, f32[3,8,768]{2,1,0:T(8,128)S(1)}) custom-call(bf16[1344,1024]{1,0:T(8,128)(2,1)S(1)} %get-tuple-element.56.dev, bf16[1344,1024]{1,0:T(8,128)(2,1)S(1)} %bitcast.81, f32[80,256]{1,0:T(8,128)S(1)} %add.85.mine, f32[80,256]{1,0:T(8,128)S(1)} %collective-permute-done.20.theirs, ...), custom_call_target="tpu_custom_call" | custom-call | tf_op jit(solution)/shard_map/final_part/pallas_call | solution.py:419
  89.1 0.6 fusion.6
  (46 shorter events, 1.0 us)
Async XLA Ops:
  9.0 7.0 %collective-permute-start.5 = (f32[512,768]{1,0:T(8,128)S(1)}, f32[512,768]{1,0:T(8,128)S(1)}, u32[]{:S(2)}, u32[]{:S(2)}) collective-permute-start(f32[512,768]{1,0:T(8,128)S(1)} %get-tuple-element.60), channel_id=1, source_target_pairs={{0,4},{1,5},{2,6},{3,7},{4,0},{5,1},{6,2},{7,3},{8,12},{9,13},{10,... | collective-permute-start | bytes 4718600 | tf_op jit(solution)/shard_map/ppermute | solution.py:450
  12.2 6.3 %collective-permute-start = (f32[512,768]{1,0:T(8,128)S(1)}, f32[512,768]{1,0:T(8,128)S(1)}, u32[]{:S(2)}, u32[]{:S(2)}) collective-permute-start(f32[512,768]{1,0:T(8,128)S(1)} %get-tuple-element.44), channel_id=1, source_target_pairs={{0,4},{1,5},{2,6},{3,7},{4,0},{5,1},{6,2},{7,3},{8,12},{9,13},{10,... | collective-permute-start | bytes 4718600 | tf_op jit(solution)/shard_map/ppermute | solution.py:450
  15.9 4.7 %collective-permute-start.1 = (f32[512,768]{1,0:T(8,128)S(1)}, f32[512,768]{1,0:T(8,128)S(1)}, u32[]{:S(2)}, u32[]{:S(2)}) collective-permute-start(f32[512,768]{1,0:T(8,128)S(1)} %get-tuple-element.46), channel_id=1, source_target_pairs={{0,4},{1,5},{2,6},{3,7},{4,0},{5,1},{6,2},{7,3},{8,12},{9,13},{10,... | collective-permute-start | bytes 4718600 | tf_op jit(solution)/shard_map/ppermute | solution.py:450
  16.4 19.4 %collective-permute-start.6 = (f32[2,2,2,2,2,8,768]{6,5,0,2,4,1,3:T(8,128)S(1)}, f32[2,2,2,2,2,8,768]{6,5,0,2,4,1,3:T(8,128)S(1)}, u32[]{:S(2)}, u32[]{:S(2)}) collective-permute-start(f32[2,2,2,2,2,8,768]{6,5,0,2,4,1,3:T(8,128)S(1)} %copy.11), channel_id=1, source_target_pairs={{0,32},{1,33},{2,34},{3,35},{4,100},{5,101},{6,102},{7,103},{8,40}... | collective-permute-start | bytes 2359304 | tf_op jit(solution)/shard_map/ppermute | solution.py:450
  18.9 17.0 %collective-permute-start.3 = (f32[2,2,2,2,2,8,768]{6,5,1,3,4,0,2:T(8,128)S(1)}, f32[2,2,2,2,2,8,768]{6,5,1,3,4,0,2:T(8,128)S(1)}, u32[]{:S(2)}, u32[]{:S(2)}) collective-permute-start(f32[2,2,2,2,2,8,768]{6,5,1,3,4,0,2:T(8,128)S(1)} %bitcast.89), channel_id=1, source_target_pairs={{0,1},{1,0},{2,3},{3,2},{4,7},{5,6},{6,5},{7,4},{8,9},{9,8},{10,11... | collective-permute-start | bytes 2359304 | tf_op jit(solution)/shard_map/ppermute | solution.py:450
  21.0 3.2 %copy-start = (f32[16,64,64]{2,1,0:T(8,128)S(1)}, f32[16,64,64]{2,1,0:T(8,128)}, u32[]{:S(2)}) copy-start(f32[16,64,64]{2,1,0:T(8,128)} %vectors.1) | copy-start | bytes 786436
  21.0 3.2 %copy-start.1 = (f32[16,64]{1,0:T(8,128)S(1)}, f32[16,64]{1,0:T(8,128)}, u32[]{:S(2)}) copy-start(f32[16,64]{1,0:T(8,128)} %values.1) | copy-start | bytes 12292
  21.1 14.9 %collective-permute-start.4 = (f32[2,2,2,2,2,8,768]{6,5,1,2,4,3,0:T(8,128)S(1)}, f32[2,2,2,2,2,8,768]{6,5,1,2,4,3,0:T(8,128)S(1)}, u32[]{:S(2)}, u32[]{:S(2)}) collective-permute-start(f32[2,2,2,2,2,8,768]{6,5,1,2,4,3,0:T(8,128)S(1)} %bitcast.90), channel_id=1, source_target_pairs={{0,24},{1,25},{2,26},{3,27},{4,12},{5,13},{6,14},{7,15},{8,16},{9,... | collective-permute-start | bytes 2359304 | tf_op jit(solution)/shard_map/ppermute | solution.py:450
  33.2 2.6 %collective-permute-start.2 = (f32[80,256]{1,0:T(8,128)S(1)}, f32[80,256]{1,0:T(8,128)S(1)}, u32[]{:S(2)}, u32[]{:S(2)}) collective-permute-start(f32[80,256]{1,0:T(8,128)S(1)} %get-tuple-element.58), channel_id=1, source_target_pairs={{0,4},{1,5},{2,6},{3,7},{4,0},{5,1},{6,2},{7,3},{8,12},{9,13},{10,... | collective-permute-start | bytes 245768 | tf_op jit(solution)/shard_map/ppermute | solution.py:450
  36.1 4.5 %collective-permute-start.7 = (f32[80,256]{1,0:T(8,128)S(1)}, f32[80,256]{1,0:T(8,128)S(1)}, u32[]{:S(2)}, u32[]{:S(2)}) collective-permute-start(f32[80,256]{1,0:T(8,128)S(1)} %add.68), channel_id=1, source_target_pairs={{0,1},{1,0},{2,3},{3,2},{4,7},{5,6},{6,5},{7,4},{8,9},{9,8},{10,11... | collective-permute-start | bytes 245768 | tf_op jit(solution)/shard_map/ppermute | solution.py:450
  36.5 9.9 %collective-permute-start.11 = (f32[2,2,2,2,8,768]{5,4,0,2,3,1:T(8,128)S(1)}, f32[2,2,2,2,8,768]{5,4,0,2,3,1:T(8,128)S(1)}, u32[]{:S(2)}, u32[]{:S(2)}) collective-permute-start(f32[2,2,2,2,8,768]{5,4,0,2,3,1:T(8,128)S(1)} %slice_bitcast_fusion), channel_id=1, source_target_pairs={{0,1},{1,0},{2,3},{3,2},{4,7},{5,6},{6,5},{7,4},{8,9},{9,8},{10,11... | collective-permute-start | bytes 1179656 | tf_op jit(solution)/shard_map/ppermute | solution.py:450
  38.4 8.1 %collective-permute-start.10 = (f32[2,2,2,2,8,768]{5,4,0,1,3,2:T(8,128)S(1)}, f32[2,2,2,2,8,768]{5,4,0,1,3,2:T(8,128)S(1)}, u32[]{:S(2)}, u32[]{:S(2)}) collective-permute-start(f32[2,2,2,2,8,768]{5,4,0,1,3,2:T(8,128)S(1)} %slice_bitcast_fusion.1), channel_id=1, source_target_pairs={{0,32},{1,33},{2,34},{3,35},{4,100},{5,101},{6,102},{7,103},{8,40}... | collective-permute-start | bytes 1179656 | tf_op jit(solution)/shard_map/ppermute | solution.py:450
  40.7 5.7 %collective-permute-start.8 = (f32[80,256]{1,0:T(8,128)S(1)}, f32[80,256]{1,0:T(8,128)S(1)}, u32[]{:S(2)}, u32[]{:S(2)}) collective-permute-start(f32[80,256]{1,0:T(8,128)S(1)} %add.73), channel_id=1, source_target_pairs={{0,3},{1,2},{2,1},{3,0},{4,5},{5,4},{6,7},{7,6},{8,11},{9,10},{10,... | collective-permute-start | bytes 245768 | tf_op jit(solution)/shard_map/ppermute | solution.py:450
  41.7 9.1 %collective-permute-start.9 = (f32[2,2,2,2,8,768]{5,4,1,2,3,0:T(8,128)S(1)}, f32[2,2,2,2,8,768]{5,4,1,2,3,0:T(8,128)S(1)}, u32[]{:S(2)}, u32[]{:S(2)}) collective-permute-start(f32[2,2,2,2,8,768]{5,4,1,2,3,0:T(8,128)S(1)} %slice_bitcast_fusion.2), channel_id=1, source_target_pairs={{0,24},{1,25},{2,26},{3,27},{4,12},{5,13},{6,14},{7,15},{8,16},{9,... | collective-permute-start | bytes 1179656 | tf_op jit(solution)/shard_map/ppermute | solution.py:450
  50.8 6.5 %collective-permute-start.12 = (f32[80,256]{1,0:T(8,128)S(1)}, f32[80,256]{1,0:T(8,128)S(1)}, u32[]{:S(2)}, u32[]{:S(2)}) collective-permute-start(f32[80,256]{1,0:T(8,128)S(1)} %add.74), channel_id=1, source_target_pairs={{0,24},{1,25},{2,26},{3,27},{4,12},{5,13},{6,14},{7,15},{8,16},{9,... | collective-permute-start | bytes 245768 | tf_op jit(solution)/shard_map/ppermute | solution.py:450
  53.5 8.4 %collective-permute-start.17 = (f32[2,2,2,8,768]{4,3,0,1,2:T(8,128)S(1)}, f32[2,2,2,8,768]{4,3,0,1,2:T(8,128)S(1)}, u32[]{:S(2)}, u32[]{:S(2)}) collective-permute-start(f32[2,2,2,8,768]{4,3,0,1,2:T(8,128)S(1)} %slice_bitcast_fusion.4), channel_id=1, source_target_pairs={{0,24},{1,25},{2,26},{3,27},{4,12},{5,13},{6,14},{7,15},{8,16},{9,... | collective-permute-start | bytes 589832 | tf_op jit(solution)/shard_map/ppermute | solution.py:450
  57.3 4.5 %collective-permute-start.13 = (f32[80,256]{1,0:T(8,128)S(1)}, f32[80,256]{1,0:T(8,128)S(1)}, u32[]{:S(2)}, u32[]{:S(2)}) collective-permute-start(f32[80,256]{1,0:T(8,128)S(1)} %add.78), channel_id=1, source_target_pairs={{0,8},{1,9},{2,10},{3,11},{4,28},{5,29},{6,30},{7,31},{8,0},{9,1},... | collective-permute-start | bytes 245768 | tf_op jit(solution)/shard_map/ppermute | solution.py:450
  57.4 5.7 %collective-permute-start.16 = (f32[2,2,2,8,768]{4,3,0,1,2:T(8,128)S(1)}, f32[2,2,2,8,768]{4,3,0,1,2:T(8,128)S(1)}, u32[]{:S(2)}, u32[]{:S(2)}) collective-permute-start(f32[2,2,2,8,768]{4,3,0,1,2:T(8,128)S(1)} %slice_bitcast_fusion.5), channel_id=1, source_target_pairs={{0,1},{1,0},{2,3},{3,2},{4,7},{5,6},{6,5},{7,4},{8,9},{9,8},{10,11... | collective-permute-start | bytes 589832 | tf_op jit(solution)/shard_map/ppermute | solution.py:450
  57.5 5.8 %collective-permute-start.15 = (f32[2,2,2,8,768]{4,3,0,1,2:T(8,128)S(1)}, f32[2,2,2,8,768]{4,3,0,1,2:T(8,128)S(1)}, u32[]{:S(2)}, u32[]{:S(2)}) collective-permute-start(f32[2,2,2,8,768]{4,3,0,1,2:T(8,128)S(1)} %slice_bitcast_fusion.6), channel_id=1, source_target_pairs={{0,32},{1,33},{2,34},{3,35},{4,100},{5,101},{6,102},{7,103},{8,40}... | collective-permute-start | bytes 589832 | tf_op jit(solution)/shard_map/ppermute | solution.py:450
  63.4 8.0 %collective-permute-start.18 = (f32[2,2,3,8,768]{4,3,2,0,1:T(8,128)S(1)}, f32[2,2,3,8,768]{4,3,2,0,1:T(8,128)S(1)}, u32[]{:S(2)}, u32[]{:S(2)}) collective-permute-start(f32[2,2,3,8,768]{4,3,2,0,1:T(8,128)S(1)} %slice_bitcast_fusion.3), channel_id=1, source_target_pairs={{0,3},{1,2},{2,1},{3,0},{4,5},{5,4},{6,7},{7,6},{8,11},{9,10},{10,... | collective-permute-start | bytes 884744 | tf_op jit(solution)/shard_map/ppermute | solution.py:450
  65.8 4.4 %collective-permute-start.14 = (f32[80,256]{1,0:T(8,128)S(1)}, f32[80,256]{1,0:T(8,128)S(1)}, u32[]{:S(2)}, u32[]{:S(2)}) collective-permute-start(f32[80,256]{1,0:T(8,128)S(1)} %add.79), channel_id=1, source_target_pairs={{0,32},{1,33},{2,34},{3,35},{4,100},{5,101},{6,102},{7,103},{8,40}... | collective-permute-start | bytes 245768 | tf_op jit(solution)/shard_map/ppermute | solution.py:450
  71.4 9.8 %collective-permute-start.21 = (f32[2,3,8,768]{3,2,1,0:T(8,128)S(1)}, f32[2,3,8,768]{3,2,1,0:T(8,128)S(1)}, u32[]{:S(2)}, u32[]{:S(2)}) collective-permute-start(f32[2,3,8,768]{3,2,1,0:T(8,128)S(1)} %slice_bitcast_fusion.7), channel_id=1, source_target_pairs={{0,8},{1,9},{2,10},{3,11},{4,28},{5,29},{6,30},{7,31},{8,0},{9,1},... | collective-permute-start | bytes 442376 | tf_op jit(solution)/shard_map/ppermute | solution.py:450
  75.4 5.7 %collective-permute-start.19 = (f32[80,256]{1,0:T(8,128)S(1)}, f32[80,256]{1,0:T(8,128)S(1)}, u32[]{:S(2)}, u32[]{:S(2)}) collective-permute-start(f32[80,256]{1,0:T(8,128)S(1)} %add.80), channel_id=1, source_target_pairs={{0,96},{1,97},{2,98},{3,99},{4,36},{5,37},{6,38},{7,39},{8,104},{9... | collective-permute-start | bytes 245768 | tf_op jit(solution)/shard_map/ppermute | solution.py:450
  81.1 3.1 %collective-permute-start.20 = (f32[80,256]{1,0:T(8,128)S(1)}, f32[80,256]{1,0:T(8,128)S(1)}, u32[]{:S(2)}, u32[]{:S(2)}) collective-permute-start(f32[80,256]{1,0:T(8,128)S(1)} %add.85.mine), channel_id=1, source_target_pairs={{0,4},{1,5},{2,6},{3,7},{4,0},{5,1},{6,2},{7,3},{8,12},{9,13},{10,... | collective-permute-start | bytes 245768 | tf_op jit(solution)/shard_map/ppermute | solution.py:450
  81.3 7.8 %collective-permute-start.22 = (f32[3,8,768]{2,1,0:T(8,128)S(1)}, f32[3,8,768]{2,1,0:T(8,128)S(1)}, u32[]{:S(2)}, u32[]{:S(2)}) collective-permute-start(f32[3,8,768]{2,1,0:T(8,128)S(1)} %slice_bitcast_fusion.8), channel_id=1, source_target_pairs={{0,96},{1,97},{2,98},{3,99},{4,36},{5,37},{6,38},{7,39},{8,104},{9... | collective-permute-start | bytes 221192 | tf_op jit(solution)/shard_map/ppermute | solution.py:450

commit v9 on v8

--- a/solution.py
+++ b/solution.py
@@ -13,7 +13,7 @@
 SIZE = {"z": 4, "y": 4, "c": 2, "x": 4}
 STRIDE = {"z": 32, "y": 8, "c": 4, "x": 1}
 ORDERS = ((0, 3, 1, 2), (0, 1, 3, 2))
-FLIP = {"z": 0, "y": 1, "x": 0}
+FLIP = {"z": 0, "y": 0, "x": 0}
 RING = [{axis: ORDERS[(c + FLIP[axis]) % 2] for axis in "zyx"} for c in range(2)]
 F32 = jnp.float32
 BF16 = jnp.bfloat16
@@ -496,7 +496,7 @@
             keep, send = halves(parts[a], dim)
             parts[a] = keep + exchange(send, ring(axis, 0))
 
-    moves = [ring(axis, step) for axis in "xyz" for step in range(2)]
+    moves = [ring(axis, step) for step in (1, 0) for axis in "xyz"]
 
     def after(value, *others):
         return lax.optimization_barrier((value, *others))[0]

time: 89.9 us -> 89.8 us (level); the launches traced: 89.8 us -> 88.7 us
  starting transfers between devices: 33.3 us -> 19.1 us
  waiting for transfers between devices: 24.3 us -> 37.3 us
    ppermute x23, starting transfers between devices: 33.3 us -> 19.1 us  [exchange(): return lax.ppermute(value, ALL, permutation(move))]
    ppermute x23, waiting for transfers between devices: 24.3 us -> 37.3 us  [exchange(): return lax.ppermute(value, ALL, permutation(move))]
  transfers between devices with their start and end apart: 23 -> 23, of which waited for: 11 -> 12; matrix products, arithmetic and copies ran while one was open for 2% -> 2% of each run, Pallas kernels for 22% -> 23%
where the time goes in v9:
time: 89.8 us; the launch traced here: 88.7 us
  waiting for transfers between devices  37.3 us (42%)
  Pallas kernels  28.5 us (32%)
  starting transfers between devices  19.1 us (21%)
  other arithmetic  1.93 us (2%)
  between operations  1.01 us (1%)
    ppermute x23, waiting for transfers between devices, exchange(): return lax.ppermute(value, ALL, permutation(move))  37.3 us
    ppermute x23, starting transfers between devices, exchange(): return lax.ppermute(value, ALL, permutation(move))  19.1 us
    pallas_call x3, Pallas kernels, weight_part(): pl.pallas_call(functools.partial(weight_kernel, a), in_specs=[ON_CHIP] *...  9.37 us
    pallas_call x1, Pallas kernels, back_part(): pl.pallas_call(back_kernel, in_specs=[ON_CHIP] * 11, out_specs=(ON_CHIP,)...  8.98 us
    pallas_call x1, Pallas kernels, prep(): pl.pallas_call(prep_kernel, out_shape=(jax.ShapeDtypeStruct((IMAGES * H,...  5.23 us
    pallas_call x1, Pallas kernels, final_part(): pl.pallas_call(final_kernel, in_specs=[ON_CHIP] * 8, out_specs=(IN_HBM, O...  4.92 us
  transfers between devices with their start and end apart: 23, of which 12 were waited for; matrix products, arithmetic and copies ran while one was open for 2% of the time, Pallas kernels for 23%

profile of v9, /device:TPU:0, one launch (start us, length us, event | category | flops | bytes accessed | tf_op | source)
XLA Modules:
  0.0 88.7 jit_solution(17867123871237739255)
XLA Ops:
  0.6 5.2 %prep.1 = (bf16[84,16,2304]{2,1,0:T(8,128)(2,1)S(1)}, bf16[84,16,1024]{2,1,0:T(8,128)(2,1)S(1)}, bf16[1040,1344]{1,0:T(8,128)(2,1)S(1)}, f32[1024,128]{1,0:T(8,1...) custom-call(bf16[6,14,14,1024]{3,2,1,0:T(8,128)(2,1)} %features_hbm.1, ...), custom_call_target="tpu_custom_call" | custom-call | tf_op jit(solution)/shard_map/prep/pallas_call | solution.py:184
  5.9 3.1 %weight_part_2.1 = (f32[512,768]{1,0:T(8,128)S(1)}, f32[512,768]{1,0:T(8,128)S(1)}, f32[8,768]{1,0:T(8,128)S(1)}, bf16[768,1024]{1,0:T(8,128)(2,1)S(1)}) custom-call(bf16[1040,1344]{1,0:T(8,128)(2,1)S(1)} %get-tuple-element.41.wht, bf16[1344,2304]{1,0:T(8,128)(2,1)S(1)} %bitcast.76, f32[1024,128]{1,0:T(8,128)S(1)} %get-tuple-element.42.u, ...), custom_call_target="tpu_custom_call" | custom-call | tf_op jit(solution)/shard_map/weight_part_2/pallas_call | solution.py:227
  9.0 0.1 collective-permute-start.5
  9.1 3.1 %weight_part_0.1 = (f32[512,768]{1,0:T(8,128)S(1)}, f32[512,768]{1,0:T(8,128)S(1)}, f32[8,768]{1,0:T(8,128)S(1)}, bf16[768,1024]{1,0:T(8,128)(2,1)S(1)}) custom-call(bf16[1040,1344]{1,0:T(8,128)(2,1)S(1)} %get-tuple-element.41.wht, bf16[1344,2304]{1,0:T(8,128)(2,1)S(1)} %bitcast.77, f32[1024,128]{1,0:T(8,128)S(1)} %get-tuple-element.42.u, ...), custom_call_target="tpu_custom_call" | custom-call | tf_op jit(solution)/shard_map/weight_part_0/pallas_call | solution.py:227
  12.2 0.6 collective-permute-start
  12.8 3.1 %weight_part_1.1 = (f32[512,768]{1,0:T(8,128)S(1)}, f32[512,768]{1,0:T(8,128)S(1)}, f32[8,768]{1,0:T(8,128)S(1)}, bf16[768,1024]{1,0:T(8,128)(2,1)S(1)}) custom-call(bf16[1040,1344]{1,0:T(8,128)(2,1)S(1)} %get-tuple-element.41.wht, bf16[1344,2304]{1,0:T(8,128)(2,1)S(1)} %bitcast.78, f32[1024,128]{1,0:T(8,128)S(1)} %get-tuple-element.42.u, ...), custom_call_target="tpu_custom_call" | custom-call | tf_op jit(solution)/shard_map/weight_part_1/pallas_call | solution.py:227
  15.9 0.1 collective-permute-start.1
  16.0 0.2 add.71
  16.2 0.1 fusion.7
  16.4 2.1 %collective-permute-start.6 = (f32[2,2,2,2,2,8,768]{6,5,0,2,4,1,3:T(8,128)S(1)}, f32[2,2,2,2,2,8,768]{6,5,0,2,4,1,3:T(8,128)S(1)}, u32[]{:S(2)}, u32[]{:S(2)}) collective-permute-start(f32[2,2,2,2,2,8,768]{6,5,0,2,4,1,3:T(8,128)S(1)} %copy.11), channel_id=1, source_target_pairs={{0,32},{1,33},{2,34},{3,35},{4,100},{5,101},{6,102},{7,103},{8,40}... | collective-permute-start | bytes 2359304 | tf_op jit(solution)/shard_map/ppermute | solution.py:450
  18.5 0.2 add.66
  18.7 0.1 fusion.9
  18.9 1.7 %collective-permute-start.3 = (f32[2,2,2,2,2,8,768]{6,5,1,3,4,0,2:T(8,128)S(1)}, f32[2,2,2,2,2,8,768]{6,5,1,3,4,0,2:T(8,128)S(1)}, u32[]{:S(2)}, u32[]{:S(2)}) collective-permute-start(f32[2,2,2,2,2,8,768]{6,5,1,3,4,0,2:T(8,128)S(1)} %bitcast.89), channel_id=1, source_target_pairs={{0,1},{1,0},{2,3},{3,2},{4,7},{5,6},{6,5},{7,4},{8,9},{9,8},{10,11... | collective-permute-start | bytes 2359304 | tf_op jit(solution)/shard_map/ppermute | solution.py:450
  20.7 0.2 add.67
  20.9 0.1 fusion.8
  21.1 1.6 %collective-permute-start.4 = (f32[2,2,2,2,2,8,768]{6,5,1,2,4,3,0:T(8,128)S(1)}, f32[2,2,2,2,2,8,768]{6,5,1,2,4,3,0:T(8,128)S(1)}, u32[]{:S(2)}, u32[]{:S(2)}) collective-permute-start(f32[2,2,2,2,2,8,768]{6,5,1,2,4,3,0:T(8,128)S(1)} %bitcast.90), channel_id=1, source_target_pairs={{0,8},{1,9},{2,10},{3,11},{4,28},{5,29},{6,30},{7,31},{8,0},{9,1},... | collective-permute-start | bytes 2359304 | tf_op jit(solution)/shard_map/ppermute | solution.py:450
  22.8 9.0 %back_part.1 = (bf16[1344,1024]{1,0:T(8,128)(2,1)S(1)}, f32[8,1024]{1,0:T(8,128)S(1)}, f32[80,256]{1,0:T(8,128)S(1)}, f32[80,256]{1,0:T(8,128)S(1)}, bf16[4,4,25...) custom-call(bf16[1344,2304]{1,0:T(8,128)(2,1)S(1)} %bitcast.79, bf16[768,1024]{1,0:T(8,128)(2,1)S(1)} %get-tuple-element.48.slab0, ...), custom_call_target="tpu_custom_call" | custom-call | tf_op jit(solution)/shard_map/back_part/pallas_call | solution.py:315
  31.8 4.5 %collective-permute-start.2 = (f32[80,256]{1,0:T(8,128)S(1)}, f32[80,256]{1,0:T(8,128)S(1)}, u32[]{:S(2)}, u32[]{:S(2)}) collective-permute-start(f32[80,256]{1,0:T(8,128)S(1)} %get-tuple-element.58), channel_id=1, source_target_pairs={{0,4},{1,5},{2,6},{3,7},{4,0},{5,1},{6,2},{7,3},{8,12},{9,13},{10,... | collective-permute-start | bytes 245768 | tf_op jit(solution)/shard_map/ppermute | solution.py:450
  36.3 0.9 %collective-permute-done.2 = f32[80,256]{1,0:T(8,128)S(1)} collective-permute-done((f32[80,256]{1,0:T(8,128)S(1)}, f32[80,256]{1,0:T(8,128)S(1)}, u32[]{:S(2)}, u32[]{:S(2)}) %collective-permute-start.2) | collective-permute-done | bytes 81952 | tf_op jit(solution)/shard_map/ppermute | solution.py:450
  37.2 0.1 copy_add_fusion
  37.3 0.1 fusion.1
  37.5 0.1 fusion
  37.6 0.6 collective-permute-start.7
  38.2 0.4 collective-permute-start.11
  38.6 0.1 collective-permute-start.10
  38.7 5.5 %collective-permute-done.7 = f32[80,256]{1,0:T(8,128)S(1)} collective-permute-done((f32[80,256]{1,0:T(8,128)S(1)}, f32[80,256]{1,0:T(8,128)S(1)}, u32[]{:S(2)}, u32[]{:S(2)}) %collective-permute-start.7) | collective-permute-done | bytes 81952 | tf_op jit(solution)/shard_map/ppermute | solution.py:450
  44.1 1.2 %collective-permute-start.8 = (f32[80,256]{1,0:T(8,128)S(1)}, f32[80,256]{1,0:T(8,128)S(1)}, u32[]{:S(2)}, u32[]{:S(2)}) collective-permute-start(f32[80,256]{1,0:T(8,128)S(1)} %add.73), channel_id=1, source_target_pairs={{0,24},{1,25},{2,26},{3,27},{4,12},{5,13},{6,14},{7,15},{8,16},{9,... | collective-permute-start | bytes 245768 | tf_op jit(solution)/shard_map/ppermute | solution.py:450
  45.4 0.2 collective-permute-start.9
  45.6 4.8 %collective-permute-done.8 = f32[80,256]{1,0:T(8,128)S(1)} collective-permute-done((f32[80,256]{1,0:T(8,128)S(1)}, f32[80,256]{1,0:T(8,128)S(1)}, u32[]{:S(2)}, u32[]{:S(2)}) %collective-permute-start.8) | collective-permute-done | bytes 81952 | tf_op jit(solution)/shard_map/ppermute | solution.py:450
  50.6 2.7 %collective-permute-done.9 = f32[2,2,2,2,8,768]{5,4,1,2,3,0:T(8,128)S(1)} collective-permute-done((f32[2,2,2,2,8,768]{5,4,1,2,3,0:T(8,128)S(1)}, f32[2,2,2,2,8,768]{5,4,1,2,3,0:T(8,128)S(1)}, u32[]{:S(2)}, u32[]{:S(2)}) %collective-permute-start.9) | collective-permute-done | bytes 393248 | tf_op jit(solution)/shard_map/ppermute | solution.py:450
  53.3 0.1 collective-permute-start.12
  53.4 0.4 collective-permute-start.17
  53.8 5.2 %collective-permute-done.12 = f32[80,256]{1,0:T(8,128)S(1)} collective-permute-done((f32[80,256]{1,0:T(8,128)S(1)}, f32[80,256]{1,0:T(8,128)S(1)}, u32[]{:S(2)}, u32[]{:S(2)}) %collective-permute-start.12) | collective-permute-done | bytes 81952 | tf_op jit(solution)/shard_map/ppermute | solution.py:450
  59.2 2.1 %collective-permute-start.16 = (f32[2,2,2,8,768]{4,3,0,1,2:T(8,128)S(1)}, f32[2,2,2,8,768]{4,3,0,1,2:T(8,128)S(1)}, u32[]{:S(2)}, u32[]{:S(2)}) collective-permute-start(f32[2,2,2,8,768]{4,3,0,1,2:T(8,128)S(1)} %slice_bitcast_fusion.5), channel_id=1, source_target_pairs={{0,1},{1,0},{2,3},{3,2},{4,7},{5,6},{6,5},{7,4},{8,9},{9,8},{10,11... | collective-permute-start | bytes 589832 | tf_op jit(solution)/shard_map/ppermute | solution.py:450
  61.3 2.3 %collective-permute-done.13 = f32[80,256]{1,0:T(8,128)S(1)} collective-permute-done((f32[80,256]{1,0:T(8,128)S(1)}, f32[80,256]{1,0:T(8,128)S(1)}, u32[]{:S(2)}, u32[]{:S(2)}) %collective-permute-start.13) | collective-permute-done | bytes 81952 | tf_op jit(solution)/shard_map/ppermute | solution.py:450
  63.6 2.7 %collective-permute-done.16 = f32[2,2,2,8,768]{4,3,0,1,2:T(8,128)S(1)} collective-permute-done((f32[2,2,2,8,768]{4,3,0,1,2:T(8,128)S(1)}, f32[2,2,2,8,768]{4,3,0,1,2:T(8,128)S(1)}, u32[]{:S(2)}, u32[]{:S(2)}) %collective-permute-start.16) | collective-permute-done | bytes 196640 | tf_op jit(solution)/shard_map/ppermute | solution.py:450
  66.3 0.6 collective-permute-done.15
  67.0 0.1 collective-permute-start.18
  67.1 0.5 collective-permute-start.14
  67.7 4.7 %collective-permute-done.14 = f32[80,256]{1,0:T(8,128)S(1)} collective-permute-done((f32[80,256]{1,0:T(8,128)S(1)}, f32[80,256]{1,0:T(8,128)S(1)}, u32[]{:S(2)}, u32[]{:S(2)}) %collective-permute-start.14) | collective-permute-done | bytes 81952 | tf_op jit(solution)/shard_map/ppermute | solution.py:450
  72.4 2.6 %collective-permute-done.18 = f32[2,2,3,8,768]{4,3,2,0,1:T(8,128)S(1)} collective-permute-done((f32[2,2,3,8,768]{4,3,2,0,1:T(8,128)S(1)}, f32[2,2,3,8,768]{4,3,2,0,1:T(8,128)S(1)}, u32[]{:S(2)}, u32[]{:S(2)}) %collective-permute-start.18) | collective-permute-done | bytes 294944 | tf_op jit(solution)/shard_map/ppermute | solution.py:450
  75.1 2.2 %collective-permute-start.21 = (f32[2,3,8,768]{3,2,1,0:T(8,128)S(1)}, f32[2,3,8,768]{3,2,1,0:T(8,128)S(1)}, u32[]{:S(2)}, u32[]{:S(2)}) collective-permute-start(f32[2,3,8,768]{3,2,1,0:T(8,128)S(1)} %slice_bitcast_fusion.7), channel_id=1, source_target_pairs={{0,24},{1,25},{2,26},{3,27},{4,12},{5,13},{6,14},{7,15},{8,16},{9,... | collective-permute-start | bytes 442376 | tf_op jit(solution)/shard_map/ppermute | solution.py:450
  77.3 4.4 %collective-permute-done.19 = f32[80,256]{1,0:T(8,128)S(1)} collective-permute-done((f32[80,256]{1,0:T(8,128)S(1)}, f32[80,256]{1,0:T(8,128)S(1)}, u32[]{:S(2)}, u32[]{:S(2)}) %collective-permute-start.19) | collective-permute-done | bytes 81952 | tf_op jit(solution)/shard_map/ppermute | solution.py:450
  81.7 0.1 collective-permute-start.20
  81.9 0.4 collective-permute-start.22
  82.3 0.8 collective-permute-done.20.theirs
  83.1 4.9 %final_part.1 = (bf16[6,14,14,1024]{3,2,1,0:T(8,128)(2,1)}, f32[3,8,768]{2,1,0:T(8,128)S(1)}) custom-call(bf16[1344,1024]{1,0:T(8,128)(2,1)S(1)} %get-tuple-element.56.dev, bf16[1344,1024]{1,0:T(8,128)(2,1)S(1)} %bitcast.81, f32[80,256]{1,0:T(8,128)S(1)} %add.85.mine, f32[80,256]{1,0:T(8,128)S(1)} %collective-permute-done.20.theirs, ...), custom_call_target="tpu_custom_call" | custom-call | tf_op jit(solution)/shard_map/final_part/pallas_call | solution.py:419
  88.0 0.6 fusion.6
  (46 shorter events, 0.9 us)
Async XLA Ops:
  9.0 7.0 %collective-permute-start.5 = (f32[512,768]{1,0:T(8,128)S(1)}, f32[512,768]{1,0:T(8,128)S(1)}, u32[]{:S(2)}, u32[]{:S(2)}) collective-permute-start(f32[512,768]{1,0:T(8,128)S(1)} %get-tuple-element.60), channel_id=1, source_target_pairs={{0,4},{1,5},{2,6},{3,7},{4,0},{5,1},{6,2},{7,3},{8,12},{9,13},{10,... | collective-permute-start | bytes 4718600 | tf_op jit(solution)/shard_map/ppermute | solution.py:450
  12.2 6.3 %collective-permute-start = (f32[512,768]{1,0:T(8,128)S(1)}, f32[512,768]{1,0:T(8,128)S(1)}, u32[]{:S(2)}, u32[]{:S(2)}) collective-permute-start(f32[512,768]{1,0:T(8,128)S(1)} %get-tuple-element.44), channel_id=1, source_target_pairs={{0,4},{1,5},{2,6},{3,7},{4,0},{5,1},{6,2},{7,3},{8,12},{9,13},{10,... | collective-permute-start | bytes 4718600 | tf_op jit(solution)/shard_map/ppermute | solution.py:450
  15.9 4.7 %collective-permute-start.1 = (f32[512,768]{1,0:T(8,128)S(1)}, f32[512,768]{1,0:T(8,128)S(1)}, u32[]{:S(2)}, u32[]{:S(2)}) collective-permute-start(f32[512,768]{1,0:T(8,128)S(1)} %get-tuple-element.46), channel_id=1, source_target_pairs={{0,4},{1,5},{2,6},{3,7},{4,0},{5,1},{6,2},{7,3},{8,12},{9,13},{10,... | collective-permute-start | bytes 4718600 | tf_op jit(solution)/shard_map/ppermute | solution.py:450
  16.4 20.8 %collective-permute-start.6 = (f32[2,2,2,2,2,8,768]{6,5,0,2,4,1,3:T(8,128)S(1)}, f32[2,2,2,2,2,8,768]{6,5,0,2,4,1,3:T(8,128)S(1)}, u32[]{:S(2)}, u32[]{:S(2)}) collective-permute-start(f32[2,2,2,2,2,8,768]{6,5,0,2,4,1,3:T(8,128)S(1)} %copy.11), channel_id=1, source_target_pairs={{0,32},{1,33},{2,34},{3,35},{4,100},{5,101},{6,102},{7,103},{8,40}... | collective-permute-start | bytes 2359304 | tf_op jit(solution)/shard_map/ppermute | solution.py:450
  18.9 18.4 %collective-permute-start.3 = (f32[2,2,2,2,2,8,768]{6,5,1,3,4,0,2:T(8,128)S(1)}, f32[2,2,2,2,2,8,768]{6,5,1,3,4,0,2:T(8,128)S(1)}, u32[]{:S(2)}, u32[]{:S(2)}) collective-permute-start(f32[2,2,2,2,2,8,768]{6,5,1,3,4,0,2:T(8,128)S(1)} %bitcast.89), channel_id=1, source_target_pairs={{0,1},{1,0},{2,3},{3,2},{4,7},{5,6},{6,5},{7,4},{8,9},{9,8},{10,11... | collective-permute-start | bytes 2359304 | tf_op jit(solution)/shard_map/ppermute | solution.py:450
  21.0 1.8 %copy-start = (f32[16,64,64]{2,1,0:T(8,128)S(1)}, f32[16,64,64]{2,1,0:T(8,128)}, u32[]{:S(2)}) copy-start(f32[16,64,64]{2,1,0:T(8,128)} %vectors.1) | copy-start | bytes 786436
  21.0 1.8 %copy-start.1 = (f32[16,64]{1,0:T(8,128)S(1)}, f32[16,64]{1,0:T(8,128)}, u32[]{:S(2)}) copy-start(f32[16,64]{1,0:T(8,128)} %values.1) | copy-start | bytes 12292
  21.1 16.4 %collective-permute-start.4 = (f32[2,2,2,2,2,8,768]{6,5,1,2,4,3,0:T(8,128)S(1)}, f32[2,2,2,2,2,8,768]{6,5,1,2,4,3,0:T(8,128)S(1)}, u32[]{:S(2)}, u32[]{:S(2)}) collective-permute-start(f32[2,2,2,2,2,8,768]{6,5,1,2,4,3,0:T(8,128)S(1)} %bitcast.90), channel_id=1, source_target_pairs={{0,8},{1,9},{2,10},{3,11},{4,28},{5,29},{6,30},{7,31},{8,0},{9,1},... | collective-permute-start | bytes 2359304 | tf_op jit(solution)/shard_map/ppermute | solution.py:450
  31.8 5.5 %collective-permute-start.2 = (f32[80,256]{1,0:T(8,128)S(1)}, f32[80,256]{1,0:T(8,128)S(1)}, u32[]{:S(2)}, u32[]{:S(2)}) collective-permute-start(f32[80,256]{1,0:T(8,128)S(1)} %get-tuple-element.58), channel_id=1, source_target_pairs={{0,4},{1,5},{2,6},{3,7},{4,0},{5,1},{6,2},{7,3},{8,12},{9,13},{10,... | collective-permute-start | bytes 245768 | tf_op jit(solution)/shard_map/ppermute | solution.py:450
  37.6 6.5 %collective-permute-start.7 = (f32[80,256]{1,0:T(8,128)S(1)}, f32[80,256]{1,0:T(8,128)S(1)}, u32[]{:S(2)}, u32[]{:S(2)}) collective-permute-start(f32[80,256]{1,0:T(8,128)S(1)} %add.68), channel_id=1, source_target_pairs={{0,3},{1,2},{2,1},{3,0},{4,5},{5,4},{6,7},{7,6},{8,11},{9,10},{10,... | collective-permute-start | bytes 245768 | tf_op jit(solution)/shard_map/ppermute | solution.py:450
  38.2 12.3 %collective-permute-start.11 = (f32[2,2,2,2,8,768]{5,4,0,2,3,1:T(8,128)S(1)}, f32[2,2,2,2,8,768]{5,4,0,2,3,1:T(8,128)S(1)}, u32[]{:S(2)}, u32[]{:S(2)}) collective-permute-start(f32[2,2,2,2,8,768]{5,4,0,2,3,1:T(8,128)S(1)} %slice_bitcast_fusion), channel_id=1, source_target_pairs={{0,1},{1,0},{2,3},{3,2},{4,7},{5,6},{6,5},{7,4},{8,9},{9,8},{10,11... | collective-permute-start | bytes 1179656 | tf_op jit(solution)/shard_map/ppermute | solution.py:450
  38.6 11.9 %collective-permute-start.10 = (f32[2,2,2,2,8,768]{5,4,0,1,3,2:T(8,128)S(1)}, f32[2,2,2,2,8,768]{5,4,0,1,3,2:T(8,128)S(1)}, u32[]{:S(2)}, u32[]{:S(2)}) collective-permute-start(f32[2,2,2,2,8,768]{5,4,0,1,3,2:T(8,128)S(1)} %slice_bitcast_fusion.1), channel_id=1, source_target_pairs={{0,32},{1,33},{2,34},{3,35},{4,100},{5,101},{6,102},{7,103},{8,40}... | collective-permute-start | bytes 1179656 | tf_op jit(solution)/shard_map/ppermute | solution.py:450
  44.1 6.3 %collective-permute-start.8 = (f32[80,256]{1,0:T(8,128)S(1)}, f32[80,256]{1,0:T(8,128)S(1)}, u32[]{:S(2)}, u32[]{:S(2)}) collective-permute-start(f32[80,256]{1,0:T(8,128)S(1)} %add.73), channel_id=1, source_target_pairs={{0,24},{1,25},{2,26},{3,27},{4,12},{5,13},{6,14},{7,15},{8,16},{9,... | collective-permute-start | bytes 245768 | tf_op jit(solution)/shard_map/ppermute | solution.py:450
  45.4 7.9 %collective-permute-start.9 = (f32[2,2,2,2,8,768]{5,4,1,2,3,0:T(8,128)S(1)}, f32[2,2,2,2,8,768]{5,4,1,2,3,0:T(8,128)S(1)}, u32[]{:S(2)}, u32[]{:S(2)}) collective-permute-start(f32[2,2,2,2,8,768]{5,4,1,2,3,0:T(8,128)S(1)} %slice_bitcast_fusion.2), channel_id=1, source_target_pairs={{0,8},{1,9},{2,10},{3,11},{4,28},{5,29},{6,30},{7,31},{8,0},{9,1},... | collective-permute-start | bytes 1179656 | tf_op jit(solution)/shard_map/ppermute | solution.py:450
  53.3 5.7 %collective-permute-start.12 = (f32[80,256]{1,0:T(8,128)S(1)}, f32[80,256]{1,0:T(8,128)S(1)}, u32[]{:S(2)}, u32[]{:S(2)}) collective-permute-start(f32[80,256]{1,0:T(8,128)S(1)} %add.74), channel_id=1, source_target_pairs={{0,96},{1,97},{2,98},{3,99},{4,36},{5,37},{6,38},{7,39},{8,104},{9... | collective-permute-start | bytes 245768 | tf_op jit(solution)/shard_map/ppermute | solution.py:450
  53.4 10.1 %collective-permute-start.17 = (f32[2,2,2,8,768]{4,3,0,1,2:T(8,128)S(1)}, f32[2,2,2,8,768]{4,3,0,1,2:T(8,128)S(1)}, u32[]{:S(2)}, u32[]{:S(2)}) collective-permute-start(f32[2,2,2,8,768]{4,3,0,1,2:T(8,128)S(1)} %slice_bitcast_fusion.4), channel_id=1, source_target_pairs={{0,8},{1,9},{2,10},{3,11},{4,28},{5,29},{6,30},{7,31},{8,0},{9,1},... | collective-permute-start | bytes 589832 | tf_op jit(solution)/shard_map/ppermute | solution.py:450
  59.0 4.5 %collective-permute-start.13 = (f32[80,256]{1,0:T(8,128)S(1)}, f32[80,256]{1,0:T(8,128)S(1)}, u32[]{:S(2)}, u32[]{:S(2)}) collective-permute-start(f32[80,256]{1,0:T(8,128)S(1)} %add.78), channel_id=1, source_target_pairs={{0,1},{1,0},{2,3},{3,2},{4,7},{5,6},{6,5},{7,4},{8,9},{9,8},{10,11... | collective-permute-start | bytes 245768 | tf_op jit(solution)/shard_map/ppermute | solution.py:450
  59.2 7.2 %collective-permute-start.16 = (f32[2,2,2,8,768]{4,3,0,1,2:T(8,128)S(1)}, f32[2,2,2,8,768]{4,3,0,1,2:T(8,128)S(1)}, u32[]{:S(2)}, u32[]{:S(2)}) collective-permute-start(f32[2,2,2,8,768]{4,3,0,1,2:T(8,128)S(1)} %slice_bitcast_fusion.5), channel_id=1, source_target_pairs={{0,1},{1,0},{2,3},{3,2},{4,7},{5,6},{6,5},{7,4},{8,9},{9,8},{10,11... | collective-permute-start | bytes 589832 | tf_op jit(solution)/shard_map/ppermute | solution.py:450
  61.2 5.7 %collective-permute-start.15 = (f32[2,2,2,8,768]{4,3,0,1,2:T(8,128)S(1)}, f32[2,2,2,8,768]{4,3,0,1,2:T(8,128)S(1)}, u32[]{:S(2)}, u32[]{:S(2)}) collective-permute-start(f32[2,2,2,8,768]{4,3,0,1,2:T(8,128)S(1)} %slice_bitcast_fusion.6), channel_id=1, source_target_pairs={{0,32},{1,33},{2,34},{3,35},{4,100},{5,101},{6,102},{7,103},{8,40}... | collective-permute-start | bytes 589832 | tf_op jit(solution)/shard_map/ppermute | solution.py:450
  67.0 8.0 %collective-permute-start.18 = (f32[2,2,3,8,768]{4,3,2,0,1:T(8,128)S(1)}, f32[2,2,3,8,768]{4,3,2,0,1:T(8,128)S(1)}, u32[]{:S(2)}, u32[]{:S(2)}) collective-permute-start(f32[2,2,3,8,768]{4,3,2,0,1:T(8,128)S(1)} %slice_bitcast_fusion.3), channel_id=1, source_target_pairs={{0,3},{1,2},{2,1},{3,0},{4,5},{5,4},{6,7},{7,6},{8,11},{9,10},{10,... | collective-permute-start | bytes 884744 | tf_op jit(solution)/shard_map/ppermute | solution.py:450
  67.1 5.3 %collective-permute-start.14 = (f32[80,256]{1,0:T(8,128)S(1)}, f32[80,256]{1,0:T(8,128)S(1)}, u32[]{:S(2)}, u32[]{:S(2)}) collective-permute-start(f32[80,256]{1,0:T(8,128)S(1)} %add.79), channel_id=1, source_target_pairs={{0,8},{1,9},{2,10},{3,11},{4,28},{5,29},{6,30},{7,31},{8,0},{9,1},... | collective-permute-start | bytes 245768 | tf_op jit(solution)/shard_map/ppermute | solution.py:450
  75.1 6.7 %collective-permute-start.21 = (f32[2,3,8,768]{3,2,1,0:T(8,128)S(1)}, f32[2,3,8,768]{3,2,1,0:T(8,128)S(1)}, u32[]{:S(2)}, u32[]{:S(2)}) collective-permute-start(f32[2,3,8,768]{3,2,1,0:T(8,128)S(1)} %slice_bitcast_fusion.7), channel_id=1, source_target_pairs={{0,24},{1,25},{2,26},{3,27},{4,12},{5,13},{6,14},{7,15},{8,16},{9,... | collective-permute-start | bytes 442376 | tf_op jit(solution)/shard_map/ppermute | solution.py:450
  77.3 4.4 %collective-permute-start.19 = (f32[80,256]{1,0:T(8,128)S(1)}, f32[80,256]{1,0:T(8,128)S(1)}, u32[]{:S(2)}, u32[]{:S(2)}) collective-permute-start(f32[80,256]{1,0:T(8,128)S(1)} %add.80), channel_id=1, source_target_pairs={{0,32},{1,33},{2,34},{3,35},{4,100},{5,101},{6,102},{7,103},{8,40}... | collective-permute-start | bytes 245768 | tf_op jit(solution)/shard_map/ppermute | solution.py:450
  81.7 1.4 %collective-permute-start.20 = (f32[80,256]{1,0:T(8,128)S(1)}, f32[80,256]{1,0:T(8,128)S(1)}, u32[]{:S(2)}, u32[]{:S(2)}) collective-permute-start(f32[80,256]{1,0:T(8,128)S(1)} %add.85.mine), channel_id=1, source_target_pairs={{0,4},{1,5},{2,6},{3,7},{4,0},{5,1},{6,2},{7,3},{8,12},{9,13},{10,... | collective-permute-start | bytes 245768 | tf_op jit(solution)/shard_map/ppermute | solution.py:450
  81.9 6.1 %collective-permute-start.22 = (f32[3,8,768]{2,1,0:T(8,128)S(1)}, f32[3,8,768]{2,1,0:T(8,128)S(1)}, u32[]{:S(2)}, u32[]{:S(2)}) collective-permute-start(f32[3,8,768]{2,1,0:T(8,128)S(1)} %slice_bitcast_fusion.8), channel_id=1, source_target_pairs={{0,96},{1,97},{2,98},{3,99},{4,36},{5,37},{6,38},{7,39},{8,104},{9... | collective-permute-start | bytes 221192 | tf_op jit(solution)/shard_map/ppermute | solution.py:450

commit v10 on v9

--- a/solution.py
+++ b/solution.py
@@ -496,7 +496,7 @@
             keep, send = halves(parts[a], dim)
             parts[a] = keep + exchange(send, ring(axis, 0))
 
-    moves = [ring(axis, step) for step in (1, 0) for axis in "xyz"]
+    moves = [ring(axis, step) for axis in "xyz" for step in range(2)]
 
     def after(value, *others):
         return lax.optimization_barrier((value, *others))[0]

time: 89.8 us -> 86.6 us (0.964)
  waiting for transfers between devices: 37.3 us -> 27 us
  starting transfers between devices: 19.1 us -> 27 us
    ppermute x23, waiting for transfers between devices: 37.3 us -> 27 us  [exchange(): return lax.ppermute(value, ALL, permutation(move))]
    ppermute x23, starting transfers between devices: 19.1 us -> 27 us  [exchange(): return lax.ppermute(value, ALL, permutation(move))]
  transfers between devices with their start and end apart: 23 -> 23, of which waited for: 12 -> 11; matrix products, arithmetic and copies ran while one was open for 2% -> 2% of each run, Pallas kernels for 23% -> 23%
where the time goes in v10:
time: 86.6 us; the launch traced here: 86.2 us
  Pallas kernels  28.5 us (33%)
  starting transfers between devices  27 us (31%)
  waiting for transfers between devices  27 us (31%)
  other arithmetic  1.93 us (2%)
  between operations  0.98 us (1%)
    ppermute x23, waiting for transfers between devices, exchange(): return lax.ppermute(value, ALL, permutation(move))  27 us
    ppermute x23, starting transfers between devices, exchange(): return lax.ppermute(value, ALL, permutation(move))  27 us
    pallas_call x3, Pallas kernels, weight_part(): pl.pallas_call(functools.partial(weight_kernel, a), in_specs=[ON_CHIP] *...  9.37 us
    pallas_call x1, Pallas kernels, back_part(): pl.pallas_call(back_kernel, in_specs=[ON_CHIP] * 11, out_specs=(ON_CHIP,)...  8.98 us
    pallas_call x1, Pallas kernels, prep(): pl.pallas_call(prep_kernel, out_shape=(jax.ShapeDtypeStruct((IMAGES * H,...  5.23 us
    pallas_call x1, Pallas kernels, final_part(): pl.pallas_call(final_kernel, in_specs=[ON_CHIP] * 8, out_specs=(IN_HBM, O...  4.92 us
  transfers between devices with their start and end apart: 23, of which 11 were waited for; matrix products, arithmetic and copies ran while one was open for 2% of the time, Pallas kernels for 23%

profile of v10, /device:TPU:0, one launch (start us, length us, event | category | flops | bytes accessed | tf_op | source)
XLA Modules:
  0.0 86.2 jit_solution(16161090275001577025)
XLA Ops:
  0.6 5.2 %prep.1 = (bf16[84,16,2304]{2,1,0:T(8,128)(2,1)S(1)}, bf16[84,16,1024]{2,1,0:T(8,128)(2,1)S(1)}, bf16[1040,1344]{1,0:T(8,128)(2,1)S(1)}, f32[1024,128]{1,0:T(8,1...) custom-call(bf16[6,14,14,1024]{3,2,1,0:T(8,128)(2,1)} %features_hbm.1, ...), custom_call_target="tpu_custom_call" | custom-call | tf_op jit(solution)/shard_map/prep/pallas_call | solution.py:184
  5.9 3.1 %weight_part_2.1 = (f32[512,768]{1,0:T(8,128)S(1)}, f32[512,768]{1,0:T(8,128)S(1)}, f32[8,768]{1,0:T(8,128)S(1)}, bf16[768,1024]{1,0:T(8,128)(2,1)S(1)}) custom-call(bf16[1040,1344]{1,0:T(8,128)(2,1)S(1)} %get-tuple-element.41.wht, bf16[1344,2304]{1,0:T(8,128)(2,1)S(1)} %bitcast.76, f32[1024,128]{1,0:T(8,128)S(1)} %get-tuple-element.42.u, ...), custom_call_target="tpu_custom_call" | custom-call | tf_op jit(solution)/shard_map/weight_part_2/pallas_call | solution.py:227
  9.1 3.1 %weight_part_0.1 = (f32[512,768]{1,0:T(8,128)S(1)}, f32[512,768]{1,0:T(8,128)S(1)}, f32[8,768]{1,0:T(8,128)S(1)}, bf16[768,1024]{1,0:T(8,128)(2,1)S(1)}) custom-call(bf16[1040,1344]{1,0:T(8,128)(2,1)S(1)} %get-tuple-element.41.wht, bf16[1344,2304]{1,0:T(8,128)(2,1)S(1)} %bitcast.77, f32[1024,128]{1,0:T(8,128)S(1)} %get-tuple-element.42.u, ...), custom_call_target="tpu_custom_call" | custom-call | tf_op jit(solution)/shard_map/weight_part_0/pallas_call | solution.py:227
  12.2 0.6 collective-permute-start
  12.8 3.1 %weight_part_1.1 = (f32[512,768]{1,0:T(8,128)S(1)}, f32[512,768]{1,0:T(8,128)S(1)}, f32[8,768]{1,0:T(8,128)S(1)}, bf16[768,1024]{1,0:T(8,128)(2,1)S(1)}) custom-call(bf16[1040,1344]{1,0:T(8,128)(2,1)S(1)} %get-tuple-element.41.wht, bf16[1344,2304]{1,0:T(8,128)(2,1)S(1)} %bitcast.78, f32[1024,128]{1,0:T(8,128)S(1)} %get-tuple-element.42.u, ...), custom_call_target="tpu_custom_call" | custom-call | tf_op jit(solution)/shard_map/weight_part_1/pallas_call | solution.py:227
  15.9 0.1 collective-permute-start.1
  16.0 0.2 add.71
  16.2 0.1 fusion.7
  16.4 2.1 %collective-permute-start.6 = (f32[2,2,2,2,2,8,768]{6,5,0,2,4,1,3:T(8,128)S(1)}, f32[2,2,2,2,2,8,768]{6,5,0,2,4,1,3:T(8,128)S(1)}, u32[]{:S(2)}, u32[]{:S(2)}) collective-permute-start(f32[2,2,2,2,2,8,768]{6,5,0,2,4,1,3:T(8,128)S(1)} %copy.11), channel_id=1, source_target_pairs={{0,32},{1,33},{2,34},{3,35},{4,100},{5,101},{6,102},{7,103},{8,40}... | collective-permute-start | bytes 2359304 | tf_op jit(solution)/shard_map/ppermute | solution.py:450
  18.5 0.2 add.66
  18.7 0.1 fusion.9
  18.9 1.7 %collective-permute-start.3 = (f32[2,2,2,2,2,8,768]{6,5,1,3,4,0,2:T(8,128)S(1)}, f32[2,2,2,2,2,8,768]{6,5,1,3,4,0,2:T(8,128)S(1)}, u32[]{:S(2)}, u32[]{:S(2)}) collective-permute-start(f32[2,2,2,2,2,8,768]{6,5,1,3,4,0,2:T(8,128)S(1)} %bitcast.89), channel_id=1, source_target_pairs={{0,1},{1,0},{2,3},{3,2},{4,7},{5,6},{6,5},{7,4},{8,9},{9,8},{10,11... | collective-permute-start | bytes 2359304 | tf_op jit(solution)/shard_map/ppermute | solution.py:450
  20.7 0.2 add.67
  20.9 0.1 fusion.8
  21.1 1.6 %collective-permute-start.4 = (f32[2,2,2,2,2,8,768]{6,5,1,2,4,3,0:T(8,128)S(1)}, f32[2,2,2,2,2,8,768]{6,5,1,2,4,3,0:T(8,128)S(1)}, u32[]{:S(2)}, u32[]{:S(2)}) collective-permute-start(f32[2,2,2,2,2,8,768]{6,5,1,2,4,3,0:T(8,128)S(1)} %bitcast.90), channel_id=1, source_target_pairs={{0,8},{1,9},{2,10},{3,11},{4,28},{5,29},{6,30},{7,31},{8,0},{9,1},... | collective-permute-start | bytes 2359304 | tf_op jit(solution)/shard_map/ppermute | solution.py:450
  22.8 9.0 %back_part.1 = (bf16[1344,1024]{1,0:T(8,128)(2,1)S(1)}, f32[8,1024]{1,0:T(8,128)S(1)}, f32[80,256]{1,0:T(8,128)S(1)}, f32[80,256]{1,0:T(8,128)S(1)}, bf16[4,4,25...) custom-call(bf16[1344,2304]{1,0:T(8,128)(2,1)S(1)} %bitcast.79, bf16[768,1024]{1,0:T(8,128)(2,1)S(1)} %get-tuple-element.48.slab0, ...), custom_call_target="tpu_custom_call" | custom-call | tf_op jit(solution)/shard_map/back_part/pallas_call | solution.py:315
  31.8 4.5 %collective-permute-start.2 = (f32[80,256]{1,0:T(8,128)S(1)}, f32[80,256]{1,0:T(8,128)S(1)}, u32[]{:S(2)}, u32[]{:S(2)}) collective-permute-start(f32[80,256]{1,0:T(8,128)S(1)} %get-tuple-element.58), channel_id=1, source_target_pairs={{0,4},{1,5},{2,6},{3,7},{4,0},{5,1},{6,2},{7,3},{8,12},{9,13},{10,... | collective-permute-start | bytes 245768 | tf_op jit(solution)/shard_map/ppermute | solution.py:450
  36.3 0.9 %collective-permute-done.2 = f32[80,256]{1,0:T(8,128)S(1)} collective-permute-done((f32[80,256]{1,0:T(8,128)S(1)}, f32[80,256]{1,0:T(8,128)S(1)}, u32[]{:S(2)}, u32[]{:S(2)}) %collective-permute-start.2) | collective-permute-done | bytes 81952 | tf_op jit(solution)/shard_map/ppermute | solution.py:450
  37.2 0.1 copy_add_fusion
  37.3 0.1 fusion.1
  37.5 0.1 fusion
  37.6 0.3 collective-permute-start.7
  37.9 1.9 %collective-permute-start.11 = (f32[2,2,2,2,8,768]{5,4,0,2,3,1:T(8,128)S(1)}, f32[2,2,2,2,8,768]{5,4,0,2,3,1:T(8,128)S(1)}, u32[]{:S(2)}, u32[]{:S(2)}) collective-permute-start(f32[2,2,2,2,8,768]{5,4,0,2,3,1:T(8,128)S(1)} %slice_bitcast_fusion), channel_id=1, source_target_pairs={{0,1},{1,0},{2,3},{3,2},{4,7},{5,6},{6,5},{7,4},{8,9},{9,8},{10,11... | collective-permute-start | bytes 1179656 | tf_op jit(solution)/shard_map/ppermute | solution.py:450
  39.8 0.1 collective-permute-start.10
  39.9 2.2 %collective-permute-done.7 = f32[80,256]{1,0:T(8,128)S(1)} collective-permute-done((f32[80,256]{1,0:T(8,128)S(1)}, f32[80,256]{1,0:T(8,128)S(1)}, u32[]{:S(2)}, u32[]{:S(2)}) %collective-permute-start.7) | collective-permute-done | bytes 81952 | tf_op jit(solution)/shard_map/ppermute | solution.py:450
  42.1 0.6 collective-permute-start.8
  42.7 0.2 collective-permute-start.9
  42.9 4.9 %collective-permute-done.8 = f32[80,256]{1,0:T(8,128)S(1)} collective-permute-done((f32[80,256]{1,0:T(8,128)S(1)}, f32[80,256]{1,0:T(8,128)S(1)}, u32[]{:S(2)}, u32[]{:S(2)}) %collective-permute-start.8) | collective-permute-done | bytes 81952 | tf_op jit(solution)/shard_map/ppermute | solution.py:450
  48.0 2.6 %collective-permute-done.9 = f32[2,2,2,2,8,768]{5,4,1,2,3,0:T(8,128)S(1)} collective-permute-done((f32[2,2,2,2,8,768]{5,4,1,2,3,0:T(8,128)S(1)}, f32[2,2,2,2,8,768]{5,4,1,2,3,0:T(8,128)S(1)}, u32[]{:S(2)}, u32[]{:S(2)}) %collective-permute-start.9) | collective-permute-done | bytes 393248 | tf_op jit(solution)/shard_map/ppermute | solution.py:450
  50.6 0.2 collective-permute-start.12
  50.9 2.0 %collective-permute-start.17 = (f32[2,2,2,8,768]{4,3,0,1,2:T(8,128)S(1)}, f32[2,2,2,8,768]{4,3,0,1,2:T(8,128)S(1)}, u32[]{:S(2)}, u32[]{:S(2)}) collective-permute-start(f32[2,2,2,8,768]{4,3,0,1,2:T(8,128)S(1)} %slice_bitcast_fusion.4), channel_id=1, source_target_pairs={{0,8},{1,9},{2,10},{3,11},{4,28},{5,29},{6,30},{7,31},{8,0},{9,1},... | collective-permute-start | bytes 589832 | tf_op jit(solution)/shard_map/ppermute | solution.py:450
  52.8 2.3 %collective-permute-done.12 = f32[80,256]{1,0:T(8,128)S(1)} collective-permute-done((f32[80,256]{1,0:T(8,128)S(1)}, f32[80,256]{1,0:T(8,128)S(1)}, u32[]{:S(2)}, u32[]{:S(2)}) %collective-permute-start.12) | collective-permute-done | bytes 81952 | tf_op jit(solution)/shard_map/ppermute | solution.py:450
  55.2 1.2 %collective-permute-start.13 = (f32[80,256]{1,0:T(8,128)S(1)}, f32[80,256]{1,0:T(8,128)S(1)}, u32[]{:S(2)}, u32[]{:S(2)}) collective-permute-start(f32[80,256]{1,0:T(8,128)S(1)} %add.78), channel_id=1, source_target_pairs={{0,24},{1,25},{2,26},{3,27},{4,12},{5,13},{6,14},{7,15},{8,16},{9,... | collective-permute-start | bytes 245768 | tf_op jit(solution)/shard_map/ppermute | solution.py:450
  56.4 0.4 collective-permute-start.16
  56.8 0.5 collective-permute-start.15
  57.3 3.6 %collective-permute-done.13 = f32[80,256]{1,0:T(8,128)S(1)} collective-permute-done((f32[80,256]{1,0:T(8,128)S(1)}, f32[80,256]{1,0:T(8,128)S(1)}, u32[]{:S(2)}, u32[]{:S(2)}) %collective-permute-start.13) | collective-permute-done | bytes 81952 | tf_op jit(solution)/shard_map/ppermute | solution.py:450
  60.9 1.2 %collective-permute-done.16 = f32[2,2,2,8,768]{4,3,0,1,2:T(8,128)S(1)} collective-permute-done((f32[2,2,2,8,768]{4,3,0,1,2:T(8,128)S(1)}, f32[2,2,2,8,768]{4,3,0,1,2:T(8,128)S(1)}, u32[]{:S(2)}, u32[]{:S(2)}) %collective-permute-start.16) | collective-permute-done | bytes 196640 | tf_op jit(solution)/shard_map/ppermute | solution.py:450
  62.2 0.3 collective-permute-done.15
  62.5 2.7 %collective-permute-start.18 = (f32[2,2,3,8,768]{4,3,2,0,1:T(8,128)S(1)}, f32[2,2,3,8,768]{4,3,2,0,1:T(8,128)S(1)}, u32[]{:S(2)}, u32[]{:S(2)}) collective-permute-start(f32[2,2,3,8,768]{4,3,2,0,1:T(8,128)S(1)} %slice_bitcast_fusion.3), channel_id=1, source_target_pairs={{0,3},{1,2},{2,1},{3,0},{4,5},{5,4},{6,7},{7,6},{8,11},{9,10},{10,... | collective-permute-start | bytes 884744 | tf_op jit(solution)/shard_map/ppermute | solution.py:450
  65.2 4.4 %collective-permute-done.14 = f32[80,256]{1,0:T(8,128)S(1)} collective-permute-done((f32[80,256]{1,0:T(8,128)S(1)}, f32[80,256]{1,0:T(8,128)S(1)}, u32[]{:S(2)}, u32[]{:S(2)}) %collective-permute-start.14) | collective-permute-done | bytes 81952 | tf_op jit(solution)/shard_map/ppermute | solution.py:450
  69.6 0.9 %collective-permute-done.18 = f32[2,2,3,8,768]{4,3,2,0,1:T(8,128)S(1)} collective-permute-done((f32[2,2,3,8,768]{4,3,2,0,1:T(8,128)S(1)}, f32[2,2,3,8,768]{4,3,2,0,1:T(8,128)S(1)}, u32[]{:S(2)}, u32[]{:S(2)}) %collective-permute-start.18) | collective-permute-done | bytes 294944 | tf_op jit(solution)/shard_map/ppermute | solution.py:450
  70.6 2.2 %collective-permute-start.21 = (f32[2,3,8,768]{3,2,1,0:T(8,128)S(1)}, f32[2,3,8,768]{3,2,1,0:T(8,128)S(1)}, u32[]{:S(2)}, u32[]{:S(2)}) collective-permute-start(f32[2,3,8,768]{3,2,1,0:T(8,128)S(1)} %slice_bitcast_fusion.7), channel_id=1, source_target_pairs={{0,24},{1,25},{2,26},{3,27},{4,12},{5,13},{6,14},{7,15},{8,16},{9,... | collective-permute-start | bytes 442376 | tf_op jit(solution)/shard_map/ppermute | solution.py:450
  72.8 1.9 %collective-permute-start.19 = (f32[80,256]{1,0:T(8,128)S(1)}, f32[80,256]{1,0:T(8,128)S(1)}, u32[]{:S(2)}, u32[]{:S(2)}) collective-permute-start(f32[80,256]{1,0:T(8,128)S(1)} %add.80), channel_id=1, source_target_pairs={{0,96},{1,97},{2,98},{3,99},{4,36},{5,37},{6,38},{7,39},{8,104},{9... | collective-permute-start | bytes 245768 | tf_op jit(solution)/shard_map/ppermute | solution.py:450
  74.7 3.7 %collective-permute-done.19 = f32[80,256]{1,0:T(8,128)S(1)} collective-permute-done((f32[80,256]{1,0:T(8,128)S(1)}, f32[80,256]{1,0:T(8,128)S(1)}, u32[]{:S(2)}, u32[]{:S(2)}) %collective-permute-start.19) | collective-permute-done | bytes 81952 | tf_op jit(solution)/shard_map/ppermute | solution.py:450
  78.4 0.1 collective-permute-start.20
  78.6 2.0 %collective-permute-start.22 = (f32[3,8,768]{2,1,0:T(8,128)S(1)}, f32[3,8,768]{2,1,0:T(8,128)S(1)}, u32[]{:S(2)}, u32[]{:S(2)}) collective-permute-start(f32[3,8,768]{2,1,0:T(8,128)S(1)} %slice_bitcast_fusion.8), channel_id=1, source_target_pairs={{0,96},{1,97},{2,98},{3,99},{4,36},{5,37},{6,38},{7,39},{8,104},{9... | collective-permute-start | bytes 221192 | tf_op jit(solution)/shard_map/ppermute | solution.py:450
  80.6 4.9 %final_part.1 = (bf16[6,14,14,1024]{3,2,1,0:T(8,128)(2,1)}, f32[3,8,768]{2,1,0:T(8,128)S(1)}) custom-call(bf16[1344,1024]{1,0:T(8,128)(2,1)S(1)} %get-tuple-element.56.dev, bf16[1344,1024]{1,0:T(8,128)(2,1)S(1)} %bitcast.81, f32[80,256]{1,0:T(8,128)S(1)} %add.85.mine, f32[80,256]{1,0:T(8,128)S(1)} %collective-permute-done.20.theirs, ...), custom_call_target="tpu_custom_call" | custom-call | tf_op jit(solution)/shard_map/final_part/pallas_call | solution.py:419
  85.5 0.6 fusion.6
  (46 shorter events, 0.9 us)
Async XLA Ops:
  9.0 7.0 %collective-permute-start.5 = (f32[512,768]{1,0:T(8,128)S(1)}, f32[512,768]{1,0:T(8,128)S(1)}, u32[]{:S(2)}, u32[]{:S(2)}) collective-permute-start(f32[512,768]{1,0:T(8,128)S(1)} %get-tuple-element.60), channel_id=1, source_target_pairs={{0,4},{1,5},{2,6},{3,7},{4,0},{5,1},{6,2},{7,3},{8,12},{9,13},{10,... | collective-permute-start | bytes 4718600 | tf_op jit(solution)/shard_map/ppermute | solution.py:450
  12.2 6.3 %collective-permute-start = (f32[512,768]{1,0:T(8,128)S(1)}, f32[512,768]{1,0:T(8,128)S(1)}, u32[]{:S(2)}, u32[]{:S(2)}) collective-permute-start(f32[512,768]{1,0:T(8,128)S(1)} %get-tuple-element.44), channel_id=1, source_target_pairs={{0,4},{1,5},{2,6},{3,7},{4,0},{5,1},{6,2},{7,3},{8,12},{9,13},{10,... | collective-permute-start | bytes 4718600 | tf_op jit(solution)/shard_map/ppermute | solution.py:450
  15.9 4.7 %collective-permute-start.1 = (f32[512,768]{1,0:T(8,128)S(1)}, f32[512,768]{1,0:T(8,128)S(1)}, u32[]{:S(2)}, u32[]{:S(2)}) collective-permute-start(f32[512,768]{1,0:T(8,128)S(1)} %get-tuple-element.46), channel_id=1, source_target_pairs={{0,4},{1,5},{2,6},{3,7},{4,0},{5,1},{6,2},{7,3},{8,12},{9,13},{10,... | collective-permute-start | bytes 4718600 | tf_op jit(solution)/shard_map/ppermute | solution.py:450
  16.4 20.8 %collective-permute-start.6 = (f32[2,2,2,2,2,8,768]{6,5,0,2,4,1,3:T(8,128)S(1)}, f32[2,2,2,2,2,8,768]{6,5,0,2,4,1,3:T(8,128)S(1)}, u32[]{:S(2)}, u32[]{:S(2)}) collective-permute-start(f32[2,2,2,2,2,8,768]{6,5,0,2,4,1,3:T(8,128)S(1)} %copy.11), channel_id=1, source_target_pairs={{0,32},{1,33},{2,34},{3,35},{4,100},{5,101},{6,102},{7,103},{8,40}... | collective-permute-start | bytes 2359304 | tf_op jit(solution)/shard_map/ppermute | solution.py:450
  18.9 18.4 %collective-permute-start.3 = (f32[2,2,2,2,2,8,768]{6,5,1,3,4,0,2:T(8,128)S(1)}, f32[2,2,2,2,2,8,768]{6,5,1,3,4,0,2:T(8,128)S(1)}, u32[]{:S(2)}, u32[]{:S(2)}) collective-permute-start(f32[2,2,2,2,2,8,768]{6,5,1,3,4,0,2:T(8,128)S(1)} %bitcast.89), channel_id=1, source_target_pairs={{0,1},{1,0},{2,3},{3,2},{4,7},{5,6},{6,5},{7,4},{8,9},{9,8},{10,11... | collective-permute-start | bytes 2359304 | tf_op jit(solution)/shard_map/ppermute | solution.py:450
  21.0 1.8 %copy-start = (f32[16,64,64]{2,1,0:T(8,128)S(1)}, f32[16,64,64]{2,1,0:T(8,128)}, u32[]{:S(2)}) copy-start(f32[16,64,64]{2,1,0:T(8,128)} %vectors.1) | copy-start | bytes 786436
  21.0 1.8 %copy-start.1 = (f32[16,64]{1,0:T(8,128)S(1)}, f32[16,64]{1,0:T(8,128)}, u32[]{:S(2)}) copy-start(f32[16,64]{1,0:T(8,128)} %values.1) | copy-start | bytes 12292
  21.1 16.4 %collective-permute-start.4 = (f32[2,2,2,2,2,8,768]{6,5,1,2,4,3,0:T(8,128)S(1)}, f32[2,2,2,2,2,8,768]{6,5,1,2,4,3,0:T(8,128)S(1)}, u32[]{:S(2)}, u32[]{:S(2)}) collective-permute-start(f32[2,2,2,2,2,8,768]{6,5,1,2,4,3,0:T(8,128)S(1)} %bitcast.90), channel_id=1, source_target_pairs={{0,8},{1,9},{2,10},{3,11},{4,28},{5,29},{6,30},{7,31},{8,0},{9,1},... | collective-permute-start | bytes 2359304 | tf_op jit(solution)/shard_map/ppermute | solution.py:450
  31.8 5.5 %collective-permute-start.2 = (f32[80,256]{1,0:T(8,128)S(1)}, f32[80,256]{1,0:T(8,128)S(1)}, u32[]{:S(2)}, u32[]{:S(2)}) collective-permute-start(f32[80,256]{1,0:T(8,128)S(1)} %get-tuple-element.58), channel_id=1, source_target_pairs={{0,4},{1,5},{2,6},{3,7},{4,0},{5,1},{6,2},{7,3},{8,12},{9,13},{10,... | collective-permute-start | bytes 245768 | tf_op jit(solution)/shard_map/ppermute | solution.py:450
  37.6 4.5 %collective-permute-start.7 = (f32[80,256]{1,0:T(8,128)S(1)}, f32[80,256]{1,0:T(8,128)S(1)}, u32[]{:S(2)}, u32[]{:S(2)}) collective-permute-start(f32[80,256]{1,0:T(8,128)S(1)} %add.68), channel_id=1, source_target_pairs={{0,1},{1,0},{2,3},{3,2},{4,7},{5,6},{6,5},{7,4},{8,9},{9,8},{10,11... | collective-permute-start | bytes 245768 | tf_op jit(solution)/shard_map/ppermute | solution.py:450
  37.9 9.9 %collective-permute-start.11 = (f32[2,2,2,2,8,768]{5,4,0,2,3,1:T(8,128)S(1)}, f32[2,2,2,2,8,768]{5,4,0,2,3,1:T(8,128)S(1)}, u32[]{:S(2)}, u32[]{:S(2)}) collective-permute-start(f32[2,2,2,2,8,768]{5,4,0,2,3,1:T(8,128)S(1)} %slice_bitcast_fusion), channel_id=1, source_target_pairs={{0,1},{1,0},{2,3},{3,2},{4,7},{5,6},{6,5},{7,4},{8,9},{9,8},{10,11... | collective-permute-start | bytes 1179656 | tf_op jit(solution)/shard_map/ppermute | solution.py:450
  39.8 8.1 %collective-permute-start.10 = (f32[2,2,2,2,8,768]{5,4,0,1,3,2:T(8,128)S(1)}, f32[2,2,2,2,8,768]{5,4,0,1,3,2:T(8,128)S(1)}, u32[]{:S(2)}, u32[]{:S(2)}) collective-permute-start(f32[2,2,2,2,8,768]{5,4,0,1,3,2:T(8,128)S(1)} %slice_bitcast_fusion.1), channel_id=1, source_target_pairs={{0,32},{1,33},{2,34},{3,35},{4,100},{5,101},{6,102},{7,103},{8,40}... | collective-permute-start | bytes 1179656 | tf_op jit(solution)/shard_map/ppermute | solution.py:450
  42.1 5.7 %collective-permute-start.8 = (f32[80,256]{1,0:T(8,128)S(1)}, f32[80,256]{1,0:T(8,128)S(1)}, u32[]{:S(2)}, u32[]{:S(2)}) collective-permute-start(f32[80,256]{1,0:T(8,128)S(1)} %add.73), channel_id=1, source_target_pairs={{0,3},{1,2},{2,1},{3,0},{4,5},{5,4},{6,7},{7,6},{8,11},{9,10},{10,... | collective-permute-start | bytes 245768 | tf_op jit(solution)/shard_map/ppermute | solution.py:450
  42.7 7.9 %collective-permute-start.9 = (f32[2,2,2,2,8,768]{5,4,1,2,3,0:T(8,128)S(1)}, f32[2,2,2,2,8,768]{5,4,1,2,3,0:T(8,128)S(1)}, u32[]{:S(2)}, u32[]{:S(2)}) collective-permute-start(f32[2,2,2,2,8,768]{5,4,1,2,3,0:T(8,128)S(1)} %slice_bitcast_fusion.2), channel_id=1, source_target_pairs={{0,8},{1,9},{2,10},{3,11},{4,28},{5,29},{6,30},{7,31},{8,0},{9,1},... | collective-permute-start | bytes 1179656 | tf_op jit(solution)/shard_map/ppermute | solution.py:450
  50.6 4.5 %collective-permute-start.12 = (f32[80,256]{1,0:T(8,128)S(1)}, f32[80,256]{1,0:T(8,128)S(1)}, u32[]{:S(2)}, u32[]{:S(2)}) collective-permute-start(f32[80,256]{1,0:T(8,128)S(1)} %add.74), channel_id=1, source_target_pairs={{0,8},{1,9},{2,10},{3,11},{4,28},{5,29},{6,30},{7,31},{8,0},{9,1},... | collective-permute-start | bytes 245768 | tf_op jit(solution)/shard_map/ppermute | solution.py:450
  50.9 10.0 %collective-permute-start.17 = (f32[2,2,2,8,768]{4,3,0,1,2:T(8,128)S(1)}, f32[2,2,2,8,768]{4,3,0,1,2:T(8,128)S(1)}, u32[]{:S(2)}, u32[]{:S(2)}) collective-permute-start(f32[2,2,2,8,768]{4,3,0,1,2:T(8,128)S(1)} %slice_bitcast_fusion.4), channel_id=1, source_target_pairs={{0,8},{1,9},{2,10},{3,11},{4,28},{5,29},{6,30},{7,31},{8,0},{9,1},... | collective-permute-start | bytes 589832 | tf_op jit(solution)/shard_map/ppermute | solution.py:450
  55.2 5.7 %collective-permute-start.13 = (f32[80,256]{1,0:T(8,128)S(1)}, f32[80,256]{1,0:T(8,128)S(1)}, u32[]{:S(2)}, u32[]{:S(2)}) collective-permute-start(f32[80,256]{1,0:T(8,128)S(1)} %add.78), channel_id=1, source_target_pairs={{0,24},{1,25},{2,26},{3,27},{4,12},{5,13},{6,14},{7,15},{8,16},{9,... | collective-permute-start | bytes 245768 | tf_op jit(solution)/shard_map/ppermute | solution.py:450
  56.4 5.7 %collective-permute-start.16 = (f32[2,2,2,8,768]{4,3,0,1,2:T(8,128)S(1)}, f32[2,2,2,8,768]{4,3,0,1,2:T(8,128)S(1)}, u32[]{:S(2)}, u32[]{:S(2)}) collective-permute-start(f32[2,2,2,8,768]{4,3,0,1,2:T(8,128)S(1)} %slice_bitcast_fusion.5), channel_id=1, source_target_pairs={{0,1},{1,0},{2,3},{3,2},{4,7},{5,6},{6,5},{7,4},{8,9},{9,8},{10,11... | collective-permute-start | bytes 589832 | tf_op jit(solution)/shard_map/ppermute | solution.py:450
  56.8 5.7 %collective-permute-start.15 = (f32[2,2,2,8,768]{4,3,0,1,2:T(8,128)S(1)}, f32[2,2,2,8,768]{4,3,0,1,2:T(8,128)S(1)}, u32[]{:S(2)}, u32[]{:S(2)}) collective-permute-start(f32[2,2,2,8,768]{4,3,0,1,2:T(8,128)S(1)} %slice_bitcast_fusion.6), channel_id=1, source_target_pairs={{0,32},{1,33},{2,34},{3,35},{4,100},{5,101},{6,102},{7,103},{8,40}... | collective-permute-start | bytes 589832 | tf_op jit(solution)/shard_map/ppermute | solution.py:450
  62.5 8.0 %collective-permute-start.18 = (f32[2,2,3,8,768]{4,3,2,0,1:T(8,128)S(1)}, f32[2,2,3,8,768]{4,3,2,0,1:T(8,128)S(1)}, u32[]{:S(2)}, u32[]{:S(2)}) collective-permute-start(f32[2,2,3,8,768]{4,3,2,0,1:T(8,128)S(1)} %slice_bitcast_fusion.3), channel_id=1, source_target_pairs={{0,3},{1,2},{2,1},{3,0},{4,5},{5,4},{6,7},{7,6},{8,11},{9,10},{10,... | collective-permute-start | bytes 884744 | tf_op jit(solution)/shard_map/ppermute | solution.py:450
  65.2 4.4 %collective-permute-start.14 = (f32[80,256]{1,0:T(8,128)S(1)}, f32[80,256]{1,0:T(8,128)S(1)}, u32[]{:S(2)}, u32[]{:S(2)}) collective-permute-start(f32[80,256]{1,0:T(8,128)S(1)} %add.79), channel_id=1, source_target_pairs={{0,32},{1,33},{2,34},{3,35},{4,100},{5,101},{6,102},{7,103},{8,40}... | collective-permute-start | bytes 245768 | tf_op jit(solution)/shard_map/ppermute | solution.py:450
  70.6 7.9 %collective-permute-start.21 = (f32[2,3,8,768]{3,2,1,0:T(8,128)S(1)}, f32[2,3,8,768]{3,2,1,0:T(8,128)S(1)}, u32[]{:S(2)}, u32[]{:S(2)}) collective-permute-start(f32[2,3,8,768]{3,2,1,0:T(8,128)S(1)} %slice_bitcast_fusion.7), channel_id=1, source_target_pairs={{0,24},{1,25},{2,26},{3,27},{4,12},{5,13},{6,14},{7,15},{8,16},{9,... | collective-permute-start | bytes 442376 | tf_op jit(solution)/shard_map/ppermute | solution.py:450
  72.8 5.7 %collective-permute-start.19 = (f32[80,256]{1,0:T(8,128)S(1)}, f32[80,256]{1,0:T(8,128)S(1)}, u32[]{:S(2)}, u32[]{:S(2)}) collective-permute-start(f32[80,256]{1,0:T(8,128)S(1)} %add.80), channel_id=1, source_target_pairs={{0,96},{1,97},{2,98},{3,99},{4,36},{5,37},{6,38},{7,39},{8,104},{9... | collective-permute-start | bytes 245768 | tf_op jit(solution)/shard_map/ppermute | solution.py:450
  78.4 2.1 %collective-permute-start.20 = (f32[80,256]{1,0:T(8,128)S(1)}, f32[80,256]{1,0:T(8,128)S(1)}, u32[]{:S(2)}, u32[]{:S(2)}) collective-permute-start(f32[80,256]{1,0:T(8,128)S(1)} %add.85.mine), channel_id=1, source_target_pairs={{0,4},{1,5},{2,6},{3,7},{4,0},{5,1},{6,2},{7,3},{8,12},{9,13},{10,... | collective-permute-start | bytes 245768 | tf_op jit(solution)/shard_map/ppermute | solution.py:450
  78.6 6.9 %collective-permute-start.22 = (f32[3,8,768]{2,1,0:T(8,128)S(1)}, f32[3,8,768]{2,1,0:T(8,128)S(1)}, u32[]{:S(2)}, u32[]{:S(2)}) collective-permute-start(f32[3,8,768]{2,1,0:T(8,128)S(1)} %slice_bitcast_fusion.8), channel_id=1, source_target_pairs={{0,96},{1,97},{2,98},{3,99},{4,36},{5,37},{6,38},{7,39},{8,104},{9... | collective-permute-start | bytes 221192 | tf_op jit(solution)/shard_map/ppermute | solution.py:450

commit v11 on v10

--- a/solution.py
+++ b/solution.py
@@ -93,12 +93,15 @@
     grads_hbm,
     vectors_hbm,
     values_hbm,
+    kernel_hbm,
     cols,
     xc,
     wht,
     u,
     sums,
     whiten,
+    kernel,
+    colsum,
     wide,
     wp32,
     features,
@@ -109,6 +112,7 @@
 ):
     moves = [(values_hbm, values), (vectors_hbm, vectors), (grads_hbm, grads)]
     moves += [(features_hbm.at[b], features.at[b]) for b in range(IMAGES)]
+    moves += [(kernel_hbm, kernel)]
     copies = [
         pltpu.make_async_copy(source, target, arrived.at[k])
         for k, (source, target) in enumerate(moves)
@@ -136,12 +140,18 @@
                 wp32[4 * c + z, pl.ds(row, 8), :] = full[channel : channel + 8, :]
     copies[2].wait()
     inside = lax.broadcasted_iota(jnp.int32, (H, 16, O), 1) < W
+    taps = [[jnp.zeros((1, O), F32)] * 3 for _ in range(3)]
     for b in range(IMAGES):
         wide[:, 8 : 8 + W, :] = grads[b].astype(F32)
         for c in range(3):
             shifted = wide[:, 9 - c : 25 - c, :]
             if c == 2:
                 shifted = jnp.where(inside, shifted, 0.0)
+            lines = jnp.sum(shifted, axis=1)
+            every = jnp.sum(lines, axis=0, keepdims=True)
+            taps[0][c] = taps[0][c] + (every - lines[0:1])
+            taps[1][c] = taps[1][c] + every
+            taps[2][c] = taps[2][c] + (every - lines[H - 1 : H])
             shifted = shifted.astype(BF16)
             for a in range(3):
                 lane = (3 * a + c) * O
@@ -152,6 +162,10 @@
                     cols[b * H + H - 1, :, lane : lane + O] = jnp.zeros((16, O), BF16)
                 if a == 2:
                     cols[b * H, :, lane : lane + O] = jnp.zeros((16, O), BF16)
+    colsum[...] = jnp.zeros_like(colsum)
+    for a in range(3):
+        for c in range(3):
+            colsum[a : a + 1, O * c : O * c + O] = taps[a][c]
     total = jnp.zeros((1, D), F32)
     for b in range(IMAGES):
         copies[3 + b].wait()
@@ -178,9 +192,10 @@
         wht[pl.ds(row, 128), :] = part.astype(BF16)
         shift = part[:, 14:15] + part[:, 15:16] + part[:, 30:31]
         u[pl.ds(row, 128), :] = jnp.broadcast_to(shift, (128, 128))
-
-
-def prep(features, grads, vectors, values):
+    copies[3 + IMAGES].wait()
+
+
+def prep(features, grads, vectors, values, kernel):
     return pl.pallas_call(
         prep_kernel,
         out_shape=(
@@ -190,9 +205,11 @@
             jax.ShapeDtypeStruct((1024, 128), F32),
             jax.ShapeDtypeStruct((1, D), F32),
             jax.ShapeDtypeStruct((4, 256, 256), BF16),
+            jax.ShapeDtypeStruct((9 * O, D), BF16),
+            jax.ShapeDtypeStruct((8, 768), F32),
         ),
-        in_specs=[IN_HBM] * 4,
-        out_specs=(ON_CHIP,) * 6,
+        in_specs=[IN_HBM] * 5,
+        out_specs=(ON_CHIP,) * 8,
         scratch_shapes=[
             pltpu.VMEM((H, 32, O), F32),
             pltpu.VMEM((8, 128, 256), F32),
@@ -200,56 +217,45 @@
             pltpu.VMEM((IMAGES, H, W, O), BF16),
             pltpu.VMEM((16, 64, 64), F32),
             pltpu.VMEM((16, 64), F32),
-            pltpu.SemaphoreType.DMA((3 + IMAGES,)),
+            pltpu.SemaphoreType.DMA((4 + IMAGES,)),
         ],
         compiler_params=pltpu.CompilerParams(vmem_limit_bytes=10 << 20),
         name="prep",
-    )(features, grads, vectors, values)
-
-
-def weight_kernel(a, wht, cols, u, kernel_hbm, keep, send, colsum, slab, arrived):
-    copy = pltpu.make_async_copy(kernel_hbm.at[pl.ds(768 * a, 768)], slab, arrived)
-    copy.start()
+    )(features, grads, vectors, values, kernel)
+
+
+def weight_kernel(a, wht, cols, u, keep, send):
     for n in range(3):
         start = 768 * a + 256 * n
         full = nn(wht[...], cols[:, start : start + 256])
-        colsum[:, 256 * n : 256 * n + 256] = full[1024:1032, :]
         for k in range(2):
             ones = full[1024:1025, 128 * k : 128 * k + 128]
             lanes = slice(256 * n + 128 * k, 256 * n + 128 * k + 128)
             part = full[0:1024, 128 * k : 128 * k + 128] + u[...] * ones
             keep[:, lanes] = part[0:512]
             send[:, lanes] = part[512:1024]
-    copy.wait()
-
-
-def weight_part(wht, cols, u, kernel, a):
+
+
+def weight_part(wht, cols, u, a):
     return pl.pallas_call(
         functools.partial(weight_kernel, a),
-        in_specs=[ON_CHIP] * 3 + [IN_HBM],
-        out_specs=(ON_CHIP,) * 4,
+        in_specs=[ON_CHIP] * 3,
+        out_specs=(ON_CHIP,) * 2,
         out_shape=(
             jax.ShapeDtypeStruct((512, 768), F32),
             jax.ShapeDtypeStruct((512, 768), F32),
-            jax.ShapeDtypeStruct((8, 768), F32),
-            jax.ShapeDtypeStruct((768, D), BF16),
         ),
-        scratch_shapes=[pltpu.SemaphoreType.DMA],
         compiler_params=pltpu.CompilerParams(vmem_limit_bytes=6 << 20),
         name=f"weight_part_{a}",
-    )(wht, cols, u, kernel)
+    )(wht, cols, u)
 
 
 def back_kernel(
     cols,
-    slab0,
-    slab1,
-    slab2,
+    kernel,
     xc,
     sums,
-    sum0,
-    sum1,
-    sum2,
+    colsum,
     vectors,
     values,
     dev,
@@ -271,9 +277,7 @@
     upper = None
     for z in range(4):
         lanes = slice(256 * z, 256 * z + 256)
-        back = nn(cols[:, 0:768], slab0[:, lanes])
-        back = back + nn(cols[:, 768:1536], slab1[:, lanes])
-        back = back + nn(cols[:, 1536:2304], slab2[:, lanes])
+        back = nn(cols[...], kernel[:, lanes])
         total = jnp.sum(back, axis=0, keepdims=True)
         low = jnp.where(real, back - total * (1.0 / PIXELS), 0.0).astype(BF16)
         dev[:, lanes] = low
@@ -297,8 +301,8 @@
         tail = jnp.where(row == 0, total, jnp.where(row == 1, sums[:, lanes], 0.0))
         tail = jnp.where(row == 5, diagonal, tail)
         if z < 3:
-            for a, part in enumerate((sum0, sum1, sum2)):
-                tail = jnp.where(row == 2 + a, part[0:1, lanes], tail)
+            for a in range(3):
+                tail = jnp.where(row == 2 + a, colsum[a : a + 1, lanes], tail)
         own[:, lanes] = tail
         blocks[z // 2, 64 + 8 * (z % 2) : 72 + 8 * (z % 2), :] = tail
         basis = block_vectors(vectors, z, same)
@@ -311,10 +315,10 @@
     theirs[...] = blocks[1 - core]
 
 
-def back_part(cols, slabs, xc, sums, colsums, vectors, values):
+def back_part(cols, kernel, xc, sums, colsum, vectors, values):
     return pl.pallas_call(
         back_kernel,
-        in_specs=[ON_CHIP] * 11,
+        in_specs=[ON_CHIP] * 7,
         out_specs=(ON_CHIP,) * 6,
         out_shape=(
             jax.ShapeDtypeStruct((ROWS, D), BF16),
@@ -327,7 +331,7 @@
         scratch_shapes=[pltpu.VMEM((2, 80, 256), F32), pltpu.VMEM((8, 256), F32)],
         compiler_params=pltpu.CompilerParams(vmem_limit_bytes=14 << 20),
         name="back_part",
-    )(cols, *slabs, xc, sums, *colsums, vectors, values)
+    )(cols, kernel, xc, sums, colsum, vectors, values)
 
 
 def final_kernel(
@@ -466,27 +470,34 @@
     return pick(0), pick(1)
 
 
+def after(value, *others):
+    return lax.optimization_barrier((value, *others))[0]
+
+
 def local(features, grads, kernel, vectors, values):
     stay = lambda array: pltpu.with_memory_space_constraint(array, pltpu.HBM)
-    cols, xc, wht, u, sums, whiten = prep(
-        stay(features), stay(grads), stay(vectors), stay(values)
+    cols, xc, wht, u, sums, whiten, kernel, colsum = prep(
+        stay(features),
+        stay(grads),
+        stay(vectors),
+        stay(values),
+        stay(kernel.reshape(9 * O, D)),
     )
     cols, xc = cols.reshape(ROWS, 9 * O), xc.reshape(ROWS, D)
-    kernel = stay(kernel.reshape(9 * O, D))
-
-    parts, colsums, slabs = [], [], []
-    for a in range(3):
-        keep, send, colsum, slab = weight_part(wht, cols, u, kernel, a)
-        colsums.append(colsum)
-        slabs.append(slab)
+    dev, own, mine, theirs, bases, factors = back_part(
+        cols, kernel, xc, sums, colsum, vectors, values
+    )
+
+    moves = [ring(axis, step) for axis in "xyz" for step in range(2)]
+    names = [["z1", "z2", "y1", "y2", "x1", "x2"] for _ in range(3)]
+    parts = []
+
+    def more(k):
+        totals.append(totals[-1] + exchange(totals[-1], moves[k]))
+
+    def weights(a, ahead):
+        keep, send = weight_part(after(wht, ahead), cols, u, a)
         parts.append((keep + exchange(send, other_core)).reshape(2, 2, 2, 2, 2, 2, 8, 768))
-    cols = lax.optimization_barrier((cols, *parts))[0]
-    dev, own, mine, theirs, bases, factors = back_part(
-        cols, slabs, xc, sums, colsums, vectors, values
-    )
-    mine = mine + exchange(theirs, other_core)
-
-    names = [["z1", "z2", "y1", "y2", "x1", "x2"] for _ in range(3)]
 
     def turn(k):
         for a in range(3):
@@ -496,35 +507,32 @@
             keep, send = halves(parts[a], dim)
             parts[a] = keep + exchange(send, ring(axis, 0))
 
-    moves = [ring(axis, step) for axis in "xyz" for step in range(2)]
-
-    def after(value, *others):
-        return lax.optimization_barrier((value, *others))[0]
-
+    totals = [mine + exchange(theirs, other_core)]
+    weights(0, totals[0])
+    more(0)
+    weights(1, totals[1])
+    weights(2, totals[1])
+    more(1)
+    totals[-1] = after(totals[-1], *parts)
+    more(2)
     turn(0)
-    mine, *parts = lax.optimization_barrier((mine, *parts))
-    one = mine + exchange(mine, moves[0])
-    two = one + exchange(one, moves[1])
+    totals[-1], *parts = lax.optimization_barrier((totals[-1], *parts))
+    more(3)
+    more(4)
     turn(1)
-    two, *parts = lax.optimization_barrier((two, *parts))
-    three = two + exchange(two, moves[2])
-    four = three + exchange(three, moves[3])
+    totals[-1], *parts = lax.optimization_barrier((totals[-1], *parts))
+    more(5)
+    mine, theirs = totals[-1], exchange(totals[-1], other_core)
     turn(2)
-    share = after(jnp.stack(parts, axis=3), four)
-    five = four + exchange(four, moves[4])
+    input_grad, fix = final_part(dev, xc, mine, theirs, own, bases, factors, whiten)
+    share = after(jnp.stack(parts, axis=3), fix)
     order = ["z", "y", "x"]
     for axis in "xyz":
-        if axis == "y":
-            share = after(share, five)
-            six = after(five, share)
-            six = six + exchange(six, moves[5])
         dim = order.index(axis)
         order.pop(dim)
         keep, send = halves(share, dim)
         share = keep + exchange(send, ring(axis, 1))
-    mine, theirs = six, exchange(six, other_core)
-
-    input_grad, fix = final_part(dev, xc, mine, theirs, own, bases, factors, whiten)
+
     kernel_grad = (share - fix).transpose(1, 0, 2).reshape(8, 3, 3, O)
     return input_grad, kernel_grad
 

time: 86.6 us -> 101 us (1.17)
  waiting for transfers between devices: 27 us -> 36.8 us
  starting transfers between devices: 27 us -> 31.3 us
    ppermute x23, waiting for transfers between devices: 27 us -> 36.8 us  [exchange(): return lax.ppermute(value, ALL, permutation(move))]
    ppermute x23, starting transfers between devices: 27 us -> 31.3 us  [exchange(): return lax.ppermute(value, ALL, permutation(move))]
  transfers between devices with their start and end apart: 23 -> 23, of which waited for: 11 -> 12; matrix products, arithmetic and copies ran while one was open for 2% -> 2% of each run, Pallas kernels for 23% -> 11%
where the time goes in v11:
time: 101 us
  waiting for transfers between devices  36.8 us (36%)
  starting transfers between devices  31.3 us (31%)
  Pallas kernels  29.3 us (29%)
  other arithmetic  2.07 us (2%)
    ppermute x23, waiting for transfers between devices, exchange(): return lax.ppermute(value, ALL, permutation(move))  36.8 us
    ppermute x23, starting transfers between devices, exchange(): return lax.ppermute(value, ALL, permutation(move))  31.3 us
    pallas_call x3, Pallas kernels, weight_part(): pl.pallas_call(functools.partial(weight_kernel, a), in_specs=[ON_CHIP] *...  9.3 us
    pallas_call x1, Pallas kernels, back_part(): pl.pallas_call(back_kernel, in_specs=[ON_CHIP] * 7, out_specs=(ON_CHIP,)...  9.02 us
    pallas_call x1, Pallas kernels, prep(): pl.pallas_call(prep_kernel, out_shape=(jax.ShapeDtypeStruct((IMAGES * H,...  5.96 us
    pallas_call x1, Pallas kernels, final_part(): pl.pallas_call(final_kernel, in_specs=[ON_CHIP] * 8, out_specs=(IN_HBM, O...  5.06 us
  transfers between devices with their start and end apart: 23, of which 12 were waited for; matrix products, arithmetic and copies ran while one was open for 2% of the time, Pallas kernels for 11%

profile of v11, /device:TPU:0, one launch (start us, length us, event | category | flops | bytes accessed | tf_op | source)
XLA Modules:
  0.0 101.2 jit_solution(1363227355148948499)
XLA Ops:
  0.7 6.0 %prep.1 = (bf16[84,16,2304]{2,1,0:T(8,128)(2,1)S(1)}, bf16[84,16,1024]{2,1,0:T(8,128)(2,1)S(1)}, bf16[1040,1344]{1,0:T(8,128)(2,1)S(1)}, f32[1024,128]{1,0:T(8,1...) custom-call(bf16[6,14,14,1024]{3,2,1,0:T(8,128)(2,1)} %features_hbm., ...), custom_call_target="tpu_custom_call" | custom-call | tf_op jit(solution)/shard_map/prep/pallas_call | solution.py:199
  6.6 9.0 %back_part.1 = (bf16[1344,1024]{1,0:T(8,128)(2,1)S(1)}, f32[8,1024]{1,0:T(8,128)S(1)}, f32[80,256]{1,0:T(8,128)S(1)}, f32[80,256]{1,0:T(8,128)S(1)}, bf16[4,4,25...) custom-call(bf16[1344,2304]{1,0:T(8,128)(2,1)S(1)} %bitcast.78, bf16[2304,1024]{1,0:T(8,128)(2,1)S(1)} %get-tuple-element.37.kernel, ...), custom_call_target="tpu_custom_call" | custom-call | tf_op jit(solution)/shard_map/back_part/pallas_call | solution.py:319
  15.7 0.3 collective-permute-start
  15.9 1.3 %collective-permute-done = f32[80,256]{1,0:T(8,128)S(1)} collective-permute-done((f32[80,256]{1,0:T(8,128)S(1)}, f32[80,256]{1,0:T(8,128)S(1)}, u32[]{:S(2)}, u32[]{:S(2)}) %collective-permute-start) | collective-permute-done | bytes 81952 | tf_op jit(solution)/shard_map/ppermute | solution.py:454
  17.2 3.1 %weight_part_0.1 = (f32[512,768]{1,0:T(8,128)S(1)}, f32[512,768]{1,0:T(8,128)S(1)}) custom-call(bf16[1040,1344]{1,0:T(8,128)(2,1)S(1)} %get-tuple-element.49.wht, bf16[1344,2304]{1,0:T(8,128)(2,1)S(1)} %bitcast.79, f32[1024,128]{1,0:T(8,128)S(1)} %get-tuple-element.46.u), custom_call_target="tpu_custom_call" | custom-call | tf_op jit(solution)/shard_map/weight_part_0/pallas_call | solution.py:240
  20.3 0.2 collective-permute-start.3
  20.6 1.6 %collective-permute-start.1 = (f32[80,256]{1,0:T(8,128)S(1)}, f32[80,256]{1,0:T(8,128)S(1)}, u32[]{:S(2)}, u32[]{:S(2)}) collective-permute-start(f32[80,256]{1,0:T(8,128)S(1)} %add.66), channel_id=1, source_target_pairs={{0,1},{1,0},{2,3},{3,2},{4,7},{5,6},{6,5},{7,4},{8,9},{9,8},{10,11... | collective-permute-start | bytes 245768 | tf_op jit(solution)/shard_map/ppermute | solution.py:454
  22.1 2.9 %collective-permute-done.1 = f32[80,256]{1,0:T(8,128)S(1)} collective-permute-done((f32[80,256]{1,0:T(8,128)S(1)}, f32[80,256]{1,0:T(8,128)S(1)}, u32[]{:S(2)}, u32[]{:S(2)}) %collective-permute-start.1) | collective-permute-done | bytes 81952 | tf_op jit(solution)/shard_map/ppermute | solution.py:454
  25.0 3.1 %weight_part_2.1 = (f32[512,768]{1,0:T(8,128)S(1)}, f32[512,768]{1,0:T(8,128)S(1)}) custom-call(bf16[1040,1344]{1,0:T(8,128)(2,1)S(1)} %get-tuple-element.49.wht, bf16[1344,2304]{1,0:T(8,128)(2,1)S(1)} %bitcast.80, f32[1024,128]{1,0:T(8,128)S(1)} %get-tuple-element.46.u), custom_call_target="tpu_custom_call" | custom-call | tf_op jit(solution)/shard_map/weight_part_2/pallas_call | solution.py:240
  28.1 0.5 collective-permute-start.8
  28.6 3.1 %weight_part_1.1 = (f32[512,768]{1,0:T(8,128)S(1)}, f32[512,768]{1,0:T(8,128)S(1)}) custom-call(bf16[1040,1344]{1,0:T(8,128)(2,1)S(1)} %get-tuple-element.49.wht, bf16[1344,2304]{1,0:T(8,128)(2,1)S(1)} %bitcast.81, f32[1024,128]{1,0:T(8,128)S(1)} %get-tuple-element.46.u), custom_call_target="tpu_custom_call" | custom-call | tf_op jit(solution)/shard_map/weight_part_1/pallas_call | solution.py:240
  31.7 0.2 collective-permute-start.4
  31.9 0.2 add.69
  32.1 0.1 fusion.10
  32.3 1.7 %collective-permute-start.6 = (f32[2,2,2,2,2,8,768]{6,5,1,3,4,0,2:T(8,128)S(1)}, f32[2,2,2,2,2,8,768]{6,5,1,3,4,0,2:T(8,128)S(1)}, u32[]{:S(2)}, u32[]{:S(2)}) collective-permute-start(f32[2,2,2,2,2,8,768]{6,5,1,3,4,0,2:T(8,128)S(1)} %bitcast.89), channel_id=1, source_target_pairs={{0,1},{1,0},{2,3},{3,2},{4,7},{5,6},{6,5},{7,4},{8,9},{9,8},{10,11... | collective-permute-start | bytes 2359304 | tf_op jit(solution)/shard_map/ppermute | solution.py:454
  34.0 0.2 add.74
  34.4 2.0 %collective-permute-start.9 = (f32[2,2,2,2,2,8,768]{6,5,0,2,4,1,3:T(8,128)S(1)}, f32[2,2,2,2,2,8,768]{6,5,0,2,4,1,3:T(8,128)S(1)}, u32[]{:S(2)}, u32[]{:S(2)}) collective-permute-start(f32[2,2,2,2,2,8,768]{6,5,0,2,4,1,3:T(8,128)S(1)} %copy.11), channel_id=1, source_target_pairs={{0,32},{1,33},{2,34},{3,35},{4,100},{5,101},{6,102},{7,103},{8,40}... | collective-permute-start | bytes 2359304 | tf_op jit(solution)/shard_map/ppermute | solution.py:454
  36.4 0.3 add.70
  36.9 1.7 %collective-permute-start.7 = (f32[2,2,2,2,2,8,768]{6,5,1,2,4,3,0:T(8,128)S(1)}, f32[2,2,2,2,2,8,768]{6,5,1,2,4,3,0:T(8,128)S(1)}, u32[]{:S(2)}, u32[]{:S(2)}) collective-permute-start(f32[2,2,2,2,2,8,768]{6,5,1,2,4,3,0:T(8,128)S(1)} %bitcast.90), channel_id=1, source_target_pairs={{0,8},{1,9},{2,10},{3,11},{4,28},{5,29},{6,30},{7,31},{8,0},{9,1},... | collective-permute-start | bytes 2359304 | tf_op jit(solution)/shard_map/ppermute | solution.py:454
  38.5 2.1 %collective-permute-start.2 = (f32[80,256]{1,0:T(8,128)S(1)}, f32[80,256]{1,0:T(8,128)S(1)}, u32[]{:S(2)}, u32[]{:S(2)}) collective-permute-start(f32[80,256]{1,0:T(8,128)S(1)} %add.67), channel_id=1, source_target_pairs={{0,3},{1,2},{2,1},{3,0},{4,5},{5,4},{6,7},{7,6},{8,11},{9,10},{10,... | collective-permute-start | bytes 245768 | tf_op jit(solution)/shard_map/ppermute | solution.py:454
  40.6 4.5 %collective-permute-done.2 = f32[80,256]{1,0:T(8,128)S(1)} collective-permute-done((f32[80,256]{1,0:T(8,128)S(1)}, f32[80,256]{1,0:T(8,128)S(1)}, u32[]{:S(2)}, u32[]{:S(2)}) %collective-permute-start.2) | collective-permute-done | bytes 81952 | tf_op jit(solution)/shard_map/ppermute | solution.py:454
  45.1 0.5 collective-permute-start.5
  45.7 4.2 %collective-permute-done.5 = f32[80,256]{1,0:T(8,128)S(1)} collective-permute-done((f32[80,256]{1,0:T(8,128)S(1)}, f32[80,256]{1,0:T(8,128)S(1)}, u32[]{:S(2)}, u32[]{:S(2)}) %collective-permute-start.5) | collective-permute-done | bytes 81952 | tf_op jit(solution)/shard_map/ppermute | solution.py:454
  50.0 0.1 copy_add_fusion
  50.1 0.1 fusion
  50.3 0.6 collective-permute-start.14
  50.9 3.0 %collective-permute-start.10 = (f32[80,256]{1,0:T(8,128)S(1)}, f32[80,256]{1,0:T(8,128)S(1)}, u32[]{:S(2)}, u32[]{:S(2)}) collective-permute-start(f32[80,256]{1,0:T(8,128)S(1)} %add.71), channel_id=1, source_target_pairs={{0,24},{1,25},{2,26},{3,27},{4,12},{5,13},{6,14},{7,15},{8,16},{9,... | collective-permute-start | bytes 245768 | tf_op jit(solution)/shard_map/ppermute | solution.py:454
  53.9 1.6 %collective-permute-start.13 = (f32[2,2,2,2,8,768]{5,4,0,1,3,2:T(8,128)S(1)}, f32[2,2,2,2,8,768]{5,4,0,1,3,2:T(8,128)S(1)}, u32[]{:S(2)}, u32[]{:S(2)}) collective-permute-start(f32[2,2,2,2,8,768]{5,4,0,1,3,2:T(8,128)S(1)} %slice_bitcast_fusion.1), channel_id=1, source_target_pairs={{0,32},{1,33},{2,34},{3,35},{4,100},{5,101},{6,102},{7,103},{8,40}... | collective-permute-start | bytes 1179656 | tf_op jit(solution)/shard_map/ppermute | solution.py:454
  55.5 1.0 %collective-permute-done.10 = f32[80,256]{1,0:T(8,128)S(1)} collective-permute-done((f32[80,256]{1,0:T(8,128)S(1)}, f32[80,256]{1,0:T(8,128)S(1)}, u32[]{:S(2)}, u32[]{:S(2)}) %collective-permute-start.10) | collective-permute-done | bytes 81952 | tf_op jit(solution)/shard_map/ppermute | solution.py:454
  56.5 1.6 %collective-permute-start.11 = (f32[80,256]{1,0:T(8,128)S(1)}, f32[80,256]{1,0:T(8,128)S(1)}, u32[]{:S(2)}, u32[]{:S(2)}) collective-permute-start(f32[80,256]{1,0:T(8,128)S(1)} %add.76), channel_id=1, source_target_pairs={{0,32},{1,33},{2,34},{3,35},{4,100},{5,101},{6,102},{7,103},{8,40}... | collective-permute-start | bytes 245768 | tf_op jit(solution)/shard_map/ppermute | solution.py:454
  58.2 0.4 collective-permute-start.12
  58.6 4.1 %collective-permute-done.11 = f32[80,256]{1,0:T(8,128)S(1)} collective-permute-done((f32[80,256]{1,0:T(8,128)S(1)}, f32[80,256]{1,0:T(8,128)S(1)}, u32[]{:S(2)}, u32[]{:S(2)}) %collective-permute-start.11) | collective-permute-done | bytes 81952 | tf_op jit(solution)/shard_map/ppermute | solution.py:454
  62.8 3.2 %collective-permute-done.12 = f32[2,2,2,2,8,768]{5,4,1,2,3,0:T(8,128)S(1)} collective-permute-done((f32[2,2,2,2,8,768]{5,4,1,2,3,0:T(8,128)S(1)}, f32[2,2,2,2,8,768]{5,4,1,2,3,0:T(8,128)S(1)}, u32[]{:S(2)}, u32[]{:S(2)}) %collective-permute-start.12) | collective-permute-done | bytes 393248 | tf_op jit(solution)/shard_map/ppermute | solution.py:454
  66.1 0.6 collective-permute-start.17
  66.7 3.6 %collective-permute-start.15 = (f32[80,256]{1,0:T(8,128)S(1)}, f32[80,256]{1,0:T(8,128)S(1)}, u32[]{:S(2)}, u32[]{:S(2)}) collective-permute-start(f32[80,256]{1,0:T(8,128)S(1)} %add.77), channel_id=1, source_target_pairs={{0,96},{1,97},{2,98},{3,99},{4,36},{5,37},{6,38},{7,39},{8,104},{9... | collective-permute-start | bytes 245768 | tf_op jit(solution)/shard_map/ppermute | solution.py:454
  70.3 0.9 collective-permute-start.18
  71.2 2.3 %collective-permute-done.15 = f32[80,256]{1,0:T(8,128)S(1)} collective-permute-done((f32[80,256]{1,0:T(8,128)S(1)}, f32[80,256]{1,0:T(8,128)S(1)}, u32[]{:S(2)}, u32[]{:S(2)}) %collective-permute-start.15) | collective-permute-done | bytes 81952 | tf_op jit(solution)/shard_map/ppermute | solution.py:454
  73.5 0.3 collective-permute-start.16
  73.9 0.5 collective-permute-start.19
  74.4 0.7 collective-permute-done.16.theirs
  75.1 5.1 %final_part.1 = (bf16[6,14,14,1024]{3,2,1,0:T(8,128)(2,1)}, f32[3,8,768]{2,1,0:T(8,128)S(1)}) custom-call(bf16[1344,1024]{1,0:T(8,128)(2,1)S(1)} %get-tuple-element.41.dev, bf16[1344,1024]{1,0:T(8,128)(2,1)S(1)} %bitcast.83, f32[80,256]{1,0:T(8,128)S(1)} %add.81.mine, f32[80,256]{1,0:T(8,128)S(1)} %collective-permute-done.16.theirs, ...), custom_call_target="tpu_custom_call" | custom-call | tf_op jit(solution)/shard_map/final_part/pallas_call | solution.py:423
  80.4 1.8 %collective-permute-start.20 = (f32[2,2,3,8,768]{4,3,2,0,1:T(8,128)S(1)}, f32[2,2,3,8,768]{4,3,2,0,1:T(8,128)S(1)}, u32[]{:S(2)}, u32[]{:S(2)}) collective-permute-start(f32[2,2,3,8,768]{4,3,2,0,1:T(8,128)S(1)} %slice_bitcast_fusion.3), channel_id=1, source_target_pairs={{0,3},{1,2},{2,1},{3,0},{4,5},{5,4},{6,7},{7,6},{8,11},{9,10},{10,... | collective-permute-start | bytes 884744 | tf_op jit(solution)/shard_map/ppermute | solution.py:454
  82.2 6.2 %collective-permute-done.20 = f32[2,2,3,8,768]{4,3,2,0,1:T(8,128)S(1)} collective-permute-done((f32[2,2,3,8,768]{4,3,2,0,1:T(8,128)S(1)}, f32[2,2,3,8,768]{4,3,2,0,1:T(8,128)S(1)}, u32[]{:S(2)}, u32[]{:S(2)}) %collective-permute-start.20) | collective-permute-done | bytes 294944 | tf_op jit(solution)/shard_map/ppermute | solution.py:454
  88.5 3.1 %collective-permute-start.21 = (f32[2,3,8,768]{3,2,1,0:T(8,128)S(1)}, f32[2,3,8,768]{3,2,1,0:T(8,128)S(1)}, u32[]{:S(2)}, u32[]{:S(2)}) collective-permute-start(f32[2,3,8,768]{3,2,1,0:T(8,128)S(1)} %slice_bitcast_fusion.7), channel_id=1, source_target_pairs={{0,24},{1,25},{2,26},{3,27},{4,12},{5,13},{6,14},{7,15},{8,16},{9,... | collective-permute-start | bytes 442376 | tf_op jit(solution)/shard_map/ppermute | solution.py:454
  91.6 3.3 %collective-permute-done.21 = f32[2,3,8,768]{3,2,1,0:T(8,128)S(1)} collective-permute-done((f32[2,3,8,768]{3,2,1,0:T(8,128)S(1)}, f32[2,3,8,768]{3,2,1,0:T(8,128)S(1)}, u32[]{:S(2)}, u32[]{:S(2)}) %collective-permute-start.21) | collective-permute-done | bytes 147488 | tf_op jit(solution)/shard_map/ppermute | solution.py:454
  94.9 2.5 %collective-permute-start.22 = (f32[3,8,768]{2,1,0:T(8,128)S(1)}, f32[3,8,768]{2,1,0:T(8,128)S(1)}, u32[]{:S(2)}, u32[]{:S(2)}) collective-permute-start(f32[3,8,768]{2,1,0:T(8,128)S(1)} %slice_bitcast_fusion.9), channel_id=1, source_target_pairs={{0,96},{1,97},{2,98},{3,99},{4,36},{5,37},{6,38},{7,39},{8,104},{9... | collective-permute-start | bytes 221192 | tf_op jit(solution)/shard_map/ppermute | solution.py:454
  97.4 3.1 %collective-permute-done.22 = f32[3,8,768]{2,1,0:T(8,128)S(1)} collective-permute-done((f32[3,8,768]{2,1,0:T(8,128)S(1)}, f32[3,8,768]{2,1,0:T(8,128)S(1)}, u32[]{:S(2)}, u32[]{:S(2)}) %collective-permute-start.22) | collective-permute-done | bytes 73760 | tf_op jit(solution)/shard_map/ppermute | solution.py:454
  100.6 0.6 fusion.7
  (46 shorter events, 1.1 us)
Async XLA Ops:
  0.6 6.0 %copy-start = (f32[16,64,64]{2,1,0:T(8,128)S(1)}, f32[16,64,64]{2,1,0:T(8,128)}, u32[]{:S(2)}) copy-start(f32[16,64,64]{2,1,0:T(8,128)} %vectors.1) | copy-start | bytes 786436
  0.6 6.0 %copy-start.1 = (f32[16,64]{1,0:T(8,128)S(1)}, f32[16,64]{1,0:T(8,128)}, u32[]{:S(2)}) copy-start(f32[16,64]{1,0:T(8,128)} %values.1) | copy-start | bytes 12292
  15.7 1.5 %collective-permute-start = (f32[80,256]{1,0:T(8,128)S(1)}, f32[80,256]{1,0:T(8,128)S(1)}, u32[]{:S(2)}, u32[]{:S(2)}) collective-permute-start(f32[80,256]{1,0:T(8,128)S(1)} %get-tuple-element.43), channel_id=1, source_target_pairs={{0,4},{1,5},{2,6},{3,7},{4,0},{5,1},{6,2},{7,3},{8,12},{9,13},{10,... | collective-permute-start | bytes 245768 | tf_op jit(solution)/shard_map/ppermute | solution.py:454
  20.3 11.6 %collective-permute-start.3 = (f32[512,768]{1,0:T(8,128)S(1)}, f32[512,768]{1,0:T(8,128)S(1)}, u32[]{:S(2)}, u32[]{:S(2)}) collective-permute-start(f32[512,768]{1,0:T(8,128)S(1)} %get-tuple-element.48), channel_id=1, source_target_pairs={{0,4},{1,5},{2,6},{3,7},{4,0},{5,1},{6,2},{7,3},{8,12},{9,13},{10,... | collective-permute-start | bytes 4718600 | tf_op jit(solution)/shard_map/ppermute | solution.py:454
  20.6 4.4 %collective-permute-start.1 = (f32[80,256]{1,0:T(8,128)S(1)}, f32[80,256]{1,0:T(8,128)S(1)}, u32[]{:S(2)}, u32[]{:S(2)}) collective-permute-start(f32[80,256]{1,0:T(8,128)S(1)} %add.66), channel_id=1, source_target_pairs={{0,1},{1,0},{2,3},{3,2},{4,7},{5,6},{6,5},{7,4},{8,9},{9,8},{10,11... | collective-permute-start | bytes 245768 | tf_op jit(solution)/shard_map/ppermute | solution.py:454
  28.1 5.9 %collective-permute-start.8 = (f32[512,768]{1,0:T(8,128)S(1)}, f32[512,768]{1,0:T(8,128)S(1)}, u32[]{:S(2)}, u32[]{:S(2)}) collective-permute-start(f32[512,768]{1,0:T(8,128)S(1)} %get-tuple-element.54), channel_id=1, source_target_pairs={{0,4},{1,5},{2,6},{3,7},{4,0},{5,1},{6,2},{7,3},{8,12},{9,13},{10,... | collective-permute-start | bytes 4718600 | tf_op jit(solution)/shard_map/ppermute | solution.py:454
  31.7 4.7 %collective-permute-start.4 = (f32[512,768]{1,0:T(8,128)S(1)}, f32[512,768]{1,0:T(8,128)S(1)}, u32[]{:S(2)}, u32[]{:S(2)}) collective-permute-start(f32[512,768]{1,0:T(8,128)S(1)} %get-tuple-element.51), channel_id=1, source_target_pairs={{0,4},{1,5},{2,6},{3,7},{4,0},{5,1},{6,2},{7,3},{8,12},{9,13},{10,... | collective-permute-start | bytes 4718600 | tf_op jit(solution)/shard_map/ppermute | solution.py:454
  32.3 17.5 %collective-permute-start.6 = (f32[2,2,2,2,2,8,768]{6,5,1,3,4,0,2:T(8,128)S(1)}, f32[2,2,2,2,2,8,768]{6,5,1,3,4,0,2:T(8,128)S(1)}, u32[]{:S(2)}, u32[]{:S(2)}) collective-permute-start(f32[2,2,2,2,2,8,768]{6,5,1,3,4,0,2:T(8,128)S(1)} %bitcast.89), channel_id=1, source_target_pairs={{0,1},{1,0},{2,3},{3,2},{4,7},{5,6},{6,5},{7,4},{8,9},{9,8},{10,11... | collective-permute-start | bytes 2359304 | tf_op jit(solution)/shard_map/ppermute | solution.py:454
  34.4 15.6 %collective-permute-start.9 = (f32[2,2,2,2,2,8,768]{6,5,0,2,4,1,3:T(8,128)S(1)}, f32[2,2,2,2,2,8,768]{6,5,0,2,4,1,3:T(8,128)S(1)}, u32[]{:S(2)}, u32[]{:S(2)}) collective-permute-start(f32[2,2,2,2,2,8,768]{6,5,0,2,4,1,3:T(8,128)S(1)} %copy.11), channel_id=1, source_target_pairs={{0,32},{1,33},{2,34},{3,35},{4,100},{5,101},{6,102},{7,103},{8,40}... | collective-permute-start | bytes 2359304 | tf_op jit(solution)/shard_map/ppermute | solution.py:454
  36.9 13.2 %collective-permute-start.7 = (f32[2,2,2,2,2,8,768]{6,5,1,2,4,3,0:T(8,128)S(1)}, f32[2,2,2,2,2,8,768]{6,5,1,2,4,3,0:T(8,128)S(1)}, u32[]{:S(2)}, u32[]{:S(2)}) collective-permute-start(f32[2,2,2,2,2,8,768]{6,5,1,2,4,3,0:T(8,128)S(1)} %bitcast.90), channel_id=1, source_target_pairs={{0,8},{1,9},{2,10},{3,11},{4,28},{5,29},{6,30},{7,31},{8,0},{9,1},... | collective-permute-start | bytes 2359304 | tf_op jit(solution)/shard_map/ppermute | solution.py:454
  38.5 6.6 %collective-permute-start.2 = (f32[80,256]{1,0:T(8,128)S(1)}, f32[80,256]{1,0:T(8,128)S(1)}, u32[]{:S(2)}, u32[]{:S(2)}) collective-permute-start(f32[80,256]{1,0:T(8,128)S(1)} %add.67), channel_id=1, source_target_pairs={{0,3},{1,2},{2,1},{3,0},{4,5},{5,4},{6,7},{7,6},{8,11},{9,10},{10,... | collective-permute-start | bytes 245768 | tf_op jit(solution)/shard_map/ppermute | solution.py:454
  45.1 4.7 %collective-permute-start.5 = (f32[80,256]{1,0:T(8,128)S(1)}, f32[80,256]{1,0:T(8,128)S(1)}, u32[]{:S(2)}, u32[]{:S(2)}) collective-permute-start(f32[80,256]{1,0:T(8,128)S(1)} %add.68), channel_id=1, source_target_pairs={{0,8},{1,9},{2,10},{3,11},{4,28},{5,29},{6,30},{7,31},{8,0},{9,1},... | collective-permute-start | bytes 245768 | tf_op jit(solution)/shard_map/ppermute | solution.py:454
  50.3 12.4 %collective-permute-start.14 = (f32[2,2,2,2,8,768]{5,4,0,2,3,1:T(8,128)S(1)}, f32[2,2,2,2,8,768]{5,4,0,2,3,1:T(8,128)S(1)}, u32[]{:S(2)}, u32[]{:S(2)}) collective-permute-start(f32[2,2,2,2,8,768]{5,4,0,2,3,1:T(8,128)S(1)} %slice_bitcast_fusion), channel_id=1, source_target_pairs={{0,1},{1,0},{2,3},{3,2},{4,7},{5,6},{6,5},{7,4},{8,9},{9,8},{10,11... | collective-permute-start | bytes 1179656 | tf_op jit(solution)/shard_map/ppermute | solution.py:454
  50.9 5.7 %collective-permute-start.10 = (f32[80,256]{1,0:T(8,128)S(1)}, f32[80,256]{1,0:T(8,128)S(1)}, u32[]{:S(2)}, u32[]{:S(2)}) collective-permute-start(f32[80,256]{1,0:T(8,128)S(1)} %add.71), channel_id=1, source_target_pairs={{0,24},{1,25},{2,26},{3,27},{4,12},{5,13},{6,14},{7,15},{8,16},{9,... | collective-permute-start | bytes 245768 | tf_op jit(solution)/shard_map/ppermute | solution.py:454
  53.9 8.8 %collective-permute-start.13 = (f32[2,2,2,2,8,768]{5,4,0,1,3,2:T(8,128)S(1)}, f32[2,2,2,2,8,768]{5,4,0,1,3,2:T(8,128)S(1)}, u32[]{:S(2)}, u32[]{:S(2)}) collective-permute-start(f32[2,2,2,2,8,768]{5,4,0,1,3,2:T(8,128)S(1)} %slice_bitcast_fusion.1), channel_id=1, source_target_pairs={{0,32},{1,33},{2,34},{3,35},{4,100},{5,101},{6,102},{7,103},{8,40}... | collective-permute-start | bytes 1179656 | tf_op jit(solution)/shard_map/ppermute | solution.py:454
  56.5 6.1 %collective-permute-start.11 = (f32[80,256]{1,0:T(8,128)S(1)}, f32[80,256]{1,0:T(8,128)S(1)}, u32[]{:S(2)}, u32[]{:S(2)}) collective-permute-start(f32[80,256]{1,0:T(8,128)S(1)} %add.76), channel_id=1, source_target_pairs={{0,32},{1,33},{2,34},{3,35},{4,100},{5,101},{6,102},{7,103},{8,40}... | collective-permute-start | bytes 245768 | tf_op jit(solution)/shard_map/ppermute | solution.py:454
  58.2 7.9 %collective-permute-start.12 = (f32[2,2,2,2,8,768]{5,4,1,2,3,0:T(8,128)S(1)}, f32[2,2,2,2,8,768]{5,4,1,2,3,0:T(8,128)S(1)}, u32[]{:S(2)}, u32[]{:S(2)}) collective-permute-start(f32[2,2,2,2,8,768]{5,4,1,2,3,0:T(8,128)S(1)} %slice_bitcast_fusion.2), channel_id=1, source_target_pairs={{0,8},{1,9},{2,10},{3,11},{4,28},{5,29},{6,30},{7,31},{8,0},{9,1},... | collective-permute-start | bytes 1179656 | tf_op jit(solution)/shard_map/ppermute | solution.py:454
  66.1 14.1 %collective-permute-start.17 = (f32[2,2,2,8,768]{4,3,0,1,2:T(8,128)S(1)}, f32[2,2,2,8,768]{4,3,0,1,2:T(8,128)S(1)}, u32[]{:S(2)}, u32[]{:S(2)}) collective-permute-start(f32[2,2,2,8,768]{4,3,0,1,2:T(8,128)S(1)} %slice_bitcast_fusion.6), channel_id=1, source_target_pairs={{0,32},{1,33},{2,34},{3,35},{4,100},{5,101},{6,102},{7,103},{8,40}... | collective-permute-start | bytes 589832 | tf_op jit(solution)/shard_map/ppermute | solution.py:454
  66.7 6.8 %collective-permute-start.15 = (f32[80,256]{1,0:T(8,128)S(1)}, f32[80,256]{1,0:T(8,128)S(1)}, u32[]{:S(2)}, u32[]{:S(2)}) collective-permute-start(f32[80,256]{1,0:T(8,128)S(1)} %add.77), channel_id=1, source_target_pairs={{0,96},{1,97},{2,98},{3,99},{4,36},{5,37},{6,38},{7,39},{8,104},{9... | collective-permute-start | bytes 245768 | tf_op jit(solution)/shard_map/ppermute | solution.py:454
  70.3 9.9 %collective-permute-start.18 = (f32[2,2,2,8,768]{4,3,0,1,2:T(8,128)S(1)}, f32[2,2,2,8,768]{4,3,0,1,2:T(8,128)S(1)}, u32[]{:S(2)}, u32[]{:S(2)}) collective-permute-start(f32[2,2,2,8,768]{4,3,0,1,2:T(8,128)S(1)} %slice_bitcast_fusion.5), channel_id=1, source_target_pairs={{0,1},{1,0},{2,3},{3,2},{4,7},{5,6},{6,5},{7,4},{8,9},{9,8},{10,11... | collective-permute-start | bytes 589832 | tf_op jit(solution)/shard_map/ppermute | solution.py:454
  73.5 1.6 %collective-permute-start.16 = (f32[80,256]{1,0:T(8,128)S(1)}, f32[80,256]{1,0:T(8,128)S(1)}, u32[]{:S(2)}, u32[]{:S(2)}) collective-permute-start(f32[80,256]{1,0:T(8,128)S(1)} %add.81.mine), channel_id=1, source_target_pairs={{0,4},{1,5},{2,6},{3,7},{4,0},{5,1},{6,2},{7,3},{8,12},{9,13},{10,... | collective-permute-start | bytes 245768 | tf_op jit(solution)/shard_map/ppermute | solution.py:454
  73.9 6.4 %collective-permute-start.19 = (f32[2,2,2,8,768]{4,3,0,1,2:T(8,128)S(1)}, f32[2,2,2,8,768]{4,3,0,1,2:T(8,128)S(1)}, u32[]{:S(2)}, u32[]{:S(2)}) collective-permute-start(f32[2,2,2,8,768]{4,3,0,1,2:T(8,128)S(1)} %slice_bitcast_fusion.4), channel_id=1, source_target_pairs={{0,8},{1,9},{2,10},{3,11},{4,28},{5,29},{6,30},{7,31},{8,0},{9,1},... | collective-permute-start | bytes 589832 | tf_op jit(solution)/shard_map/ppermute | solution.py:454
  80.4 8.0 %collective-permute-start.20 = (f32[2,2,3,8,768]{4,3,2,0,1:T(8,128)S(1)}, f32[2,2,3,8,768]{4,3,2,0,1:T(8,128)S(1)}, u32[]{:S(2)}, u32[]{:S(2)}) collective-permute-start(f32[2,2,3,8,768]{4,3,2,0,1:T(8,128)S(1)} %slice_bitcast_fusion.3), channel_id=1, source_target_pairs={{0,3},{1,2},{2,1},{3,0},{4,5},{5,4},{6,7},{7,6},{8,11},{9,10},{10,... | collective-permute-start | bytes 884744 | tf_op jit(solution)/shard_map/ppermute | solution.py:454
  88.5 6.4 %collective-permute-start.21 = (f32[2,3,8,768]{3,2,1,0:T(8,128)S(1)}, f32[2,3,8,768]{3,2,1,0:T(8,128)S(1)}, u32[]{:S(2)}, u32[]{:S(2)}) collective-permute-start(f32[2,3,8,768]{3,2,1,0:T(8,128)S(1)} %slice_bitcast_fusion.7), channel_id=1, source_target_pairs={{0,24},{1,25},{2,26},{3,27},{4,12},{5,13},{6,14},{7,15},{8,16},{9,... | collective-permute-start | bytes 442376 | tf_op jit(solution)/shard_map/ppermute | solution.py:454
  94.9 5.6 %collective-permute-start.22 = (f32[3,8,768]{2,1,0:T(8,128)S(1)}, f32[3,8,768]{2,1,0:T(8,128)S(1)}, u32[]{:S(2)}, u32[]{:S(2)}) collective-permute-start(f32[3,8,768]{2,1,0:T(8,128)S(1)} %slice_bitcast_fusion.9), channel_id=1, source_target_pairs={{0,96},{1,97},{2,98},{3,99},{4,36},{5,37},{6,38},{7,39},{8,104},{9... | collective-permute-start | bytes 221192 | tf_op jit(solution)/shard_map/ppermute | solution.py:454
